TPU v7x, 32 devices: a whole 2x2x4 slice. The times are simulated.
32 devices in a mesh: row: 4 (over y, core), col: 8 (over z, x).
Axes of the slice: x: 2, y: 2, z: 4, core: 2. Of those that a mesh axis runs over, the one named last changes fastest.
Arguments:
- object_field: float32 [2, 1024, 2048], P(None, 'row', 'col'), may hold values from -4 to 4
- modes: bfloat16 [4, 12, 2, 256, 256], P('row', None, None, 'col'), may hold values from -5 to 5
- coeffs: float32 [4, 8, 4, 12], P('row', 'col'), may hold values from -1.5 to 1.5
- offsets: int32 [4, 8, 4, 2], P('row', 'col'), may hold values from -128 to 128, as said below
- region: int32 [4, 8, 4], P('row', 'col'), may hold values from 0 to 3, as said below
- counts: int32 [4, 8], P('row', 'col'), may hold values from 1 to 4, as said below
- intensity: bfloat16 [4, 8, 4, 256, 256], P('row', 'col'), may hold values from 0.049804688 to 4
Outputs:
- object_grad: float32 [2, 1024, 2048], P(None, 'row', 'col')
- mode_grad: float32 [4, 12, 2, 256, 256], P('row', None, None, 'col')
Inputs may be any that keep to these rules, and one draw needn't show every extreme that they name: `offsets`: every window reaches at most 128 cells beyond its tile on each side; every tile has a live slot whose window starts at row offset -128 and column offset 256 - 256 / 2. A position's region is its tile's row index or the next one; slot 0 of every tile has its own row's region. Slots 0 to counts - 1 of a tile are live, the rest are ignored; some tile is full and some tile has one live slot.
All inputs are finite; a program needn't handle non-finite values.
Results may differ from a plain program's by a relative error of at most 0.014.
Values may be sent and summed in bfloat16 or wider, within the bound.
No kernel may reach another device: no remote copies, remote signals or barrier semaphores. Data moves between devices by JAX's collectives and lax.ppermute only.
A program may use at most 64 MiB of HBM per device.

v0:
```python
import functools
import math

import jax
import jax.numpy as jnp
import numpy as np
from jax import lax
from jax.experimental import pallas as pl
from jax.experimental.pallas import tpu as pltpu
from jax.sharding import PartitionSpec as P


FLOOR = 0.25
LANES = 128
SUBLANES = 8

VMEM = pl.BlockSpec(memory_space=pltpu.VMEM)
SMEM = pl.BlockSpec(memory_space=pltpu.SMEM)


def shift(value, axis, steps):
    count = lax.axis_size(axis)
    leading, last = (max(0, -steps), min(count, count - steps))
    pairs = [(source, source + steps) for source in range(leading, last)]
    return lax.ppermute(value, axis, pairs)


def dft_tables(length):
    indices = np.arange(length)
    phases = indices[:, None] * indices[None, :] % length
    angles = phases * (2.0 * math.pi / length)
    scaling = 1.0 / math.sqrt(length)
    re = (np.cos(angles) * scaling).astype(np.float32)
    im = (-np.sin(angles) * scaling).astype(np.float32)
    forward = np.block([[re, -im], [im, re]])
    inverse = np.block([[re, im], [-im, re]])
    return jnp.asarray(forward, jnp.bfloat16), jnp.asarray(inverse, jnp.bfloat16)


def partners(axis):
    count = lax.axis_size(axis)
    steps = list(range(count // 2, count)) + list(range(1, count // 2))
    paired = count & (count - 1) == 0

    def goes_to(index, step):
        return index ^ step if paired else (index + step) % count

    def comes_from(index, step):
        return index ^ step if paired else (index - step + count) % count

    return steps, goes_to, comes_from


def call(body, outs, *operands, scratch=(), limit=20):
    arrays = [o[0] if isinstance(o, tuple) else o for o in operands]
    specs = [o[1] if isinstance(o, tuple) else VMEM for o in operands]
    outs = [jax.ShapeDtypeStruct(shape, dtype) for shape, dtype in outs]
    return pl.pallas_call(
        body,
        out_shape=tuple(outs),
        in_specs=specs,
        out_specs=tuple(VMEM for _ in outs),
        scratch_shapes=list(scratch),
        compiler_params=pltpu.CompilerParams(vmem_limit_bytes=limit * 1024 * 1024),
    )(*arrays)


def fetch(arrays, held, sem):
    copies = [pltpu.make_async_copy(a, held.at[at], sem.at[at]) for at, a in enumerate(arrays)]
    for copy in copies:
        copy.start()
    return copies


def held_weights(count, weights):
    return [pltpu.SMEM((count,) + weights.shape, jnp.float32), pltpu.SemaphoreType.DMA((count,))]


def slab_kernel(count, row, *refs):
    own, follower = refs[count : count + 2]
    outs = refs[count + 2 : -3]
    table, held, sem = refs[-3:]
    copies = fetch(refs[:count], held, sem)
    num_modes = own.shape[1]
    table[0] = own[0].astype(jnp.float32)
    table[1] = follower[0].astype(jnp.float32)
    next_row = (row[0] + 1).astype(jnp.float32)
    for copy in copies:
        copy.wait()
    for at, out in enumerate(outs):

        def slot_step(slot, carry, at=at, out=out):
            region = held[at, slot, num_modes]
            which = jnp.where(region == next_row, 1, 0)
            known = jnp.where(jnp.abs(region - next_row + 0.5) < 1.0, 1.0, 0.0)
            scales = [held[at, slot, k] * known for k in range(num_modes)]
            for part in range(2):
                total = scales[0] * table[which, 0, part]
                for k in range(1, num_modes):
                    total += scales[k] * table[which, k, part]
                out[slot, part] = total.astype(jnp.bfloat16)
            return carry

        lax.fori_loop(0, out.shape[0], slot_step, 0)


def slabs(row, weights, own, follower):
    shape = (weights[0].shape[0],) + own.shape[2:]
    return call(
        functools.partial(slab_kernel, len(weights)),
        [(shape, jnp.bfloat16)] * len(weights),
        (row, SMEM),
        *weights,
        own,
        follower,
        scratch=[pltpu.VMEM((2,) + own.shape[1:], jnp.float32)]
        + held_weights(len(weights), weights[0]),
    )


def widen_kernel(tile, left, right, top, bottom):
    half = left.shape[-1]
    rows, cols = tile.shape[1:]
    for out, start in ((top, 0), (bottom, rows - half)):
        out[:, :, :half] = left[:, start : start + half]
        out[:, :, half : half + cols] = tile[:, start : start + half].astype(jnp.bfloat16)
        out[:, :, half + cols :] = right[:, start : start + half]


def corner_of(corners, slot, half, limit):
    row = jnp.clip(corners[slot, 0] + half, 0, limit)
    col = jnp.clip(corners[slot, 1] + half, 0, limit)
    rest_row, rest_col = (row & (SUBLANES - 1), col & (LANES - 1))
    base_row = pl.multiple_of(row - rest_row, SUBLANES)
    base_col = pl.multiple_of(col - rest_col, LANES)
    return base_row, rest_row, base_col, rest_col


def window_kernel(corners, tile, left, right, top, bottom, intensity, out, measured, ext):
    size = out.shape[-1]
    half = left.shape[-1]
    rows, cols = tile.shape[1:]
    for part in range(2):
        ext[part, :half, : cols + 2 * half] = top[part].astype(jnp.float32)
        ext[part, half : half + rows, :half] = left[part].astype(jnp.float32)
        low = tile[part].astype(jnp.bfloat16)
        ext[part, half : half + rows, half : half + cols] = low.astype(jnp.float32)
        ext[part, half : half + rows, half + cols : cols + 2 * half] = right[part].astype(jnp.float32)
        ext[part, half + rows : 2 * half + rows, : cols + 2 * half] = bottom[part].astype(jnp.float32)
    tall = size + SUBLANES
    wide = size + LANES

    def slot_step(slot, carry):
        base_row, rest_row, base_col, rest_col = corner_of(
            corners, slot, half, rows + 2 * half - size
        )
        for part in range(2):
            block = ext[part, pl.ds(base_row, tall), pl.ds(base_col, wide)]
            block = pltpu.roll(block, lax.rem(tall - rest_row, tall), 0)[:size]
            block = pltpu.roll(block, lax.rem(wide - rest_col, wide), 1)[:, :size]
            out[slot, part] = block.astype(jnp.bfloat16)
        measured[slot] = jnp.sqrt(intensity[0, 0, slot].astype(jnp.float32))
        return carry

    lax.fori_loop(0, out.shape[0], slot_step, 0)


def windows_of(corners, tile, left, right, top, bottom, intensity):
    slot_count = corners.shape[0]
    size = intensity.shape[-1]
    half = left.shape[-1]
    extent = (2, tile.shape[1] + 2 * half + SUBLANES, tile.shape[2] + 2 * half + LANES)
    return call(
        window_kernel,
        [((slot_count, 2, size, size), jnp.bfloat16), ((slot_count, size, size), jnp.float32)],
        (corners, SMEM),
        tile,
        left,
        right,
        top,
        bottom,
        intensity,
        scratch=[pltpu.VMEM(extent, jnp.float32)],
    )


def dft_kernel(goes_to, comes_from, steps, counts, me, *refs):
    blocks = refs[: len(steps)]
    windows, measured, forward, inverse = refs[len(steps) : len(steps) + 4]
    outs = refs[len(steps) + 4 : 2 * len(steps) + 4]
    placed, probes, terms = refs[2 * len(steps) + 4 :]
    size = windows.shape[-1]
    rows = blocks[0].shape[2]
    starts = [pl.multiple_of(comes_from(me[0], step) * rows, rows) for step in steps]
    targets = [pl.multiple_of(goes_to(me[0], step) * rows, rows) for step in steps]

    def dot(left, right):
        return jnp.dot(left, right, preferred_element_type=jnp.float32)

    for block, start in zip(blocks, starts):
        probes[:, :, pl.ds(start, rows)] = block[...]
    for slot in range(windows.shape[0]):
        probe_re = probes[slot, 0].astype(jnp.float32)
        probe_im = probes[slot, 1].astype(jnp.float32)
        window_re = windows[slot, 0].astype(jnp.float32)
        window_im = windows[slot, 1].astype(jnp.float32)
        leaving = jnp.concatenate(
            [
                (probe_re * window_re - probe_im * window_im).astype(jnp.bfloat16),
                (probe_re * window_im + probe_im * window_re).astype(jnp.bfloat16),
            ],
            axis=0,
        )
        half = dot(forward[...], leaving).astype(jnp.bfloat16)
        far = dot(jnp.concatenate([half[:size], half[size:]], axis=1), inverse[...])
        far_re, far_im = (far[:, :size], far[:, size:])
        power = jnp.maximum(far_re * far_re + far_im * far_im, FLOOR * FLOOR)
        live = jnp.where(slot < counts[0, 0], 1.0, 0.0).astype(jnp.float32)
        factor = (measured[slot] * lax.rsqrt(power) - 1.0) * live
        change = jnp.concatenate(
            [(far_re * factor).astype(jnp.bfloat16), (far_im * factor).astype(jnp.bfloat16)], axis=0
        )
        back = dot(inverse[...], change).astype(jnp.bfloat16)
        update = dot(jnp.concatenate([back[:size], back[size:]], axis=1), forward[...])
        update_re, update_im = (update[:, :size], update[:, size:])
        terms[slot, 0] = (window_re * update_re + window_im * update_im).astype(jnp.bfloat16)
        terms[slot, 1] = (window_re * update_im - window_im * update_re).astype(jnp.bfloat16)
        placed[slot, 0] = probe_re * update_re + probe_im * update_im
        placed[slot, 1] = probe_re * update_im - probe_im * update_re
    for out, start in zip(outs, targets):
        out[...] = terms[:, :, pl.ds(start, rows)]


def place_kernel(half, corners, pieces, top, middle, bottom, accum):
    size = pieces.shape[-1]
    rows = middle.shape[1]
    width = middle.shape[2]
    accum[...] = jnp.zeros_like(accum)
    for slot in range(pieces.shape[0]):
        base_row, rest_row, base_col, rest_col = corner_of(
            corners, slot, half, rows + 2 * half - size
        )
        for part in range(2):
            block = jnp.concatenate(
                [pieces[slot, part], jnp.zeros((size, LANES), jnp.float32)], axis=1
            )
            block = pltpu.roll(block, rest_col, 1)
            block = jnp.concatenate(
                [block, jnp.zeros((SUBLANES, size + LANES), jnp.float32)], axis=0
            )
            block = pltpu.roll(block, rest_row, 0)
            where = (part, pl.ds(base_row, size + SUBLANES), pl.ds(base_col, size + LANES))
            accum[where] += block
    top[...] = accum[:, :half, :width].astype(jnp.bfloat16)
    middle[...] = accum[:, half : half + rows, :width]
    bottom[...] = accum[:, half + rows : 2 * half + rows, :width].astype(jnp.bfloat16)


def rows_kernel(middle, got_top, got_bottom, left, center, right, total):
    half = got_top.shape[1]
    rows = middle.shape[1]
    cols = center.shape[2]
    total[...] = middle[...]
    total[:, :half] += got_top[...].astype(jnp.float32)
    total[:, rows - half :] += got_bottom[...].astype(jnp.float32)
    left[...] = total[:, :, :half].astype(jnp.bfloat16)
    center[...] = total[:, :, half : half + cols]
    right[...] = total[:, :, half + cols :].astype(jnp.bfloat16)


def cols_kernel(center, got_left, got_right, out):
    half = got_left.shape[2]
    cols = out.shape[2]
    out[...] = center[...]
    out[:, :, :half] += got_left[...].astype(jnp.float32)
    out[:, :, cols - half :] += got_right[...].astype(jnp.float32)


def sums_kernel(count, goals, row, *refs):
    received = refs[count : 2 * count]
    added = refs[2 * count : 2 * count + sum(goal[2] for goal in goals)]
    outs = refs[2 * count + len(added) : -3]
    terms, held, sem = refs[-3:]
    copies = fetch(refs[:count], held, sem)
    num_modes = outs[0].shape[-4]
    slot_count = received[0].shape[0]
    first = min(goal[1] for goal in goals)
    for at in range(count):
        terms[at, first:] = received[at][first:].astype(jnp.float32)
    for copy in copies:
        copy.wait()

    def mode_step(k, carry):
        rest = list(added)
        for (step, first, adds), out in zip(goals, outs):
            region = (row[0] + step).astype(jnp.float32)
            addend = rest.pop(0) if adds else None
            scales = [
                jnp.where(held[at, slot, num_modes] == region, held[at, slot, k], 0.0)
                for at in range(count)
                for slot in range(first, slot_count)
            ]
            for part in range(2):
                pieces = [
                    terms[at, slot, part] for at in range(count) for slot in range(first, slot_count)
                ]
                total = scales[0] * pieces[0]
                for scale, piece in zip(scales[1:], pieces[1:]):
                    total += scale * piece
                if adds:
                    total += addend[k, part].astype(jnp.float32)
                out[k, part] = total.astype(out.dtype)
        return carry

    lax.fori_loop(0, num_modes, mode_step, 0)


def sums(row, goals, weights, received, added, num_modes, dtypes):
    shape = (num_modes,) + received[0].shape[1:]
    return call(
        functools.partial(sums_kernel, len(received), goals),
        [(shape, dtype) for dtype in dtypes],
        (row, SMEM),
        *weights,
        *received,
        *added,
        scratch=[pltpu.VMEM((len(received),) + received[0].shape, jnp.float32)]
        + held_weights(len(weights), weights[0]),
    )


def gradients(object_field, modes, coeffs, offsets, region, counts, intensity):
    size = modes.shape[-1]
    half = size // 2
    num_modes = modes.shape[1]
    slot_count = coeffs.shape[2]
    rows, cols = object_field.shape[1:]
    block = (slot_count,) + modes.shape[2:]
    row = lax.axis_index("row").reshape(1)
    me = lax.axis_index("col").reshape(1)
    steps, goes_to, comes_from = partners("col")
    count = lax.axis_size("col")
    crossing = steps[: count - count // 2]
    staying = steps[count - count // 2 :]

    def move(value, step):
        return lax.ppermute(value, "col", [(i, goes_to(i, step)) for i in range(count)])

    follower = shift(modes, "row", -1)
    lanes = lax.broadcasted_iota(jnp.int32, (slot_count, LANES), 1)
    payload = jnp.where(
        lanes < num_modes,
        jnp.pad(coeffs[0, 0], ((0, 0), (0, LANES - num_modes))),
        region[0, 0].astype(jnp.float32)[:, None],
    )
    weights = {0: payload}
    for step in steps:
        weights[step] = move(payload, step)

    def made_for(step):
        return weights[step] if goes_to(1, step) == comes_from(1, step) else weights[count - step]

    low = object_field.astype(jnp.bfloat16)
    left = shift(low[:, :, cols - half :], "col", 1)
    right = shift(low[:, :, :half], "col", -1)
    wide = (2, half, cols + 2 * half)
    wide_top, wide_bottom = call(
        widen_kernel, [(wide, jnp.bfloat16)] * 2, object_field, left, right
    )
    top = shift(wide_bottom, "row", 1)
    bottom = shift(wide_top, "row", -1)

    blocks = {}
    for group in (crossing, [0] + staying):
        made = slabs(row, [made_for(step) for step in group], modes, follower)
        for step, slab in zip(group, made):
            blocks[step] = move(slab, step) if step else slab

    corners = offsets[0, 0]
    windows, measured = windows_of(corners, object_field, left, right, top, bottom, intensity)
    every = [0] + steps
    whole = (slot_count, 2, size, size)
    *terms, placed = call(
        functools.partial(dft_kernel, goes_to, comes_from, every),
        [(block, jnp.bfloat16)] * count + [(whole, jnp.float32)],
        (counts, SMEM),
        (me, SMEM),
        *[blocks[step] for step in every],
        windows,
        measured,
        *dft_tables(size),
        scratch=[pltpu.VMEM(whole, jnp.bfloat16)] * 2,
        limit=32,
    )
    terms = dict(zip(every, terms))
    received = {step: move(terms[step], step) if step else terms[step] for step in every}

    extent = (2, rows + 2 * half + SUBLANES, cols + 2 * half + LANES)
    over_top, middle, over_bottom = call(
        functools.partial(place_kernel, half),
        [(wide, jnp.bfloat16), ((2, rows, cols + 2 * half), jnp.float32), (wide, jnp.bfloat16)],
        (corners, SMEM),
        placed,
        scratch=[pltpu.VMEM(extent, jnp.float32)],
    )
    got_top = shift(over_bottom, "row", 1)
    got_bottom = shift(over_top, "row", -1)
    side = ((2, rows, half), jnp.bfloat16)
    over_left, center, over_right = call(
        rows_kernel,
        [side, ((2, rows, cols), jnp.float32), side],
        middle,
        got_top,
        got_bottom,
        scratch=[pltpu.VMEM((2, rows, cols + 2 * half), jnp.float32)],
    )
    got_left = shift(over_right, "col", 1)
    got_right = shift(over_left, "col", -1)
    (object_grad,) = call(
        cols_kernel, [(object_field.shape, jnp.float32)], center, got_left, got_right
    )

    def add_up(group, goals, added, dtypes):
        return sums(
            row,
            goals,
            [came_from(step) for step in group],
            [received[step] for step in group],
            added,
            num_modes,
            dtypes,
        )

    def came_from(step):
        return weights[step]

    own, following = add_up(
        [0] + staying, ((0, 0, False), (1, 1, False)), [], [jnp.float32, jnp.float32]
    )
    (following,) = add_up(crossing, ((1, 1, True),), [following], [jnp.bfloat16])
    passed = shift(following, "row", 1)
    (own,) = add_up(crossing, ((0, 0, True),), [own], [jnp.float32])
    mode_grad = (own + passed.astype(jnp.float32))[None]
    return (object_grad, mode_grad)


def solution(mesh):
    in_specs = (
        P(None, "row", "col"),
        P("row", None, None, "col", None),
        P("row", "col", None, None),
        P("row", "col", None, None),
        P("row", "col", None),
        P("row", "col"),
        P("row", "col", None, None, None),
    )
    out_specs = (P(None, "row", "col"), P("row", None, None, "col", None))
    return jax.shard_map(gradients, mesh=mesh, in_specs=in_specs, out_specs=out_specs, check_vma=False)
```

profile of v0, /device:TPU:3, one launch (start us, length us, event | category | flops | bytes accessed | tf_op | source)
XLA Modules:
  0.0 126.1 jit_solution(18029753938251962220)
XLA Ops:
  3.8 4.3 %collective-permute-start.15 = (bf16[2,256,128]{2,1,0:T(8,128)(2,1)S(1)}, bf16[2,256,128]{2,1,0:T(8,128)(2,1)S(1)}, u32[]{:S(2)}, u32[]{:S(2)}) collective-permute-start(bf16[2,256,128]{2,1,0:T(8,128)(2,1)S(1)} %get-tuple-element.61), channel_id=1, source_target_pairs={{0,1},{1,2},{2,3},{3,4},{4,5},{5,6},{6,7},{8,9},{9,10},{10,11},{11... | collective-permute-start | bytes 393224 | tf_op jit(solution)/shard_map/ppermute | solution.py:25
  8.1 3.1 %collective-permute-start.3 = (bf16[1,12,2,32,256]{4,3,2,1,0:T(8,128)(2,1)}, bf16[1,12,2,32,256]{4,3,2,1,0:T(8,128)(2,1)S(1)}, u32[]{:S(2)}, u32[]{:S(2)}) collective-permute-start(bf16[1,12,2,32,256]{4,3,2,1,0:T(8,128)(2,1)} %refs_4_.3), channel_id=1, source_target_pairs={{8,0},{16,8},{24,16},{9,1},{17,9},{25,17},{10,2},{18,10},{26,18},{... | collective-permute-start | bytes 1179656 | tf_op jit(solution)/shard_map/ppermute | solution.py:25
  14.8 3.5 %collective-permute-start.17 = (bf16[2,128,512]{2,1,0:T(8,128)(2,1)}, bf16[2,128,512]{2,1,0:T(8,128)(2,1)S(1)}, u32[]{:S(2)}, u32[]{:S(2)}) collective-permute-start(bf16[2,128,512]{2,1,0:T(8,128)(2,1)} %get-tuple-element.39), channel_id=1, source_target_pairs={{0,8},{8,16},{16,24},{1,9},{9,17},{17,25},{2,10},{10,18},{18,26},{... | collective-permute-start | bytes 786440 | tf_op jit(solution)/shard_map/ppermute | solution.py:25
  24.3 2.0 %collective-permute-done.refs_1_ = f32[4,128]{1,0:T(4,128)S(1)} collective-permute-done((f32[4,128]{1,0:T(4,128)S(1)}, f32[4,128]{1,0:T(4,128)S(1)}, u32[]{:S(2)}, u32[]{:S(2)}) %collective-permute-start) | collective-permute-done | bytes 2080 | tf_op jit(solution)/shard_map/ppermute | solution.py:347
  26.3 2.5 %shard_map.104 = (bf16[4,2,32,256]{3,2,1,0:T(8,128)(2,1)S(1)}, bf16[4,2,32,256]{3,2,1,0:T(8,128)(2,1)S(1)}, bf16[4,2,32,256]{3,2,1,0:T(8,128)(2,1)S(1)}, bf16[4,2,32,256]{3,2,1,0:T(8,128)(2,1)}) custom-call(s32[1]{0:T(128)} %bitcast.2.row, f32[4,128]{1,0:T(4,128)S(1)} %pad_select_fusion.refs_0_, f32[4,128]{1,0:T(4,128)S(1)} %collective-permute-done.refs_1_, ...), custom_call_target="tpu_custom_call" | custom-call | tf_op jit(solution)/shard_map/pallas_call | solution.py:58
  30.5 3.1 %collective-permute-start.7 = (f32[4,128]{1,0:T(4,128)S(1)}, f32[4,128]{1,0:T(4,128)S(1)}, u32[]{:S(2)}, u32[]{:S(2)}) collective-permute-start(f32[4,128]{1,0:T(4,128)S(1)} %pad_select_fusion.refs_0_), channel_id=1, source_target_pairs={{0,7},{1,6},{2,5},{3,4},{4,3},{5,2},{6,1},{7,0},{8,15},{9,14},{10,... | collective-permute-start | bytes 6152 | tf_op jit(solution)/shard_map/ppermute | solution.py:347
  33.6 2.7 %collective-permute-done.7.refs_3_ = f32[4,128]{1,0:T(4,128)S(1)} collective-permute-done((f32[4,128]{1,0:T(4,128)S(1)}, f32[4,128]{1,0:T(4,128)S(1)}, u32[]{:S(2)}, u32[]{:S(2)}) %collective-permute-start.7) | collective-permute-done | bytes 2080 | tf_op jit(solution)/shard_map/ppermute | solution.py:347
  37.8 2.6 %collective-permute-done.6.refs_2_ = f32[4,128]{1,0:T(4,128)S(1)} collective-permute-done((f32[4,128]{1,0:T(4,128)S(1)}, f32[4,128]{1,0:T(4,128)S(1)}, u32[]{:S(2)}, u32[]{:S(2)}) %collective-permute-start.6) | collective-permute-done | bytes 2080 | tf_op jit(solution)/shard_map/ppermute | solution.py:347
  40.5 4.2 %collective-permute-done.5.refs_1_ = f32[4,128]{1,0:T(4,128)S(1)} collective-permute-done((f32[4,128]{1,0:T(4,128)S(1)}, f32[4,128]{1,0:T(4,128)S(1)}, u32[]{:S(2)}, u32[]{:S(2)}) %collective-permute-start.5) | collective-permute-done | bytes 2080 | tf_op jit(solution)/shard_map/ppermute | solution.py:347
  44.7 3.7 %collective-permute-done.4.refs_0_ = f32[4,128]{1,0:T(4,128)S(1)} collective-permute-done((f32[4,128]{1,0:T(4,128)}, f32[4,128]{1,0:T(4,128)S(1)}, u32[]{:S(2)}, u32[]{:S(2)}) %collective-permute-start.4) | collective-permute-done | bytes 2080 | tf_op jit(solution)/shard_map/ppermute | solution.py:347
  48.6 2.6 %shard_map.105 = (bf16[4,2,32,256]{3,2,1,0:T(8,128)(2,1)}, bf16[4,2,32,256]{3,2,1,0:T(8,128)(2,1)}, bf16[4,2,32,256]{3,2,1,0:T(8,128)(2,1)}, bf16[4,2,32,256]{3,2,1,0:T(8,128)(2,1)}) custom-call(s32[1]{0:T(128)} %bitcast.2.row, f32[4,128]{1,0:T(4,128)S(1)} %collective-permute-done.4.refs_0_, f32[4,128]{1,0:T(4,128)S(1)} %collective-permute-done.5.refs_1_, ...), custom_call_target="tpu_custom_call" | custom-call | tf_op jit(solution)/shard_map/pallas_call | solution.py:58
  51.3 2.7 %collective-permute-start.8 = (bf16[4,2,32,256]{3,2,1,0:T(8,128)(2,1)}, bf16[4,2,32,256]{3,2,1,0:T(8,128)(2,1)S(1)}, u32[]{:S(2)}, u32[]{:S(2)}) collective-permute-start(bf16[4,2,32,256]{3,2,1,0:T(8,128)(2,1)} %get-tuple-element.32), channel_id=1, source_target_pairs={{0,4},{1,5},{2,6},{3,7},{4,0},{5,1},{6,2},{7,3},{8,12},{9,13},{10,... | collective-permute-start | bytes 393224 | tf_op jit(solution)/shard_map/ppermute | solution.py:347
  57.4 2.2 %collective-permute-start.11 = (bf16[4,2,32,256]{3,2,1,0:T(8,128)(2,1)}, bf16[4,2,32,256]{3,2,1,0:T(8,128)(2,1)S(1)}, u32[]{:S(2)}, u32[]{:S(2)}) collective-permute-start(bf16[4,2,32,256]{3,2,1,0:T(8,128)(2,1)} %get-tuple-element.35), channel_id=1, source_target_pairs={{0,7},{1,6},{2,5},{3,4},{4,3},{5,2},{6,1},{7,0},{8,15},{9,14},{10,... | collective-permute-start | bytes 393224 | tf_op jit(solution)/shard_map/ppermute | solution.py:347
  61.0 2.9 %shard_map.107 = (bf16[4,2,256,256]{3,2,1,0:T(8,128)(2,1)S(1)}, f32[4,256,256]{2,1,0:T(8,128)S(1)}) custom-call(s32[4,2]{1,0:T(4,128)S(1)} %copy.12.corners, f32[2,256,256]{2,1,0:T(8,128)S(1)} %copy-done.1, bf16[2,256,128]{2,1,0:T(8,128)(2,1)S(1)} %collective-permute-done.15.left, bf16[2,256,128]{2,1,0:T(8,128)(2,1)S(1)} %collective-permute-done.16.right, ...), custom_call_target="tpu_custom_call" | custom-call | tf_op jit(solution)/shard_map/pallas_call | solution.py:58
  63.9 4.8 %collective-permute-done.9.refs_2_ = bf16[4,2,32,256]{3,2,1,0:T(8,128)(2,1)S(1)} collective-permute-done((bf16[4,2,32,256]{3,2,1,0:T(8,128)(2,1)}, bf16[4,2,32,256]{3,2,1,0:T(8,128)(2,1)S(1)}, u32[]{:S(2)}, u32[]{:S(2)}) %collective-permute-start.9) | collective-permute-done | bytes 131104 | tf_op jit(solution)/shard_map/ppermute | solution.py:347
  70.6 5.5 %shard_map.108 = (bf16[4,2,32,256]{3,2,1,0:T(8,128)(2,1)S(1)}, bf16[4,2,32,256]{3,2,1,0:T(8,128)(2,1)S(1)}, bf16[4,2,32,256]{3,2,1,0:T(8,128)(2,1)S(1)}, bf16[4,...) custom-call(s32[1,1]{1,0:T(1,128)S(6)} %copy.13.counts, ...), custom_call_target="tpu_custom_call" | custom-call | tf_op jit(solution)/shard_map/pallas_call | solution.py:58
  76.2 7.8 %collective-permute-start.23 = (bf16[4,2,32,256]{3,2,1,0:T(8,128)(2,1)S(1)}, bf16[4,2,32,256]{3,2,1,0:T(8,128)(2,1)S(1)}, u32[]{:S(2)}, u32[]{:S(2)}) collective-permute-start(bf16[4,2,32,256]{3,2,1,0:T(8,128)(2,1)S(1)} %get-tuple-element.50), channel_id=1, source_target_pairs={{0,4},{1,5},{2,6},{3,7},{4,0},{5,1},{6,2},{7,3},{8,12},{9,13},{10,... | collective-permute-start | bytes 393224 | tf_op jit(solution)/shard_map/ppermute | solution.py:347
  89.1 2.1 %collective-permute-start.26 = (bf16[4,2,32,256]{3,2,1,0:T(8,128)(2,1)S(1)}, bf16[4,2,32,256]{3,2,1,0:T(8,128)(2,1)S(1)}, u32[]{:S(2)}, u32[]{:S(2)}) collective-permute-start(bf16[4,2,32,256]{3,2,1,0:T(8,128)(2,1)S(1)} %get-tuple-element.53), channel_id=1, source_target_pairs={{0,7},{1,6},{2,5},{3,4},{4,3},{5,2},{6,1},{7,0},{8,15},{9,14},{10,... | collective-permute-start | bytes 393224 | tf_op jit(solution)/shard_map/ppermute | solution.py:347
  91.3 2.9 %shard_map.109 = (bf16[2,128,512]{2,1,0:T(8,128)(2,1)S(1)}, f32[2,256,512]{2,1,0:T(8,128)S(1)}, bf16[2,128,512]{2,1,0:T(8,128)(2,1)S(1)}) custom-call(s32[4,2]{1,0:T(4,128)S(1)} %copy.12.corners, f32[4,2,256,256]{3,2,1,0:T(8,128)S(1)} %get-tuple-element.43.pieces), custom_call_target="tpu_custom_call" | custom-call | tf_op jit(solution)/shard_map/pallas_call | solution.py:58
  94.1 7.5 %collective-permute-start.19 = (bf16[2,128,512]{2,1,0:T(8,128)(2,1)S(1)}, bf16[2,128,512]{2,1,0:T(8,128)(2,1)S(1)}, u32[]{:S(2)}, u32[]{:S(2)}) collective-permute-start(bf16[2,128,512]{2,1,0:T(8,128)(2,1)S(1)} %get-tuple-element.45), channel_id=1, source_target_pairs={{0,8},{8,16},{16,24},{1,9},{9,17},{17,25},{2,10},{10,18},{18,26},{... | collective-permute-start | bytes 786440 | tf_op jit(solution)/shard_map/ppermute | solution.py:25
  103.7 2.3 %shard_map.112 = (f32[12,2,32,256]{3,2,1,0:T(8,128)S(1)}, f32[12,2,32,256]{3,2,1,0:T(8,128)S(1)}) custom-call(s32[1]{0:T(128)} %bitcast.2.row, f32[4,128]{1,0:T(4,128)S(1)} %copy-done.11, f32[4,128]{1,0:T(4,128)S(1)} %copy-done.17, f32[4,128]{1,0:T(4,128)S(1)} %copy-done.15, f32[4,128]{1,0:T(4,128)S(1)} %copy-done.13, ...), custom_call_target="tpu_custom_call" | custom-call | tf_op jit(solution)/shard_map/pallas_call | solution.py:58
  107.5 3.6 %collective-permute-start.30 = (bf16[12,2,32,256]{3,2,1,0:T(8,128)(2,1)S(1)}, bf16[12,2,32,256]{3,2,1,0:T(8,128)(2,1)S(1)}, u32[]{:S(2)}, u32[]{:S(2)}) collective-permute-start(bf16[12,2,32,256]{3,2,1,0:T(8,128)(2,1)S(1)} %shard_map.114), channel_id=1, source_target_pairs={{0,8},{8,16},{16,24},{1,9},{9,17},{17,25},{2,10},{10,18},{18,26},{... | collective-permute-start | bytes 1179656 | tf_op jit(solution)/shard_map/ppermute | solution.py:25
  111.3 4.8 %collective-permute-start.21 = (bf16[2,256,128]{2,1,0:T(8,128)(2,1)S(1)}, bf16[2,256,128]{2,1,0:T(8,128)(2,1)S(1)}, u32[]{:S(2)}, u32[]{:S(2)}) collective-permute-start(bf16[2,256,128]{2,1,0:T(8,128)(2,1)S(1)} %get-tuple-element.48), channel_id=1, source_target_pairs={{0,1},{1,2},{2,3},{3,4},{4,5},{5,6},{6,7},{8,9},{9,10},{10,11},{11... | collective-permute-start | bytes 393224 | tf_op jit(solution)/shard_map/ppermute | solution.py:25
  119.8 4.5 %collective-permute-done.22.got_right = bf16[2,256,128]{2,1,0:T(8,128)(2,1)S(1)} collective-permute-done((bf16[2,256,128]{2,1,0:T(8,128)(2,1)S(1)}, bf16[2,256,128]{2,1,0:T(8,128)(2,1)S(1)}, u32[]{:S(2)}, u32[]{:S(2)}) %collective-permute-start.22) | collective-permute-done | bytes 131104 | tf_op jit(solution)/shard_map/ppermute | solution.py:25
  (94 shorter events, 36.3 us)
Async XLA Ops:
  1.9 10.0 %collective-permute-start.16 = (bf16[2,256,128]{2,1,0:T(8,128)(2,1)S(1)}, bf16[2,256,128]{2,1,0:T(8,128)(2,1)S(1)}, u32[]{:S(2)}, u32[]{:S(2)}) collective-permute-start(bf16[2,256,128]{2,1,0:T(8,128)(2,1)S(1)} %get-tuple-element.60), channel_id=1, source_target_pairs={{1,0},{2,1},{3,2},{4,3},{5,4},{6,5},{7,6},{9,8},{10,9},{11,10},{12... | collective-permute-start | bytes 393224 | tf_op jit(solution)/shard_map/ppermute | solution.py:25
  3.8 9.1 %collective-permute-start.15 = (bf16[2,256,128]{2,1,0:T(8,128)(2,1)S(1)}, bf16[2,256,128]{2,1,0:T(8,128)(2,1)S(1)}, u32[]{:S(2)}, u32[]{:S(2)}) collective-permute-start(bf16[2,256,128]{2,1,0:T(8,128)(2,1)S(1)} %get-tuple-element.61), channel_id=1, source_target_pairs={{0,1},{1,2},{2,3},{3,4},{4,5},{5,6},{6,7},{8,9},{9,10},{10,11},{11... | collective-permute-start | bytes 393224 | tf_op jit(solution)/shard_map/ppermute | solution.py:25
  8.1 18.2 %collective-permute-start.3 = (bf16[1,12,2,32,256]{4,3,2,1,0:T(8,128)(2,1)}, bf16[1,12,2,32,256]{4,3,2,1,0:T(8,128)(2,1)S(1)}, u32[]{:S(2)}, u32[]{:S(2)}) collective-permute-start(bf16[1,12,2,32,256]{4,3,2,1,0:T(8,128)(2,1)} %refs_4_.3), channel_id=1, source_target_pairs={{8,0},{16,8},{24,16},{9,1},{17,9},{25,17},{10,2},{18,10},{26,18},{... | collective-permute-start | bytes 1179656 | tf_op jit(solution)/shard_map/ppermute | solution.py:25
  14.8 36.5 %collective-permute-start.17 = (bf16[2,128,512]{2,1,0:T(8,128)(2,1)}, bf16[2,128,512]{2,1,0:T(8,128)(2,1)S(1)}, u32[]{:S(2)}, u32[]{:S(2)}) collective-permute-start(bf16[2,128,512]{2,1,0:T(8,128)(2,1)} %get-tuple-element.39), channel_id=1, source_target_pairs={{0,8},{8,16},{16,24},{1,9},{9,17},{17,25},{2,10},{10,18},{18,26},{... | collective-permute-start | bytes 786440 | tf_op jit(solution)/shard_map/ppermute | solution.py:25
  18.3 35.7 %collective-permute-start.18 = (bf16[2,128,512]{2,1,0:T(8,128)(2,1)}, bf16[2,128,512]{2,1,0:T(8,128)(2,1)}, u32[]{:S(2)}, u32[]{:S(2)}) collective-permute-start(bf16[2,128,512]{2,1,0:T(8,128)(2,1)} %get-tuple-element.40), channel_id=1, source_target_pairs={{8,0},{16,8},{24,16},{9,1},{17,9},{25,17},{10,2},{18,10},{26,18},{... | collective-permute-start | bytes 786440 | tf_op jit(solution)/shard_map/ppermute | solution.py:25
  28.8 25.3 %collective-permute-start.12 = (bf16[4,2,32,256]{3,2,1,0:T(8,128)(2,1)S(1)}, bf16[4,2,32,256]{3,2,1,0:T(8,128)(2,1)S(1)}, u32[]{:S(2)}, u32[]{:S(2)}) collective-permute-start(bf16[4,2,32,256]{3,2,1,0:T(8,128)(2,1)S(1)} %get-tuple-element.36), channel_id=1, source_target_pairs={{0,1},{1,0},{2,3},{3,2},{4,5},{5,4},{6,7},{7,6},{8,9},{9,8},{10,11... | collective-permute-start | bytes 393224 | tf_op jit(solution)/shard_map/ppermute | solution.py:347
  28.9 27.9 %collective-permute-start.13 = (bf16[4,2,32,256]{3,2,1,0:T(8,128)(2,1)S(1)}, bf16[4,2,32,256]{3,2,1,0:T(8,128)(2,1)S(1)}, u32[]{:S(2)}, u32[]{:S(2)}) collective-permute-start(bf16[4,2,32,256]{3,2,1,0:T(8,128)(2,1)S(1)} %get-tuple-element.37), channel_id=1, source_target_pairs={{0,2},{1,3},{2,0},{3,1},{4,6},{5,7},{6,4},{7,5},{8,10},{9,11},{10,... | collective-permute-start | bytes 393224 | tf_op jit(solution)/shard_map/ppermute | solution.py:347
  30.5 5.7 %collective-permute-start.7 = (f32[4,128]{1,0:T(4,128)S(1)}, f32[4,128]{1,0:T(4,128)S(1)}, u32[]{:S(2)}, u32[]{:S(2)}) collective-permute-start(f32[4,128]{1,0:T(4,128)S(1)} %pad_select_fusion.refs_0_), channel_id=1, source_target_pairs={{0,7},{1,6},{2,5},{3,4},{4,3},{5,2},{6,1},{7,0},{8,15},{9,14},{10,... | collective-permute-start | bytes 6152 | tf_op jit(solution)/shard_map/ppermute | solution.py:347
  48.4 15.5 %collective-permute-start.14 = (bf16[4,2,32,256]{3,2,1,0:T(8,128)(2,1)}, bf16[4,2,32,256]{3,2,1,0:T(8,128)(2,1)}, u32[]{:S(2)}, u32[]{:S(2)}) collective-permute-start(bf16[4,2,32,256]{3,2,1,0:T(8,128)(2,1)} %get-tuple-element.38), channel_id=1, source_target_pairs={{0,3},{1,2},{2,1},{3,0},{4,7},{5,6},{6,5},{7,4},{8,11},{9,10},{10,... | collective-permute-start | bytes 393224 | tf_op jit(solution)/shard_map/ppermute | solution.py:347
  51.3 12.6 %collective-permute-start.8 = (bf16[4,2,32,256]{3,2,1,0:T(8,128)(2,1)}, bf16[4,2,32,256]{3,2,1,0:T(8,128)(2,1)S(1)}, u32[]{:S(2)}, u32[]{:S(2)}) collective-permute-start(bf16[4,2,32,256]{3,2,1,0:T(8,128)(2,1)} %get-tuple-element.32), channel_id=1, source_target_pairs={{0,4},{1,5},{2,6},{3,7},{4,0},{5,1},{6,2},{7,3},{8,12},{9,13},{10,... | collective-permute-start | bytes 393224 | tf_op jit(solution)/shard_map/ppermute | solution.py:347
  54.0 14.7 %collective-permute-start.9 = (bf16[4,2,32,256]{3,2,1,0:T(8,128)(2,1)}, bf16[4,2,32,256]{3,2,1,0:T(8,128)(2,1)S(1)}, u32[]{:S(2)}, u32[]{:S(2)}) collective-permute-start(bf16[4,2,32,256]{3,2,1,0:T(8,128)(2,1)} %get-tuple-element.33), channel_id=1, source_target_pairs={{0,5},{1,4},{2,7},{3,6},{4,1},{5,0},{6,3},{7,2},{8,13},{9,12},{10,... | collective-permute-start | bytes 393224 | tf_op jit(solution)/shard_map/ppermute | solution.py:347
  54.8 14.0 %collective-permute-start.10 = (bf16[4,2,32,256]{3,2,1,0:T(8,128)(2,1)}, bf16[4,2,32,256]{3,2,1,0:T(8,128)(2,1)S(1)}, u32[]{:S(2)}, u32[]{:S(2)}) collective-permute-start(bf16[4,2,32,256]{3,2,1,0:T(8,128)(2,1)} %get-tuple-element.34), channel_id=1, source_target_pairs={{0,6},{1,7},{2,4},{3,5},{4,2},{5,3},{6,0},{7,1},{8,14},{9,15},{10,... | collective-permute-start | bytes 393224 | tf_op jit(solution)/shard_map/ppermute | solution.py:347
  57.4 11.3 %collective-permute-start.11 = (bf16[4,2,32,256]{3,2,1,0:T(8,128)(2,1)}, bf16[4,2,32,256]{3,2,1,0:T(8,128)(2,1)S(1)}, u32[]{:S(2)}, u32[]{:S(2)}) collective-permute-start(bf16[4,2,32,256]{3,2,1,0:T(8,128)(2,1)} %get-tuple-element.35), channel_id=1, source_target_pairs={{0,7},{1,6},{2,5},{3,4},{4,3},{5,2},{6,1},{7,0},{8,15},{9,14},{10,... | collective-permute-start | bytes 393224 | tf_op jit(solution)/shard_map/ppermute | solution.py:347
  76.2 11.4 %collective-permute-start.23 = (bf16[4,2,32,256]{3,2,1,0:T(8,128)(2,1)S(1)}, bf16[4,2,32,256]{3,2,1,0:T(8,128)(2,1)S(1)}, u32[]{:S(2)}, u32[]{:S(2)}) collective-permute-start(bf16[4,2,32,256]{3,2,1,0:T(8,128)(2,1)S(1)} %get-tuple-element.50), channel_id=1, source_target_pairs={{0,4},{1,5},{2,6},{3,7},{4,0},{5,1},{6,2},{7,3},{8,12},{9,13},{10,... | collective-permute-start | bytes 393224 | tf_op jit(solution)/shard_map/ppermute | solution.py:347
  84.7 9.4 %collective-permute-start.28 = (bf16[4,2,32,256]{3,2,1,0:T(8,128)(2,1)S(1)}, bf16[4,2,32,256]{3,2,1,0:T(8,128)(2,1)S(1)}, u32[]{:S(2)}, u32[]{:S(2)}) collective-permute-start(bf16[4,2,32,256]{3,2,1,0:T(8,128)(2,1)S(1)} %get-tuple-element.56), channel_id=1, source_target_pairs={{0,2},{1,3},{2,0},{3,1},{4,6},{5,7},{6,4},{7,5},{8,10},{9,11},{10,... | collective-permute-start | bytes 393224 | tf_op jit(solution)/shard_map/ppermute | solution.py:347
  84.7 17.0 %collective-permute-start.29 = (bf16[4,2,32,256]{3,2,1,0:T(8,128)(2,1)S(1)}, bf16[4,2,32,256]{3,2,1,0:T(8,128)(2,1)S(1)}, u32[]{:S(2)}, u32[]{:S(2)}) collective-permute-start(bf16[4,2,32,256]{3,2,1,0:T(8,128)(2,1)S(1)} %get-tuple-element.57), channel_id=1, source_target_pairs={{0,3},{1,2},{2,1},{3,0},{4,7},{5,6},{6,5},{7,4},{8,11},{9,10},{10,... | collective-permute-start | bytes 393224 | tf_op jit(solution)/shard_map/ppermute | solution.py:347
  86.6 19.3 %collective-permute-start.24 = (bf16[4,2,32,256]{3,2,1,0:T(8,128)(2,1)S(1)}, bf16[4,2,32,256]{3,2,1,0:T(8,128)(2,1)S(1)}, u32[]{:S(2)}, u32[]{:S(2)}) collective-permute-start(bf16[4,2,32,256]{3,2,1,0:T(8,128)(2,1)S(1)} %get-tuple-element.51), channel_id=1, source_target_pairs={{0,5},{1,4},{2,7},{3,6},{4,1},{5,0},{6,3},{7,2},{8,13},{9,12},{10,... | collective-permute-start | bytes 393224 | tf_op jit(solution)/shard_map/ppermute | solution.py:347
  87.6 18.4 %collective-permute-start.25 = (bf16[4,2,32,256]{3,2,1,0:T(8,128)(2,1)S(1)}, bf16[4,2,32,256]{3,2,1,0:T(8,128)(2,1)S(1)}, u32[]{:S(2)}, u32[]{:S(2)}) collective-permute-start(bf16[4,2,32,256]{3,2,1,0:T(8,128)(2,1)S(1)} %get-tuple-element.52), channel_id=1, source_target_pairs={{0,6},{1,7},{2,4},{3,5},{4,2},{5,3},{6,0},{7,1},{8,14},{9,15},{10,... | collective-permute-start | bytes 393224 | tf_op jit(solution)/shard_map/ppermute | solution.py:347
  89.1 16.8 %collective-permute-start.26 = (bf16[4,2,32,256]{3,2,1,0:T(8,128)(2,1)S(1)}, bf16[4,2,32,256]{3,2,1,0:T(8,128)(2,1)S(1)}, u32[]{:S(2)}, u32[]{:S(2)}) collective-permute-start(bf16[4,2,32,256]{3,2,1,0:T(8,128)(2,1)S(1)} %get-tuple-element.53), channel_id=1, source_target_pairs={{0,7},{1,6},{2,5},{3,4},{4,3},{5,2},{6,1},{7,0},{8,15},{9,14},{10,... | collective-permute-start | bytes 393224 | tf_op jit(solution)/shard_map/ppermute | solution.py:347
  94.1 17.0 %collective-permute-start.19 = (bf16[2,128,512]{2,1,0:T(8,128)(2,1)S(1)}, bf16[2,128,512]{2,1,0:T(8,128)(2,1)S(1)}, u32[]{:S(2)}, u32[]{:S(2)}) collective-permute-start(bf16[2,128,512]{2,1,0:T(8,128)(2,1)S(1)} %get-tuple-element.45), channel_id=1, source_target_pairs={{0,8},{8,16},{16,24},{1,9},{9,17},{17,25},{2,10},{10,18},{18,26},{... | collective-permute-start | bytes 786440 | tf_op jit(solution)/shard_map/ppermute | solution.py:25
  101.7 9.4 %collective-permute-start.20 = (bf16[2,128,512]{2,1,0:T(8,128)(2,1)S(1)}, bf16[2,128,512]{2,1,0:T(8,128)(2,1)S(1)}, u32[]{:S(2)}, u32[]{:S(2)}) collective-permute-start(bf16[2,128,512]{2,1,0:T(8,128)(2,1)S(1)} %get-tuple-element.46), channel_id=1, source_target_pairs={{8,0},{16,8},{24,16},{9,1},{17,9},{25,17},{10,2},{18,10},{26,18},{... | collective-permute-start | bytes 786440 | tf_op jit(solution)/shard_map/ppermute | solution.py:25
  107.5 17.7 %collective-permute-start.30 = (bf16[12,2,32,256]{3,2,1,0:T(8,128)(2,1)S(1)}, bf16[12,2,32,256]{3,2,1,0:T(8,128)(2,1)S(1)}, u32[]{:S(2)}, u32[]{:S(2)}) collective-permute-start(bf16[12,2,32,256]{3,2,1,0:T(8,128)(2,1)S(1)} %shard_map.114), channel_id=1, source_target_pairs={{0,8},{8,16},{16,24},{1,9},{9,17},{17,25},{2,10},{10,18},{18,26},{... | collective-permute-start | bytes 1179656 | tf_op jit(solution)/shard_map/ppermute | solution.py:25
  111.3 8.5 %collective-permute-start.21 = (bf16[2,256,128]{2,1,0:T(8,128)(2,1)S(1)}, bf16[2,256,128]{2,1,0:T(8,128)(2,1)S(1)}, u32[]{:S(2)}, u32[]{:S(2)}) collective-permute-start(bf16[2,256,128]{2,1,0:T(8,128)(2,1)S(1)} %get-tuple-element.48), channel_id=1, source_target_pairs={{0,1},{1,2},{2,3},{3,4},{4,5},{5,6},{6,7},{8,9},{9,10},{10,11},{11... | collective-permute-start | bytes 393224 | tf_op jit(solution)/shard_map/ppermute | solution.py:25
  116.1 8.1 %collective-permute-start.22 = (bf16[2,256,128]{2,1,0:T(8,128)(2,1)S(1)}, bf16[2,256,128]{2,1,0:T(8,128)(2,1)S(1)}, u32[]{:S(2)}, u32[]{:S(2)}) collective-permute-start(bf16[2,256,128]{2,1,0:T(8,128)(2,1)S(1)} %get-tuple-element.49), channel_id=1, source_target_pairs={{1,0},{2,1},{3,2},{4,3},{5,4},{6,5},{7,6},{9,8},{10,9},{11,10},{12... | collective-permute-start | bytes 393224 | tf_op jit(solution)/shard_map/ppermute | solution.py:25
  (26 other events, 448.5 us)
where the time goes:
time: 127 us; the launch traced here: 126 us
  starting transfers between devices  64.8 us (51%)
  waiting for transfers between devices  27.9 us (22%)
  Pallas kernels  23.8 us (19%)
  local copies, waits for them, and re-layouts  5.03 us (4%)
  other arithmetic  2.9 us (2%)
  between operations  1.69 us (1%)
    ppermute x10, starting transfers between devices, shift(): return lax.ppermute(value, axis, pairs)  34.6 us
    ppermute x21, starting transfers between devices, move(): lax.ppermute(value, 'col', [(i, goes_to(i, step)) for i in range(count)])  30.2 us
    pallas_call x11, Pallas kernels, call(): pl.pallas_call(body, out_shape=tuple(outs), in_specs=specs, out_specs=tup...  23.8 us
    ppermute x21, waiting for transfers between devices, move(): lax.ppermute(value, 'col', [(i, goes_to(i, step)) for i in range(count)])  22.4 us
    ppermute x10, waiting for transfers between devices, shift(): return lax.ppermute(value, axis, pairs)  5.49 us
    unnamed x38, local copies, waits for them, and re-layouts  4.21 us
  transfers between devices with their start and end apart: 31, of which 10 were waited for; matrix products, arithmetic and copies ran while one was open for 1% of the time, Pallas kernels for 14%

commit v1 on v0

--- a/solution.py
+++ b/solution.py
@@ -85,12 +85,13 @@
     table[0] = own[0].astype(jnp.float32)
     table[1] = follower[0].astype(jnp.float32)
     next_row = (row[0] + 1).astype(jnp.float32)
+    slots = outs[0].shape[0]
     for copy in copies:
         copy.wait()
     for at, out in enumerate(outs):
 
         def slot_step(slot, carry, at=at, out=out):
-            region = held[at, slot, num_modes]
+            region = held[at, slots, slot]
             which = jnp.where(region == next_row, 1, 0)
             known = jnp.where(jnp.abs(region - next_row + 0.5) < 1.0, 1.0, 0.0)
             scales = [held[at, slot, k] * known for k in range(num_modes)]
@@ -105,7 +106,7 @@
 
 
 def slabs(row, weights, own, follower):
-    shape = (weights[0].shape[0],) + own.shape[2:]
+    shape = (weights[0].shape[0] - 1,) + own.shape[2:]
     return call(
         functools.partial(slab_kernel, len(weights)),
         [(shape, jnp.bfloat16)] * len(weights),
@@ -128,8 +129,8 @@
 
 
 def corner_of(corners, slot, half, limit):
-    row = jnp.clip(corners[slot, 0] + half, 0, limit)
-    col = jnp.clip(corners[slot, 1] + half, 0, limit)
+    row = jnp.clip(corners[0, slot] + half, 0, limit)
+    col = jnp.clip(corners[1, slot] + half, 0, limit)
     rest_row, rest_col = (row & (SUBLANES - 1), col & (LANES - 1))
     base_row = pl.multiple_of(row - rest_row, SUBLANES)
     base_col = pl.multiple_of(col - rest_col, LANES)
@@ -166,7 +167,7 @@
 
 
 def windows_of(corners, tile, left, right, top, bottom, intensity):
-    slot_count = corners.shape[0]
+    slot_count = intensity.shape[2]
     size = intensity.shape[-1]
     half = left.shape[-1]
     extent = (2, tile.shape[1] + 2 * half + SUBLANES, tile.shape[2] + 2 * half + LANES)
@@ -284,6 +285,7 @@
     copies = fetch(refs[:count], held, sem)
     num_modes = outs[0].shape[-4]
     slot_count = received[0].shape[0]
+    slots = slot_count
     first = min(goal[1] for goal in goals)
     for at in range(count):
         terms[at, first:] = received[at][first:].astype(jnp.float32)
@@ -296,7 +298,7 @@
             region = (row[0] + step).astype(jnp.float32)
             addend = rest.pop(0) if adds else None
             scales = [
-                jnp.where(held[at, slot, num_modes] == region, held[at, slot, k], 0.0)
+                jnp.where(held[at, slots, slot] == region, held[at, slot, k], 0.0)
                 for at in range(count)
                 for slot in range(first, slot_count)
             ]
@@ -339,6 +341,7 @@
     row = lax.axis_index("row").reshape(1)
     me = lax.axis_index("col").reshape(1)
     steps, goes_to, comes_from = partners("col")
+    every = [0] + steps
     count = lax.axis_size("col")
     crossing = steps[: count - count // 2]
     staying = steps[count - count // 2 :]
@@ -347,11 +350,8 @@
         return lax.ppermute(value, "col", [(i, goes_to(i, step)) for i in range(count)])
 
     follower = shift(modes, "row", -1)
-    lanes = lax.broadcasted_iota(jnp.int32, (slot_count, LANES), 1)
-    payload = jnp.where(
-        lanes < num_modes,
-        jnp.pad(coeffs[0, 0], ((0, 0), (0, LANES - num_modes))),
-        region[0, 0].astype(jnp.float32)[:, None],
+    payload = jnp.pad(coeffs[0, 0], ((0, 1), (0, LANES - num_modes))) + jnp.pad(
+        region[0].astype(jnp.float32), ((slot_count, 0), (0, LANES - slot_count))
     )
     weights = {0: payload}
     for step in steps:
@@ -371,14 +371,12 @@
     bottom = shift(wide_top, "row", -1)
 
     blocks = {}
-    for group in (crossing, [0] + staying):
-        made = slabs(row, [made_for(step) for step in group], modes, follower)
-        for step, slab in zip(group, made):
-            blocks[step] = move(slab, step) if step else slab
-
-    corners = offsets[0, 0]
+    made = slabs(row, [made_for(step) for step in every], modes, follower)
+    for step, slab in zip(every, made):
+        blocks[step] = move(slab, step) if step else slab
+
+    corners = offsets[0, 0].T
     windows, measured = windows_of(corners, object_field, left, right, top, bottom, intensity)
-    every = [0] + steps
     whole = (slot_count, 2, size, size)
     *terms, placed = call(
         functools.partial(dft_kernel, goes_to, comes_from, every),

time: 127 us -> 120 us (0.945)
  the two profiles are of different devices: /device:TPU:3 before, /device:TPU:0 now
where the time goes in v1:
time: 120 us
  starting transfers between devices  56.8 us (47%)
  waiting for transfers between devices  33.5 us (28%)
  Pallas kernels  22.5 us (19%)
  local copies, waits for them, and re-layouts  2.82 us (2%)
  other arithmetic  2.15 us (2%)
  between operations  1.71 us (1%)
    ppermute x21, starting transfers between devices, move(): lax.ppermute(value, 'col', [(i, goes_to(i, step)) for i in range(count)])  33.7 us
    ppermute x21, waiting for transfers between devices, move(): lax.ppermute(value, 'col', [(i, goes_to(i, step)) for i in range(count)])  25.6 us
    ppermute x10, starting transfers between devices, shift(): return lax.ppermute(value, axis, pairs)  23 us
    pallas_call x10, Pallas kernels, call(): pl.pallas_call(body, out_shape=tuple(outs), in_specs=specs, out_specs=tup...  22.5 us
    ppermute x10, waiting for transfers between devices, shift(): return lax.ppermute(value, axis, pairs)  7.92 us
    unnamed x36, local copies, waits for them, and re-layouts  2.77 us
  transfers between devices with their start and end apart: 31, of which 13 were waited for; matrix products, arithmetic and copies ran while one was open for 0% of the time, Pallas kernels for 14%

profile of v1, /device:TPU:0, one launch (start us, length us, event | category | flops | bytes accessed | tf_op | source)
XLA Modules:
  0.0 119.5 jit_solution(16100697440769388597)
XLA Ops:
  3.2 5.5 %collective-permute-start.15 = (bf16[2,256,128]{2,1,0:T(8,128)(2,1)S(1)}, bf16[2,256,128]{2,1,0:T(8,128)(2,1)S(1)}, u32[]{:S(2)}, u32[]{:S(2)}) collective-permute-start(bf16[2,256,128]{2,1,0:T(8,128)(2,1)S(1)} %get-tuple-element.61), channel_id=1, source_target_pairs={{0,1},{1,2},{2,3},{3,4},{4,5},{5,6},{6,7},{8,9},{9,10},{10,11},{11... | collective-permute-start | bytes 393224 | tf_op jit(solution)/shard_map/ppermute | solution.py:25
  10.2 3.0 %collective-permute-done.15.left = bf16[2,256,128]{2,1,0:T(8,128)(2,1)S(1)} collective-permute-done((bf16[2,256,128]{2,1,0:T(8,128)(2,1)S(1)}, bf16[2,256,128]{2,1,0:T(8,128)(2,1)S(1)}, u32[]{:S(2)}, u32[]{:S(2)}) %collective-permute-start.15) | collective-permute-done | bytes 131104 | tf_op jit(solution)/shard_map/ppermute | solution.py:25
  15.1 1.9 %collective-permute-start.17 = (bf16[2,128,512]{2,1,0:T(8,128)(2,1)}, bf16[2,128,512]{2,1,0:T(8,128)(2,1)S(1)}, u32[]{:S(2)}, u32[]{:S(2)}) collective-permute-start(bf16[2,128,512]{2,1,0:T(8,128)(2,1)} %get-tuple-element.39), channel_id=1, source_target_pairs={{0,8},{8,16},{16,24},{1,9},{9,17},{17,25},{2,10},{10,18},{18,26},{... | collective-permute-start | bytes 786440 | tf_op jit(solution)/shard_map/ppermute | solution.py:25
  18.4 3.6 %collective-permute-start.6 = (f32[5,128]{1,0:T(8,128)S(1)}, f32[5,128]{1,0:T(8,128)S(1)}, u32[]{:S(2)}, u32[]{:S(2)}) collective-permute-start(f32[5,128]{1,0:T(8,128)S(1)} %pad_add_fusion.refs_0_), channel_id=1, source_target_pairs={{0,3},{1,2},{2,1},{3,0},{4,7},{5,6},{6,5},{7,4},{8,11},{9,10},{10,... | collective-permute-start | bytes 7688 | tf_op jit(solution)/shard_map/ppermute | solution.py:350
  25.6 3.0 %collective-permute-start.3 = (f32[5,128]{1,0:T(8,128)S(1)}, f32[5,128]{1,0:T(8,128)S(1)}, u32[]{:S(2)}, u32[]{:S(2)}) collective-permute-start(f32[5,128]{1,0:T(8,128)S(1)} %pad_add_fusion.refs_0_), channel_id=1, source_target_pairs={{0,7},{1,6},{2,5},{3,4},{4,3},{5,2},{6,1},{7,0},{8,15},{9,14},{10,... | collective-permute-start | bytes 7688 | tf_op jit(solution)/shard_map/ppermute | solution.py:350
  28.6 2.1 %collective-permute-start.2 = (f32[5,128]{1,0:T(8,128)S(1)}, f32[5,128]{1,0:T(8,128)S(1)}, u32[]{:S(2)}, u32[]{:S(2)}) collective-permute-start(f32[5,128]{1,0:T(8,128)S(1)} %pad_add_fusion.refs_0_), channel_id=1, source_target_pairs={{0,6},{1,7},{2,4},{3,5},{4,2},{5,3},{6,0},{7,1},{8,14},{9,15},{10,... | collective-permute-start | bytes 7688 | tf_op jit(solution)/shard_map/ppermute | solution.py:350
  34.4 2.9 %collective-permute-done.1.refs_2_.refs_1_ = f32[5,128]{1,0:T(8,128)S(1)} collective-permute-done((f32[5,128]{1,0:T(8,128)S(1)}, f32[5,128]{1,0:T(8,128)S(1)}, u32[]{:S(2)}, u32[]{:S(2)}) %collective-permute-start.1) | collective-permute-done | bytes 2592 | tf_op jit(solution)/shard_map/ppermute | solution.py:350
  39.5 4.0 %shard_map.104 = (bf16[4,2,32,256]{3,2,1,0:T(8,128)(2,1)S(1)}, bf16[4,2,32,256]{3,2,1,0:T(8,128)(2,1)S(1)}, bf16[4,2,32,256]{3,2,1,0:T(8,128)(2,1)S(1)}, bf16[4,...) custom-call(s32[1]{0:T(128)} %bitcast.3.row, ...), custom_call_target="tpu_custom_call" | custom-call | tf_op jit(solution)/shard_map/pallas_call | solution.py:58
  44.0 2.9 %collective-permute-start.9 = (bf16[4,2,32,256]{3,2,1,0:T(8,128)(2,1)S(1)}, bf16[4,2,32,256]{3,2,1,0:T(8,128)(2,1)S(1)}, u32[]{:S(2)}, u32[]{:S(2)}) collective-permute-start(bf16[4,2,32,256]{3,2,1,0:T(8,128)(2,1)S(1)} %get-tuple-element.33), channel_id=1, source_target_pairs={{0,5},{1,4},{2,7},{3,6},{4,1},{5,0},{6,3},{7,2},{8,13},{9,12},{10,... | collective-permute-start | bytes 393224 | tf_op jit(solution)/shard_map/ppermute | solution.py:350
  48.4 3.0 %collective-permute-start.11 = (bf16[4,2,32,256]{3,2,1,0:T(8,128)(2,1)}, bf16[4,2,32,256]{3,2,1,0:T(8,128)(2,1)S(1)}, u32[]{:S(2)}, u32[]{:S(2)}) collective-permute-start(bf16[4,2,32,256]{3,2,1,0:T(8,128)(2,1)} %get-tuple-element.35), channel_id=1, source_target_pairs={{0,7},{1,6},{2,5},{3,4},{4,3},{5,2},{6,1},{7,0},{8,15},{9,14},{10,... | collective-permute-start | bytes 393224 | tf_op jit(solution)/shard_map/ppermute | solution.py:350
  52.2 8.7 %collective-permute-done.8.refs_1_ = bf16[4,2,32,256]{3,2,1,0:T(8,128)(2,1)S(1)} collective-permute-done((bf16[4,2,32,256]{3,2,1,0:T(8,128)(2,1)S(1)}, bf16[4,2,32,256]{3,2,1,0:T(8,128)(2,1)S(1)}, u32[]{:S(2)}, u32[]{:S(2)}) %collective-permute-start.8) | collective-permute-done | bytes 131104 | tf_op jit(solution)/shard_map/ppermute | solution.py:350
  61.0 2.6 %collective-permute-done.9.refs_2_ = bf16[4,2,32,256]{3,2,1,0:T(8,128)(2,1)S(1)} collective-permute-done((bf16[4,2,32,256]{3,2,1,0:T(8,128)(2,1)S(1)}, bf16[4,2,32,256]{3,2,1,0:T(8,128)(2,1)S(1)}, u32[]{:S(2)}, u32[]{:S(2)}) %collective-permute-start.9) | collective-permute-done | bytes 131104 | tf_op jit(solution)/shard_map/ppermute | solution.py:350
  65.0 2.5 %shard_map.106 = (bf16[4,2,256,256]{3,2,1,0:T(8,128)(2,1)S(1)}, f32[4,256,256]{2,1,0:T(8,128)S(1)}) custom-call(s32[2,4]{1,0:T(2,128)S(1)} %bitcast.10, f32[2,256,256]{2,1,0:T(8,128)S(1)} %copy-done.1, bf16[2,256,128]{2,1,0:T(8,128)(2,1)S(1)} %collective-permute-done.15.left, bf16[2,256,128]{2,1,0:T(8,128)(2,1)S(1)} %collective-permute-done.16.right, ...), custom_call_target="tpu_custom_call" | custom-call | tf_op jit(solution)/shard_map/pallas_call | solution.py:58
  67.5 2.3 %collective-permute-done.14.refs_7_ = bf16[4,2,32,256]{3,2,1,0:T(8,128)(2,1)} collective-permute-done((bf16[4,2,32,256]{3,2,1,0:T(8,128)(2,1)}, bf16[4,2,32,256]{3,2,1,0:T(8,128)(2,1)}, u32[]{:S(2)}, u32[]{:S(2)}) %collective-permute-start.14) | collective-permute-done | bytes 131104 | tf_op jit(solution)/shard_map/ppermute | solution.py:350
  69.8 5.7 %shard_map.107 = (bf16[4,2,32,256]{3,2,1,0:T(8,128)(2,1)S(1)}, bf16[4,2,32,256]{3,2,1,0:T(8,128)(2,1)S(1)}, bf16[4,2,32,256]{3,2,1,0:T(8,128)(2,1)S(1)}, bf16[4,...) custom-call(s32[1,1]{1,0:T(1,128)S(6)} %copy.11.counts, ...), custom_call_target="tpu_custom_call" | custom-call | tf_op jit(solution)/shard_map/pallas_call | solution.py:58
  75.5 2.3 %collective-permute-start.23 = (bf16[4,2,32,256]{3,2,1,0:T(8,128)(2,1)S(1)}, bf16[4,2,32,256]{3,2,1,0:T(8,128)(2,1)S(1)}, u32[]{:S(2)}, u32[]{:S(2)}) collective-permute-start(bf16[4,2,32,256]{3,2,1,0:T(8,128)(2,1)S(1)} %get-tuple-element.50), channel_id=1, source_target_pairs={{0,4},{1,5},{2,6},{3,7},{4,0},{5,1},{6,2},{7,3},{8,12},{9,13},{10,... | collective-permute-start | bytes 393224 | tf_op jit(solution)/shard_map/ppermute | solution.py:350
  78.8 2.5 %collective-permute-start.29 = (bf16[4,2,32,256]{3,2,1,0:T(8,128)(2,1)S(1)}, bf16[4,2,32,256]{3,2,1,0:T(8,128)(2,1)S(1)}, u32[]{:S(2)}, u32[]{:S(2)}) collective-permute-start(bf16[4,2,32,256]{3,2,1,0:T(8,128)(2,1)S(1)} %get-tuple-element.57), channel_id=1, source_target_pairs={{0,3},{1,2},{2,1},{3,0},{4,7},{5,6},{6,5},{7,4},{8,11},{9,10},{10,... | collective-permute-start | bytes 393224 | tf_op jit(solution)/shard_map/ppermute | solution.py:350
  84.4 4.4 %collective-permute-start.26 = (bf16[4,2,32,256]{3,2,1,0:T(8,128)(2,1)S(1)}, bf16[4,2,32,256]{3,2,1,0:T(8,128)(2,1)S(1)}, u32[]{:S(2)}, u32[]{:S(2)}) collective-permute-start(bf16[4,2,32,256]{3,2,1,0:T(8,128)(2,1)S(1)} %get-tuple-element.53), channel_id=1, source_target_pairs={{0,7},{1,6},{2,5},{3,4},{4,3},{5,2},{6,1},{7,0},{8,15},{9,14},{10,... | collective-permute-start | bytes 393224 | tf_op jit(solution)/shard_map/ppermute | solution.py:350
  88.8 2.9 %shard_map.108 = (bf16[2,128,512]{2,1,0:T(8,128)(2,1)S(1)}, f32[2,256,512]{2,1,0:T(8,128)S(1)}, bf16[2,128,512]{2,1,0:T(8,128)(2,1)S(1)}) custom-call(s32[2,4]{1,0:T(2,128)S(1)} %bitcast.11, f32[4,2,256,256]{3,2,1,0:T(8,128)S(1)} %get-tuple-element.43.pieces), custom_call_target="tpu_custom_call" | custom-call | tf_op jit(solution)/shard_map/pallas_call | solution.py:58
  93.1 3.6 %collective-permute-done.29.refs_7_ = bf16[4,2,32,256]{3,2,1,0:T(8,128)(2,1)S(1)} collective-permute-done((bf16[4,2,32,256]{3,2,1,0:T(8,128)(2,1)S(1)}, bf16[4,2,32,256]{3,2,1,0:T(8,128)(2,1)S(1)}, u32[]{:S(2)}, u32[]{:S(2)}) %collective-permute-start.29) | collective-permute-done | bytes 131104 | tf_op jit(solution)/shard_map/ppermute | solution.py:350
  97.9 2.3 %shard_map.111 = (f32[12,2,32,256]{3,2,1,0:T(8,128)S(1)}, f32[12,2,32,256]{3,2,1,0:T(8,128)S(1)}) custom-call(s32[1]{0:T(128)} %bitcast.3.row, f32[5,128]{1,0:T(8,128)S(1)} %copy-done.7, f32[5,128]{1,0:T(8,128)S(1)} %copy-done.13, f32[5,128]{1,0:T(8,128)S(1)} %copy-done.11, f32[5,128]{1,0:T(8,128)S(1)} %copy-done.9, ...), custom_call_target="tpu_custom_call" | custom-call | tf_op jit(solution)/shard_map/pallas_call | solution.py:58
  101.8 4.0 %collective-permute-start.30 = (bf16[12,2,32,256]{3,2,1,0:T(8,128)(2,1)S(1)}, bf16[12,2,32,256]{3,2,1,0:T(8,128)(2,1)S(1)}, u32[]{:S(2)}, u32[]{:S(2)}) collective-permute-start(bf16[12,2,32,256]{3,2,1,0:T(8,128)(2,1)S(1)} %shard_map.113), channel_id=1, source_target_pairs={{0,8},{8,16},{16,24},{1,9},{9,17},{17,25},{2,10},{10,18},{18,26},{... | collective-permute-start | bytes 1179656 | tf_op jit(solution)/shard_map/ppermute | solution.py:25
  106.1 3.8 %collective-permute-start.21 = (bf16[2,256,128]{2,1,0:T(8,128)(2,1)S(1)}, bf16[2,256,128]{2,1,0:T(8,128)(2,1)S(1)}, u32[]{:S(2)}, u32[]{:S(2)}) collective-permute-start(bf16[2,256,128]{2,1,0:T(8,128)(2,1)S(1)} %get-tuple-element.48), channel_id=1, source_target_pairs={{0,1},{1,2},{2,3},{3,4},{4,5},{5,6},{6,7},{8,9},{9,10},{10,11},{11... | collective-permute-start | bytes 393224 | tf_op jit(solution)/shard_map/ppermute | solution.py:25
  113.0 4.7 %collective-permute-done.22.got_right = bf16[2,256,128]{2,1,0:T(8,128)(2,1)S(1)} collective-permute-done((bf16[2,256,128]{2,1,0:T(8,128)(2,1)S(1)}, bf16[2,256,128]{2,1,0:T(8,128)(2,1)S(1)}, u32[]{:S(2)}, u32[]{:S(2)}) %collective-permute-start.22) | collective-permute-done | bytes 131104 | tf_op jit(solution)/shard_map/ppermute | solution.py:25
  (89 shorter events, 33.5 us)
Async XLA Ops:
  1.9 8.4 %collective-permute-start.16 = (bf16[2,256,128]{2,1,0:T(8,128)(2,1)S(1)}, bf16[2,256,128]{2,1,0:T(8,128)(2,1)S(1)}, u32[]{:S(2)}, u32[]{:S(2)}) collective-permute-start(bf16[2,256,128]{2,1,0:T(8,128)(2,1)S(1)} %get-tuple-element.60), channel_id=1, source_target_pairs={{1,0},{2,1},{3,2},{4,3},{5,4},{6,5},{7,6},{9,8},{10,9},{11,10},{12... | collective-permute-start | bytes 393224 | tf_op jit(solution)/shard_map/ppermute | solution.py:25
  3.2 10.0 %collective-permute-start.15 = (bf16[2,256,128]{2,1,0:T(8,128)(2,1)S(1)}, bf16[2,256,128]{2,1,0:T(8,128)(2,1)S(1)}, u32[]{:S(2)}, u32[]{:S(2)}) collective-permute-start(bf16[2,256,128]{2,1,0:T(8,128)(2,1)S(1)} %get-tuple-element.61), channel_id=1, source_target_pairs={{0,1},{1,2},{2,3},{3,4},{4,5},{5,6},{6,7},{8,9},{9,10},{10,11},{11... | collective-permute-start | bytes 393224 | tf_op jit(solution)/shard_map/ppermute | solution.py:25
  8.7 29.8 %collective-permute-start.7 = (bf16[1,12,2,32,256]{4,3,2,1,0:T(8,128)(2,1)}, bf16[1,12,2,32,256]{4,3,2,1,0:T(8,128)(2,1)S(1)}, u32[]{:S(2)}, u32[]{:S(2)}) collective-permute-start(bf16[1,12,2,32,256]{4,3,2,1,0:T(8,128)(2,1)} %refs_8_.1), channel_id=1, source_target_pairs={{8,0},{16,8},{24,16},{9,1},{17,9},{25,17},{10,2},{18,10},{26,18},{... | collective-permute-start | bytes 1179656 | tf_op jit(solution)/shard_map/ppermute | solution.py:25
  15.1 33.2 %collective-permute-start.17 = (bf16[2,128,512]{2,1,0:T(8,128)(2,1)}, bf16[2,128,512]{2,1,0:T(8,128)(2,1)S(1)}, u32[]{:S(2)}, u32[]{:S(2)}) collective-permute-start(bf16[2,128,512]{2,1,0:T(8,128)(2,1)} %get-tuple-element.39), channel_id=1, source_target_pairs={{0,8},{8,16},{16,24},{1,9},{9,17},{17,25},{2,10},{10,18},{18,26},{... | collective-permute-start | bytes 786440 | tf_op jit(solution)/shard_map/ppermute | solution.py:25
  17.0 34.3 %collective-permute-start.18 = (bf16[2,128,512]{2,1,0:T(8,128)(2,1)}, bf16[2,128,512]{2,1,0:T(8,128)(2,1)S(1)}, u32[]{:S(2)}, u32[]{:S(2)}) collective-permute-start(bf16[2,128,512]{2,1,0:T(8,128)(2,1)} %get-tuple-element.40), channel_id=1, source_target_pairs={{8,0},{16,8},{24,16},{9,1},{17,9},{25,17},{10,2},{18,10},{26,18},{... | collective-permute-start | bytes 786440 | tf_op jit(solution)/shard_map/ppermute | solution.py:25
  25.6 6.3 %collective-permute-start.3 = (f32[5,128]{1,0:T(8,128)S(1)}, f32[5,128]{1,0:T(8,128)S(1)}, u32[]{:S(2)}, u32[]{:S(2)}) collective-permute-start(f32[5,128]{1,0:T(8,128)S(1)} %pad_add_fusion.refs_0_), channel_id=1, source_target_pairs={{0,7},{1,6},{2,5},{3,4},{4,3},{5,2},{6,1},{7,0},{8,15},{9,14},{10,... | collective-permute-start | bytes 7688 | tf_op jit(solution)/shard_map/ppermute | solution.py:350
  43.5 17.5 %collective-permute-start.8 = (bf16[4,2,32,256]{3,2,1,0:T(8,128)(2,1)S(1)}, bf16[4,2,32,256]{3,2,1,0:T(8,128)(2,1)S(1)}, u32[]{:S(2)}, u32[]{:S(2)}) collective-permute-start(bf16[4,2,32,256]{3,2,1,0:T(8,128)(2,1)S(1)} %get-tuple-element.32), channel_id=1, source_target_pairs={{0,4},{1,5},{2,6},{3,7},{4,0},{5,1},{6,2},{7,3},{8,12},{9,13},{10,... | collective-permute-start | bytes 393224 | tf_op jit(solution)/shard_map/ppermute | solution.py:350
  44.0 19.6 %collective-permute-start.9 = (bf16[4,2,32,256]{3,2,1,0:T(8,128)(2,1)S(1)}, bf16[4,2,32,256]{3,2,1,0:T(8,128)(2,1)S(1)}, u32[]{:S(2)}, u32[]{:S(2)}) collective-permute-start(bf16[4,2,32,256]{3,2,1,0:T(8,128)(2,1)S(1)} %get-tuple-element.33), channel_id=1, source_target_pairs={{0,5},{1,4},{2,7},{3,6},{4,1},{5,0},{6,3},{7,2},{8,13},{9,12},{10,... | collective-permute-start | bytes 393224 | tf_op jit(solution)/shard_map/ppermute | solution.py:350
  46.9 20.6 %collective-permute-start.10 = (bf16[4,2,32,256]{3,2,1,0:T(8,128)(2,1)}, bf16[4,2,32,256]{3,2,1,0:T(8,128)(2,1)S(1)}, u32[]{:S(2)}, u32[]{:S(2)}) collective-permute-start(bf16[4,2,32,256]{3,2,1,0:T(8,128)(2,1)} %get-tuple-element.34), channel_id=1, source_target_pairs={{0,6},{1,7},{2,4},{3,5},{4,2},{5,3},{6,0},{7,1},{8,14},{9,15},{10,... | collective-permute-start | bytes 393224 | tf_op jit(solution)/shard_map/ppermute | solution.py:350
  48.4 19.1 %collective-permute-start.11 = (bf16[4,2,32,256]{3,2,1,0:T(8,128)(2,1)}, bf16[4,2,32,256]{3,2,1,0:T(8,128)(2,1)S(1)}, u32[]{:S(2)}, u32[]{:S(2)}) collective-permute-start(bf16[4,2,32,256]{3,2,1,0:T(8,128)(2,1)} %get-tuple-element.35), channel_id=1, source_target_pairs={{0,7},{1,6},{2,5},{3,4},{4,3},{5,2},{6,1},{7,0},{8,15},{9,14},{10,... | collective-permute-start | bytes 393224 | tf_op jit(solution)/shard_map/ppermute | solution.py:350
  51.4 16.1 %collective-permute-start.12 = (bf16[4,2,32,256]{3,2,1,0:T(8,128)(2,1)}, bf16[4,2,32,256]{3,2,1,0:T(8,128)(2,1)}, u32[]{:S(2)}, u32[]{:S(2)}) collective-permute-start(bf16[4,2,32,256]{3,2,1,0:T(8,128)(2,1)} %get-tuple-element.36), channel_id=1, source_target_pairs={{0,1},{1,0},{2,3},{3,2},{4,5},{5,4},{6,7},{7,6},{8,9},{9,8},{10,11... | collective-permute-start | bytes 393224 | tf_op jit(solution)/shard_map/ppermute | solution.py:350
  61.0 6.5 %collective-permute-start.13 = (bf16[4,2,32,256]{3,2,1,0:T(8,128)(2,1)}, bf16[4,2,32,256]{3,2,1,0:T(8,128)(2,1)}, u32[]{:S(2)}, u32[]{:S(2)}) collective-permute-start(bf16[4,2,32,256]{3,2,1,0:T(8,128)(2,1)} %get-tuple-element.37), channel_id=1, source_target_pairs={{0,2},{1,3},{2,0},{3,1},{4,6},{5,7},{6,4},{7,5},{8,10},{9,11},{10,... | collective-permute-start | bytes 393224 | tf_op jit(solution)/shard_map/ppermute | solution.py:350
  75.5 7.6 %collective-permute-start.23 = (bf16[4,2,32,256]{3,2,1,0:T(8,128)(2,1)S(1)}, bf16[4,2,32,256]{3,2,1,0:T(8,128)(2,1)S(1)}, u32[]{:S(2)}, u32[]{:S(2)}) collective-permute-start(bf16[4,2,32,256]{3,2,1,0:T(8,128)(2,1)S(1)} %get-tuple-element.50), channel_id=1, source_target_pairs={{0,4},{1,5},{2,6},{3,7},{4,0},{5,1},{6,2},{7,3},{8,12},{9,13},{10,... | collective-permute-start | bytes 393224 | tf_op jit(solution)/shard_map/ppermute | solution.py:350
  77.8 6.6 %collective-permute-start.27 = (bf16[4,2,32,256]{3,2,1,0:T(8,128)(2,1)S(1)}, bf16[4,2,32,256]{3,2,1,0:T(8,128)(2,1)S(1)}, u32[]{:S(2)}, u32[]{:S(2)}) collective-permute-start(bf16[4,2,32,256]{3,2,1,0:T(8,128)(2,1)S(1)} %get-tuple-element.55), channel_id=1, source_target_pairs={{0,1},{1,0},{2,3},{3,2},{4,5},{5,4},{6,7},{7,6},{8,9},{9,8},{10,11... | collective-permute-start | bytes 393224 | tf_op jit(solution)/shard_map/ppermute | solution.py:350
  78.8 12.9 %collective-permute-start.28 = (bf16[4,2,32,256]{3,2,1,0:T(8,128)(2,1)S(1)}, bf16[4,2,32,256]{3,2,1,0:T(8,128)(2,1)S(1)}, u32[]{:S(2)}, u32[]{:S(2)}) collective-permute-start(bf16[4,2,32,256]{3,2,1,0:T(8,128)(2,1)S(1)} %get-tuple-element.56), channel_id=1, source_target_pairs={{0,2},{1,3},{2,0},{3,1},{4,6},{5,7},{6,4},{7,5},{8,10},{9,11},{10,... | collective-permute-start | bytes 393224 | tf_op jit(solution)/shard_map/ppermute | solution.py:350
  78.8 17.8 %collective-permute-start.29 = (bf16[4,2,32,256]{3,2,1,0:T(8,128)(2,1)S(1)}, bf16[4,2,32,256]{3,2,1,0:T(8,128)(2,1)S(1)}, u32[]{:S(2)}, u32[]{:S(2)}) collective-permute-start(bf16[4,2,32,256]{3,2,1,0:T(8,128)(2,1)S(1)} %get-tuple-element.57), channel_id=1, source_target_pairs={{0,3},{1,2},{2,1},{3,0},{4,7},{5,6},{6,5},{7,4},{8,11},{9,10},{10,... | collective-permute-start | bytes 393224 | tf_op jit(solution)/shard_map/ppermute | solution.py:350
  81.3 19.0 %collective-permute-start.24 = (bf16[4,2,32,256]{3,2,1,0:T(8,128)(2,1)S(1)}, bf16[4,2,32,256]{3,2,1,0:T(8,128)(2,1)S(1)}, u32[]{:S(2)}, u32[]{:S(2)}) collective-permute-start(bf16[4,2,32,256]{3,2,1,0:T(8,128)(2,1)S(1)} %get-tuple-element.51), channel_id=1, source_target_pairs={{0,5},{1,4},{2,7},{3,6},{4,1},{5,0},{6,3},{7,2},{8,13},{9,12},{10,... | collective-permute-start | bytes 393224 | tf_op jit(solution)/shard_map/ppermute | solution.py:350
  83.1 17.2 %collective-permute-start.25 = (bf16[4,2,32,256]{3,2,1,0:T(8,128)(2,1)S(1)}, bf16[4,2,32,256]{3,2,1,0:T(8,128)(2,1)S(1)}, u32[]{:S(2)}, u32[]{:S(2)}) collective-permute-start(bf16[4,2,32,256]{3,2,1,0:T(8,128)(2,1)S(1)} %get-tuple-element.52), channel_id=1, source_target_pairs={{0,6},{1,7},{2,4},{3,5},{4,2},{5,3},{6,0},{7,1},{8,14},{9,15},{10,... | collective-permute-start | bytes 393224 | tf_op jit(solution)/shard_map/ppermute | solution.py:350
  84.4 15.9 %collective-permute-start.26 = (bf16[4,2,32,256]{3,2,1,0:T(8,128)(2,1)S(1)}, bf16[4,2,32,256]{3,2,1,0:T(8,128)(2,1)S(1)}, u32[]{:S(2)}, u32[]{:S(2)}) collective-permute-start(bf16[4,2,32,256]{3,2,1,0:T(8,128)(2,1)S(1)} %get-tuple-element.53), channel_id=1, source_target_pairs={{0,7},{1,6},{2,5},{3,4},{4,3},{5,2},{6,1},{7,0},{8,15},{9,14},{10,... | collective-permute-start | bytes 393224 | tf_op jit(solution)/shard_map/ppermute | solution.py:350
  91.7 14.1 %collective-permute-start.19 = (bf16[2,128,512]{2,1,0:T(8,128)(2,1)S(1)}, bf16[2,128,512]{2,1,0:T(8,128)(2,1)S(1)}, u32[]{:S(2)}, u32[]{:S(2)}) collective-permute-start(bf16[2,128,512]{2,1,0:T(8,128)(2,1)S(1)} %get-tuple-element.45), channel_id=1, source_target_pairs={{0,8},{8,16},{16,24},{1,9},{9,17},{17,25},{2,10},{10,18},{18,26},{... | collective-permute-start | bytes 786440 | tf_op jit(solution)/shard_map/ppermute | solution.py:25
  96.6 9.3 %collective-permute-start.20 = (bf16[2,128,512]{2,1,0:T(8,128)(2,1)S(1)}, bf16[2,128,512]{2,1,0:T(8,128)(2,1)S(1)}, u32[]{:S(2)}, u32[]{:S(2)}) collective-permute-start(bf16[2,128,512]{2,1,0:T(8,128)(2,1)S(1)} %get-tuple-element.46), channel_id=1, source_target_pairs={{8,0},{16,8},{24,16},{9,1},{17,9},{25,17},{10,2},{18,10},{26,18},{... | collective-permute-start | bytes 786440 | tf_op jit(solution)/shard_map/ppermute | solution.py:25
  101.8 16.7 %collective-permute-start.30 = (bf16[12,2,32,256]{3,2,1,0:T(8,128)(2,1)S(1)}, bf16[12,2,32,256]{3,2,1,0:T(8,128)(2,1)S(1)}, u32[]{:S(2)}, u32[]{:S(2)}) collective-permute-start(bf16[12,2,32,256]{3,2,1,0:T(8,128)(2,1)S(1)} %shard_map.113), channel_id=1, source_target_pairs={{0,8},{8,16},{16,24},{1,9},{9,17},{17,25},{2,10},{10,18},{18,26},{... | collective-permute-start | bytes 1179656 | tf_op jit(solution)/shard_map/ppermute | solution.py:25
  106.1 6.9 %collective-permute-start.21 = (bf16[2,256,128]{2,1,0:T(8,128)(2,1)S(1)}, bf16[2,256,128]{2,1,0:T(8,128)(2,1)S(1)}, u32[]{:S(2)}, u32[]{:S(2)}) collective-permute-start(bf16[2,256,128]{2,1,0:T(8,128)(2,1)S(1)} %get-tuple-element.48), channel_id=1, source_target_pairs={{0,1},{1,2},{2,3},{3,4},{4,5},{5,6},{6,7},{8,9},{9,10},{10,11},{11... | collective-permute-start | bytes 393224 | tf_op jit(solution)/shard_map/ppermute | solution.py:25
  109.9 7.8 %collective-permute-start.22 = (bf16[2,256,128]{2,1,0:T(8,128)(2,1)S(1)}, bf16[2,256,128]{2,1,0:T(8,128)(2,1)S(1)}, u32[]{:S(2)}, u32[]{:S(2)}) collective-permute-start(bf16[2,256,128]{2,1,0:T(8,128)(2,1)S(1)} %get-tuple-element.49), channel_id=1, source_target_pairs={{1,0},{2,1},{3,2},{4,3},{5,4},{6,5},{7,6},{9,8},{10,9},{11,10},{12... | collective-permute-start | bytes 393224 | tf_op jit(solution)/shard_map/ppermute | solution.py:25
  (25 other events, 517.8 us)

commit v2 on v1

--- a/solution.py
+++ b/solution.py
@@ -16,6 +16,7 @@
 
 VMEM = pl.BlockSpec(memory_space=pltpu.VMEM)
 SMEM = pl.BlockSpec(memory_space=pltpu.SMEM)
+HBM = pl.BlockSpec(memory_space=pltpu.HBM)
 
 
 def shift(value, axis, steps):
@@ -23,6 +24,27 @@
     leading, last = (max(0, -steps), min(count, count - steps))
     pairs = [(source, source + steps) for source in range(leading, last)]
     return lax.ppermute(value, axis, pairs)
+
+
+def swap(values, axis):
+    count = lax.axis_size(axis)
+    got = []
+    for odd, value in enumerate(values):
+        pairs = []
+        for i in range(odd, count - 1, 2):
+            pairs += [(i, i + 1), (i + 1, i)]
+        got.append(lax.ppermute(value, axis, pairs) if pairs else jnp.zeros_like(value))
+    return got
+
+
+def by_side(index, low, high):
+    even = index % 2 == 0
+    return jnp.where(even, high, low), jnp.where(even, low, high)
+
+
+def from_sides(index, first, second):
+    high, low = by_side(index, second, first)
+    return low, high
 
 
 def dft_tables(length):
@@ -39,7 +61,7 @@
 
 def partners(axis):
     count = lax.axis_size(axis)
-    steps = list(range(count // 2, count)) + list(range(1, count // 2))
+    steps = list(range(1, count))
     paired = count & (count - 1) == 0
 
     def goes_to(index, step):
@@ -53,6 +75,12 @@
 
 def call(body, outs, *operands, scratch=(), limit=20):
     arrays = [o[0] if isinstance(o, tuple) else o for o in operands]
+    arrays = [
+        pltpu.with_memory_space_constraint(a, pltpu.HBM)
+        if isinstance(o, tuple) and o[1] is HBM
+        else a
+        for a, o in zip(arrays, operands)
+    ]
     specs = [o[1] if isinstance(o, tuple) else VMEM for o in operands]
     outs = [jax.ShapeDtypeStruct(shape, dtype) for shape, dtype in outs]
     return pl.pallas_call(
@@ -78,12 +106,15 @@
 
 def slab_kernel(count, row, *refs):
     own, follower = refs[count : count + 2]
-    outs = refs[count + 2 : -3]
-    table, held, sem = refs[-3:]
+    outs = refs[count + 2 : -5]
+    table, near, held, sem, near_sem = refs[-5:]
+    copy_own = pltpu.make_async_copy(own, near, near_sem)
+    copy_own.start()
     copies = fetch(refs[:count], held, sem)
     num_modes = own.shape[1]
-    table[0] = own[0].astype(jnp.float32)
     table[1] = follower[0].astype(jnp.float32)
+    copy_own.wait()
+    table[0] = near[0].astype(jnp.float32)
     next_row = (row[0] + 1).astype(jnp.float32)
     slots = outs[0].shape[0]
     for copy in copies:
@@ -112,20 +143,49 @@
         [(shape, jnp.bfloat16)] * len(weights),
         (row, SMEM),
         *weights,
-        own,
+        (own, HBM),
         follower,
-        scratch=[pltpu.VMEM((2,) + own.shape[1:], jnp.float32)]
-        + held_weights(len(weights), weights[0]),
-    )
-
-
-def widen_kernel(tile, left, right, top, bottom):
-    half = left.shape[-1]
-    rows, cols = tile.shape[1:]
-    for out, start in ((top, 0), (bottom, rows - half)):
-        out[:, :, :half] = left[:, start : start + half]
-        out[:, :, half : half + cols] = tile[:, start : start + half].astype(jnp.bfloat16)
-        out[:, :, half + cols :] = right[:, start : start + half]
+        scratch=[pltpu.VMEM((2,) + own.shape[1:], jnp.float32), pltpu.VMEM(own.shape, own.dtype)]
+        + held_weights(len(weights), weights[0])
+        + [pltpu.SemaphoreType.DMA],
+    )
+
+
+def prepare_kernel(
+    me, coeffs, region, tile, payload, low, even, odd, coeffs_held, region_held, tile_held, sem
+):
+    slots, num_modes = coeffs.shape[2:]
+    half = even.shape[2]
+    copies = [
+        pltpu.make_async_copy(source, held, sem.at[at])
+        for at, (source, held) in enumerate(
+            ((coeffs, coeffs_held), (region, region_held), (tile, tile_held))
+        )
+    ]
+    for copy in copies:
+        copy.start()
+    payload[...] = jnp.zeros_like(payload)
+    for copy in copies:
+        copy.wait()
+    payload[:slots, :num_modes] = coeffs_held[0, 0]
+    payload[slots:, :slots] = region_held[0].astype(jnp.float32)
+    low[...] = tile_held[...].astype(jnp.bfloat16)
+    first, second = by_side(me[0], low[:, :, :half], low[:, :, low.shape[2] - half :])
+    even[...] = first
+    odd[...] = second
+
+
+def widen_kernel(row, me, tile, even, odd, first, second):
+    half = even.shape[2]
+    rows, _ = tile.shape[1:]
+
+    def extended(start):
+        left, right = from_sides(
+            me[0], even[:, start : start + half], odd[:, start : start + half]
+        )
+        return jnp.concatenate([left, tile[:, start : start + half], right], axis=2)
+
+    first[...], second[...] = by_side(row[0], extended(0), extended(rows - half))
 
 
 def corner_of(corners, slot, half, limit):
@@ -137,15 +197,21 @@
     return base_row, rest_row, base_col, rest_col
 
 
-def window_kernel(corners, tile, left, right, top, bottom, intensity, out, measured, ext):
+def window_kernel(
+    row, me, corners, tile, side_even, side_odd, end_even, end_odd, intensity, out, measured, ext,
+    held, sem,
+):
+    copy = pltpu.make_async_copy(intensity, held, sem)
+    copy.start()
     size = out.shape[-1]
-    half = left.shape[-1]
+    half = side_even.shape[-1]
     rows, cols = tile.shape[1:]
+    left, right = from_sides(me[0], side_even[...], side_odd[...])
+    top, bottom = from_sides(row[0], end_even[...], end_odd[...])
     for part in range(2):
         ext[part, :half, : cols + 2 * half] = top[part].astype(jnp.float32)
         ext[part, half : half + rows, :half] = left[part].astype(jnp.float32)
-        low = tile[part].astype(jnp.bfloat16)
-        ext[part, half : half + rows, half : half + cols] = low.astype(jnp.float32)
+        ext[part, half : half + rows, half : half + cols] = tile[part].astype(jnp.float32)
         ext[part, half : half + rows, half + cols : cols + 2 * half] = right[part].astype(jnp.float32)
         ext[part, half + rows : 2 * half + rows, : cols + 2 * half] = bottom[part].astype(jnp.float32)
     tall = size + SUBLANES
@@ -160,28 +226,34 @@
             block = pltpu.roll(block, lax.rem(tall - rest_row, tall), 0)[:size]
             block = pltpu.roll(block, lax.rem(wide - rest_col, wide), 1)[:, :size]
             out[slot, part] = block.astype(jnp.bfloat16)
-        measured[slot] = jnp.sqrt(intensity[0, 0, slot].astype(jnp.float32))
         return carry
 
     lax.fori_loop(0, out.shape[0], slot_step, 0)
-
-
-def windows_of(corners, tile, left, right, top, bottom, intensity):
+    copy.wait()
+    for slot in range(out.shape[0]):
+        measured[slot] = jnp.sqrt(held[0, 0, slot].astype(jnp.float32))
+
+
+def windows_of(row, me, corners, tile, sides, ends, intensity):
     slot_count = intensity.shape[2]
     size = intensity.shape[-1]
-    half = left.shape[-1]
+    half = sides[0].shape[-1]
     extent = (2, tile.shape[1] + 2 * half + SUBLANES, tile.shape[2] + 2 * half + LANES)
     return call(
         window_kernel,
         [((slot_count, 2, size, size), jnp.bfloat16), ((slot_count, size, size), jnp.float32)],
+        (row, SMEM),
+        (me, SMEM),
         (corners, SMEM),
         tile,
-        left,
-        right,
-        top,
-        bottom,
-        intensity,
-        scratch=[pltpu.VMEM(extent, jnp.float32)],
+        *sides,
+        *ends,
+        (intensity, HBM),
+        scratch=[
+            pltpu.VMEM(extent, jnp.float32),
+            pltpu.VMEM(intensity.shape, intensity.dtype),
+            pltpu.SemaphoreType.DMA,
+        ],
     )
 
 
@@ -232,7 +304,7 @@
         out[...] = terms[:, :, pl.ds(start, rows)]
 
 
-def place_kernel(half, corners, pieces, top, middle, bottom, accum):
+def place_kernel(half, row, corners, pieces, first, middle, second, accum):
     size = pieces.shape[-1]
     rows = middle.shape[1]
     width = middle.shape[2]
@@ -252,29 +324,33 @@
             block = pltpu.roll(block, rest_row, 0)
             where = (part, pl.ds(base_row, size + SUBLANES), pl.ds(base_col, size + LANES))
             accum[where] += block
-    top[...] = accum[:, :half, :width].astype(jnp.bfloat16)
     middle[...] = accum[:, half : half + rows, :width]
-    bottom[...] = accum[:, half + rows : 2 * half + rows, :width].astype(jnp.bfloat16)
-
-
-def rows_kernel(middle, got_top, got_bottom, left, center, right, total):
-    half = got_top.shape[1]
+    top = accum[:, :half, :width].astype(jnp.bfloat16)
+    bottom = accum[:, half + rows : 2 * half + rows, :width].astype(jnp.bfloat16)
+    first[...], second[...] = by_side(row[0], top, bottom)
+
+
+def rows_kernel(row, me, middle, even, odd, first, center, second, total):
+    half = even.shape[1]
     rows = middle.shape[1]
     cols = center.shape[2]
+    got_top, got_bottom = from_sides(row[0], even[...], odd[...])
     total[...] = middle[...]
-    total[:, :half] += got_top[...].astype(jnp.float32)
-    total[:, rows - half :] += got_bottom[...].astype(jnp.float32)
-    left[...] = total[:, :, :half].astype(jnp.bfloat16)
+    total[:, :half] += got_top.astype(jnp.float32)
+    total[:, rows - half :] += got_bottom.astype(jnp.float32)
     center[...] = total[:, :, half : half + cols]
-    right[...] = total[:, :, half + cols :].astype(jnp.bfloat16)
-
-
-def cols_kernel(center, got_left, got_right, out):
-    half = got_left.shape[2]
+    left = total[:, :, :half].astype(jnp.bfloat16)
+    right = total[:, :, half + cols :].astype(jnp.bfloat16)
+    first[...], second[...] = by_side(me[0], left, right)
+
+
+def cols_kernel(me, center, even, odd, out):
+    half = even.shape[2]
     cols = out.shape[2]
+    got_left, got_right = from_sides(me[0], even[...], odd[...])
     out[...] = center[...]
-    out[:, :, :half] += got_left[...].astype(jnp.float32)
-    out[:, :, cols - half :] += got_right[...].astype(jnp.float32)
+    out[:, :, :half] += got_left.astype(jnp.float32)
+    out[:, :, cols - half :] += got_right.astype(jnp.float32)
 
 
 def sums_kernel(count, goals, row, *refs):
@@ -343,15 +419,24 @@
     steps, goes_to, comes_from = partners("col")
     every = [0] + steps
     count = lax.axis_size("col")
-    crossing = steps[: count - count // 2]
-    staying = steps[count - count // 2 :]
+    staying = steps[: count // 2 - 1]
+    crossing = steps[count // 2 - 1 :]
 
     def move(value, step):
         return lax.ppermute(value, "col", [(i, goes_to(i, step)) for i in range(count)])
 
     follower = shift(modes, "row", -1)
-    payload = jnp.pad(coeffs[0, 0], ((0, 1), (0, LANES - num_modes))) + jnp.pad(
-        region[0].astype(jnp.float32), ((slot_count, 0), (0, LANES - slot_count))
+    side = (2, rows, half)
+    payload, low, *edges = call(
+        prepare_kernel,
+        [((slot_count + 1, LANES), jnp.float32), (object_field.shape, jnp.bfloat16)]
+        + [(side, jnp.bfloat16)] * 2,
+        (me, SMEM),
+        (coeffs, HBM),
+        (region, HBM),
+        (object_field, HBM),
+        scratch=[pltpu.VMEM(x.shape, x.dtype) for x in (coeffs, region, object_field)]
+        + [pltpu.SemaphoreType.DMA((3,))],
     )
     weights = {0: payload}
     for step in steps:
@@ -360,23 +445,18 @@
     def made_for(step):
         return weights[step] if goes_to(1, step) == comes_from(1, step) else weights[count - step]
 
-    low = object_field.astype(jnp.bfloat16)
-    left = shift(low[:, :, cols - half :], "col", 1)
-    right = shift(low[:, :, :half], "col", -1)
+    sides = swap(edges, "col")
     wide = (2, half, cols + 2 * half)
-    wide_top, wide_bottom = call(
-        widen_kernel, [(wide, jnp.bfloat16)] * 2, object_field, left, right
-    )
-    top = shift(wide_bottom, "row", 1)
-    bottom = shift(wide_top, "row", -1)
+    ends = call(widen_kernel, [(wide, jnp.bfloat16)] * 2, (row, SMEM), (me, SMEM), low, *sides)
+    ends = swap(ends, "row")
 
     blocks = {}
     made = slabs(row, [made_for(step) for step in every], modes, follower)
     for step, slab in zip(every, made):
         blocks[step] = move(slab, step) if step else slab
 
-    corners = offsets[0, 0].T
-    windows, measured = windows_of(corners, object_field, left, right, top, bottom, intensity)
+    corners = pltpu.with_memory_space_constraint(offsets[0, 0].T, pltpu.HBM)
+    windows, measured = windows_of(row, me, corners, low, sides, ends, intensity)
     whole = (slot_count, 2, size, size)
     *terms, placed = call(
         functools.partial(dft_kernel, goes_to, comes_from, every),
@@ -394,28 +474,27 @@
     received = {step: move(terms[step], step) if step else terms[step] for step in every}
 
     extent = (2, rows + 2 * half + SUBLANES, cols + 2 * half + LANES)
-    over_top, middle, over_bottom = call(
+    even, middle, odd = call(
         functools.partial(place_kernel, half),
         [(wide, jnp.bfloat16), ((2, rows, cols + 2 * half), jnp.float32), (wide, jnp.bfloat16)],
+        (row, SMEM),
         (corners, SMEM),
         placed,
         scratch=[pltpu.VMEM(extent, jnp.float32)],
     )
-    got_top = shift(over_bottom, "row", 1)
-    got_bottom = shift(over_top, "row", -1)
-    side = ((2, rows, half), jnp.bfloat16)
-    over_left, center, over_right = call(
+    over_ends = swap([even, odd], "row")
+    even, center, odd = call(
         rows_kernel,
-        [side, ((2, rows, cols), jnp.float32), side],
+        [(side, jnp.bfloat16), ((2, rows, cols), jnp.float32), (side, jnp.bfloat16)],
+        (row, SMEM),
+        (me, SMEM),
         middle,
-        got_top,
-        got_bottom,
+        *over_ends,
         scratch=[pltpu.VMEM((2, rows, cols + 2 * half), jnp.float32)],
     )
-    got_left = shift(over_right, "col", 1)
-    got_right = shift(over_left, "col", -1)
+    over_sides = swap([even, odd], "col")
     (object_grad,) = call(
-        cols_kernel, [(object_field.shape, jnp.float32)], center, got_left, got_right
+        cols_kernel, [(object_field.shape, jnp.float32)], (me, SMEM), center, *over_sides
     )
 
     def add_up(group, goals, added, dtypes):

time: 120 us -> 108 us (0.900)
  the two profiles are of different devices: /device:TPU:0 before, /device:TPU:8 now
where the time goes in v2:
time: 108 us
  starting transfers between devices  43.1 us (40%)
  waiting for transfers between devices  40.4 us (37%)
  Pallas kernels  21.8 us (20%)
  between operations  1.51 us (1%)
    ppermute x21, starting transfers between devices, move(): lax.ppermute(value, 'col', [(i, goes_to(i, step)) for i in range(count)])  32.2 us
    ppermute x21, waiting for transfers between devices, move(): lax.ppermute(value, 'col', [(i, goes_to(i, step)) for i in range(count)])  29.3 us
    pallas_call x11, Pallas kernels, call(): pl.pallas_call(body, out_shape=tuple(outs), in_specs=specs, out_specs=tup...  21.8 us
    ppermute x8, waiting for transfers between devices, swap(): lax.ppermute(value, axis, pairs)  11.2 us
    ppermute x8, starting transfers between devices, swap(): lax.ppermute(value, axis, pairs)  8.17 us
    ppermute x2, starting transfers between devices, shift(): return lax.ppermute(value, axis, pairs)  2.74 us
  transfers between devices with their start and end apart: 31, of which 17 were waited for; matrix products, arithmetic and copies ran while one was open for 0% of the time, Pallas kernels for 16%

profile of v2, /device:TPU:8, one launch (start us, length us, event | category | flops | bytes accessed | tf_op | source)
XLA Modules:
  0.0 107.9 jit_solution(13934870153046235384)
XLA Ops:
  4.8 1.9 %collective-permute-start.16 = (bf16[2,256,128]{2,1,0:T(8,128)(2,1)S(1)}, bf16[2,256,128]{2,1,0:T(8,128)(2,1)S(1)}, u32[]{:S(2)}, u32[]{:S(2)}) collective-permute-start(bf16[2,256,128]{2,1,0:T(8,128)(2,1)S(1)} %get-tuple-element.46), channel_id=1, source_target_pairs={{1,2},{2,1},{3,4},{4,3},{5,6},{6,5},{9,10},{10,9},{11,12},{12,11},... | collective-permute-start | bytes 393224 | tf_op jit(solution)/shard_map/ppermute | solution.py:36
  6.8 2.8 %collective-permute-done.15.even.side_even = bf16[2,256,128]{2,1,0:T(8,128)(2,1)S(1)} collective-permute-done((bf16[2,256,128]{2,1,0:T(8,128)(2,1)S(1)}, bf16[2,256,128]{2,1,0:T(8,128)(2,1)S(1)}, u32[]{:S(2)}, u32[]{:S(2)}) %collective-permute-start.15) | collective-permute-done | bytes 131104 | tf_op jit(solution)/shard_map/ppermute | solution.py:36
  9.6 4.3 %collective-permute-done.16.odd.side_odd = bf16[2,256,128]{2,1,0:T(8,128)(2,1)S(1)} collective-permute-done((bf16[2,256,128]{2,1,0:T(8,128)(2,1)S(1)}, bf16[2,256,128]{2,1,0:T(8,128)(2,1)S(1)}, u32[]{:S(2)}, u32[]{:S(2)}) %collective-permute-start.16) | collective-permute-done | bytes 131104 | tf_op jit(solution)/shard_map/ppermute | solution.py:36
  16.8 2.5 %collective-permute-done.6.refs_7_.refs_3_ = f32[5,128]{1,0:T(8,128)S(1)} collective-permute-done((f32[5,128]{1,0:T(8,128)S(1)}, f32[5,128]{1,0:T(8,128)S(1)}, u32[]{:S(2)}, u32[]{:S(2)}) %collective-permute-start.6) | collective-permute-done | bytes 2592 | tf_op jit(solution)/shard_map/ppermute | solution.py:426
  19.3 2.8 %collective-permute-start.4 = (f32[5,128]{1,0:T(8,128)S(1)}, f32[5,128]{1,0:T(8,128)S(1)}, u32[]{:S(2)}, u32[]{:S(2)}) collective-permute-start(f32[5,128]{1,0:T(8,128)S(1)} %get-tuple-element.35.refs_0_), channel_id=1, source_target_pairs={{0,5},{1,4},{2,7},{3,6},{4,1},{5,0},{6,3},{7,2},{8,13},{9,12},{10,... | collective-permute-start | bytes 7688 | tf_op jit(solution)/shard_map/ppermute | solution.py:426
  24.7 2.0 %collective-permute-start.2 = (f32[5,128]{1,0:T(8,128)S(1)}, f32[5,128]{1,0:T(8,128)S(1)}, u32[]{:S(2)}, u32[]{:S(2)}) collective-permute-start(f32[5,128]{1,0:T(8,128)S(1)} %get-tuple-element.35.refs_0_), channel_id=1, source_target_pairs={{0,3},{1,2},{2,1},{3,0},{4,7},{5,6},{6,5},{7,4},{8,11},{9,10},{10,... | collective-permute-start | bytes 7688 | tf_op jit(solution)/shard_map/ppermute | solution.py:426
  29.2 2.0 %collective-permute-start = (f32[5,128]{1,0:T(8,128)S(1)}, f32[5,128]{1,0:T(8,128)S(1)}, u32[]{:S(2)}, u32[]{:S(2)}) collective-permute-start(f32[5,128]{1,0:T(8,128)S(1)} %get-tuple-element.35.refs_0_), channel_id=1, source_target_pairs={{0,1},{1,0},{2,3},{3,2},{4,5},{5,4},{6,7},{7,6},{8,9},{9,8},{10,11... | collective-permute-start | bytes 7688 | tf_op jit(solution)/shard_map/ppermute | solution.py:426
  32.8 3.5 %shard_map.105 = (bf16[4,2,32,256]{3,2,1,0:T(8,128)(2,1)S(1)}, bf16[4,2,32,256]{3,2,1,0:T(8,128)(2,1)S(1)}, bf16[4,2,32,256]{3,2,1,0:T(8,128)(2,1)S(1)}, bf16[4,...) custom-call(s32[1]{0:T(128)} %bitcast.1.row, ...), custom_call_target="tpu_custom_call" | custom-call | tf_op jit(solution)/shard_map/pallas_call | solution.py:86
  36.3 2.1 %collective-permute-start.8 = (bf16[4,2,32,256]{3,2,1,0:T(8,128)(2,1)S(1)}, bf16[4,2,32,256]{3,2,1,0:T(8,128)(2,1)S(1)}, u32[]{:S(2)}, u32[]{:S(2)}) collective-permute-start(bf16[4,2,32,256]{3,2,1,0:T(8,128)(2,1)S(1)} %get-tuple-element.37), channel_id=1, source_target_pairs={{0,1},{1,0},{2,3},{3,2},{4,5},{5,4},{6,7},{7,6},{8,9},{9,8},{10,11... | collective-permute-start | bytes 393224 | tf_op jit(solution)/shard_map/ppermute | solution.py:426
  39.9 4.3 %collective-permute-start.11 = (bf16[4,2,32,256]{3,2,1,0:T(8,128)(2,1)S(1)}, bf16[4,2,32,256]{3,2,1,0:T(8,128)(2,1)S(1)}, u32[]{:S(2)}, u32[]{:S(2)}) collective-permute-start(bf16[4,2,32,256]{3,2,1,0:T(8,128)(2,1)S(1)} %get-tuple-element.40), channel_id=1, source_target_pairs={{0,4},{1,5},{2,6},{3,7},{4,0},{5,1},{6,2},{7,3},{8,12},{9,13},{10,... | collective-permute-start | bytes 393224 | tf_op jit(solution)/shard_map/ppermute | solution.py:426
  47.9 2.6 %shard_map.107 = (bf16[4,2,256,256]{3,2,1,0:T(8,128)(2,1)S(1)}, f32[4,256,256]{2,1,0:T(8,128)S(1)}) custom-call(s32[1]{0:T(128)} %bitcast.1.row, s32[1]{0:T(128)} %bitcast.me, s32[2,4]{1,0:T(2,128)} %bitcast.7, bf16[2,256,256]{2,1,0:T(8,128)(2,1)S(1)} %get-tuple-element.44.tile, bf16[2,256,128]{2,1,0:T(8,128)(2,1)S(1)} %collective-permute-done.15.even.side_even, ...), custom_call_target="tpu_custom_call" | custom-call | tf_op jit(solution)/shard_map/pallas_call | solution.py:86
  50.5 6.9 %collective-permute-done.11.refs_4_ = bf16[4,2,32,256]{3,2,1,0:T(8,128)(2,1)S(1)} collective-permute-done((bf16[4,2,32,256]{3,2,1,0:T(8,128)(2,1)S(1)}, bf16[4,2,32,256]{3,2,1,0:T(8,128)(2,1)S(1)}, u32[]{:S(2)}, u32[]{:S(2)}) %collective-permute-start.11) | collective-permute-done | bytes 131104 | tf_op jit(solution)/shard_map/ppermute | solution.py:426
  57.4 2.8 %collective-permute-done.12.refs_5_ = bf16[4,2,32,256]{3,2,1,0:T(8,128)(2,1)S(1)} collective-permute-done((bf16[4,2,32,256]{3,2,1,0:T(8,128)(2,1)S(1)}, bf16[4,2,32,256]{3,2,1,0:T(8,128)(2,1)S(1)}, u32[]{:S(2)}, u32[]{:S(2)}) %collective-permute-start.12) | collective-permute-done | bytes 131104 | tf_op jit(solution)/shard_map/ppermute | solution.py:426
  60.2 3.2 %collective-permute-done.13.refs_6_ = bf16[4,2,32,256]{3,2,1,0:T(8,128)(2,1)S(1)} collective-permute-done((bf16[4,2,32,256]{3,2,1,0:T(8,128)(2,1)S(1)}, bf16[4,2,32,256]{3,2,1,0:T(8,128)(2,1)S(1)}, u32[]{:S(2)}, u32[]{:S(2)}) %collective-permute-start.13) | collective-permute-done | bytes 131104 | tf_op jit(solution)/shard_map/ppermute | solution.py:426
  63.4 1.9 %collective-permute-done.14.refs_7_ = bf16[4,2,32,256]{3,2,1,0:T(8,128)(2,1)S(1)} collective-permute-done((bf16[4,2,32,256]{3,2,1,0:T(8,128)(2,1)S(1)}, bf16[4,2,32,256]{3,2,1,0:T(8,128)(2,1)S(1)}, u32[]{:S(2)}, u32[]{:S(2)}) %collective-permute-start.14) | collective-permute-done | bytes 131104 | tf_op jit(solution)/shard_map/ppermute | solution.py:426
  65.4 4.7 %shard_map.108 = (bf16[4,2,32,256]{3,2,1,0:T(8,128)(2,1)S(1)}, bf16[4,2,32,256]{3,2,1,0:T(8,128)(2,1)S(1)}, bf16[4,2,32,256]{3,2,1,0:T(8,128)(2,1)S(1)}, bf16[4,...) custom-call(s32[1,1]{1,0:T(1,128)S(6)} %copy.11.counts, ...), custom_call_target="tpu_custom_call" | custom-call | tf_op jit(solution)/shard_map/pallas_call | solution.py:86
  71.1 3.2 %collective-permute-start.28 = (bf16[4,2,32,256]{3,2,1,0:T(8,128)(2,1)S(1)}, bf16[4,2,32,256]{3,2,1,0:T(8,128)(2,1)S(1)}, u32[]{:S(2)}, u32[]{:S(2)}) collective-permute-start(bf16[4,2,32,256]{3,2,1,0:T(8,128)(2,1)S(1)} %get-tuple-element.64), channel_id=1, source_target_pairs={{0,2},{1,3},{2,0},{3,1},{4,6},{5,7},{6,4},{7,5},{8,10},{9,11},{10,... | collective-permute-start | bytes 393224 | tf_op jit(solution)/shard_map/ppermute | solution.py:426
  74.3 2.6 %collective-permute-start.24 = (bf16[4,2,32,256]{3,2,1,0:T(8,128)(2,1)S(1)}, bf16[4,2,32,256]{3,2,1,0:T(8,128)(2,1)S(1)}, u32[]{:S(2)}, u32[]{:S(2)}) collective-permute-start(bf16[4,2,32,256]{3,2,1,0:T(8,128)(2,1)S(1)} %get-tuple-element.59), channel_id=1, source_target_pairs={{0,5},{1,4},{2,7},{3,6},{4,1},{5,0},{6,3},{7,2},{8,13},{9,12},{10,... | collective-permute-start | bytes 393224 | tf_op jit(solution)/shard_map/ppermute | solution.py:426
  79.8 3.1 %shard_map.109 = (bf16[2,128,512]{2,1,0:T(8,128)(2,1)S(1)}, f32[2,256,512]{2,1,0:T(8,128)S(1)}, bf16[2,128,512]{2,1,0:T(8,128)(2,1)S(1)}) custom-call(s32[1]{0:T(128)} %bitcast.1.row, s32[2,4]{1,0:T(2,128)} %bitcast.8, f32[4,2,256,256]{3,2,1,0:T(8,128)S(1)} %get-tuple-element.51.pieces), custom_call_target="tpu_custom_call" | custom-call | tf_op jit(solution)/shard_map/pallas_call | solution.py:86
  84.3 2.3 %shard_map.112 = (f32[12,2,32,256]{3,2,1,0:T(8,128)S(1)}, f32[12,2,32,256]{3,2,1,0:T(8,128)S(1)}) custom-call(s32[1]{0:T(128)} %bitcast.1.row, f32[5,128]{1,0:T(8,128)S(1)} %get-tuple-element.35.refs_0_, f32[5,128]{1,0:T(8,128)S(1)} %collective-permute-done.refs_1_, f32[5,128]{1,0:T(8,128)S(1)} %collective-permute-done.1.refs_2_, ...), custom_call_target="tpu_custom_call" | custom-call | tf_op jit(solution)/shard_map/pallas_call | solution.py:86
  88.2 4.0 %collective-permute-done.25.refs_6_ = bf16[4,2,32,256]{3,2,1,0:T(8,128)(2,1)S(1)} collective-permute-done((bf16[4,2,32,256]{3,2,1,0:T(8,128)(2,1)S(1)}, bf16[4,2,32,256]{3,2,1,0:T(8,128)(2,1)S(1)}, u32[]{:S(2)}, u32[]{:S(2)}) %collective-permute-start.25) | collective-permute-done | bytes 131104 | tf_op jit(solution)/shard_map/ppermute | solution.py:426
  98.2 1.9 %collective-permute-start.22 = (bf16[2,256,128]{2,1,0:T(8,128)(2,1)S(1)}, bf16[2,256,128]{2,1,0:T(8,128)(2,1)S(1)}, u32[]{:S(2)}, u32[]{:S(2)}) collective-permute-start(bf16[2,256,128]{2,1,0:T(8,128)(2,1)S(1)} %get-tuple-element.57), channel_id=1, source_target_pairs={{1,2},{2,1},{3,4},{4,3},{5,6},{6,5},{9,10},{10,9},{11,12},{12,11},... | collective-permute-start | bytes 393224 | tf_op jit(solution)/shard_map/ppermute | solution.py:36
  100.1 1.8 %shard_map.113 = f32[12,2,32,256]{3,2,1,0:T(8,128)S(1)} custom-call(s32[1]{0:T(128)} %bitcast.1.row, f32[5,128]{1,0:T(8,128)S(1)} %collective-permute-done.3.refs_4_.refs_0_, f32[5,128]{1,0:T(8,128)S(1)} %collective-permute-done.4.refs_5_.refs_1_, f32[5,128]{1,0:T(8,128)S(1)} %collective-permute-done.5.refs_6_.refs_2_, ...), custom_call_target="tpu_custom_call" | custom-call | tf_op jit(solution)/shard_map/pallas_call | solution.py:86
  102.1 3.9 %collective-permute-done.22.odd = bf16[2,256,128]{2,1,0:T(8,128)(2,1)S(1)} collective-permute-done((bf16[2,256,128]{2,1,0:T(8,128)(2,1)S(1)}, bf16[2,256,128]{2,1,0:T(8,128)(2,1)S(1)}, u32[]{:S(2)}, u32[]{:S(2)}) %collective-permute-start.22) | collective-permute-done | bytes 131104 | tf_op jit(solution)/shard_map/ppermute | solution.py:36
  (54 shorter events, 33.4 us)
Async XLA Ops:
  0.7 32.2 %collective-permute-start.7 = (bf16[1,12,2,32,256]{4,3,2,1,0:T(8,128)(2,1)}, bf16[1,12,2,32,256]{4,3,2,1,0:T(8,128)(2,1)S(1)}, u32[]{:S(2)}, u32[]{:S(2)}) collective-permute-start(bf16[1,12,2,32,256]{4,3,2,1,0:T(8,128)(2,1)} %refs_8_.1), channel_id=1, source_target_pairs={{8,0},{16,8},{24,16},{9,1},{17,9},{25,17},{10,2},{18,10},{26,18},{... | collective-permute-start | bytes 1179656 | tf_op jit(solution)/shard_map/ppermute | solution.py:26
  3.3 6.3 %collective-permute-start.15 = (bf16[2,256,128]{2,1,0:T(8,128)(2,1)S(1)}, bf16[2,256,128]{2,1,0:T(8,128)(2,1)S(1)}, u32[]{:S(2)}, u32[]{:S(2)}) collective-permute-start(bf16[2,256,128]{2,1,0:T(8,128)(2,1)S(1)} %get-tuple-element.45), channel_id=1, source_target_pairs={{0,1},{1,0},{2,3},{3,2},{4,5},{5,4},{6,7},{7,6},{8,9},{9,8},{10,11... | collective-permute-start | bytes 393224 | tf_op jit(solution)/shard_map/ppermute | solution.py:36
  4.8 9.0 %collective-permute-start.16 = (bf16[2,256,128]{2,1,0:T(8,128)(2,1)S(1)}, bf16[2,256,128]{2,1,0:T(8,128)(2,1)S(1)}, u32[]{:S(2)}, u32[]{:S(2)}) collective-permute-start(bf16[2,256,128]{2,1,0:T(8,128)(2,1)S(1)} %get-tuple-element.46), channel_id=1, source_target_pairs={{1,2},{2,1},{3,4},{4,3},{5,6},{6,5},{9,10},{10,9},{11,12},{12,11},... | collective-permute-start | bytes 393224 | tf_op jit(solution)/shard_map/ppermute | solution.py:36
  14.0 26.0 %collective-permute-start.17 = (bf16[2,128,512]{2,1,0:T(8,128)(2,1)S(1)}, bf16[2,128,512]{2,1,0:T(8,128)(2,1)S(1)}, u32[]{:S(2)}, u32[]{:S(2)}) collective-permute-start(bf16[2,128,512]{2,1,0:T(8,128)(2,1)S(1)} %get-tuple-element.47), channel_id=1, source_target_pairs={{0,8},{8,0},{16,24},{24,16},{1,9},{9,1},{17,25},{25,17},{2,10},{10... | collective-permute-start | bytes 786440 | tf_op jit(solution)/shard_map/ppermute | solution.py:36
  14.0 30.2 %collective-permute-start.18 = (bf16[2,128,512]{2,1,0:T(8,128)(2,1)S(1)}, bf16[2,128,512]{2,1,0:T(8,128)(2,1)S(1)}, u32[]{:S(2)}, u32[]{:S(2)}) collective-permute-start(bf16[2,128,512]{2,1,0:T(8,128)(2,1)S(1)} %get-tuple-element.48), channel_id=1, source_target_pairs={{8,16},{16,8},{9,17},{17,9},{10,18},{18,10},{11,19},{19,11},{12,20... | collective-permute-start | bytes 786440 | tf_op jit(solution)/shard_map/ppermute | solution.py:36
  16.3 5.8 %collective-permute-start.5 = (f32[5,128]{1,0:T(8,128)S(1)}, f32[5,128]{1,0:T(8,128)S(1)}, u32[]{:S(2)}, u32[]{:S(2)}) collective-permute-start(f32[5,128]{1,0:T(8,128)S(1)} %get-tuple-element.35.refs_0_), channel_id=1, source_target_pairs={{0,6},{1,7},{2,4},{3,5},{4,2},{5,3},{6,0},{7,1},{8,14},{9,15},{10,... | collective-permute-start | bytes 7688 | tf_op jit(solution)/shard_map/ppermute | solution.py:426
  36.3 8.0 %collective-permute-start.8 = (bf16[4,2,32,256]{3,2,1,0:T(8,128)(2,1)S(1)}, bf16[4,2,32,256]{3,2,1,0:T(8,128)(2,1)S(1)}, u32[]{:S(2)}, u32[]{:S(2)}) collective-permute-start(bf16[4,2,32,256]{3,2,1,0:T(8,128)(2,1)S(1)} %get-tuple-element.37), channel_id=1, source_target_pairs={{0,1},{1,0},{2,3},{3,2},{4,5},{5,4},{6,7},{7,6},{8,9},{9,8},{10,11... | collective-permute-start | bytes 393224 | tf_op jit(solution)/shard_map/ppermute | solution.py:426
  38.4 7.3 %collective-permute-start.9 = (bf16[4,2,32,256]{3,2,1,0:T(8,128)(2,1)S(1)}, bf16[4,2,32,256]{3,2,1,0:T(8,128)(2,1)S(1)}, u32[]{:S(2)}, u32[]{:S(2)}) collective-permute-start(bf16[4,2,32,256]{3,2,1,0:T(8,128)(2,1)S(1)} %get-tuple-element.38), channel_id=1, source_target_pairs={{0,2},{1,3},{2,0},{3,1},{4,6},{5,7},{6,4},{7,5},{8,10},{9,11},{10,... | collective-permute-start | bytes 393224 | tf_op jit(solution)/shard_map/ppermute | solution.py:426
  38.9 11.6 %collective-permute-start.10 = (bf16[4,2,32,256]{3,2,1,0:T(8,128)(2,1)S(1)}, bf16[4,2,32,256]{3,2,1,0:T(8,128)(2,1)S(1)}, u32[]{:S(2)}, u32[]{:S(2)}) collective-permute-start(bf16[4,2,32,256]{3,2,1,0:T(8,128)(2,1)S(1)} %get-tuple-element.39), channel_id=1, source_target_pairs={{0,3},{1,2},{2,1},{3,0},{4,7},{5,6},{6,5},{7,4},{8,11},{9,10},{10,... | collective-permute-start | bytes 393224 | tf_op jit(solution)/shard_map/ppermute | solution.py:426
  39.9 17.5 %collective-permute-start.11 = (bf16[4,2,32,256]{3,2,1,0:T(8,128)(2,1)S(1)}, bf16[4,2,32,256]{3,2,1,0:T(8,128)(2,1)S(1)}, u32[]{:S(2)}, u32[]{:S(2)}) collective-permute-start(bf16[4,2,32,256]{3,2,1,0:T(8,128)(2,1)S(1)} %get-tuple-element.40), channel_id=1, source_target_pairs={{0,4},{1,5},{2,6},{3,7},{4,0},{5,1},{6,2},{7,3},{8,12},{9,13},{10,... | collective-permute-start | bytes 393224 | tf_op jit(solution)/shard_map/ppermute | solution.py:426
  44.2 16.0 %collective-permute-start.12 = (bf16[4,2,32,256]{3,2,1,0:T(8,128)(2,1)S(1)}, bf16[4,2,32,256]{3,2,1,0:T(8,128)(2,1)S(1)}, u32[]{:S(2)}, u32[]{:S(2)}) collective-permute-start(bf16[4,2,32,256]{3,2,1,0:T(8,128)(2,1)S(1)} %get-tuple-element.41), channel_id=1, source_target_pairs={{0,5},{1,4},{2,7},{3,6},{4,1},{5,0},{6,3},{7,2},{8,13},{9,12},{10,... | collective-permute-start | bytes 393224 | tf_op jit(solution)/shard_map/ppermute | solution.py:426
  44.2 19.2 %collective-permute-start.13 = (bf16[4,2,32,256]{3,2,1,0:T(8,128)(2,1)S(1)}, bf16[4,2,32,256]{3,2,1,0:T(8,128)(2,1)S(1)}, u32[]{:S(2)}, u32[]{:S(2)}) collective-permute-start(bf16[4,2,32,256]{3,2,1,0:T(8,128)(2,1)S(1)} %get-tuple-element.42), channel_id=1, source_target_pairs={{0,6},{1,7},{2,4},{3,5},{4,2},{5,3},{6,0},{7,1},{8,14},{9,15},{10,... | collective-permute-start | bytes 393224 | tf_op jit(solution)/shard_map/ppermute | solution.py:426
  45.7 19.6 %collective-permute-start.14 = (bf16[4,2,32,256]{3,2,1,0:T(8,128)(2,1)S(1)}, bf16[4,2,32,256]{3,2,1,0:T(8,128)(2,1)S(1)}, u32[]{:S(2)}, u32[]{:S(2)}) collective-permute-start(bf16[4,2,32,256]{3,2,1,0:T(8,128)(2,1)S(1)} %get-tuple-element.43), channel_id=1, source_target_pairs={{0,7},{1,6},{2,5},{3,4},{4,3},{5,2},{6,1},{7,0},{8,15},{9,14},{10,... | collective-permute-start | bytes 393224 | tf_op jit(solution)/shard_map/ppermute | solution.py:426
  70.0 7.3 %collective-permute-start.23 = (bf16[4,2,32,256]{3,2,1,0:T(8,128)(2,1)S(1)}, bf16[4,2,32,256]{3,2,1,0:T(8,128)(2,1)S(1)}, u32[]{:S(2)}, u32[]{:S(2)}) collective-permute-start(bf16[4,2,32,256]{3,2,1,0:T(8,128)(2,1)S(1)} %get-tuple-element.58), channel_id=1, source_target_pairs={{0,4},{1,5},{2,6},{3,7},{4,0},{5,1},{6,2},{7,3},{8,12},{9,13},{10,... | collective-permute-start | bytes 393224 | tf_op jit(solution)/shard_map/ppermute | solution.py:426
  70.1 8.5 %collective-permute-start.27 = (bf16[4,2,32,256]{3,2,1,0:T(8,128)(2,1)S(1)}, bf16[4,2,32,256]{3,2,1,0:T(8,128)(2,1)S(1)}, u32[]{:S(2)}, u32[]{:S(2)}) collective-permute-start(bf16[4,2,32,256]{3,2,1,0:T(8,128)(2,1)S(1)} %get-tuple-element.63), channel_id=1, source_target_pairs={{0,1},{1,0},{2,3},{3,2},{4,5},{5,4},{6,7},{7,6},{8,9},{9,8},{10,11... | collective-permute-start | bytes 393224 | tf_op jit(solution)/shard_map/ppermute | solution.py:426
  71.1 11.8 %collective-permute-start.28 = (bf16[4,2,32,256]{3,2,1,0:T(8,128)(2,1)S(1)}, bf16[4,2,32,256]{3,2,1,0:T(8,128)(2,1)S(1)}, u32[]{:S(2)}, u32[]{:S(2)}) collective-permute-start(bf16[4,2,32,256]{3,2,1,0:T(8,128)(2,1)S(1)} %get-tuple-element.64), channel_id=1, source_target_pairs={{0,2},{1,3},{2,0},{3,1},{4,6},{5,7},{6,4},{7,5},{8,10},{9,11},{10,... | collective-permute-start | bytes 393224 | tf_op jit(solution)/shard_map/ppermute | solution.py:426
  74.2 9.4 %collective-permute-start.29 = (bf16[4,2,32,256]{3,2,1,0:T(8,128)(2,1)S(1)}, bf16[4,2,32,256]{3,2,1,0:T(8,128)(2,1)S(1)}, u32[]{:S(2)}, u32[]{:S(2)}) collective-permute-start(bf16[4,2,32,256]{3,2,1,0:T(8,128)(2,1)S(1)} %get-tuple-element.65), channel_id=1, source_target_pairs={{0,3},{1,2},{2,1},{3,0},{4,7},{5,6},{6,5},{7,4},{8,11},{9,10},{10,... | collective-permute-start | bytes 393224 | tf_op jit(solution)/shard_map/ppermute | solution.py:426
  74.3 14.0 %collective-permute-start.24 = (bf16[4,2,32,256]{3,2,1,0:T(8,128)(2,1)S(1)}, bf16[4,2,32,256]{3,2,1,0:T(8,128)(2,1)S(1)}, u32[]{:S(2)}, u32[]{:S(2)}) collective-permute-start(bf16[4,2,32,256]{3,2,1,0:T(8,128)(2,1)S(1)} %get-tuple-element.59), channel_id=1, source_target_pairs={{0,5},{1,4},{2,7},{3,6},{4,1},{5,0},{6,3},{7,2},{8,13},{9,12},{10,... | collective-permute-start | bytes 393224 | tf_op jit(solution)/shard_map/ppermute | solution.py:426
  77.4 14.8 %collective-permute-start.25 = (bf16[4,2,32,256]{3,2,1,0:T(8,128)(2,1)S(1)}, bf16[4,2,32,256]{3,2,1,0:T(8,128)(2,1)S(1)}, u32[]{:S(2)}, u32[]{:S(2)}) collective-permute-start(bf16[4,2,32,256]{3,2,1,0:T(8,128)(2,1)S(1)} %get-tuple-element.60), channel_id=1, source_target_pairs={{0,6},{1,7},{2,4},{3,5},{4,2},{5,3},{6,0},{7,1},{8,14},{9,15},{10,... | collective-permute-start | bytes 393224 | tf_op jit(solution)/shard_map/ppermute | solution.py:426
  78.6 15.2 %collective-permute-start.26 = (bf16[4,2,32,256]{3,2,1,0:T(8,128)(2,1)S(1)}, bf16[4,2,32,256]{3,2,1,0:T(8,128)(2,1)S(1)}, u32[]{:S(2)}, u32[]{:S(2)}) collective-permute-start(bf16[4,2,32,256]{3,2,1,0:T(8,128)(2,1)S(1)} %get-tuple-element.61), channel_id=1, source_target_pairs={{0,7},{1,6},{2,5},{3,4},{4,3},{5,2},{6,1},{7,0},{8,15},{9,14},{10,... | collective-permute-start | bytes 393224 | tf_op jit(solution)/shard_map/ppermute | solution.py:426
  82.9 13.8 %collective-permute-start.19 = (bf16[2,128,512]{2,1,0:T(8,128)(2,1)S(1)}, bf16[2,128,512]{2,1,0:T(8,128)(2,1)S(1)}, u32[]{:S(2)}, u32[]{:S(2)}) collective-permute-start(bf16[2,128,512]{2,1,0:T(8,128)(2,1)S(1)} %get-tuple-element.53), channel_id=1, source_target_pairs={{0,8},{8,0},{16,24},{24,16},{1,9},{9,1},{17,25},{25,17},{2,10},{10... | collective-permute-start | bytes 786440 | tf_op jit(solution)/shard_map/ppermute | solution.py:36
  83.6 13.0 %collective-permute-start.20 = (bf16[2,128,512]{2,1,0:T(8,128)(2,1)S(1)}, bf16[2,128,512]{2,1,0:T(8,128)(2,1)S(1)}, u32[]{:S(2)}, u32[]{:S(2)}) collective-permute-start(bf16[2,128,512]{2,1,0:T(8,128)(2,1)S(1)} %get-tuple-element.54), channel_id=1, source_target_pairs={{8,16},{16,8},{9,17},{17,9},{10,18},{18,10},{11,19},{19,11},{12,20... | collective-permute-start | bytes 786440 | tf_op jit(solution)/shard_map/ppermute | solution.py:36
  95.4 11.5 %collective-permute-start.30 = (bf16[12,2,32,256]{3,2,1,0:T(8,128)(2,1)S(1)}, bf16[12,2,32,256]{3,2,1,0:T(8,128)(2,1)S(1)}, u32[]{:S(2)}, u32[]{:S(2)}) collective-permute-start(bf16[12,2,32,256]{3,2,1,0:T(8,128)(2,1)S(1)} %shard_map.114), channel_id=1, source_target_pairs={{0,8},{8,16},{16,24},{1,9},{9,17},{17,25},{2,10},{10,18},{18,26},{... | collective-permute-start | bytes 1179656 | tf_op jit(solution)/shard_map/ppermute | solution.py:26
  98.2 7.7 %collective-permute-start.22 = (bf16[2,256,128]{2,1,0:T(8,128)(2,1)S(1)}, bf16[2,256,128]{2,1,0:T(8,128)(2,1)S(1)}, u32[]{:S(2)}, u32[]{:S(2)}) collective-permute-start(bf16[2,256,128]{2,1,0:T(8,128)(2,1)S(1)} %get-tuple-element.57), channel_id=1, source_target_pairs={{1,2},{2,1},{3,4},{4,3},{5,6},{6,5},{9,10},{10,9},{11,12},{12,11},... | collective-permute-start | bytes 393224 | tf_op jit(solution)/shard_map/ppermute | solution.py:36
  (9 other events, 161.8 us)

commit v3 on v2

--- a/solution.py
+++ b/solution.py
@@ -59,9 +59,14 @@
     return jnp.asarray(forward, jnp.bfloat16), jnp.asarray(inverse, jnp.bfloat16)
 
 
+def transfer_order(count):
+    half = count // 2
+    return [half] * (half > 0) + list(range(1, half)) + list(range(half + 1, count))
+
+
 def partners(axis):
     count = lax.axis_size(axis)
-    steps = list(range(1, count))
+    steps = transfer_order(count)
     paired = count & (count - 1) == 0
 
     def goes_to(index, step):
@@ -93,24 +98,28 @@
     )(*arrays)
 
 
-def fetch(arrays, held, sem):
-    copies = [pltpu.make_async_copy(a, held.at[at], sem.at[at]) for at, a in enumerate(arrays)]
+def fetch(arrays, places, held, sem):
+    copies = [
+        pltpu.make_async_copy(arrays[i].at[block], held.at[at], sem.at[at])
+        for at, (i, block) in enumerate(places)
+    ]
     for copy in copies:
         copy.start()
     return copies
 
 
 def held_weights(count, weights):
-    return [pltpu.SMEM((count,) + weights.shape, jnp.float32), pltpu.SemaphoreType.DMA((count,))]
-
-
-def slab_kernel(count, row, *refs):
+    shape = (count,) + weights.shape[1:]
+    return [pltpu.SMEM(shape, jnp.float32), pltpu.SemaphoreType.DMA((count,))]
+
+
+def slab_kernel(count, places, row, *refs):
     own, follower = refs[count : count + 2]
     outs = refs[count + 2 : -5]
     table, near, held, sem, near_sem = refs[-5:]
     copy_own = pltpu.make_async_copy(own, near, near_sem)
     copy_own.start()
-    copies = fetch(refs[:count], held, sem)
+    copies = fetch(refs[:count], places, held, sem)
     num_modes = own.shape[1]
     table[1] = follower[0].astype(jnp.float32)
     copy_own.wait()
@@ -136,17 +145,17 @@
         lax.fori_loop(0, out.shape[0], slot_step, 0)
 
 
-def slabs(row, weights, own, follower):
-    shape = (weights[0].shape[0] - 1,) + own.shape[2:]
+def slabs(row, weights, places, own, follower):
+    shape = (weights[0].shape[1] - 1,) + own.shape[2:]
     return call(
-        functools.partial(slab_kernel, len(weights)),
-        [(shape, jnp.bfloat16)] * len(weights),
+        functools.partial(slab_kernel, len(weights), places),
+        [(shape, jnp.bfloat16)] * len(places),
         (row, SMEM),
         *weights,
         (own, HBM),
         follower,
         scratch=[pltpu.VMEM((2,) + own.shape[1:], jnp.float32), pltpu.VMEM(own.shape, own.dtype)]
-        + held_weights(len(weights), weights[0])
+        + held_weights(len(places), weights[0])
         + [pltpu.SemaphoreType.DMA],
     )
 
@@ -173,6 +182,11 @@
     first, second = by_side(me[0], low[:, :, :half], low[:, :, low.shape[2] - half :])
     even[...] = first
     odd[...] = second
+
+
+def pair_kernel(mine, across, out):
+    out[0] = mine[...]
+    out[1] = across[...]
 
 
 def widen_kernel(row, me, tile, even, odd, first, second):
@@ -353,12 +367,13 @@
     out[:, :, cols - half :] += got_right.astype(jnp.float32)
 
 
-def sums_kernel(count, goals, row, *refs):
-    received = refs[count : 2 * count]
-    added = refs[2 * count : 2 * count + sum(goal[2] for goal in goals)]
-    outs = refs[2 * count + len(added) : -3]
+def sums_kernel(held_in, places, goals, row, *refs):
+    count = len(places)
+    received = refs[held_in : held_in + count]
+    added = refs[held_in + count : held_in + count + sum(goal[2] for goal in goals)]
+    outs = refs[held_in + count + len(added) : -3]
     terms, held, sem = refs[-3:]
-    copies = fetch(refs[:count], held, sem)
+    copies = fetch(refs[:held_in], places, held, sem)
     num_modes = outs[0].shape[-4]
     slot_count = received[0].shape[0]
     slots = slot_count
@@ -393,17 +408,17 @@
     lax.fori_loop(0, num_modes, mode_step, 0)
 
 
-def sums(row, goals, weights, received, added, num_modes, dtypes):
+def sums(row, goals, weights, places, received, added, num_modes, dtypes):
     shape = (num_modes,) + received[0].shape[1:]
     return call(
-        functools.partial(sums_kernel, len(received), goals),
+        functools.partial(sums_kernel, len(weights), places, goals),
         [(shape, dtype) for dtype in dtypes],
         (row, SMEM),
         *weights,
         *received,
         *added,
         scratch=[pltpu.VMEM((len(received),) + received[0].shape, jnp.float32)]
-        + held_weights(len(weights), weights[0]),
+        + held_weights(len(places), weights[0]),
     )
 
 
@@ -419,13 +434,13 @@
     steps, goes_to, comes_from = partners("col")
     every = [0] + steps
     count = lax.axis_size("col")
-    staying = steps[: count // 2 - 1]
-    crossing = steps[count // 2 - 1 :]
+    middle_step = count // 2
+    near = list(range(1, middle_step))
+    crossing = list(range(max(middle_step, 1), count))
 
     def move(value, step):
         return lax.ppermute(value, "col", [(i, goes_to(i, step)) for i in range(count)])
 
-    follower = shift(modes, "row", -1)
     side = (2, rows, half)
     payload, low, *edges = call(
         prepare_kernel,
@@ -438,12 +453,27 @@
         scratch=[pltpu.VMEM(x.shape, x.dtype) for x in (coeffs, region, object_field)]
         + [pltpu.SemaphoreType.DMA((3,))],
     )
-    weights = {0: payload}
-    for step in steps:
-        weights[step] = move(payload, step)
-
-    def made_for(step):
-        return weights[step] if goes_to(1, step) == comes_from(1, step) else weights[count - step]
+    if count > 1 and count & (count - 1) == 0:
+        across = move(payload, middle_step)
+        blocks_shape = (2,) + payload.shape
+        (pair,) = call(pair_kernel, [(blocks_shape, jnp.float32)], payload, across)
+        weights = [pair] + [move(pair, step) for step in near]
+
+        def made_at(step):
+            return step % middle_step, step // middle_step
+
+        came_at = made_at
+    else:
+        weights = [payload[None]]
+        weights += [move(payload[None], step) for step in range(1, count)]
+
+        def made_at(step):
+            return -step % count, 0
+
+        def came_at(step):
+            return step, 0
+
+    follower = shift(modes, "row", -1)
 
     sides = swap(edges, "col")
     wide = (2, half, cols + 2 * half)
@@ -451,7 +481,7 @@
     ends = swap(ends, "row")
 
     blocks = {}
-    made = slabs(row, [made_for(step) for step in every], modes, follower)
+    made = slabs(row, weights, [made_at(step) for step in every], modes, follower)
     for step, slab in zip(every, made):
         blocks[step] = move(slab, step) if step else slab
 
@@ -501,18 +531,16 @@
         return sums(
             row,
             goals,
-            [came_from(step) for step in group],
+            weights,
+            [came_at(step) for step in group],
             [received[step] for step in group],
             added,
             num_modes,
             dtypes,
         )
 
-    def came_from(step):
-        return weights[step]
-
     own, following = add_up(
-        [0] + staying, ((0, 0, False), (1, 1, False)), [], [jnp.float32, jnp.float32]
+        [0] + near, ((0, 0, False), (1, 1, False)), [], [jnp.float32, jnp.float32]
     )
     (following,) = add_up(crossing, ((1, 1, True),), [following], [jnp.bfloat16])
     passed = shift(following, "row", 1)

time: 108 us -> 101 us (0.935)
  starting transfers between devices: 43.1 us -> 34.8 us
  waiting for transfers between devices: 40.4 us -> 41.5 us
    ppermute x21 -> x18, starting transfers between devices: 32.2 us -> 23.4 us  [move(): lax.ppermute(value, 'col', [(i, goes_to(i, step)) for i in range(count)])]
    ppermute x21 -> x18, waiting for transfers between devices: 29.3 us -> 31.1 us  [move(): lax.ppermute(value, 'col', [(i, goes_to(i, step)) for i in range(count)])]
    pallas_call x11 -> x12, Pallas kernels: 21.8 us -> 21.8 us  [call(): pl.pallas_call(body, out_shape=tuple(outs), in_specs=specs, out_specs=tup...]
  transfers between devices with their start and end apart: 31 -> 28, of which waited for: 17 -> 15; matrix products, arithmetic and copies ran while one was open for 0% -> 0% of each run, Pallas kernels for 16% -> 17%
where the time goes in v3:
time: 101 us
  waiting for transfers between devices  41.5 us (41%)
  starting transfers between devices  34.8 us (34%)
  Pallas kernels  21.8 us (22%)
  between operations  1.51 us (1%)
    ppermute x18, waiting for transfers between devices, move(): lax.ppermute(value, 'col', [(i, goes_to(i, step)) for i in range(count)])  31.1 us
    ppermute x18, starting transfers between devices, move(): lax.ppermute(value, 'col', [(i, goes_to(i, step)) for i in range(count)])  23.4 us
    pallas_call x12, Pallas kernels, call(): pl.pallas_call(body, out_shape=tuple(outs), in_specs=specs, out_specs=tup...  21.8 us
    ppermute x8, waiting for transfers between devices, swap(): lax.ppermute(value, axis, pairs)  10.3 us
    ppermute x8, starting transfers between devices, swap(): lax.ppermute(value, axis, pairs)  8.71 us
    ppermute x2, starting transfers between devices, shift(): return lax.ppermute(value, axis, pairs)  2.74 us
  transfers between devices with their start and end apart: 28, of which 15 were waited for; matrix products, arithmetic and copies ran while one was open for 0% of the time, Pallas kernels for 17%

profile of v3, /device:TPU:8, one launch (start us, length us, event | category | flops | bytes accessed | tf_op | source)
XLA Modules:
  0.0 100.6 jit_solution(4543629760295398208)
XLA Ops:
  4.8 1.9 %collective-permute-start.13 = (bf16[2,256,128]{2,1,0:T(8,128)(2,1)S(1)}, bf16[2,256,128]{2,1,0:T(8,128)(2,1)S(1)}, u32[]{:S(2)}, u32[]{:S(2)}) collective-permute-start(bf16[2,256,128]{2,1,0:T(8,128)(2,1)S(1)} %get-tuple-element.46), channel_id=1, source_target_pairs={{1,2},{2,1},{3,4},{4,3},{5,6},{6,5},{9,10},{10,9},{11,12},{12,11},... | collective-permute-start | bytes 393224 | tf_op jit(solution)/shard_map/ppermute | solution.py:36
  6.8 2.8 %collective-permute-done.12.even.side_even = bf16[2,256,128]{2,1,0:T(8,128)(2,1)S(1)} collective-permute-done((bf16[2,256,128]{2,1,0:T(8,128)(2,1)S(1)}, bf16[2,256,128]{2,1,0:T(8,128)(2,1)S(1)}, u32[]{:S(2)}, u32[]{:S(2)}) %collective-permute-start.12) | collective-permute-done | bytes 131104 | tf_op jit(solution)/shard_map/ppermute | solution.py:36
  9.6 4.3 %collective-permute-done.13.odd.side_odd = bf16[2,256,128]{2,1,0:T(8,128)(2,1)S(1)} collective-permute-done((bf16[2,256,128]{2,1,0:T(8,128)(2,1)S(1)}, bf16[2,256,128]{2,1,0:T(8,128)(2,1)S(1)}, u32[]{:S(2)}, u32[]{:S(2)}) %collective-permute-start.13) | collective-permute-done | bytes 131104 | tf_op jit(solution)/shard_map/ppermute | solution.py:36
  14.7 2.7 %collective-permute-start = (f32[5,128]{1,0:T(8,128)S(1)}, f32[5,128]{1,0:T(8,128)S(1)}, u32[]{:S(2)}, u32[]{:S(2)}) collective-permute-start(f32[5,128]{1,0:T(8,128)S(1)} %get-tuple-element.35.mine), channel_id=1, source_target_pairs={{0,4},{1,5},{2,6},{3,7},{4,0},{5,1},{6,2},{7,3},{8,12},{9,13},{10,... | collective-permute-start | bytes 7688 | tf_op jit(solution)/shard_map/ppermute | solution.py:442
  17.4 1.9 %collective-permute-done.across = f32[5,128]{1,0:T(8,128)S(1)} collective-permute-done((f32[5,128]{1,0:T(8,128)S(1)}, f32[5,128]{1,0:T(8,128)S(1)}, u32[]{:S(2)}, u32[]{:S(2)}) %collective-permute-start) | collective-permute-done | bytes 2592 | tf_op jit(solution)/shard_map/ppermute | solution.py:442
  19.4 1.9 %collective-permute-start.2 = (f32[2,5,128]{2,1,0:T(8,128)S(1)}, f32[2,5,128]{2,1,0:T(8,128)S(1)}, u32[]{:S(2)}, u32[]{:S(2)}) collective-permute-start(f32[2,5,128]{2,1,0:T(8,128)S(1)} %shard_map.105.refs_0_), channel_id=1, source_target_pairs={{0,2},{1,3},{2,0},{3,1},{4,6},{5,7},{6,4},{7,5},{8,10},{9,11},{10,... | collective-permute-start | bytes 15368 | tf_op jit(solution)/shard_map/ppermute | solution.py:442
  21.3 2.6 %collective-permute-done.3.refs_3_ = f32[2,5,128]{2,1,0:T(8,128)S(1)} collective-permute-done((f32[2,5,128]{2,1,0:T(8,128)S(1)}, f32[2,5,128]{2,1,0:T(8,128)S(1)}, u32[]{:S(2)}, u32[]{:S(2)}) %collective-permute-start.3) | collective-permute-done | bytes 5152 | tf_op jit(solution)/shard_map/ppermute | solution.py:442
  24.4 3.1 %collective-permute-done.1.refs_1_ = f32[2,5,128]{2,1,0:T(8,128)S(1)} collective-permute-done((f32[2,5,128]{2,1,0:T(8,128)S(1)}, f32[2,5,128]{2,1,0:T(8,128)S(1)}, u32[]{:S(2)}, u32[]{:S(2)}) %collective-permute-start.1) | collective-permute-done | bytes 5152 | tf_op jit(solution)/shard_map/ppermute | solution.py:442
  27.5 3.4 %shard_map.106 = (bf16[4,2,32,256]{3,2,1,0:T(8,128)(2,1)S(1)}, bf16[4,2,32,256]{3,2,1,0:T(8,128)(2,1)S(1)}, bf16[4,2,32,256]{3,2,1,0:T(8,128)(2,1)S(1)}, bf16[4,...) custom-call(s32[1]{0:T(128)} %bitcast.1.row, ...), custom_call_target="tpu_custom_call" | custom-call | tf_op jit(solution)/shard_map/pallas_call | solution.py:91
  30.9 2.7 %collective-permute-start.5 = (bf16[4,2,32,256]{3,2,1,0:T(8,128)(2,1)S(1)}, bf16[4,2,32,256]{3,2,1,0:T(8,128)(2,1)S(1)}, u32[]{:S(2)}, u32[]{:S(2)}) collective-permute-start(bf16[4,2,32,256]{3,2,1,0:T(8,128)(2,1)S(1)} %get-tuple-element.37), channel_id=1, source_target_pairs={{0,4},{1,5},{2,6},{3,7},{4,0},{5,1},{6,2},{7,3},{8,12},{9,13},{10,... | collective-permute-start | bytes 393224 | tf_op jit(solution)/shard_map/ppermute | solution.py:442
  34.6 2.5 %collective-permute-start.8 = (bf16[4,2,32,256]{3,2,1,0:T(8,128)(2,1)S(1)}, bf16[4,2,32,256]{3,2,1,0:T(8,128)(2,1)S(1)}, u32[]{:S(2)}, u32[]{:S(2)}) collective-permute-start(bf16[4,2,32,256]{3,2,1,0:T(8,128)(2,1)S(1)} %get-tuple-element.40), channel_id=1, source_target_pairs={{0,3},{1,2},{2,1},{3,0},{4,7},{5,6},{6,5},{7,4},{8,11},{9,10},{10,... | collective-permute-start | bytes 393224 | tf_op jit(solution)/shard_map/ppermute | solution.py:442
  41.5 2.6 %shard_map.108 = (bf16[4,2,256,256]{3,2,1,0:T(8,128)(2,1)S(1)}, f32[4,256,256]{2,1,0:T(8,128)S(1)}) custom-call(s32[1]{0:T(128)} %bitcast.1.row, s32[1]{0:T(128)} %bitcast.me, s32[2,4]{1,0:T(2,128)} %bitcast.7, bf16[2,256,256]{2,1,0:T(8,128)(2,1)S(1)} %get-tuple-element.44.tile, bf16[2,256,128]{2,1,0:T(8,128)(2,1)S(1)} %collective-permute-done.12.even.side_even, ...), custom_call_target="tpu_custom_call" | custom-call | tf_op jit(solution)/shard_map/pallas_call | solution.py:91
  44.2 2.5 %collective-permute-done.9.refs_5_ = bf16[4,2,32,256]{3,2,1,0:T(8,128)(2,1)S(1)} collective-permute-done((bf16[4,2,32,256]{3,2,1,0:T(8,128)(2,1)S(1)}, bf16[4,2,32,256]{3,2,1,0:T(8,128)(2,1)S(1)}, u32[]{:S(2)}, u32[]{:S(2)}) %collective-permute-start.9) | collective-permute-done | bytes 131104 | tf_op jit(solution)/shard_map/ppermute | solution.py:442
  46.7 7.3 %collective-permute-done.10.refs_6_ = bf16[4,2,32,256]{3,2,1,0:T(8,128)(2,1)S(1)} collective-permute-done((bf16[4,2,32,256]{3,2,1,0:T(8,128)(2,1)S(1)}, bf16[4,2,32,256]{3,2,1,0:T(8,128)(2,1)S(1)}, u32[]{:S(2)}, u32[]{:S(2)}) %collective-permute-start.10) | collective-permute-done | bytes 131104 | tf_op jit(solution)/shard_map/ppermute | solution.py:442
  54.0 2.4 %collective-permute-done.11.refs_7_ = bf16[4,2,32,256]{3,2,1,0:T(8,128)(2,1)S(1)} collective-permute-done((bf16[4,2,32,256]{3,2,1,0:T(8,128)(2,1)S(1)}, bf16[4,2,32,256]{3,2,1,0:T(8,128)(2,1)S(1)}, u32[]{:S(2)}, u32[]{:S(2)}) %collective-permute-start.11) | collective-permute-done | bytes 131104 | tf_op jit(solution)/shard_map/ppermute | solution.py:442
  56.4 4.7 %shard_map.109 = (bf16[4,2,32,256]{3,2,1,0:T(8,128)(2,1)S(1)}, bf16[4,2,32,256]{3,2,1,0:T(8,128)(2,1)S(1)}, bf16[4,2,32,256]{3,2,1,0:T(8,128)(2,1)S(1)}, bf16[4,...) custom-call(s32[1,1]{1,0:T(1,128)S(6)} %copy.11.counts, ...), custom_call_target="tpu_custom_call" | custom-call | tf_op jit(solution)/shard_map/pallas_call | solution.py:91
  62.2 3.4 %collective-permute-start.25 = (bf16[4,2,32,256]{3,2,1,0:T(8,128)(2,1)S(1)}, bf16[4,2,32,256]{3,2,1,0:T(8,128)(2,1)S(1)}, u32[]{:S(2)}, u32[]{:S(2)}) collective-permute-start(bf16[4,2,32,256]{3,2,1,0:T(8,128)(2,1)S(1)} %get-tuple-element.64), channel_id=1, source_target_pairs={{0,2},{1,3},{2,0},{3,1},{4,6},{5,7},{6,4},{7,5},{8,10},{9,11},{10,... | collective-permute-start | bytes 393224 | tf_op jit(solution)/shard_map/ppermute | solution.py:442
  65.7 2.4 %collective-permute-start.21 = (bf16[4,2,32,256]{3,2,1,0:T(8,128)(2,1)S(1)}, bf16[4,2,32,256]{3,2,1,0:T(8,128)(2,1)S(1)}, u32[]{:S(2)}, u32[]{:S(2)}) collective-permute-start(bf16[4,2,32,256]{3,2,1,0:T(8,128)(2,1)S(1)} %get-tuple-element.59), channel_id=1, source_target_pairs={{0,5},{1,4},{2,7},{3,6},{4,1},{5,0},{6,3},{7,2},{8,13},{9,12},{10,... | collective-permute-start | bytes 393224 | tf_op jit(solution)/shard_map/ppermute | solution.py:442
  68.1 2.0 %collective-permute-start.22 = (bf16[4,2,32,256]{3,2,1,0:T(8,128)(2,1)S(1)}, bf16[4,2,32,256]{3,2,1,0:T(8,128)(2,1)S(1)}, u32[]{:S(2)}, u32[]{:S(2)}) collective-permute-start(bf16[4,2,32,256]{3,2,1,0:T(8,128)(2,1)S(1)} %get-tuple-element.60), channel_id=1, source_target_pairs={{0,6},{1,7},{2,4},{3,5},{4,2},{5,3},{6,0},{7,1},{8,14},{9,15},{10,... | collective-permute-start | bytes 393224 | tf_op jit(solution)/shard_map/ppermute | solution.py:442
  70.9 3.1 %shard_map.110 = (bf16[2,128,512]{2,1,0:T(8,128)(2,1)S(1)}, f32[2,256,512]{2,1,0:T(8,128)S(1)}, bf16[2,128,512]{2,1,0:T(8,128)(2,1)S(1)}) custom-call(s32[1]{0:T(128)} %bitcast.1.row, s32[2,4]{1,0:T(2,128)} %bitcast.8, f32[4,2,256,256]{3,2,1,0:T(8,128)S(1)} %get-tuple-element.51.pieces), custom_call_target="tpu_custom_call" | custom-call | tf_op jit(solution)/shard_map/pallas_call | solution.py:91
  76.0 2.3 %shard_map.113 = (f32[12,2,32,256]{3,2,1,0:T(8,128)S(1)}, f32[12,2,32,256]{3,2,1,0:T(8,128)S(1)}) custom-call(s32[1]{0:T(128)} %bitcast.1.row, f32[2,5,128]{2,1,0:T(8,128)S(1)} %shard_map.105.refs_0_, f32[2,5,128]{2,1,0:T(8,128)S(1)} %collective-permute-done.1.refs_1_, f32[2,5,128]{2,1,0:T(8,128)S(1)} %collective-permute-done.2.refs_2_, ...), custom_call_target="tpu_custom_call" | custom-call | tf_op jit(solution)/shard_map/pallas_call | solution.py:91
  78.3 6.6 %collective-permute-done.22.refs_6_ = bf16[4,2,32,256]{3,2,1,0:T(8,128)(2,1)S(1)} collective-permute-done((bf16[4,2,32,256]{3,2,1,0:T(8,128)(2,1)S(1)}, bf16[4,2,32,256]{3,2,1,0:T(8,128)(2,1)S(1)}, u32[]{:S(2)}, u32[]{:S(2)}) %collective-permute-start.22) | collective-permute-done | bytes 131104 | tf_op jit(solution)/shard_map/ppermute | solution.py:442
  90.9 2.7 %collective-permute-start.19 = (bf16[2,256,128]{2,1,0:T(8,128)(2,1)S(1)}, bf16[2,256,128]{2,1,0:T(8,128)(2,1)S(1)}, u32[]{:S(2)}, u32[]{:S(2)}) collective-permute-start(bf16[2,256,128]{2,1,0:T(8,128)(2,1)S(1)} %get-tuple-element.57), channel_id=1, source_target_pairs={{1,2},{2,1},{3,4},{4,3},{5,6},{6,5},{9,10},{10,9},{11,12},{12,11},... | collective-permute-start | bytes 393224 | tf_op jit(solution)/shard_map/ppermute | solution.py:36
  96.3 2.3 %collective-permute-done.19.odd = bf16[2,256,128]{2,1,0:T(8,128)(2,1)S(1)} collective-permute-done((bf16[2,256,128]{2,1,0:T(8,128)(2,1)S(1)}, bf16[2,256,128]{2,1,0:T(8,128)(2,1)S(1)}, u32[]{:S(2)}, u32[]{:S(2)}) %collective-permute-start.19) | collective-permute-done | bytes 131104 | tf_op jit(solution)/shard_map/ppermute | solution.py:36
  (49 shorter events, 25.0 us)
Async XLA Ops:
  0.7 26.8 %collective-permute-start.4 = (bf16[1,12,2,32,256]{4,3,2,1,0:T(8,128)(2,1)}, bf16[1,12,2,32,256]{4,3,2,1,0:T(8,128)(2,1)S(1)}, u32[]{:S(2)}, u32[]{:S(2)}) collective-permute-start(bf16[1,12,2,32,256]{4,3,2,1,0:T(8,128)(2,1)} %refs_4_.1), channel_id=1, source_target_pairs={{8,0},{16,8},{24,16},{9,1},{17,9},{25,17},{10,2},{18,10},{26,18},{... | collective-permute-start | bytes 1179656 | tf_op jit(solution)/shard_map/ppermute | solution.py:26
  3.3 6.3 %collective-permute-start.12 = (bf16[2,256,128]{2,1,0:T(8,128)(2,1)S(1)}, bf16[2,256,128]{2,1,0:T(8,128)(2,1)S(1)}, u32[]{:S(2)}, u32[]{:S(2)}) collective-permute-start(bf16[2,256,128]{2,1,0:T(8,128)(2,1)S(1)} %get-tuple-element.45), channel_id=1, source_target_pairs={{0,1},{1,0},{2,3},{3,2},{4,5},{5,4},{6,7},{7,6},{8,9},{9,8},{10,11... | collective-permute-start | bytes 393224 | tf_op jit(solution)/shard_map/ppermute | solution.py:36
  4.8 9.0 %collective-permute-start.13 = (bf16[2,256,128]{2,1,0:T(8,128)(2,1)S(1)}, bf16[2,256,128]{2,1,0:T(8,128)(2,1)S(1)}, u32[]{:S(2)}, u32[]{:S(2)}) collective-permute-start(bf16[2,256,128]{2,1,0:T(8,128)(2,1)S(1)} %get-tuple-element.46), channel_id=1, source_target_pairs={{1,2},{2,1},{3,4},{4,3},{5,6},{6,5},{9,10},{10,9},{11,12},{12,11},... | collective-permute-start | bytes 393224 | tf_op jit(solution)/shard_map/ppermute | solution.py:36
  14.0 20.6 %collective-permute-start.14 = (bf16[2,128,512]{2,1,0:T(8,128)(2,1)S(1)}, bf16[2,128,512]{2,1,0:T(8,128)(2,1)S(1)}, u32[]{:S(2)}, u32[]{:S(2)}) collective-permute-start(bf16[2,128,512]{2,1,0:T(8,128)(2,1)S(1)} %get-tuple-element.47), channel_id=1, source_target_pairs={{0,8},{8,0},{16,24},{24,16},{1,9},{9,1},{17,25},{25,17},{2,10},{10... | collective-permute-start | bytes 786440 | tf_op jit(solution)/shard_map/ppermute | solution.py:36
  14.0 23.1 %collective-permute-start.15 = (bf16[2,128,512]{2,1,0:T(8,128)(2,1)S(1)}, bf16[2,128,512]{2,1,0:T(8,128)(2,1)S(1)}, u32[]{:S(2)}, u32[]{:S(2)}) collective-permute-start(bf16[2,128,512]{2,1,0:T(8,128)(2,1)S(1)} %get-tuple-element.48), channel_id=1, source_target_pairs={{8,16},{16,8},{9,17},{17,9},{10,18},{18,10},{11,19},{19,11},{12,20... | collective-permute-start | bytes 786440 | tf_op jit(solution)/shard_map/ppermute | solution.py:36
  30.9 7.9 %collective-permute-start.5 = (bf16[4,2,32,256]{3,2,1,0:T(8,128)(2,1)S(1)}, bf16[4,2,32,256]{3,2,1,0:T(8,128)(2,1)S(1)}, u32[]{:S(2)}, u32[]{:S(2)}) collective-permute-start(bf16[4,2,32,256]{3,2,1,0:T(8,128)(2,1)S(1)} %get-tuple-element.37), channel_id=1, source_target_pairs={{0,4},{1,5},{2,6},{3,7},{4,0},{5,1},{6,2},{7,3},{8,12},{9,13},{10,... | collective-permute-start | bytes 393224 | tf_op jit(solution)/shard_map/ppermute | solution.py:442
  33.6 6.3 %collective-permute-start.6 = (bf16[4,2,32,256]{3,2,1,0:T(8,128)(2,1)S(1)}, bf16[4,2,32,256]{3,2,1,0:T(8,128)(2,1)S(1)}, u32[]{:S(2)}, u32[]{:S(2)}) collective-permute-start(bf16[4,2,32,256]{3,2,1,0:T(8,128)(2,1)S(1)} %get-tuple-element.38), channel_id=1, source_target_pairs={{0,1},{1,0},{2,3},{3,2},{4,5},{5,4},{6,7},{7,6},{8,9},{9,8},{10,11... | collective-permute-start | bytes 393224 | tf_op jit(solution)/shard_map/ppermute | solution.py:442
  33.6 10.5 %collective-permute-start.7 = (bf16[4,2,32,256]{3,2,1,0:T(8,128)(2,1)S(1)}, bf16[4,2,32,256]{3,2,1,0:T(8,128)(2,1)S(1)}, u32[]{:S(2)}, u32[]{:S(2)}) collective-permute-start(bf16[4,2,32,256]{3,2,1,0:T(8,128)(2,1)S(1)} %get-tuple-element.39), channel_id=1, source_target_pairs={{0,2},{1,3},{2,0},{3,1},{4,6},{5,7},{6,4},{7,5},{8,10},{9,11},{10,... | collective-permute-start | bytes 393224 | tf_op jit(solution)/shard_map/ppermute | solution.py:442
  34.6 9.6 %collective-permute-start.8 = (bf16[4,2,32,256]{3,2,1,0:T(8,128)(2,1)S(1)}, bf16[4,2,32,256]{3,2,1,0:T(8,128)(2,1)S(1)}, u32[]{:S(2)}, u32[]{:S(2)}) collective-permute-start(bf16[4,2,32,256]{3,2,1,0:T(8,128)(2,1)S(1)} %get-tuple-element.40), channel_id=1, source_target_pairs={{0,3},{1,2},{2,1},{3,0},{4,7},{5,6},{6,5},{7,4},{8,11},{9,10},{10,... | collective-permute-start | bytes 393224 | tf_op jit(solution)/shard_map/ppermute | solution.py:442
  37.1 9.6 %collective-permute-start.9 = (bf16[4,2,32,256]{3,2,1,0:T(8,128)(2,1)S(1)}, bf16[4,2,32,256]{3,2,1,0:T(8,128)(2,1)S(1)}, u32[]{:S(2)}, u32[]{:S(2)}) collective-permute-start(bf16[4,2,32,256]{3,2,1,0:T(8,128)(2,1)S(1)} %get-tuple-element.41), channel_id=1, source_target_pairs={{0,5},{1,4},{2,7},{3,6},{4,1},{5,0},{6,3},{7,2},{8,13},{9,12},{10,... | collective-permute-start | bytes 393224 | tf_op jit(solution)/shard_map/ppermute | solution.py:442
  38.8 15.2 %collective-permute-start.10 = (bf16[4,2,32,256]{3,2,1,0:T(8,128)(2,1)S(1)}, bf16[4,2,32,256]{3,2,1,0:T(8,128)(2,1)S(1)}, u32[]{:S(2)}, u32[]{:S(2)}) collective-permute-start(bf16[4,2,32,256]{3,2,1,0:T(8,128)(2,1)S(1)} %get-tuple-element.42), channel_id=1, source_target_pairs={{0,6},{1,7},{2,4},{3,5},{4,2},{5,3},{6,0},{7,1},{8,14},{9,15},{10,... | collective-permute-start | bytes 393224 | tf_op jit(solution)/shard_map/ppermute | solution.py:442
  39.9 16.5 %collective-permute-start.11 = (bf16[4,2,32,256]{3,2,1,0:T(8,128)(2,1)S(1)}, bf16[4,2,32,256]{3,2,1,0:T(8,128)(2,1)S(1)}, u32[]{:S(2)}, u32[]{:S(2)}) collective-permute-start(bf16[4,2,32,256]{3,2,1,0:T(8,128)(2,1)S(1)} %get-tuple-element.43), channel_id=1, source_target_pairs={{0,7},{1,6},{2,5},{3,4},{4,3},{5,2},{6,1},{7,0},{8,15},{9,14},{10,... | collective-permute-start | bytes 393224 | tf_op jit(solution)/shard_map/ppermute | solution.py:442
  61.1 7.0 %collective-permute-start.20 = (bf16[4,2,32,256]{3,2,1,0:T(8,128)(2,1)S(1)}, bf16[4,2,32,256]{3,2,1,0:T(8,128)(2,1)S(1)}, u32[]{:S(2)}, u32[]{:S(2)}) collective-permute-start(bf16[4,2,32,256]{3,2,1,0:T(8,128)(2,1)S(1)} %get-tuple-element.58), channel_id=1, source_target_pairs={{0,4},{1,5},{2,6},{3,7},{4,0},{5,1},{6,2},{7,3},{8,12},{9,13},{10,... | collective-permute-start | bytes 393224 | tf_op jit(solution)/shard_map/ppermute | solution.py:442
  61.1 8.9 %collective-permute-start.24 = (bf16[4,2,32,256]{3,2,1,0:T(8,128)(2,1)S(1)}, bf16[4,2,32,256]{3,2,1,0:T(8,128)(2,1)S(1)}, u32[]{:S(2)}, u32[]{:S(2)}) collective-permute-start(bf16[4,2,32,256]{3,2,1,0:T(8,128)(2,1)S(1)} %get-tuple-element.63), channel_id=1, source_target_pairs={{0,1},{1,0},{2,3},{3,2},{4,5},{5,4},{6,7},{7,6},{8,9},{9,8},{10,11... | collective-permute-start | bytes 393224 | tf_op jit(solution)/shard_map/ppermute | solution.py:442
  62.2 11.7 %collective-permute-start.25 = (bf16[4,2,32,256]{3,2,1,0:T(8,128)(2,1)S(1)}, bf16[4,2,32,256]{3,2,1,0:T(8,128)(2,1)S(1)}, u32[]{:S(2)}, u32[]{:S(2)}) collective-permute-start(bf16[4,2,32,256]{3,2,1,0:T(8,128)(2,1)S(1)} %get-tuple-element.64), channel_id=1, source_target_pairs={{0,2},{1,3},{2,0},{3,1},{4,6},{5,7},{6,4},{7,5},{8,10},{9,11},{10,... | collective-permute-start | bytes 393224 | tf_op jit(solution)/shard_map/ppermute | solution.py:442
  65.7 9.7 %collective-permute-start.26 = (bf16[4,2,32,256]{3,2,1,0:T(8,128)(2,1)S(1)}, bf16[4,2,32,256]{3,2,1,0:T(8,128)(2,1)S(1)}, u32[]{:S(2)}, u32[]{:S(2)}) collective-permute-start(bf16[4,2,32,256]{3,2,1,0:T(8,128)(2,1)S(1)} %get-tuple-element.65), channel_id=1, source_target_pairs={{0,3},{1,2},{2,1},{3,0},{4,7},{5,6},{6,5},{7,4},{8,11},{9,10},{10,... | collective-permute-start | bytes 393224 | tf_op jit(solution)/shard_map/ppermute | solution.py:442
  65.7 12.7 %collective-permute-start.21 = (bf16[4,2,32,256]{3,2,1,0:T(8,128)(2,1)S(1)}, bf16[4,2,32,256]{3,2,1,0:T(8,128)(2,1)S(1)}, u32[]{:S(2)}, u32[]{:S(2)}) collective-permute-start(bf16[4,2,32,256]{3,2,1,0:T(8,128)(2,1)S(1)} %get-tuple-element.59), channel_id=1, source_target_pairs={{0,5},{1,4},{2,7},{3,6},{4,1},{5,0},{6,3},{7,2},{8,13},{9,12},{10,... | collective-permute-start | bytes 393224 | tf_op jit(solution)/shard_map/ppermute | solution.py:442
  68.1 16.9 %collective-permute-start.22 = (bf16[4,2,32,256]{3,2,1,0:T(8,128)(2,1)S(1)}, bf16[4,2,32,256]{3,2,1,0:T(8,128)(2,1)S(1)}, u32[]{:S(2)}, u32[]{:S(2)}) collective-permute-start(bf16[4,2,32,256]{3,2,1,0:T(8,128)(2,1)S(1)} %get-tuple-element.60), channel_id=1, source_target_pairs={{0,6},{1,7},{2,4},{3,5},{4,2},{5,3},{6,0},{7,1},{8,14},{9,15},{10,... | collective-permute-start | bytes 393224 | tf_op jit(solution)/shard_map/ppermute | solution.py:442
  70.0 16.8 %collective-permute-start.23 = (bf16[4,2,32,256]{3,2,1,0:T(8,128)(2,1)S(1)}, bf16[4,2,32,256]{3,2,1,0:T(8,128)(2,1)S(1)}, u32[]{:S(2)}, u32[]{:S(2)}) collective-permute-start(bf16[4,2,32,256]{3,2,1,0:T(8,128)(2,1)S(1)} %get-tuple-element.61), channel_id=1, source_target_pairs={{0,7},{1,6},{2,5},{3,4},{4,3},{5,2},{6,1},{7,0},{8,15},{9,14},{10,... | collective-permute-start | bytes 393224 | tf_op jit(solution)/shard_map/ppermute | solution.py:442
  74.0 15.7 %collective-permute-start.16 = (bf16[2,128,512]{2,1,0:T(8,128)(2,1)S(1)}, bf16[2,128,512]{2,1,0:T(8,128)(2,1)S(1)}, u32[]{:S(2)}, u32[]{:S(2)}) collective-permute-start(bf16[2,128,512]{2,1,0:T(8,128)(2,1)S(1)} %get-tuple-element.53), channel_id=1, source_target_pairs={{0,8},{8,0},{16,24},{24,16},{1,9},{9,1},{17,25},{25,17},{2,10},{10... | collective-permute-start | bytes 786440 | tf_op jit(solution)/shard_map/ppermute | solution.py:36
  75.3 14.3 %collective-permute-start.17 = (bf16[2,128,512]{2,1,0:T(8,128)(2,1)S(1)}, bf16[2,128,512]{2,1,0:T(8,128)(2,1)S(1)}, u32[]{:S(2)}, u32[]{:S(2)}) collective-permute-start(bf16[2,128,512]{2,1,0:T(8,128)(2,1)S(1)} %get-tuple-element.54), channel_id=1, source_target_pairs={{8,16},{16,8},{9,17},{17,9},{10,18},{18,10},{11,19},{19,11},{12,20... | collective-permute-start | bytes 786440 | tf_op jit(solution)/shard_map/ppermute | solution.py:36
  88.4 11.2 %collective-permute-start.27 = (bf16[12,2,32,256]{3,2,1,0:T(8,128)(2,1)S(1)}, bf16[12,2,32,256]{3,2,1,0:T(8,128)(2,1)S(1)}, u32[]{:S(2)}, u32[]{:S(2)}) collective-permute-start(bf16[12,2,32,256]{3,2,1,0:T(8,128)(2,1)S(1)} %shard_map.115), channel_id=1, source_target_pairs={{0,8},{8,16},{16,24},{1,9},{9,17},{17,25},{2,10},{10,18},{18,26},{... | collective-permute-start | bytes 1179656 | tf_op jit(solution)/shard_map/ppermute | solution.py:26
  89.9 6.4 %collective-permute-start.18 = (bf16[2,256,128]{2,1,0:T(8,128)(2,1)S(1)}, bf16[2,256,128]{2,1,0:T(8,128)(2,1)S(1)}, u32[]{:S(2)}, u32[]{:S(2)}) collective-permute-start(bf16[2,256,128]{2,1,0:T(8,128)(2,1)S(1)} %get-tuple-element.56), channel_id=1, source_target_pairs={{0,1},{1,0},{2,3},{3,2},{4,5},{5,4},{6,7},{7,6},{8,9},{9,8},{10,11... | collective-permute-start | bytes 393224 | tf_op jit(solution)/shard_map/ppermute | solution.py:36
  90.9 7.7 %collective-permute-start.19 = (bf16[2,256,128]{2,1,0:T(8,128)(2,1)S(1)}, bf16[2,256,128]{2,1,0:T(8,128)(2,1)S(1)}, u32[]{:S(2)}, u32[]{:S(2)}) collective-permute-start(bf16[2,256,128]{2,1,0:T(8,128)(2,1)S(1)} %get-tuple-element.57), channel_id=1, source_target_pairs={{1,2},{2,1},{3,4},{4,3},{5,6},{6,5},{9,10},{10,9},{11,12},{12,11},... | collective-permute-start | bytes 393224 | tf_op jit(solution)/shard_map/ppermute | solution.py:36
  (6 other events, 129.3 us)

commit v4 on v3

--- a/solution.py
+++ b/solution.py
@@ -160,33 +160,33 @@
     )
 
 
-def prepare_kernel(
-    me, coeffs, region, tile, payload, low, even, odd, coeffs_held, region_held, tile_held, sem
-):
+def prepare_kernel(me, tile, low, even, odd, held, sem):
+    half = even.shape[2]
+    copy = pltpu.make_async_copy(tile, held, sem)
+    copy.start()
+    copy.wait()
+    low[...] = held[...].astype(jnp.bfloat16)
+    first, second = by_side(me[0], low[:, :, :half], low[:, :, low.shape[2] - half :])
+    even[...] = first
+    odd[...] = second
+
+
+def pair_kernel(coeffs, region, *refs):
+    across = refs[:-4]
+    out, coeffs_held, region_held, sem = refs[-4:]
     slots, num_modes = coeffs.shape[2:]
-    half = even.shape[2]
     copies = [
-        pltpu.make_async_copy(source, held, sem.at[at])
-        for at, (source, held) in enumerate(
-            ((coeffs, coeffs_held), (region, region_held), (tile, tile_held))
-        )
+        pltpu.make_async_copy(coeffs, coeffs_held, sem.at[0]),
+        pltpu.make_async_copy(region, region_held, sem.at[1]),
     ]
     for copy in copies:
         copy.start()
-    payload[...] = jnp.zeros_like(payload)
+    out[...] = jnp.zeros_like(out)
     for copy in copies:
         copy.wait()
-    payload[:slots, :num_modes] = coeffs_held[0, 0]
-    payload[slots:, :slots] = region_held[0].astype(jnp.float32)
-    low[...] = tile_held[...].astype(jnp.bfloat16)
-    first, second = by_side(me[0], low[:, :, :half], low[:, :, low.shape[2] - half :])
-    even[...] = first
-    odd[...] = second
-
-
-def pair_kernel(mine, across, out):
-    out[0] = mine[...]
-    out[1] = across[...]
+    for at, (weights, regions) in enumerate([(coeffs_held, region_held), across][: out.shape[0]]):
+        out[at, :slots, :num_modes] = weights[0, 0]
+        out[at, slots:, :slots] = regions[0].astype(jnp.float32)
 
 
 def widen_kernel(row, me, tile, even, odd, first, second):
@@ -367,14 +367,13 @@
     out[:, :, cols - half :] += got_right.astype(jnp.float32)
 
 
-def sums_kernel(held_in, places, goals, row, *refs):
+def sums_kernel(held_in, places, goals, start, num_modes, row, *refs):
     count = len(places)
     received = refs[held_in : held_in + count]
     added = refs[held_in + count : held_in + count + sum(goal[2] for goal in goals)]
     outs = refs[held_in + count + len(added) : -3]
     terms, held, sem = refs[-3:]
     copies = fetch(refs[:held_in], places, held, sem)
-    num_modes = outs[0].shape[-4]
     slot_count = received[0].shape[0]
     slots = slot_count
     first = min(goal[1] for goal in goals)
@@ -389,7 +388,7 @@
             region = (row[0] + step).astype(jnp.float32)
             addend = rest.pop(0) if adds else None
             scales = [
-                jnp.where(held[at, slots, slot] == region, held[at, slot, k], 0.0)
+                jnp.where(held[at, slots, slot] == region, held[at, slot, start + k], 0.0)
                 for at in range(count)
                 for slot in range(first, slot_count)
             ]
@@ -401,17 +400,32 @@
                 for scale, piece in zip(scales[1:], pieces[1:]):
                     total += scale * piece
                 if adds:
-                    total += addend[k, part].astype(jnp.float32)
+                    total += addend[start + k, part].astype(jnp.float32)
                 out[k, part] = total.astype(out.dtype)
         return carry
 
     lax.fori_loop(0, num_modes, mode_step, 0)
 
 
-def sums(row, goals, weights, places, received, added, num_modes, dtypes):
+def halves(num_modes):
+    half = num_modes // 2
+    return [(0, half), (half, num_modes - half)] if half else [(0, num_modes)]
+
+
+def last_kernel(own, *refs):
+    out = refs[-1]
+    start = 0
+    for passed in refs[:-1]:
+        modes = pl.ds(start, passed.shape[0])
+        out[0, modes] = own[modes] + passed[...].astype(jnp.float32)
+        start += passed.shape[0]
+
+
+def sums(row, goals, weights, places, received, added, modes, dtypes):
+    start, num_modes = modes
     shape = (num_modes,) + received[0].shape[1:]
     return call(
-        functools.partial(sums_kernel, len(weights), places, goals),
+        functools.partial(sums_kernel, len(weights), places, goals, start, num_modes),
         [(shape, dtype) for dtype in dtypes],
         (row, SMEM),
         *weights,
@@ -442,21 +456,27 @@
         return lax.ppermute(value, "col", [(i, goes_to(i, step)) for i in range(count)])
 
     side = (2, rows, half)
-    payload, low, *edges = call(
+    low, *edges = call(
         prepare_kernel,
-        [((slot_count + 1, LANES), jnp.float32), (object_field.shape, jnp.bfloat16)]
-        + [(side, jnp.bfloat16)] * 2,
+        [(object_field.shape, jnp.bfloat16)] + [(side, jnp.bfloat16)] * 2,
         (me, SMEM),
-        (coeffs, HBM),
-        (region, HBM),
         (object_field, HBM),
-        scratch=[pltpu.VMEM(x.shape, x.dtype) for x in (coeffs, region, object_field)]
-        + [pltpu.SemaphoreType.DMA((3,))],
-    )
+        scratch=[pltpu.VMEM(object_field.shape, object_field.dtype), pltpu.SemaphoreType.DMA],
+    )
+
+    def paired(*across):
+        return call(
+            pair_kernel,
+            [((1 + len(across) // 2, slot_count + 1, LANES), jnp.float32)],
+            (coeffs, HBM),
+            (region, HBM),
+            *across,
+            scratch=[pltpu.VMEM(x.shape, x.dtype) for x in (coeffs, region)]
+            + [pltpu.SemaphoreType.DMA((2,))],
+        )[0]
+
     if count > 1 and count & (count - 1) == 0:
-        across = move(payload, middle_step)
-        blocks_shape = (2,) + payload.shape
-        (pair,) = call(pair_kernel, [(blocks_shape, jnp.float32)], payload, across)
+        pair = paired(move(coeffs, middle_step), move(region, middle_step))
         weights = [pair] + [move(pair, step) for step in near]
 
         def made_at(step):
@@ -464,8 +484,8 @@
 
         came_at = made_at
     else:
-        weights = [payload[None]]
-        weights += [move(payload[None], step) for step in range(1, count)]
+        weights = [paired()]
+        weights += [move(weights[0], step) for step in range(1, count)]
 
         def made_at(step):
             return -step % count, 0
@@ -527,7 +547,7 @@
         cols_kernel, [(object_field.shape, jnp.float32)], (me, SMEM), center, *over_sides
     )
 
-    def add_up(group, goals, added, dtypes):
+    def add_up(group, goals, added, modes, dtypes):
         return sums(
             row,
             goals,
@@ -535,17 +555,18 @@
             [came_at(step) for step in group],
             [received[step] for step in group],
             added,
-            num_modes,
+            modes,
             dtypes,
         )
 
-    own, following = add_up(
-        [0] + near, ((0, 0, False), (1, 1, False)), [], [jnp.float32, jnp.float32]
-    )
-    (following,) = add_up(crossing, ((1, 1, True),), [following], [jnp.bfloat16])
-    passed = shift(following, "row", 1)
-    (own,) = add_up(crossing, ((0, 0, True),), [own], [jnp.float32])
-    mode_grad = (own + passed.astype(jnp.float32))[None]
+    everything = (0, num_modes)
+    (following,) = add_up([0] + near, ((1, 1, False),), [], everything, [jnp.float32])
+    passed = []
+    for modes_part in halves(num_modes):
+        (part,) = add_up(crossing, ((1, 1, True),), [following], modes_part, [jnp.bfloat16])
+        passed.append(shift(part, "row", 1))
+    (own,) = add_up(every, ((0, 0, False),), [], everything, [jnp.float32])
+    (mode_grad,) = call(last_kernel, [((1,) + own.shape, jnp.float32)], own, *passed)
     return (object_grad, mode_grad)
 
 

time: 101 us -> 111 us (1.099)
  waiting for transfers between devices: 41.5 us -> 49.6 us
  Pallas kernels: 21.8 us -> 24.4 us
    ppermute x18 -> x19, waiting for transfers between devices: 31.1 us -> 40.4 us  [move(): lax.ppermute(value, 'col', [(i, goes_to(i, step)) for i in range(count)])]
    ppermute x2 -> x3, starting transfers between devices: 2.74 us -> 6.62 us  [shift(): return lax.ppermute(value, axis, pairs)]
    ppermute x18 -> x19, starting transfers between devices: 23.4 us -> 20.6 us  [move(): lax.ppermute(value, 'col', [(i, goes_to(i, step)) for i in range(count)])]
    pallas_call x12 -> x14, Pallas kernels: 21.8 us -> 24.4 us  [call(): pl.pallas_call(body, out_shape=tuple(outs), in_specs=specs, out_specs=tup...]
    ppermute x8, starting transfers between devices: 8.71 us -> 7.51 us  [swap(): lax.ppermute(value, axis, pairs)]
  transfers between devices with their start and end apart: 28 -> 30, of which waited for: 15 -> 14; matrix products, arithmetic and copies ran while one was open for 0% -> 0% of each run, Pallas kernels for 17% -> 17%
where the time goes in v4:
time: 111 us; the launch traced here: 110 us
  waiting for transfers between devices  49.6 us (45%)
  starting transfers between devices  34.8 us (31%)
  Pallas kernels  24.4 us (22%)
  between operations  1.55 us (1%)
    ppermute x19, waiting for transfers between devices, move(): lax.ppermute(value, 'col', [(i, goes_to(i, step)) for i in range(count)])  40.4 us
    pallas_call x14, Pallas kernels, call(): pl.pallas_call(body, out_shape=tuple(outs), in_specs=specs, out_specs=tup...  24.4 us
    ppermute x19, starting transfers between devices, move(): lax.ppermute(value, 'col', [(i, goes_to(i, step)) for i in range(count)])  20.6 us
    ppermute x8, waiting for transfers between devices, swap(): lax.ppermute(value, axis, pairs)  9.23 us
    ppermute x8, starting transfers between devices, swap(): lax.ppermute(value, axis, pairs)  7.51 us
    ppermute x3, starting transfers between devices, shift(): return lax.ppermute(value, axis, pairs)  6.62 us
  transfers between devices with their start and end apart: 30, of which 14 were waited for; matrix products, arithmetic and copies ran while one was open for 0% of the time, Pallas kernels for 17%

profile of v4, /device:TPU:8, one launch (start us, length us, event | category | flops | bytes accessed | tf_op | source)
XLA Modules:
  0.0 110.4 jit_solution(17355853714016442295)
XLA Ops:
  4.8 1.9 %collective-permute-start.14 = (bf16[2,256,128]{2,1,0:T(8,128)(2,1)S(1)}, bf16[2,256,128]{2,1,0:T(8,128)(2,1)S(1)}, u32[]{:S(2)}, u32[]{:S(2)}) collective-permute-start(bf16[2,256,128]{2,1,0:T(8,128)(2,1)S(1)} %get-tuple-element.42), channel_id=1, source_target_pairs={{1,2},{2,1},{3,4},{4,3},{5,6},{6,5},{9,10},{10,9},{11,12},{12,11},... | collective-permute-start | bytes 393224 | tf_op jit(solution)/shard_map/ppermute | solution.py:36
  6.7 2.8 %collective-permute-done.13.even.side_even = bf16[2,256,128]{2,1,0:T(8,128)(2,1)S(1)} collective-permute-done((bf16[2,256,128]{2,1,0:T(8,128)(2,1)S(1)}, bf16[2,256,128]{2,1,0:T(8,128)(2,1)S(1)}, u32[]{:S(2)}, u32[]{:S(2)}) %collective-permute-start.13) | collective-permute-done | bytes 131104 | tf_op jit(solution)/shard_map/ppermute | solution.py:36
  9.5 4.3 %collective-permute-done.14.odd.side_odd = bf16[2,256,128]{2,1,0:T(8,128)(2,1)S(1)} collective-permute-done((bf16[2,256,128]{2,1,0:T(8,128)(2,1)S(1)}, bf16[2,256,128]{2,1,0:T(8,128)(2,1)S(1)}, u32[]{:S(2)}, u32[]{:S(2)}) %collective-permute-start.14) | collective-permute-done | bytes 131104 | tf_op jit(solution)/shard_map/ppermute | solution.py:36
  14.7 2.7 %collective-permute-start = (f32[1,1,4,12]{3,2,1,0:T(4,128)}, f32[1,1,4,12]{3,2,1,0:T(4,128)S(1)}, u32[]{:S(2)}, u32[]{:S(2)}) collective-permute-start(f32[1,1,4,12]{3,2,1,0:T(4,128)} %coeffs.1), channel_id=1, source_target_pairs={{0,4},{1,5},{2,6},{3,7},{4,0},{5,1},{6,2},{7,3},{8,12},{9,13},{10,... | collective-permute-start | bytes 584 | tf_op jit(solution)/shard_map/ppermute | solution.py:456
  17.7 4.3 %collective-permute-done.1.refs_1_ = s32[1,1,4]{2,1,0:T(1,128)S(1)} collective-permute-done((s32[1,1,4]{2,1,0:T(1,128)}, s32[1,1,4]{2,1,0:T(1,128)S(1)}, u32[]{:S(2)}, u32[]{:S(2)}) %collective-permute-start.1) | collective-permute-done | bytes 48 | tf_op jit(solution)/shard_map/ppermute | solution.py:456
  23.2 4.0 %collective-permute-done.4.refs_3_ = f32[2,5,128]{2,1,0:T(8,128)S(1)} collective-permute-done((f32[2,5,128]{2,1,0:T(8,128)S(1)}, f32[2,5,128]{2,1,0:T(8,128)S(1)}, u32[]{:S(2)}, u32[]{:S(2)}) %collective-permute-start.4) | collective-permute-done | bytes 5152 | tf_op jit(solution)/shard_map/ppermute | solution.py:456
  27.3 3.6 %collective-permute-done.2.refs_1_ = f32[2,5,128]{2,1,0:T(8,128)S(1)} collective-permute-done((f32[2,5,128]{2,1,0:T(8,128)S(1)}, f32[2,5,128]{2,1,0:T(8,128)S(1)}, u32[]{:S(2)}, u32[]{:S(2)}) %collective-permute-start.2) | collective-permute-done | bytes 5152 | tf_op jit(solution)/shard_map/ppermute | solution.py:456
  30.9 3.4 %shard_map.105 = (bf16[4,2,32,256]{3,2,1,0:T(8,128)(2,1)S(1)}, bf16[4,2,32,256]{3,2,1,0:T(8,128)(2,1)S(1)}, bf16[4,2,32,256]{3,2,1,0:T(8,128)(2,1)S(1)}, bf16[4,...) custom-call(s32[1]{0:T(128)} %bitcast.1.row, ...), custom_call_target="tpu_custom_call" | custom-call | tf_op jit(solution)/shard_map/pallas_call | solution.py:91
  35.6 2.7 %collective-permute-start.9 = (bf16[4,2,32,256]{3,2,1,0:T(8,128)(2,1)S(1)}, bf16[4,2,32,256]{3,2,1,0:T(8,128)(2,1)S(1)}, u32[]{:S(2)}, u32[]{:S(2)}) collective-permute-start(bf16[4,2,32,256]{3,2,1,0:T(8,128)(2,1)S(1)} %get-tuple-element.36), channel_id=1, source_target_pairs={{0,3},{1,2},{2,1},{3,0},{4,7},{5,6},{6,5},{7,4},{8,11},{9,10},{10,... | collective-permute-start | bytes 393224 | tf_op jit(solution)/shard_map/ppermute | solution.py:456
  38.3 2.0 %collective-permute-start.10 = (bf16[4,2,32,256]{3,2,1,0:T(8,128)(2,1)S(1)}, bf16[4,2,32,256]{3,2,1,0:T(8,128)(2,1)S(1)}, u32[]{:S(2)}, u32[]{:S(2)}) collective-permute-start(bf16[4,2,32,256]{3,2,1,0:T(8,128)(2,1)S(1)} %get-tuple-element.37), channel_id=1, source_target_pairs={{0,5},{1,4},{2,7},{3,6},{4,1},{5,0},{6,3},{7,2},{8,13},{9,12},{10,... | collective-permute-start | bytes 393224 | tf_op jit(solution)/shard_map/ppermute | solution.py:456
  44.4 2.6 %shard_map.108 = (bf16[4,2,256,256]{3,2,1,0:T(8,128)(2,1)S(1)}, f32[4,256,256]{2,1,0:T(8,128)S(1)}) custom-call(s32[1]{0:T(128)} %bitcast.1.row, s32[1]{0:T(128)} %bitcast.me, s32[2,4]{1,0:T(2,128)} %bitcast.5, bf16[2,256,256]{2,1,0:T(8,128)(2,1)S(1)} %get-tuple-element.40.tile, bf16[2,256,128]{2,1,0:T(8,128)(2,1)S(1)} %collective-permute-done.13.even.side_even, ...), custom_call_target="tpu_custom_call" | custom-call | tf_op jit(solution)/shard_map/pallas_call | solution.py:91
  47.1 5.3 %collective-permute-done.10.refs_5_ = bf16[4,2,32,256]{3,2,1,0:T(8,128)(2,1)S(1)} collective-permute-done((bf16[4,2,32,256]{3,2,1,0:T(8,128)(2,1)S(1)}, bf16[4,2,32,256]{3,2,1,0:T(8,128)(2,1)S(1)}, u32[]{:S(2)}, u32[]{:S(2)}) %collective-permute-start.10) | collective-permute-done | bytes 131104 | tf_op jit(solution)/shard_map/ppermute | solution.py:456
  52.4 4.5 %collective-permute-done.11.refs_6_ = bf16[4,2,32,256]{3,2,1,0:T(8,128)(2,1)S(1)} collective-permute-done((bf16[4,2,32,256]{3,2,1,0:T(8,128)(2,1)S(1)}, bf16[4,2,32,256]{3,2,1,0:T(8,128)(2,1)S(1)}, u32[]{:S(2)}, u32[]{:S(2)}) %collective-permute-start.11) | collective-permute-done | bytes 131104 | tf_op jit(solution)/shard_map/ppermute | solution.py:456
  58.6 4.7 %shard_map.109 = (bf16[4,2,32,256]{3,2,1,0:T(8,128)(2,1)S(1)}, bf16[4,2,32,256]{3,2,1,0:T(8,128)(2,1)S(1)}, bf16[4,2,32,256]{3,2,1,0:T(8,128)(2,1)S(1)}, bf16[4,...) custom-call(s32[1,1]{1,0:T(1,128)S(6)} %copy.11.counts, ...), custom_call_target="tpu_custom_call" | custom-call | tf_op jit(solution)/shard_map/pallas_call | solution.py:91
  67.0 3.1 %shard_map.110 = (bf16[2,128,512]{2,1,0:T(8,128)(2,1)S(1)}, f32[2,256,512]{2,1,0:T(8,128)S(1)}, bf16[2,128,512]{2,1,0:T(8,128)(2,1)S(1)}) custom-call(s32[1]{0:T(128)} %bitcast.1.row, s32[2,4]{1,0:T(2,128)} %bitcast.6, f32[4,2,256,256]{3,2,1,0:T(8,128)S(1)} %get-tuple-element.47.pieces), custom_call_target="tpu_custom_call" | custom-call | tf_op jit(solution)/shard_map/pallas_call | solution.py:91
  71.2 3.3 %collective-permute-start.25 = (bf16[4,2,32,256]{3,2,1,0:T(8,128)(2,1)S(1)}, bf16[4,2,32,256]{3,2,1,0:T(8,128)(2,1)S(1)}, u32[]{:S(2)}, u32[]{:S(2)}) collective-permute-start(bf16[4,2,32,256]{3,2,1,0:T(8,128)(2,1)S(1)} %get-tuple-element.59), channel_id=1, source_target_pairs={{0,5},{1,4},{2,7},{3,6},{4,1},{5,0},{6,3},{7,2},{8,13},{9,12},{10,... | collective-permute-start | bytes 393224 | tf_op jit(solution)/shard_map/ppermute | solution.py:456
  78.0 8.2 %collective-permute-done.25.refs_9_.refs_5_ = bf16[4,2,32,256]{3,2,1,0:T(8,128)(2,1)S(1)} collective-permute-done((bf16[4,2,32,256]{3,2,1,0:T(8,128)(2,1)S(1)}, bf16[4,2,32,256]{3,2,1,0:T(8,128)(2,1)S(1)}, u32[]{:S(2)}, u32[]{:S(2)}) %collective-permute-start.25) | collective-permute-done | bytes 131104 | tf_op jit(solution)/shard_map/ppermute | solution.py:456
  86.3 4.0 %collective-permute-done.26.refs_10_.refs_6_ = bf16[4,2,32,256]{3,2,1,0:T(8,128)(2,1)S(1)} collective-permute-done((bf16[4,2,32,256]{3,2,1,0:T(8,128)(2,1)S(1)}, bf16[4,2,32,256]{3,2,1,0:T(8,128)(2,1)S(1)}, u32[]{:S(2)}, u32[]{:S(2)}) %collective-permute-start.26) | collective-permute-done | bytes 131104 | tf_op jit(solution)/shard_map/ppermute | solution.py:456
  90.3 2.9 %collective-permute-done.27.refs_11_.refs_7_ = bf16[4,2,32,256]{3,2,1,0:T(8,128)(2,1)S(1)} collective-permute-done((bf16[4,2,32,256]{3,2,1,0:T(8,128)(2,1)S(1)}, bf16[4,2,32,256]{3,2,1,0:T(8,128)(2,1)S(1)}, u32[]{:S(2)}, u32[]{:S(2)}) %collective-permute-start.27) | collective-permute-done | bytes 131104 | tf_op jit(solution)/shard_map/ppermute | solution.py:456
  94.3 2.1 %collective-permute-start.28 = (bf16[6,2,32,256]{3,2,1,0:T(8,128)(2,1)S(1)}, bf16[6,2,32,256]{3,2,1,0:T(8,128)(2,1)S(1)}, u32[]{:S(2)}, u32[]{:S(2)}) collective-permute-start(bf16[6,2,32,256]{3,2,1,0:T(8,128)(2,1)S(1)} %shard_map.115), channel_id=1, source_target_pairs={{0,8},{8,16},{16,24},{1,9},{9,17},{17,25},{2,10},{10,18},{18,26},{... | collective-permute-start | bytes 589832 | tf_op jit(solution)/shard_map/ppermute | solution.py:26
  97.5 3.1 %collective-permute-start.29 = (bf16[6,2,32,256]{3,2,1,0:T(8,128)(2,1)S(1)}, bf16[6,2,32,256]{3,2,1,0:T(8,128)(2,1)S(1)}, u32[]{:S(2)}, u32[]{:S(2)}) collective-permute-start(bf16[6,2,32,256]{3,2,1,0:T(8,128)(2,1)S(1)} %shard_map.116), channel_id=1, source_target_pairs={{0,8},{8,16},{16,24},{1,9},{9,17},{17,25},{2,10},{10,18},{18,26},{... | collective-permute-start | bytes 589832 | tf_op jit(solution)/shard_map/ppermute | solution.py:26
  101.5 1.9 %collective-permute-start.20 = (bf16[2,256,128]{2,1,0:T(8,128)(2,1)S(1)}, bf16[2,256,128]{2,1,0:T(8,128)(2,1)S(1)}, u32[]{:S(2)}, u32[]{:S(2)}) collective-permute-start(bf16[2,256,128]{2,1,0:T(8,128)(2,1)S(1)} %get-tuple-element.53), channel_id=1, source_target_pairs={{1,2},{2,1},{3,4},{4,3},{5,6},{6,5},{9,10},{10,9},{11,12},{12,11},... | collective-permute-start | bytes 393224 | tf_op jit(solution)/shard_map/ppermute | solution.py:36
  103.4 2.9 %shard_map.113.own = f32[12,2,32,256]{3,2,1,0:T(8,128)S(1)} custom-call(s32[1]{0:T(128)} %bitcast.1.row, f32[2,5,128]{2,1,0:T(8,128)S(1)} %shard_map.104.refs_0_, f32[2,5,128]{2,1,0:T(8,128)S(1)} %collective-permute-done.2.refs_1_, f32[2,5,128]{2,1,0:T(8,128)S(1)} %collective-permute-done.3.refs_2_, f32[2,5,128]{2,1,0:T(8,128)S(1)} %collective-permute-done.4.refs_3_, ...), custom_call_target="tpu_custom_call" | custom-call | tf_op jit(solution)/shard_map/pallas_call | solution.py:91
  107.3 2.1 %collective-permute-done.20.odd = bf16[2,256,128]{2,1,0:T(8,128)(2,1)S(1)} collective-permute-done((bf16[2,256,128]{2,1,0:T(8,128)(2,1)S(1)}, bf16[2,256,128]{2,1,0:T(8,128)(2,1)S(1)}, u32[]{:S(2)}, u32[]{:S(2)}) %collective-permute-start.20) | collective-permute-done | bytes 131104 | tf_op jit(solution)/shard_map/ppermute | solution.py:36
  (54 shorter events, 26.3 us)
Async XLA Ops:
  0.7 30.3 %collective-permute-start.5 = (bf16[1,12,2,32,256]{4,3,2,1,0:T(8,128)(2,1)}, bf16[1,12,2,32,256]{4,3,2,1,0:T(8,128)(2,1)S(1)}, u32[]{:S(2)}, u32[]{:S(2)}) collective-permute-start(bf16[1,12,2,32,256]{4,3,2,1,0:T(8,128)(2,1)} %refs_4_.1), channel_id=1, source_target_pairs={{8,0},{16,8},{24,16},{9,1},{17,9},{25,17},{10,2},{18,10},{26,18},{... | collective-permute-start | bytes 1179656 | tf_op jit(solution)/shard_map/ppermute | solution.py:26
  4.8 9.0 %collective-permute-start.14 = (bf16[2,256,128]{2,1,0:T(8,128)(2,1)S(1)}, bf16[2,256,128]{2,1,0:T(8,128)(2,1)S(1)}, u32[]{:S(2)}, u32[]{:S(2)}) collective-permute-start(bf16[2,256,128]{2,1,0:T(8,128)(2,1)S(1)} %get-tuple-element.42), channel_id=1, source_target_pairs={{1,2},{2,1},{3,4},{4,3},{5,6},{6,5},{9,10},{10,9},{11,12},{12,11},... | collective-permute-start | bytes 393224 | tf_op jit(solution)/shard_map/ppermute | solution.py:36
  13.9 21.7 %collective-permute-start.15 = (bf16[2,128,512]{2,1,0:T(8,128)(2,1)S(1)}, bf16[2,128,512]{2,1,0:T(8,128)(2,1)S(1)}, u32[]{:S(2)}, u32[]{:S(2)}) collective-permute-start(bf16[2,128,512]{2,1,0:T(8,128)(2,1)S(1)} %get-tuple-element.43), channel_id=1, source_target_pairs={{0,8},{8,0},{16,24},{24,16},{1,9},{9,1},{17,25},{25,17},{2,10},{10... | collective-permute-start | bytes 786440 | tf_op jit(solution)/shard_map/ppermute | solution.py:36
  14.0 24.3 %collective-permute-start.16 = (bf16[2,128,512]{2,1,0:T(8,128)(2,1)S(1)}, bf16[2,128,512]{2,1,0:T(8,128)(2,1)S(1)}, u32[]{:S(2)}, u32[]{:S(2)}) collective-permute-start(bf16[2,128,512]{2,1,0:T(8,128)(2,1)S(1)} %get-tuple-element.44), channel_id=1, source_target_pairs={{8,16},{16,8},{9,17},{17,9},{10,18},{18,10},{11,19},{19,11},{12,20... | collective-permute-start | bytes 786440 | tf_op jit(solution)/shard_map/ppermute | solution.py:36
  14.7 7.3 %collective-permute-start = (f32[1,1,4,12]{3,2,1,0:T(4,128)}, f32[1,1,4,12]{3,2,1,0:T(4,128)S(1)}, u32[]{:S(2)}, u32[]{:S(2)}) collective-permute-start(f32[1,1,4,12]{3,2,1,0:T(4,128)} %coeffs.1), channel_id=1, source_target_pairs={{0,4},{1,5},{2,6},{3,7},{4,0},{5,1},{6,2},{7,3},{8,12},{9,13},{10,... | collective-permute-start | bytes 584 | tf_op jit(solution)/shard_map/ppermute | solution.py:456
  34.4 7.3 %collective-permute-start.6 = (bf16[4,2,32,256]{3,2,1,0:T(8,128)(2,1)S(1)}, bf16[4,2,32,256]{3,2,1,0:T(8,128)(2,1)S(1)}, u32[]{:S(2)}, u32[]{:S(2)}) collective-permute-start(bf16[4,2,32,256]{3,2,1,0:T(8,128)(2,1)S(1)} %get-tuple-element.33), channel_id=1, source_target_pairs={{0,4},{1,5},{2,6},{3,7},{4,0},{5,1},{6,2},{7,3},{8,12},{9,13},{10,... | collective-permute-start | bytes 393224 | tf_op jit(solution)/shard_map/ppermute | solution.py:456
  34.8 7.6 %collective-permute-start.7 = (bf16[4,2,32,256]{3,2,1,0:T(8,128)(2,1)S(1)}, bf16[4,2,32,256]{3,2,1,0:T(8,128)(2,1)S(1)}, u32[]{:S(2)}, u32[]{:S(2)}) collective-permute-start(bf16[4,2,32,256]{3,2,1,0:T(8,128)(2,1)S(1)} %get-tuple-element.34), channel_id=1, source_target_pairs={{0,1},{1,0},{2,3},{3,2},{4,5},{5,4},{6,7},{7,6},{8,9},{9,8},{10,11... | collective-permute-start | bytes 393224 | tf_op jit(solution)/shard_map/ppermute | solution.py:456
  35.3 11.8 %collective-permute-start.8 = (bf16[4,2,32,256]{3,2,1,0:T(8,128)(2,1)S(1)}, bf16[4,2,32,256]{3,2,1,0:T(8,128)(2,1)S(1)}, u32[]{:S(2)}, u32[]{:S(2)}) collective-permute-start(bf16[4,2,32,256]{3,2,1,0:T(8,128)(2,1)S(1)} %get-tuple-element.35), channel_id=1, source_target_pairs={{0,2},{1,3},{2,0},{3,1},{4,6},{5,7},{6,4},{7,5},{8,10},{9,11},{10,... | collective-permute-start | bytes 393224 | tf_op jit(solution)/shard_map/ppermute | solution.py:456
  35.6 11.5 %collective-permute-start.9 = (bf16[4,2,32,256]{3,2,1,0:T(8,128)(2,1)S(1)}, bf16[4,2,32,256]{3,2,1,0:T(8,128)(2,1)S(1)}, u32[]{:S(2)}, u32[]{:S(2)}) collective-permute-start(bf16[4,2,32,256]{3,2,1,0:T(8,128)(2,1)S(1)} %get-tuple-element.36), channel_id=1, source_target_pairs={{0,3},{1,2},{2,1},{3,0},{4,7},{5,6},{6,5},{7,4},{8,11},{9,10},{10,... | collective-permute-start | bytes 393224 | tf_op jit(solution)/shard_map/ppermute | solution.py:456
  38.3 14.1 %collective-permute-start.10 = (bf16[4,2,32,256]{3,2,1,0:T(8,128)(2,1)S(1)}, bf16[4,2,32,256]{3,2,1,0:T(8,128)(2,1)S(1)}, u32[]{:S(2)}, u32[]{:S(2)}) collective-permute-start(bf16[4,2,32,256]{3,2,1,0:T(8,128)(2,1)S(1)} %get-tuple-element.37), channel_id=1, source_target_pairs={{0,5},{1,4},{2,7},{3,6},{4,1},{5,0},{6,3},{7,2},{8,13},{9,12},{10,... | collective-permute-start | bytes 393224 | tf_op jit(solution)/shard_map/ppermute | solution.py:456
  41.7 15.2 %collective-permute-start.11 = (bf16[4,2,32,256]{3,2,1,0:T(8,128)(2,1)S(1)}, bf16[4,2,32,256]{3,2,1,0:T(8,128)(2,1)S(1)}, u32[]{:S(2)}, u32[]{:S(2)}) collective-permute-start(bf16[4,2,32,256]{3,2,1,0:T(8,128)(2,1)S(1)} %get-tuple-element.38), channel_id=1, source_target_pairs={{0,6},{1,7},{2,4},{3,5},{4,2},{5,3},{6,0},{7,1},{8,14},{9,15},{10,... | collective-permute-start | bytes 393224 | tf_op jit(solution)/shard_map/ppermute | solution.py:456
  42.4 16.2 %collective-permute-start.12 = (bf16[4,2,32,256]{3,2,1,0:T(8,128)(2,1)S(1)}, bf16[4,2,32,256]{3,2,1,0:T(8,128)(2,1)S(1)}, u32[]{:S(2)}, u32[]{:S(2)}) collective-permute-start(bf16[4,2,32,256]{3,2,1,0:T(8,128)(2,1)S(1)} %get-tuple-element.39), channel_id=1, source_target_pairs={{0,7},{1,6},{2,5},{3,4},{4,3},{5,2},{6,1},{7,0},{8,15},{9,14},{10,... | collective-permute-start | bytes 393224 | tf_op jit(solution)/shard_map/ppermute | solution.py:456
  63.2 7.3 %collective-permute-start.21 = (bf16[4,2,32,256]{3,2,1,0:T(8,128)(2,1)S(1)}, bf16[4,2,32,256]{3,2,1,0:T(8,128)(2,1)S(1)}, u32[]{:S(2)}, u32[]{:S(2)}) collective-permute-start(bf16[4,2,32,256]{3,2,1,0:T(8,128)(2,1)S(1)} %get-tuple-element.55), channel_id=1, source_target_pairs={{0,4},{1,5},{2,6},{3,7},{4,0},{5,1},{6,2},{7,3},{8,12},{9,13},{10,... | collective-permute-start | bytes 393224 | tf_op jit(solution)/shard_map/ppermute | solution.py:456
  63.3 7.9 %collective-permute-start.22 = (bf16[4,2,32,256]{3,2,1,0:T(8,128)(2,1)S(1)}, bf16[4,2,32,256]{3,2,1,0:T(8,128)(2,1)S(1)}, u32[]{:S(2)}, u32[]{:S(2)}) collective-permute-start(bf16[4,2,32,256]{3,2,1,0:T(8,128)(2,1)S(1)} %get-tuple-element.56), channel_id=1, source_target_pairs={{0,1},{1,0},{2,3},{3,2},{4,5},{5,4},{6,7},{7,6},{8,9},{9,8},{10,11... | collective-permute-start | bytes 393224 | tf_op jit(solution)/shard_map/ppermute | solution.py:456
  64.9 9.7 %collective-permute-start.23 = (bf16[4,2,32,256]{3,2,1,0:T(8,128)(2,1)S(1)}, bf16[4,2,32,256]{3,2,1,0:T(8,128)(2,1)S(1)}, u32[]{:S(2)}, u32[]{:S(2)}) collective-permute-start(bf16[4,2,32,256]{3,2,1,0:T(8,128)(2,1)S(1)} %get-tuple-element.57), channel_id=1, source_target_pairs={{0,2},{1,3},{2,0},{3,1},{4,6},{5,7},{6,4},{7,5},{8,10},{9,11},{10,... | collective-permute-start | bytes 393224 | tf_op jit(solution)/shard_map/ppermute | solution.py:456
  66.7 8.3 %collective-permute-start.24 = (bf16[4,2,32,256]{3,2,1,0:T(8,128)(2,1)S(1)}, bf16[4,2,32,256]{3,2,1,0:T(8,128)(2,1)S(1)}, u32[]{:S(2)}, u32[]{:S(2)}) collective-permute-start(bf16[4,2,32,256]{3,2,1,0:T(8,128)(2,1)S(1)} %get-tuple-element.58), channel_id=1, source_target_pairs={{0,3},{1,2},{2,1},{3,0},{4,7},{5,6},{6,5},{7,4},{8,11},{9,10},{10,... | collective-permute-start | bytes 393224 | tf_op jit(solution)/shard_map/ppermute | solution.py:456
  70.1 30.6 %collective-permute-start.17 = (bf16[2,128,512]{2,1,0:T(8,128)(2,1)S(1)}, bf16[2,128,512]{2,1,0:T(8,128)(2,1)S(1)}, u32[]{:S(2)}, u32[]{:S(2)}) collective-permute-start(bf16[2,128,512]{2,1,0:T(8,128)(2,1)S(1)} %get-tuple-element.49), channel_id=1, source_target_pairs={{0,8},{8,0},{16,24},{24,16},{1,9},{9,1},{17,25},{25,17},{2,10},{10... | collective-permute-start | bytes 786440 | tf_op jit(solution)/shard_map/ppermute | solution.py:36
  70.6 30.1 %collective-permute-start.18 = (bf16[2,128,512]{2,1,0:T(8,128)(2,1)S(1)}, bf16[2,128,512]{2,1,0:T(8,128)(2,1)S(1)}, u32[]{:S(2)}, u32[]{:S(2)}) collective-permute-start(bf16[2,128,512]{2,1,0:T(8,128)(2,1)S(1)} %get-tuple-element.50), channel_id=1, source_target_pairs={{8,16},{16,8},{9,17},{17,9},{10,18},{18,10},{11,19},{19,11},{12,20... | collective-permute-start | bytes 786440 | tf_op jit(solution)/shard_map/ppermute | solution.py:36
  71.2 15.0 %collective-permute-start.25 = (bf16[4,2,32,256]{3,2,1,0:T(8,128)(2,1)S(1)}, bf16[4,2,32,256]{3,2,1,0:T(8,128)(2,1)S(1)}, u32[]{:S(2)}, u32[]{:S(2)}) collective-permute-start(bf16[4,2,32,256]{3,2,1,0:T(8,128)(2,1)S(1)} %get-tuple-element.59), channel_id=1, source_target_pairs={{0,5},{1,4},{2,7},{3,6},{4,1},{5,0},{6,3},{7,2},{8,13},{9,12},{10,... | collective-permute-start | bytes 393224 | tf_op jit(solution)/shard_map/ppermute | solution.py:456
  74.6 15.7 %collective-permute-start.26 = (bf16[4,2,32,256]{3,2,1,0:T(8,128)(2,1)S(1)}, bf16[4,2,32,256]{3,2,1,0:T(8,128)(2,1)S(1)}, u32[]{:S(2)}, u32[]{:S(2)}) collective-permute-start(bf16[4,2,32,256]{3,2,1,0:T(8,128)(2,1)S(1)} %get-tuple-element.60), channel_id=1, source_target_pairs={{0,6},{1,7},{2,4},{3,5},{4,2},{5,3},{6,0},{7,1},{8,14},{9,15},{10,... | collective-permute-start | bytes 393224 | tf_op jit(solution)/shard_map/ppermute | solution.py:456
  75.0 18.2 %collective-permute-start.27 = (bf16[4,2,32,256]{3,2,1,0:T(8,128)(2,1)S(1)}, bf16[4,2,32,256]{3,2,1,0:T(8,128)(2,1)S(1)}, u32[]{:S(2)}, u32[]{:S(2)}) collective-permute-start(bf16[4,2,32,256]{3,2,1,0:T(8,128)(2,1)S(1)} %get-tuple-element.61), channel_id=1, source_target_pairs={{0,7},{1,6},{2,5},{3,4},{4,3},{5,2},{6,1},{7,0},{8,15},{9,14},{10,... | collective-permute-start | bytes 393224 | tf_op jit(solution)/shard_map/ppermute | solution.py:456
  94.3 12.0 %collective-permute-start.28 = (bf16[6,2,32,256]{3,2,1,0:T(8,128)(2,1)S(1)}, bf16[6,2,32,256]{3,2,1,0:T(8,128)(2,1)S(1)}, u32[]{:S(2)}, u32[]{:S(2)}) collective-permute-start(bf16[6,2,32,256]{3,2,1,0:T(8,128)(2,1)S(1)} %shard_map.115), channel_id=1, source_target_pairs={{0,8},{8,16},{16,24},{1,9},{9,17},{17,25},{2,10},{10,18},{18,26},{... | collective-permute-start | bytes 589832 | tf_op jit(solution)/shard_map/ppermute | solution.py:26
  97.5 8.8 %collective-permute-start.29 = (bf16[6,2,32,256]{3,2,1,0:T(8,128)(2,1)S(1)}, bf16[6,2,32,256]{3,2,1,0:T(8,128)(2,1)S(1)}, u32[]{:S(2)}, u32[]{:S(2)}) collective-permute-start(bf16[6,2,32,256]{3,2,1,0:T(8,128)(2,1)S(1)} %shard_map.116), channel_id=1, source_target_pairs={{0,8},{8,16},{16,24},{1,9},{9,17},{17,25},{2,10},{10,18},{18,26},{... | collective-permute-start | bytes 589832 | tf_op jit(solution)/shard_map/ppermute | solution.py:26
  101.5 7.9 %collective-permute-start.20 = (bf16[2,256,128]{2,1,0:T(8,128)(2,1)S(1)}, bf16[2,256,128]{2,1,0:T(8,128)(2,1)S(1)}, u32[]{:S(2)}, u32[]{:S(2)}) collective-permute-start(bf16[2,256,128]{2,1,0:T(8,128)(2,1)S(1)} %get-tuple-element.53), channel_id=1, source_target_pairs={{1,2},{2,1},{3,4},{4,3},{5,6},{6,5},{9,10},{10,9},{11,12},{12,11},... | collective-permute-start | bytes 393224 | tf_op jit(solution)/shard_map/ppermute | solution.py:36
  (8 other events, 145.6 us)

commit v5 on v3

--- a/solution.py
+++ b/solution.py
@@ -62,6 +62,11 @@
 def transfer_order(count):
     half = count // 2
     return [half] * (half > 0) + list(range(1, half)) + list(range(half + 1, count))
+
+
+def slab_order(count, paired):
+    steps = transfer_order(count)
+    return steps[:1] + [0] + steps[1:] if paired else [0] + steps
 
 
 def partners(axis):
@@ -113,28 +118,15 @@
     return [pltpu.SMEM(shape, jnp.float32), pltpu.SemaphoreType.DMA((count,))]
 
 
-def slab_kernel(count, places, row, *refs):
-    own, follower = refs[count : count + 2]
-    outs = refs[count + 2 : -5]
-    table, near, held, sem, near_sem = refs[-5:]
-    copy_own = pltpu.make_async_copy(own, near, near_sem)
-    copy_own.start()
-    copies = fetch(refs[:count], places, held, sem)
-    num_modes = own.shape[1]
-    table[1] = follower[0].astype(jnp.float32)
-    copy_own.wait()
-    table[0] = near[0].astype(jnp.float32)
+def make_slabs(region_of, weight_of, num_modes, row, table, outs):
     next_row = (row[0] + 1).astype(jnp.float32)
-    slots = outs[0].shape[0]
-    for copy in copies:
-        copy.wait()
     for at, out in enumerate(outs):
 
         def slot_step(slot, carry, at=at, out=out):
-            region = held[at, slots, slot]
+            region = region_of(at, slot)
             which = jnp.where(region == next_row, 1, 0)
             known = jnp.where(jnp.abs(region - next_row + 0.5) < 1.0, 1.0, 0.0)
-            scales = [held[at, slot, k] * known for k in range(num_modes)]
+            scales = [weight_of(at, slot, k) * known for k in range(num_modes)]
             for part in range(2):
                 total = scales[0] * table[which, 0, part]
                 for k in range(1, num_modes):
@@ -145,19 +137,65 @@
         lax.fori_loop(0, out.shape[0], slot_step, 0)
 
 
+def first_kernel(places, row, weights, own, follower, out, table, near, held, sem, near_sem):
+    copy_own = pltpu.make_async_copy(own, near, near_sem)
+    copy_own.start()
+    copies = fetch([weights], places, held, sem)
+    num_modes, slots = (own.shape[1], out.shape[0])
+    table[1] = follower[0].astype(jnp.float32)
+    copy_own.wait()
+    table[0] = near[0].astype(jnp.float32)
+    for copy in copies:
+        copy.wait()
+    make_slabs(
+        lambda at, slot: held[at, slots, slot],
+        lambda at, slot, k: held[at, slot, k],
+        num_modes,
+        row,
+        table,
+        [out],
+    )
+
+
+def slab_kernel(count, places, row, *refs):
+    table = refs[count]
+    outs = refs[count + 1 : -2]
+    held, sem = refs[-2:]
+    slots = outs[0].shape[0]
+    for copy in fetch(refs[:count], places, held, sem):
+        copy.wait()
+    make_slabs(
+        lambda at, slot: held[at, slots, slot],
+        lambda at, slot, k: held[at, slot, k],
+        table.shape[1],
+        row,
+        table,
+        outs,
+    )
+
+
 def slabs(row, weights, places, own, follower):
     shape = (weights[0].shape[1] - 1,) + own.shape[2:]
-    return call(
-        functools.partial(slab_kernel, len(weights), places),
-        [(shape, jnp.bfloat16)] * len(places),
+    first, table = call(
+        functools.partial(first_kernel, places[:1]),
+        [(shape, jnp.bfloat16), ((2,) + own.shape[1:], jnp.float32)],
+        (row, SMEM),
+        weights[0],
+        (own, HBM),
+        follower,
+        scratch=[pltpu.VMEM(own.shape, own.dtype)]
+        + held_weights(1, weights[0])
+        + [pltpu.SemaphoreType.DMA],
+    )
+    rest = call(
+        functools.partial(slab_kernel, len(weights), places[1:]),
+        [(shape, jnp.bfloat16)] * (len(places) - 1),
         (row, SMEM),
         *weights,
-        (own, HBM),
-        follower,
-        scratch=[pltpu.VMEM((2,) + own.shape[1:], jnp.float32), pltpu.VMEM(own.shape, own.dtype)]
-        + held_weights(len(places), weights[0])
-        + [pltpu.SemaphoreType.DMA],
-    )
+        table,
+        scratch=held_weights(len(places) - 1, weights[0]),
+    )
+    return [first, *rest]
 
 
 def prepare_kernel(
@@ -453,7 +491,8 @@
         scratch=[pltpu.VMEM(x.shape, x.dtype) for x in (coeffs, region, object_field)]
         + [pltpu.SemaphoreType.DMA((3,))],
     )
-    if count > 1 and count & (count - 1) == 0:
+    paired = count > 1 and count & (count - 1) == 0
+    if paired:
         across = move(payload, middle_step)
         blocks_shape = (2,) + payload.shape
         (pair,) = call(pair_kernel, [(blocks_shape, jnp.float32)], payload, across)
@@ -481,8 +520,9 @@
     ends = swap(ends, "row")
 
     blocks = {}
-    made = slabs(row, weights, [made_at(step) for step in every], modes, follower)
-    for step, slab in zip(every, made):
+    turns = slab_order(count, paired)
+    made = slabs(row, weights, [made_at(step) for step in turns], modes, follower)
+    for step, slab in zip(turns, made):
         blocks[step] = move(slab, step) if step else slab
 
     corners = pltpu.with_memory_space_constraint(offsets[0, 0].T, pltpu.HBM)

time: 101 us -> 101 us (level)
  waiting for transfers between devices: 41.5 us -> 38.5 us
  starting transfers between devices: 34.8 us -> 36.9 us
    ppermute x18, waiting for transfers between devices: 31.1 us -> 27.3 us  [move(): lax.ppermute(value, 'col', [(i, goes_to(i, step)) for i in range(count)])]
    ppermute x18, starting transfers between devices: 23.4 us -> 26 us  [move(): lax.ppermute(value, 'col', [(i, goes_to(i, step)) for i in range(count)])]
    pallas_call x12 -> x13, Pallas kernels: 21.8 us -> 22.7 us  [call(): pl.pallas_call(body, out_shape=tuple(outs), in_specs=specs, out_specs=tup...]
  transfers between devices with their start and end apart: 28 -> 28, of which waited for: 15 -> 15; matrix products, arithmetic and copies ran while one was open for 0% -> 0% of each run, Pallas kernels for 17% -> 18%
where the time goes in v5:
time: 101 us
  waiting for transfers between devices  38.5 us (38%)
  starting transfers between devices  36.9 us (37%)
  Pallas kernels  22.7 us (22%)
  between operations  1.53 us (2%)
    ppermute x18, waiting for transfers between devices, move(): lax.ppermute(value, 'col', [(i, goes_to(i, step)) for i in range(count)])  27.3 us
    ppermute x18, starting transfers between devices, move(): lax.ppermute(value, 'col', [(i, goes_to(i, step)) for i in range(count)])  26 us
    pallas_call x13, Pallas kernels, call(): pl.pallas_call(body, out_shape=tuple(outs), in_specs=specs, out_specs=tup...  22.7 us
    ppermute x8, waiting for transfers between devices, swap(): lax.ppermute(value, axis, pairs)  11.1 us
    ppermute x8, starting transfers between devices, swap(): lax.ppermute(value, axis, pairs)  8.35 us
    ppermute x2, starting transfers between devices, shift(): return lax.ppermute(value, axis, pairs)  2.61 us
  transfers between devices with their start and end apart: 28, of which 15 were waited for; matrix products, arithmetic and copies ran while one was open for 0% of the time, Pallas kernels for 18%

profile of v5, /device:TPU:8, one launch (start us, length us, event | category | flops | bytes accessed | tf_op | source)
XLA Modules:
  0.0 100.6 jit_solution(12251674232987878956)
XLA Ops:
  4.7 1.9 %collective-permute-start.13 = (bf16[2,256,128]{2,1,0:T(8,128)(2,1)S(1)}, bf16[2,256,128]{2,1,0:T(8,128)(2,1)S(1)}, u32[]{:S(2)}, u32[]{:S(2)}) collective-permute-start(bf16[2,256,128]{2,1,0:T(8,128)(2,1)S(1)} %get-tuple-element.48), channel_id=1, source_target_pairs={{1,2},{2,1},{3,4},{4,3},{5,6},{6,5},{9,10},{10,9},{11,12},{12,11},... | collective-permute-start | bytes 393224 | tf_op jit(solution)/shard_map/ppermute | solution.py:36
  6.6 2.8 %collective-permute-done.12.even.side_even = bf16[2,256,128]{2,1,0:T(8,128)(2,1)S(1)} collective-permute-done((bf16[2,256,128]{2,1,0:T(8,128)(2,1)S(1)}, bf16[2,256,128]{2,1,0:T(8,128)(2,1)S(1)}, u32[]{:S(2)}, u32[]{:S(2)}) %collective-permute-start.12) | collective-permute-done | bytes 131104 | tf_op jit(solution)/shard_map/ppermute | solution.py:36
  9.4 4.3 %collective-permute-done.13.odd.side_odd = bf16[2,256,128]{2,1,0:T(8,128)(2,1)S(1)} collective-permute-done((bf16[2,256,128]{2,1,0:T(8,128)(2,1)S(1)}, bf16[2,256,128]{2,1,0:T(8,128)(2,1)S(1)}, u32[]{:S(2)}, u32[]{:S(2)}) %collective-permute-start.13) | collective-permute-done | bytes 131104 | tf_op jit(solution)/shard_map/ppermute | solution.py:36
  14.7 2.7 %collective-permute-start = (f32[5,128]{1,0:T(8,128)S(1)}, f32[5,128]{1,0:T(8,128)S(1)}, u32[]{:S(2)}, u32[]{:S(2)}) collective-permute-start(f32[5,128]{1,0:T(8,128)S(1)} %get-tuple-element.36.mine), channel_id=1, source_target_pairs={{0,4},{1,5},{2,6},{3,7},{4,0},{5,1},{6,2},{7,3},{8,12},{9,13},{10,... | collective-permute-start | bytes 7688 | tf_op jit(solution)/shard_map/ppermute | solution.py:480
  17.4 1.9 %collective-permute-done.across = f32[5,128]{1,0:T(8,128)S(1)} collective-permute-done((f32[5,128]{1,0:T(8,128)S(1)}, f32[5,128]{1,0:T(8,128)S(1)}, u32[]{:S(2)}, u32[]{:S(2)}) %collective-permute-start) | collective-permute-done | bytes 2592 | tf_op jit(solution)/shard_map/ppermute | solution.py:480
  19.4 1.9 %collective-permute-start.2 = (f32[2,5,128]{2,1,0:T(8,128)S(1)}, f32[2,5,128]{2,1,0:T(8,128)S(1)}, u32[]{:S(2)}, u32[]{:S(2)}) collective-permute-start(f32[2,5,128]{2,1,0:T(8,128)S(1)} %shard_map.105.weights.refs_0_), channel_id=1, source_target_pairs={{0,2},{1,3},{2,0},{3,1},{4,6},{5,7},{6,4},{7,5},{8,10},{9,11},{10,... | collective-permute-start | bytes 15368 | tf_op jit(solution)/shard_map/ppermute | solution.py:480
  24.9 2.8 %shard_map.107 = (bf16[4,2,32,256]{3,2,1,0:T(8,128)(2,1)S(1)}, bf16[4,2,32,256]{3,2,1,0:T(8,128)(2,1)S(1)}, bf16[4,2,32,256]{3,2,1,0:T(8,128)(2,1)S(1)}, bf16[4,...) custom-call(s32[1]{0:T(128)} %bitcast.1.row, ...), custom_call_target="tpu_custom_call" | custom-call | tf_op jit(solution)/shard_map/pallas_call | solution.py:96
  29.5 1.9 %collective-permute-start.8 = (bf16[4,2,32,256]{3,2,1,0:T(8,128)(2,1)S(1)}, bf16[4,2,32,256]{3,2,1,0:T(8,128)(2,1)S(1)}, u32[]{:S(2)}, u32[]{:S(2)}) collective-permute-start(bf16[4,2,32,256]{3,2,1,0:T(8,128)(2,1)S(1)} %get-tuple-element.42), channel_id=1, source_target_pairs={{0,3},{1,2},{2,1},{3,0},{4,7},{5,6},{6,5},{7,4},{8,11},{9,10},{10,... | collective-permute-start | bytes 393224 | tf_op jit(solution)/shard_map/ppermute | solution.py:480
  31.4 3.5 %collective-permute-start.9 = (bf16[4,2,32,256]{3,2,1,0:T(8,128)(2,1)S(1)}, bf16[4,2,32,256]{3,2,1,0:T(8,128)(2,1)S(1)}, u32[]{:S(2)}, u32[]{:S(2)}) collective-permute-start(bf16[4,2,32,256]{3,2,1,0:T(8,128)(2,1)S(1)} %get-tuple-element.43), channel_id=1, source_target_pairs={{0,5},{1,4},{2,7},{3,6},{4,1},{5,0},{6,3},{7,2},{8,13},{9,12},{10,... | collective-permute-start | bytes 393224 | tf_op jit(solution)/shard_map/ppermute | solution.py:480
  36.4 3.4 %collective-permute-start.5 = (bf16[4,2,32,256]{3,2,1,0:T(8,128)(2,1)S(1)}, bf16[4,2,32,256]{3,2,1,0:T(8,128)(2,1)S(1)}, u32[]{:S(2)}, u32[]{:S(2)}) collective-permute-start(bf16[4,2,32,256]{3,2,1,0:T(8,128)(2,1)S(1)} %get-tuple-element.39), channel_id=1, source_target_pairs={{0,4},{1,5},{2,6},{3,7},{4,0},{5,1},{6,2},{7,3},{8,12},{9,13},{10,... | collective-permute-start | bytes 393224 | tf_op jit(solution)/shard_map/ppermute | solution.py:480
  40.5 2.6 %shard_map.109 = (bf16[4,2,256,256]{3,2,1,0:T(8,128)(2,1)S(1)}, f32[4,256,256]{2,1,0:T(8,128)S(1)}) custom-call(s32[1]{0:T(128)} %bitcast.1.row, s32[1]{0:T(128)} %bitcast.me, s32[2,4]{1,0:T(2,128)} %bitcast.7, bf16[2,256,256]{2,1,0:T(8,128)(2,1)S(1)} %get-tuple-element.46.tile, bf16[2,256,128]{2,1,0:T(8,128)(2,1)S(1)} %collective-permute-done.12.even.side_even, ...), custom_call_target="tpu_custom_call" | custom-call | tf_op jit(solution)/shard_map/pallas_call | solution.py:96
  43.1 6.5 %collective-permute-done.9.refs_5_ = bf16[4,2,32,256]{3,2,1,0:T(8,128)(2,1)S(1)} collective-permute-done((bf16[4,2,32,256]{3,2,1,0:T(8,128)(2,1)S(1)}, bf16[4,2,32,256]{3,2,1,0:T(8,128)(2,1)S(1)}, u32[]{:S(2)}, u32[]{:S(2)}) %collective-permute-start.9) | collective-permute-done | bytes 131104 | tf_op jit(solution)/shard_map/ppermute | solution.py:480
  49.6 2.8 %collective-permute-done.10.refs_6_ = bf16[4,2,32,256]{3,2,1,0:T(8,128)(2,1)S(1)} collective-permute-done((bf16[4,2,32,256]{3,2,1,0:T(8,128)(2,1)S(1)}, bf16[4,2,32,256]{3,2,1,0:T(8,128)(2,1)S(1)}, u32[]{:S(2)}, u32[]{:S(2)}) %collective-permute-start.10) | collective-permute-done | bytes 131104 | tf_op jit(solution)/shard_map/ppermute | solution.py:480
  52.4 2.8 %collective-permute-done.11.refs_7_ = bf16[4,2,32,256]{3,2,1,0:T(8,128)(2,1)S(1)} collective-permute-done((bf16[4,2,32,256]{3,2,1,0:T(8,128)(2,1)S(1)}, bf16[4,2,32,256]{3,2,1,0:T(8,128)(2,1)S(1)}, u32[]{:S(2)}, u32[]{:S(2)}) %collective-permute-start.11) | collective-permute-done | bytes 131104 | tf_op jit(solution)/shard_map/ppermute | solution.py:480
  56.8 4.8 %shard_map.110 = (bf16[4,2,32,256]{3,2,1,0:T(8,128)(2,1)S(1)}, bf16[4,2,32,256]{3,2,1,0:T(8,128)(2,1)S(1)}, bf16[4,2,32,256]{3,2,1,0:T(8,128)(2,1)S(1)}, bf16[4,...) custom-call(s32[1,1]{1,0:T(1,128)S(6)} %copy.11.counts, ...), custom_call_target="tpu_custom_call" | custom-call | tf_op jit(solution)/shard_map/pallas_call | solution.py:96
  61.6 3.4 %collective-permute-start.20 = (bf16[4,2,32,256]{3,2,1,0:T(8,128)(2,1)S(1)}, bf16[4,2,32,256]{3,2,1,0:T(8,128)(2,1)S(1)}, u32[]{:S(2)}, u32[]{:S(2)}) collective-permute-start(bf16[4,2,32,256]{3,2,1,0:T(8,128)(2,1)S(1)} %get-tuple-element.60), channel_id=1, source_target_pairs={{0,4},{1,5},{2,6},{3,7},{4,0},{5,1},{6,2},{7,3},{8,12},{9,13},{10,... | collective-permute-start | bytes 393224 | tf_op jit(solution)/shard_map/ppermute | solution.py:480
  65.6 2.9 %collective-permute-start.26 = (bf16[4,2,32,256]{3,2,1,0:T(8,128)(2,1)S(1)}, bf16[4,2,32,256]{3,2,1,0:T(8,128)(2,1)S(1)}, u32[]{:S(2)}, u32[]{:S(2)}) collective-permute-start(bf16[4,2,32,256]{3,2,1,0:T(8,128)(2,1)S(1)} %get-tuple-element.67), channel_id=1, source_target_pairs={{0,3},{1,2},{2,1},{3,0},{4,7},{5,6},{6,5},{7,4},{8,11},{9,10},{10,... | collective-permute-start | bytes 393224 | tf_op jit(solution)/shard_map/ppermute | solution.py:480
  71.5 3.1 %shard_map.111 = (bf16[2,128,512]{2,1,0:T(8,128)(2,1)S(1)}, f32[2,256,512]{2,1,0:T(8,128)S(1)}, bf16[2,128,512]{2,1,0:T(8,128)(2,1)S(1)}) custom-call(s32[1]{0:T(128)} %bitcast.1.row, s32[2,4]{1,0:T(2,128)} %bitcast.8, f32[4,2,256,256]{3,2,1,0:T(8,128)S(1)} %get-tuple-element.53.pieces), custom_call_target="tpu_custom_call" | custom-call | tf_op jit(solution)/shard_map/pallas_call | solution.py:96
  76.4 2.3 %shard_map.114 = (f32[12,2,32,256]{3,2,1,0:T(8,128)S(1)}, f32[12,2,32,256]{3,2,1,0:T(8,128)S(1)}) custom-call(s32[1]{0:T(128)} %bitcast.1.row, f32[2,5,128]{2,1,0:T(8,128)S(1)} %shard_map.105.weights.refs_0_, f32[2,5,128]{2,1,0:T(8,128)S(1)} %collective-permute-done.1.refs_1_, f32[2,5,128]{2,1,0:T(8,128)S(1)} %collective-permute-done.2.refs_2_, ...), custom_call_target="tpu_custom_call" | custom-call | tf_op jit(solution)/shard_map/pallas_call | solution.py:96
  78.7 1.8 %collective-permute-done.21.refs_5_ = bf16[4,2,32,256]{3,2,1,0:T(8,128)(2,1)S(1)} collective-permute-done((bf16[4,2,32,256]{3,2,1,0:T(8,128)(2,1)S(1)}, bf16[4,2,32,256]{3,2,1,0:T(8,128)(2,1)S(1)}, u32[]{:S(2)}, u32[]{:S(2)}) %collective-permute-start.21) | collective-permute-done | bytes 131104 | tf_op jit(solution)/shard_map/ppermute | solution.py:480
  80.5 4.5 %collective-permute-done.22.refs_6_ = bf16[4,2,32,256]{3,2,1,0:T(8,128)(2,1)S(1)} collective-permute-done((bf16[4,2,32,256]{3,2,1,0:T(8,128)(2,1)S(1)}, bf16[4,2,32,256]{3,2,1,0:T(8,128)(2,1)S(1)}, u32[]{:S(2)}, u32[]{:S(2)}) %collective-permute-start.22) | collective-permute-done | bytes 131104 | tf_op jit(solution)/shard_map/ppermute | solution.py:480
  91.0 1.9 %collective-permute-start.19 = (bf16[2,256,128]{2,1,0:T(8,128)(2,1)S(1)}, bf16[2,256,128]{2,1,0:T(8,128)(2,1)S(1)}, u32[]{:S(2)}, u32[]{:S(2)}) collective-permute-start(bf16[2,256,128]{2,1,0:T(8,128)(2,1)S(1)} %get-tuple-element.59), channel_id=1, source_target_pairs={{1,2},{2,1},{3,4},{4,3},{5,6},{6,5},{9,10},{10,9},{11,12},{12,11},... | collective-permute-start | bytes 393224 | tf_op jit(solution)/shard_map/ppermute | solution.py:36
  92.9 1.8 %shard_map.115 = f32[12,2,32,256]{3,2,1,0:T(8,128)S(1)} custom-call(s32[1]{0:T(128)} %bitcast.1.row, f32[2,5,128]{2,1,0:T(8,128)S(1)} %shard_map.105.weights.refs_0_, f32[2,5,128]{2,1,0:T(8,128)S(1)} %collective-permute-done.1.refs_1_, f32[2,5,128]{2,1,0:T(8,128)S(1)} %collective-permute-done.2.refs_2_, f32[2,5,128]{2,1,0:T(8,128)S(1)} %collective-permute-done.3.refs_3_, ...), custom_call_target="tpu_custom_call" | custom-call | tf_op jit(solution)/shard_map/pallas_call | solution.py:96
  94.7 4.0 %collective-permute-done.19.odd = bf16[2,256,128]{2,1,0:T(8,128)(2,1)S(1)} collective-permute-done((bf16[2,256,128]{2,1,0:T(8,128)(2,1)S(1)}, bf16[2,256,128]{2,1,0:T(8,128)(2,1)S(1)}, u32[]{:S(2)}, u32[]{:S(2)}) %collective-permute-start.19) | collective-permute-done | bytes 131104 | tf_op jit(solution)/shard_map/ppermute | solution.py:36
  (50 shorter events, 26.7 us)
Async XLA Ops:
  0.6 20.7 %collective-permute-start.4 = (bf16[1,12,2,32,256]{4,3,2,1,0:T(8,128)(2,1)}, bf16[1,12,2,32,256]{4,3,2,1,0:T(8,128)(2,1)S(1)}, u32[]{:S(2)}, u32[]{:S(2)}) collective-permute-start(bf16[1,12,2,32,256]{4,3,2,1,0:T(8,128)(2,1)} %own.1), channel_id=1, source_target_pairs={{8,0},{16,8},{24,16},{9,1},{17,9},{25,17},{10,2},{18,10},{26,18},{... | collective-permute-start | bytes 1179656 | tf_op jit(solution)/shard_map/ppermute | solution.py:26
  3.1 6.3 %collective-permute-start.12 = (bf16[2,256,128]{2,1,0:T(8,128)(2,1)S(1)}, bf16[2,256,128]{2,1,0:T(8,128)(2,1)S(1)}, u32[]{:S(2)}, u32[]{:S(2)}) collective-permute-start(bf16[2,256,128]{2,1,0:T(8,128)(2,1)S(1)} %get-tuple-element.47), channel_id=1, source_target_pairs={{0,1},{1,0},{2,3},{3,2},{4,5},{5,4},{6,7},{7,6},{8,9},{9,8},{10,11... | collective-permute-start | bytes 393224 | tf_op jit(solution)/shard_map/ppermute | solution.py:36
  4.7 9.0 %collective-permute-start.13 = (bf16[2,256,128]{2,1,0:T(8,128)(2,1)S(1)}, bf16[2,256,128]{2,1,0:T(8,128)(2,1)S(1)}, u32[]{:S(2)}, u32[]{:S(2)}) collective-permute-start(bf16[2,256,128]{2,1,0:T(8,128)(2,1)S(1)} %get-tuple-element.48), channel_id=1, source_target_pairs={{1,2},{2,1},{3,4},{4,3},{5,6},{6,5},{9,10},{10,9},{11,12},{12,11},... | collective-permute-start | bytes 393224 | tf_op jit(solution)/shard_map/ppermute | solution.py:36
  13.8 17.5 %collective-permute-start.14 = (bf16[2,128,512]{2,1,0:T(8,128)(2,1)S(1)}, bf16[2,128,512]{2,1,0:T(8,128)(2,1)S(1)}, u32[]{:S(2)}, u32[]{:S(2)}) collective-permute-start(bf16[2,128,512]{2,1,0:T(8,128)(2,1)S(1)} %get-tuple-element.49), channel_id=1, source_target_pairs={{0,8},{8,0},{16,24},{24,16},{1,9},{9,1},{17,25},{25,17},{2,10},{10... | collective-permute-start | bytes 786440 | tf_op jit(solution)/shard_map/ppermute | solution.py:36
  13.9 21.0 %collective-permute-start.15 = (bf16[2,128,512]{2,1,0:T(8,128)(2,1)S(1)}, bf16[2,128,512]{2,1,0:T(8,128)(2,1)S(1)}, u32[]{:S(2)}, u32[]{:S(2)}) collective-permute-start(bf16[2,128,512]{2,1,0:T(8,128)(2,1)S(1)} %get-tuple-element.50), channel_id=1, source_target_pairs={{8,16},{16,8},{9,17},{17,9},{10,18},{18,10},{11,19},{19,11},{12,20... | collective-permute-start | bytes 786440 | tf_op jit(solution)/shard_map/ppermute | solution.py:36
  27.8 7.1 %collective-permute-start.6 = (bf16[4,2,32,256]{3,2,1,0:T(8,128)(2,1)S(1)}, bf16[4,2,32,256]{3,2,1,0:T(8,128)(2,1)S(1)}, u32[]{:S(2)}, u32[]{:S(2)}) collective-permute-start(bf16[4,2,32,256]{3,2,1,0:T(8,128)(2,1)S(1)} %get-tuple-element.40), channel_id=1, source_target_pairs={{0,1},{1,0},{2,3},{3,2},{4,5},{5,4},{6,7},{7,6},{8,9},{9,8},{10,11... | collective-permute-start | bytes 393224 | tf_op jit(solution)/shard_map/ppermute | solution.py:480
  29.4 7.1 %collective-permute-start.7 = (bf16[4,2,32,256]{3,2,1,0:T(8,128)(2,1)S(1)}, bf16[4,2,32,256]{3,2,1,0:T(8,128)(2,1)S(1)}, u32[]{:S(2)}, u32[]{:S(2)}) collective-permute-start(bf16[4,2,32,256]{3,2,1,0:T(8,128)(2,1)S(1)} %get-tuple-element.41), channel_id=1, source_target_pairs={{0,2},{1,3},{2,0},{3,1},{4,6},{5,7},{6,4},{7,5},{8,10},{9,11},{10,... | collective-permute-start | bytes 393224 | tf_op jit(solution)/shard_map/ppermute | solution.py:480
  29.5 13.7 %collective-permute-start.8 = (bf16[4,2,32,256]{3,2,1,0:T(8,128)(2,1)S(1)}, bf16[4,2,32,256]{3,2,1,0:T(8,128)(2,1)S(1)}, u32[]{:S(2)}, u32[]{:S(2)}) collective-permute-start(bf16[4,2,32,256]{3,2,1,0:T(8,128)(2,1)S(1)} %get-tuple-element.42), channel_id=1, source_target_pairs={{0,3},{1,2},{2,1},{3,0},{4,7},{5,6},{6,5},{7,4},{8,11},{9,10},{10,... | collective-permute-start | bytes 393224 | tf_op jit(solution)/shard_map/ppermute | solution.py:480
  31.4 18.3 %collective-permute-start.9 = (bf16[4,2,32,256]{3,2,1,0:T(8,128)(2,1)S(1)}, bf16[4,2,32,256]{3,2,1,0:T(8,128)(2,1)S(1)}, u32[]{:S(2)}, u32[]{:S(2)}) collective-permute-start(bf16[4,2,32,256]{3,2,1,0:T(8,128)(2,1)S(1)} %get-tuple-element.43), channel_id=1, source_target_pairs={{0,5},{1,4},{2,7},{3,6},{4,1},{5,0},{6,3},{7,2},{8,13},{9,12},{10,... | collective-permute-start | bytes 393224 | tf_op jit(solution)/shard_map/ppermute | solution.py:480
  34.9 17.6 %collective-permute-start.10 = (bf16[4,2,32,256]{3,2,1,0:T(8,128)(2,1)S(1)}, bf16[4,2,32,256]{3,2,1,0:T(8,128)(2,1)S(1)}, u32[]{:S(2)}, u32[]{:S(2)}) collective-permute-start(bf16[4,2,32,256]{3,2,1,0:T(8,128)(2,1)S(1)} %get-tuple-element.44), channel_id=1, source_target_pairs={{0,6},{1,7},{2,4},{3,5},{4,2},{5,3},{6,0},{7,1},{8,14},{9,15},{10,... | collective-permute-start | bytes 393224 | tf_op jit(solution)/shard_map/ppermute | solution.py:480
  34.9 20.4 %collective-permute-start.11 = (bf16[4,2,32,256]{3,2,1,0:T(8,128)(2,1)S(1)}, bf16[4,2,32,256]{3,2,1,0:T(8,128)(2,1)S(1)}, u32[]{:S(2)}, u32[]{:S(2)}) collective-permute-start(bf16[4,2,32,256]{3,2,1,0:T(8,128)(2,1)S(1)} %get-tuple-element.45), channel_id=1, source_target_pairs={{0,7},{1,6},{2,5},{3,4},{4,3},{5,2},{6,1},{7,0},{8,15},{9,14},{10,... | collective-permute-start | bytes 393224 | tf_op jit(solution)/shard_map/ppermute | solution.py:480
  36.4 20.3 %collective-permute-start.5 = (bf16[4,2,32,256]{3,2,1,0:T(8,128)(2,1)S(1)}, bf16[4,2,32,256]{3,2,1,0:T(8,128)(2,1)S(1)}, u32[]{:S(2)}, u32[]{:S(2)}) collective-permute-start(bf16[4,2,32,256]{3,2,1,0:T(8,128)(2,1)S(1)} %get-tuple-element.39), channel_id=1, source_target_pairs={{0,4},{1,5},{2,6},{3,7},{4,0},{5,1},{6,2},{7,3},{8,12},{9,13},{10,... | collective-permute-start | bytes 393224 | tf_op jit(solution)/shard_map/ppermute | solution.py:480
  61.6 7.8 %collective-permute-start.20 = (bf16[4,2,32,256]{3,2,1,0:T(8,128)(2,1)S(1)}, bf16[4,2,32,256]{3,2,1,0:T(8,128)(2,1)S(1)}, u32[]{:S(2)}, u32[]{:S(2)}) collective-permute-start(bf16[4,2,32,256]{3,2,1,0:T(8,128)(2,1)S(1)} %get-tuple-element.60), channel_id=1, source_target_pairs={{0,4},{1,5},{2,6},{3,7},{4,0},{5,1},{6,2},{7,3},{8,12},{9,13},{10,... | collective-permute-start | bytes 393224 | tf_op jit(solution)/shard_map/ppermute | solution.py:480
  65.0 6.3 %collective-permute-start.24 = (bf16[4,2,32,256]{3,2,1,0:T(8,128)(2,1)S(1)}, bf16[4,2,32,256]{3,2,1,0:T(8,128)(2,1)S(1)}, u32[]{:S(2)}, u32[]{:S(2)}) collective-permute-start(bf16[4,2,32,256]{3,2,1,0:T(8,128)(2,1)S(1)} %get-tuple-element.65), channel_id=1, source_target_pairs={{0,1},{1,0},{2,3},{3,2},{4,5},{5,4},{6,7},{7,6},{8,9},{9,8},{10,11... | collective-permute-start | bytes 393224 | tf_op jit(solution)/shard_map/ppermute | solution.py:480
  65.6 9.0 %collective-permute-start.25 = (bf16[4,2,32,256]{3,2,1,0:T(8,128)(2,1)S(1)}, bf16[4,2,32,256]{3,2,1,0:T(8,128)(2,1)S(1)}, u32[]{:S(2)}, u32[]{:S(2)}) collective-permute-start(bf16[4,2,32,256]{3,2,1,0:T(8,128)(2,1)S(1)} %get-tuple-element.66), channel_id=1, source_target_pairs={{0,2},{1,3},{2,0},{3,1},{4,6},{5,7},{6,4},{7,5},{8,10},{9,11},{10,... | collective-permute-start | bytes 393224 | tf_op jit(solution)/shard_map/ppermute | solution.py:480
  65.6 10.2 %collective-permute-start.26 = (bf16[4,2,32,256]{3,2,1,0:T(8,128)(2,1)S(1)}, bf16[4,2,32,256]{3,2,1,0:T(8,128)(2,1)S(1)}, u32[]{:S(2)}, u32[]{:S(2)}) collective-permute-start(bf16[4,2,32,256]{3,2,1,0:T(8,128)(2,1)S(1)} %get-tuple-element.67), channel_id=1, source_target_pairs={{0,3},{1,2},{2,1},{3,0},{4,7},{5,6},{6,5},{7,4},{8,11},{9,10},{10,... | collective-permute-start | bytes 393224 | tf_op jit(solution)/shard_map/ppermute | solution.py:480
  68.5 12.0 %collective-permute-start.21 = (bf16[4,2,32,256]{3,2,1,0:T(8,128)(2,1)S(1)}, bf16[4,2,32,256]{3,2,1,0:T(8,128)(2,1)S(1)}, u32[]{:S(2)}, u32[]{:S(2)}) collective-permute-start(bf16[4,2,32,256]{3,2,1,0:T(8,128)(2,1)S(1)} %get-tuple-element.61), channel_id=1, source_target_pairs={{0,5},{1,4},{2,7},{3,6},{4,1},{5,0},{6,3},{7,2},{8,13},{9,12},{10,... | collective-permute-start | bytes 393224 | tf_op jit(solution)/shard_map/ppermute | solution.py:480
  69.4 15.6 %collective-permute-start.22 = (bf16[4,2,32,256]{3,2,1,0:T(8,128)(2,1)S(1)}, bf16[4,2,32,256]{3,2,1,0:T(8,128)(2,1)S(1)}, u32[]{:S(2)}, u32[]{:S(2)}) collective-permute-start(bf16[4,2,32,256]{3,2,1,0:T(8,128)(2,1)S(1)} %get-tuple-element.62), channel_id=1, source_target_pairs={{0,6},{1,7},{2,4},{3,5},{4,2},{5,3},{6,0},{7,1},{8,14},{9,15},{10,... | collective-permute-start | bytes 393224 | tf_op jit(solution)/shard_map/ppermute | solution.py:480
  71.3 15.2 %collective-permute-start.23 = (bf16[4,2,32,256]{3,2,1,0:T(8,128)(2,1)S(1)}, bf16[4,2,32,256]{3,2,1,0:T(8,128)(2,1)S(1)}, u32[]{:S(2)}, u32[]{:S(2)}) collective-permute-start(bf16[4,2,32,256]{3,2,1,0:T(8,128)(2,1)S(1)} %get-tuple-element.63), channel_id=1, source_target_pairs={{0,7},{1,6},{2,5},{3,4},{4,3},{5,2},{6,1},{7,0},{8,15},{9,14},{10,... | collective-permute-start | bytes 393224 | tf_op jit(solution)/shard_map/ppermute | solution.py:480
  74.6 14.8 %collective-permute-start.16 = (bf16[2,128,512]{2,1,0:T(8,128)(2,1)S(1)}, bf16[2,128,512]{2,1,0:T(8,128)(2,1)S(1)}, u32[]{:S(2)}, u32[]{:S(2)}) collective-permute-start(bf16[2,128,512]{2,1,0:T(8,128)(2,1)S(1)} %get-tuple-element.55), channel_id=1, source_target_pairs={{0,8},{8,0},{16,24},{24,16},{1,9},{9,1},{17,25},{25,17},{2,10},{10... | collective-permute-start | bytes 786440 | tf_op jit(solution)/shard_map/ppermute | solution.py:36
  75.7 13.7 %collective-permute-start.17 = (bf16[2,128,512]{2,1,0:T(8,128)(2,1)S(1)}, bf16[2,128,512]{2,1,0:T(8,128)(2,1)S(1)}, u32[]{:S(2)}, u32[]{:S(2)}) collective-permute-start(bf16[2,128,512]{2,1,0:T(8,128)(2,1)S(1)} %get-tuple-element.56), channel_id=1, source_target_pairs={{8,16},{16,8},{9,17},{17,9},{10,18},{18,10},{11,19},{19,11},{12,20... | collective-permute-start | bytes 786440 | tf_op jit(solution)/shard_map/ppermute | solution.py:36
  88.1 11.6 %collective-permute-start.27 = (bf16[12,2,32,256]{3,2,1,0:T(8,128)(2,1)S(1)}, bf16[12,2,32,256]{3,2,1,0:T(8,128)(2,1)S(1)}, u32[]{:S(2)}, u32[]{:S(2)}) collective-permute-start(bf16[12,2,32,256]{3,2,1,0:T(8,128)(2,1)S(1)} %shard_map.116), channel_id=1, source_target_pairs={{0,8},{8,16},{16,24},{1,9},{9,17},{17,25},{2,10},{10,18},{18,26},{... | collective-permute-start | bytes 1179656 | tf_op jit(solution)/shard_map/ppermute | solution.py:26
  89.6 5.1 %collective-permute-start.18 = (bf16[2,256,128]{2,1,0:T(8,128)(2,1)S(1)}, bf16[2,256,128]{2,1,0:T(8,128)(2,1)S(1)}, u32[]{:S(2)}, u32[]{:S(2)}) collective-permute-start(bf16[2,256,128]{2,1,0:T(8,128)(2,1)S(1)} %get-tuple-element.58), channel_id=1, source_target_pairs={{0,1},{1,0},{2,3},{3,2},{4,5},{5,4},{6,7},{7,6},{8,9},{9,8},{10,11... | collective-permute-start | bytes 393224 | tf_op jit(solution)/shard_map/ppermute | solution.py:36
  91.0 7.7 %collective-permute-start.19 = (bf16[2,256,128]{2,1,0:T(8,128)(2,1)S(1)}, bf16[2,256,128]{2,1,0:T(8,128)(2,1)S(1)}, u32[]{:S(2)}, u32[]{:S(2)}) collective-permute-start(bf16[2,256,128]{2,1,0:T(8,128)(2,1)S(1)} %get-tuple-element.59), channel_id=1, source_target_pairs={{1,2},{2,1},{3,4},{4,3},{5,6},{6,5},{9,10},{10,9},{11,12},{12,11},... | collective-permute-start | bytes 393224 | tf_op jit(solution)/shard_map/ppermute | solution.py:36
  (6 other events, 103.8 us)

commit v6 on v5

--- a/solution.py
+++ b/solution.py
@@ -579,12 +579,10 @@
             dtypes,
         )
 
-    own, following = add_up(
-        [0] + near, ((0, 0, False), (1, 1, False)), [], [jnp.float32, jnp.float32]
-    )
+    (following,) = add_up([0] + near, ((1, 1, False),), [], [jnp.float32])
     (following,) = add_up(crossing, ((1, 1, True),), [following], [jnp.bfloat16])
     passed = shift(following, "row", 1)
-    (own,) = add_up(crossing, ((0, 0, True),), [own], [jnp.float32])
+    (own,) = add_up(every, ((0, 0, False),), [], [jnp.float32])
     mode_grad = (own + passed.astype(jnp.float32))[None]
     return (object_grad, mode_grad)
 

time: 101 us -> 101 us (level)
    ppermute x8, waiting for transfers between devices: 11.1 us -> 10 us  [swap(): lax.ppermute(value, axis, pairs)]
where the time goes in v6:
time: 101 us
  waiting for transfers between devices  38.2 us (38%)
  starting transfers between devices  36.9 us (37%)
  Pallas kernels  23 us (23%)
  between operations  1.53 us (2%)
    ppermute x18, waiting for transfers between devices, move(): lax.ppermute(value, 'col', [(i, goes_to(i, step)) for i in range(count)])  28.1 us
    ppermute x18, starting transfers between devices, move(): lax.ppermute(value, 'col', [(i, goes_to(i, step)) for i in range(count)])  26 us
    pallas_call x13, Pallas kernels, call(): pl.pallas_call(body, out_shape=tuple(outs), in_specs=specs, out_specs=tup...  23 us
    ppermute x8, waiting for transfers between devices, swap(): lax.ppermute(value, axis, pairs)  10 us
    ppermute x8, starting transfers between devices, swap(): lax.ppermute(value, axis, pairs)  8.35 us
    ppermute x2, starting transfers between devices, shift(): return lax.ppermute(value, axis, pairs)  2.61 us
  transfers between devices with their start and end apart: 28, of which 15 were waited for; matrix products, arithmetic and copies ran while one was open for 0% of the time, Pallas kernels for 18%

profile of v6, /device:TPU:8, one launch (start us, length us, event | category | flops | bytes accessed | tf_op | source)
XLA Modules:
  0.0 100.6 jit_solution(10994849772805654724)
XLA Ops:
  4.7 1.9 %collective-permute-start.13 = (bf16[2,256,128]{2,1,0:T(8,128)(2,1)S(1)}, bf16[2,256,128]{2,1,0:T(8,128)(2,1)S(1)}, u32[]{:S(2)}, u32[]{:S(2)}) collective-permute-start(bf16[2,256,128]{2,1,0:T(8,128)(2,1)S(1)} %get-tuple-element.46), channel_id=1, source_target_pairs={{1,2},{2,1},{3,4},{4,3},{5,6},{6,5},{9,10},{10,9},{11,12},{12,11},... | collective-permute-start | bytes 393224 | tf_op jit(solution)/shard_map/ppermute | solution.py:36
  6.6 2.8 %collective-permute-done.12.even.side_even = bf16[2,256,128]{2,1,0:T(8,128)(2,1)S(1)} collective-permute-done((bf16[2,256,128]{2,1,0:T(8,128)(2,1)S(1)}, bf16[2,256,128]{2,1,0:T(8,128)(2,1)S(1)}, u32[]{:S(2)}, u32[]{:S(2)}) %collective-permute-start.12) | collective-permute-done | bytes 131104 | tf_op jit(solution)/shard_map/ppermute | solution.py:36
  9.4 4.3 %collective-permute-done.13.odd.side_odd = bf16[2,256,128]{2,1,0:T(8,128)(2,1)S(1)} collective-permute-done((bf16[2,256,128]{2,1,0:T(8,128)(2,1)S(1)}, bf16[2,256,128]{2,1,0:T(8,128)(2,1)S(1)}, u32[]{:S(2)}, u32[]{:S(2)}) %collective-permute-start.13) | collective-permute-done | bytes 131104 | tf_op jit(solution)/shard_map/ppermute | solution.py:36
  14.7 2.7 %collective-permute-start = (f32[5,128]{1,0:T(8,128)S(1)}, f32[5,128]{1,0:T(8,128)S(1)}, u32[]{:S(2)}, u32[]{:S(2)}) collective-permute-start(f32[5,128]{1,0:T(8,128)S(1)} %get-tuple-element.34.mine), channel_id=1, source_target_pairs={{0,4},{1,5},{2,6},{3,7},{4,0},{5,1},{6,2},{7,3},{8,12},{9,13},{10,... | collective-permute-start | bytes 7688 | tf_op jit(solution)/shard_map/ppermute | solution.py:480
  17.4 1.9 %collective-permute-done.across = f32[5,128]{1,0:T(8,128)S(1)} collective-permute-done((f32[5,128]{1,0:T(8,128)S(1)}, f32[5,128]{1,0:T(8,128)S(1)}, u32[]{:S(2)}, u32[]{:S(2)}) %collective-permute-start) | collective-permute-done | bytes 2592 | tf_op jit(solution)/shard_map/ppermute | solution.py:480
  19.4 1.9 %collective-permute-start.2 = (f32[2,5,128]{2,1,0:T(8,128)S(1)}, f32[2,5,128]{2,1,0:T(8,128)S(1)}, u32[]{:S(2)}, u32[]{:S(2)}) collective-permute-start(f32[2,5,128]{2,1,0:T(8,128)S(1)} %shard_map.105.weights.refs_0_), channel_id=1, source_target_pairs={{0,2},{1,3},{2,0},{3,1},{4,6},{5,7},{6,4},{7,5},{8,10},{9,11},{10,... | collective-permute-start | bytes 15368 | tf_op jit(solution)/shard_map/ppermute | solution.py:480
  24.9 2.8 %shard_map.107 = (bf16[4,2,32,256]{3,2,1,0:T(8,128)(2,1)S(1)}, bf16[4,2,32,256]{3,2,1,0:T(8,128)(2,1)S(1)}, bf16[4,2,32,256]{3,2,1,0:T(8,128)(2,1)S(1)}, bf16[4,...) custom-call(s32[1]{0:T(128)} %bitcast.1.row, ...), custom_call_target="tpu_custom_call" | custom-call | tf_op jit(solution)/shard_map/pallas_call | solution.py:96
  29.5 1.9 %collective-permute-start.8 = (bf16[4,2,32,256]{3,2,1,0:T(8,128)(2,1)S(1)}, bf16[4,2,32,256]{3,2,1,0:T(8,128)(2,1)S(1)}, u32[]{:S(2)}, u32[]{:S(2)}) collective-permute-start(bf16[4,2,32,256]{3,2,1,0:T(8,128)(2,1)S(1)} %get-tuple-element.40), channel_id=1, source_target_pairs={{0,3},{1,2},{2,1},{3,0},{4,7},{5,6},{6,5},{7,4},{8,11},{9,10},{10,... | collective-permute-start | bytes 393224 | tf_op jit(solution)/shard_map/ppermute | solution.py:480
  31.4 3.5 %collective-permute-start.9 = (bf16[4,2,32,256]{3,2,1,0:T(8,128)(2,1)S(1)}, bf16[4,2,32,256]{3,2,1,0:T(8,128)(2,1)S(1)}, u32[]{:S(2)}, u32[]{:S(2)}) collective-permute-start(bf16[4,2,32,256]{3,2,1,0:T(8,128)(2,1)S(1)} %get-tuple-element.41), channel_id=1, source_target_pairs={{0,5},{1,4},{2,7},{3,6},{4,1},{5,0},{6,3},{7,2},{8,13},{9,12},{10,... | collective-permute-start | bytes 393224 | tf_op jit(solution)/shard_map/ppermute | solution.py:480
  36.4 3.4 %collective-permute-start.5 = (bf16[4,2,32,256]{3,2,1,0:T(8,128)(2,1)S(1)}, bf16[4,2,32,256]{3,2,1,0:T(8,128)(2,1)S(1)}, u32[]{:S(2)}, u32[]{:S(2)}) collective-permute-start(bf16[4,2,32,256]{3,2,1,0:T(8,128)(2,1)S(1)} %get-tuple-element.37), channel_id=1, source_target_pairs={{0,4},{1,5},{2,6},{3,7},{4,0},{5,1},{6,2},{7,3},{8,12},{9,13},{10,... | collective-permute-start | bytes 393224 | tf_op jit(solution)/shard_map/ppermute | solution.py:480
  40.5 2.6 %shard_map.109 = (bf16[4,2,256,256]{3,2,1,0:T(8,128)(2,1)S(1)}, f32[4,256,256]{2,1,0:T(8,128)S(1)}) custom-call(s32[1]{0:T(128)} %bitcast.1.row, s32[1]{0:T(128)} %bitcast.me, s32[2,4]{1,0:T(2,128)} %bitcast.7, bf16[2,256,256]{2,1,0:T(8,128)(2,1)S(1)} %get-tuple-element.44.tile, bf16[2,256,128]{2,1,0:T(8,128)(2,1)S(1)} %collective-permute-done.12.even.side_even, ...), custom_call_target="tpu_custom_call" | custom-call | tf_op jit(solution)/shard_map/pallas_call | solution.py:96
  43.1 6.5 %collective-permute-done.9.refs_5_ = bf16[4,2,32,256]{3,2,1,0:T(8,128)(2,1)S(1)} collective-permute-done((bf16[4,2,32,256]{3,2,1,0:T(8,128)(2,1)S(1)}, bf16[4,2,32,256]{3,2,1,0:T(8,128)(2,1)S(1)}, u32[]{:S(2)}, u32[]{:S(2)}) %collective-permute-start.9) | collective-permute-done | bytes 131104 | tf_op jit(solution)/shard_map/ppermute | solution.py:480
  49.6 2.8 %collective-permute-done.10.refs_6_ = bf16[4,2,32,256]{3,2,1,0:T(8,128)(2,1)S(1)} collective-permute-done((bf16[4,2,32,256]{3,2,1,0:T(8,128)(2,1)S(1)}, bf16[4,2,32,256]{3,2,1,0:T(8,128)(2,1)S(1)}, u32[]{:S(2)}, u32[]{:S(2)}) %collective-permute-start.10) | collective-permute-done | bytes 131104 | tf_op jit(solution)/shard_map/ppermute | solution.py:480
  52.4 2.8 %collective-permute-done.11.refs_7_ = bf16[4,2,32,256]{3,2,1,0:T(8,128)(2,1)S(1)} collective-permute-done((bf16[4,2,32,256]{3,2,1,0:T(8,128)(2,1)S(1)}, bf16[4,2,32,256]{3,2,1,0:T(8,128)(2,1)S(1)}, u32[]{:S(2)}, u32[]{:S(2)}) %collective-permute-start.11) | collective-permute-done | bytes 131104 | tf_op jit(solution)/shard_map/ppermute | solution.py:480
  56.8 4.8 %shard_map.110 = (bf16[4,2,32,256]{3,2,1,0:T(8,128)(2,1)S(1)}, bf16[4,2,32,256]{3,2,1,0:T(8,128)(2,1)S(1)}, bf16[4,2,32,256]{3,2,1,0:T(8,128)(2,1)S(1)}, bf16[4,...) custom-call(s32[1,1]{1,0:T(1,128)S(6)} %copy.11.counts, ...), custom_call_target="tpu_custom_call" | custom-call | tf_op jit(solution)/shard_map/pallas_call | solution.py:96
  61.6 3.4 %collective-permute-start.20 = (bf16[4,2,32,256]{3,2,1,0:T(8,128)(2,1)S(1)}, bf16[4,2,32,256]{3,2,1,0:T(8,128)(2,1)S(1)}, u32[]{:S(2)}, u32[]{:S(2)}) collective-permute-start(bf16[4,2,32,256]{3,2,1,0:T(8,128)(2,1)S(1)} %get-tuple-element.59), channel_id=1, source_target_pairs={{0,4},{1,5},{2,6},{3,7},{4,0},{5,1},{6,2},{7,3},{8,12},{9,13},{10,... | collective-permute-start | bytes 393224 | tf_op jit(solution)/shard_map/ppermute | solution.py:480
  65.6 2.9 %collective-permute-start.23 = (bf16[4,2,32,256]{3,2,1,0:T(8,128)(2,1)S(1)}, bf16[4,2,32,256]{3,2,1,0:T(8,128)(2,1)S(1)}, u32[]{:S(2)}, u32[]{:S(2)}) collective-permute-start(bf16[4,2,32,256]{3,2,1,0:T(8,128)(2,1)S(1)} %get-tuple-element.62), channel_id=1, source_target_pairs={{0,3},{1,2},{2,1},{3,0},{4,7},{5,6},{6,5},{7,4},{8,11},{9,10},{10,... | collective-permute-start | bytes 393224 | tf_op jit(solution)/shard_map/ppermute | solution.py:480
  71.5 3.1 %shard_map.111 = (bf16[2,128,512]{2,1,0:T(8,128)(2,1)S(1)}, f32[2,256,512]{2,1,0:T(8,128)S(1)}, bf16[2,128,512]{2,1,0:T(8,128)(2,1)S(1)}) custom-call(s32[1]{0:T(128)} %bitcast.1.row, s32[2,4]{1,0:T(2,128)} %bitcast.8, f32[4,2,256,256]{3,2,1,0:T(8,128)S(1)} %get-tuple-element.51.pieces), custom_call_target="tpu_custom_call" | custom-call | tf_op jit(solution)/shard_map/pallas_call | solution.py:96
  77.9 2.6 %collective-permute-done.24.refs_9_.refs_5_ = bf16[4,2,32,256]{3,2,1,0:T(8,128)(2,1)S(1)} collective-permute-done((bf16[4,2,32,256]{3,2,1,0:T(8,128)(2,1)S(1)}, bf16[4,2,32,256]{3,2,1,0:T(8,128)(2,1)S(1)}, u32[]{:S(2)}, u32[]{:S(2)}) %collective-permute-start.24) | collective-permute-done | bytes 131104 | tf_op jit(solution)/shard_map/ppermute | solution.py:480
  80.5 4.5 %collective-permute-done.25.refs_10_.refs_6_ = bf16[4,2,32,256]{3,2,1,0:T(8,128)(2,1)S(1)} collective-permute-done((bf16[4,2,32,256]{3,2,1,0:T(8,128)(2,1)S(1)}, bf16[4,2,32,256]{3,2,1,0:T(8,128)(2,1)S(1)}, u32[]{:S(2)}, u32[]{:S(2)}) %collective-permute-start.25) | collective-permute-done | bytes 131104 | tf_op jit(solution)/shard_map/ppermute | solution.py:480
  85.0 1.6 %collective-permute-done.26.refs_11_.refs_7_ = bf16[4,2,32,256]{3,2,1,0:T(8,128)(2,1)S(1)} collective-permute-done((bf16[4,2,32,256]{3,2,1,0:T(8,128)(2,1)S(1)}, bf16[4,2,32,256]{3,2,1,0:T(8,128)(2,1)S(1)}, u32[]{:S(2)}, u32[]{:S(2)}) %collective-permute-start.26) | collective-permute-done | bytes 131104 | tf_op jit(solution)/shard_map/ppermute | solution.py:480
  91.0 1.9 %collective-permute-start.19 = (bf16[2,256,128]{2,1,0:T(8,128)(2,1)S(1)}, bf16[2,256,128]{2,1,0:T(8,128)(2,1)S(1)}, u32[]{:S(2)}, u32[]{:S(2)}) collective-permute-start(bf16[2,256,128]{2,1,0:T(8,128)(2,1)S(1)} %get-tuple-element.57), channel_id=1, source_target_pairs={{1,2},{2,1},{3,4},{4,3},{5,6},{6,5},{9,10},{10,9},{11,12},{12,11},... | collective-permute-start | bytes 393224 | tf_op jit(solution)/shard_map/ppermute | solution.py:36
  92.9 2.9 %shard_map.114 = f32[12,2,32,256]{3,2,1,0:T(8,128)S(1)} custom-call(s32[1]{0:T(128)} %bitcast.1.row, f32[2,5,128]{2,1,0:T(8,128)S(1)} %shard_map.105.weights.refs_0_, f32[2,5,128]{2,1,0:T(8,128)S(1)} %collective-permute-done.1.refs_1_, f32[2,5,128]{2,1,0:T(8,128)S(1)} %collective-permute-done.2.refs_2_, f32[2,5,128]{2,1,0:T(8,128)S(1)} %collective-permute-done.3.refs_3_, ...), custom_call_target="tpu_custom_call" | custom-call | tf_op jit(solution)/shard_map/pallas_call | solution.py:96
  95.8 2.9 %collective-permute-done.19.odd = bf16[2,256,128]{2,1,0:T(8,128)(2,1)S(1)} collective-permute-done((bf16[2,256,128]{2,1,0:T(8,128)(2,1)S(1)}, bf16[2,256,128]{2,1,0:T(8,128)(2,1)S(1)}, u32[]{:S(2)}, u32[]{:S(2)}) %collective-permute-start.19) | collective-permute-done | bytes 131104 | tf_op jit(solution)/shard_map/ppermute | solution.py:36
  (50 shorter events, 26.6 us)
Async XLA Ops:
  0.6 20.7 %collective-permute-start.4 = (bf16[1,12,2,32,256]{4,3,2,1,0:T(8,128)(2,1)}, bf16[1,12,2,32,256]{4,3,2,1,0:T(8,128)(2,1)S(1)}, u32[]{:S(2)}, u32[]{:S(2)}) collective-permute-start(bf16[1,12,2,32,256]{4,3,2,1,0:T(8,128)(2,1)} %own.1), channel_id=1, source_target_pairs={{8,0},{16,8},{24,16},{9,1},{17,9},{25,17},{10,2},{18,10},{26,18},{... | collective-permute-start | bytes 1179656 | tf_op jit(solution)/shard_map/ppermute | solution.py:26
  3.1 6.3 %collective-permute-start.12 = (bf16[2,256,128]{2,1,0:T(8,128)(2,1)S(1)}, bf16[2,256,128]{2,1,0:T(8,128)(2,1)S(1)}, u32[]{:S(2)}, u32[]{:S(2)}) collective-permute-start(bf16[2,256,128]{2,1,0:T(8,128)(2,1)S(1)} %get-tuple-element.45), channel_id=1, source_target_pairs={{0,1},{1,0},{2,3},{3,2},{4,5},{5,4},{6,7},{7,6},{8,9},{9,8},{10,11... | collective-permute-start | bytes 393224 | tf_op jit(solution)/shard_map/ppermute | solution.py:36
  4.7 9.0 %collective-permute-start.13 = (bf16[2,256,128]{2,1,0:T(8,128)(2,1)S(1)}, bf16[2,256,128]{2,1,0:T(8,128)(2,1)S(1)}, u32[]{:S(2)}, u32[]{:S(2)}) collective-permute-start(bf16[2,256,128]{2,1,0:T(8,128)(2,1)S(1)} %get-tuple-element.46), channel_id=1, source_target_pairs={{1,2},{2,1},{3,4},{4,3},{5,6},{6,5},{9,10},{10,9},{11,12},{12,11},... | collective-permute-start | bytes 393224 | tf_op jit(solution)/shard_map/ppermute | solution.py:36
  13.8 17.5 %collective-permute-start.14 = (bf16[2,128,512]{2,1,0:T(8,128)(2,1)S(1)}, bf16[2,128,512]{2,1,0:T(8,128)(2,1)S(1)}, u32[]{:S(2)}, u32[]{:S(2)}) collective-permute-start(bf16[2,128,512]{2,1,0:T(8,128)(2,1)S(1)} %get-tuple-element.47), channel_id=1, source_target_pairs={{0,8},{8,0},{16,24},{24,16},{1,9},{9,1},{17,25},{25,17},{2,10},{10... | collective-permute-start | bytes 786440 | tf_op jit(solution)/shard_map/ppermute | solution.py:36
  13.9 21.0 %collective-permute-start.15 = (bf16[2,128,512]{2,1,0:T(8,128)(2,1)S(1)}, bf16[2,128,512]{2,1,0:T(8,128)(2,1)S(1)}, u32[]{:S(2)}, u32[]{:S(2)}) collective-permute-start(bf16[2,128,512]{2,1,0:T(8,128)(2,1)S(1)} %get-tuple-element.48), channel_id=1, source_target_pairs={{8,16},{16,8},{9,17},{17,9},{10,18},{18,10},{11,19},{19,11},{12,20... | collective-permute-start | bytes 786440 | tf_op jit(solution)/shard_map/ppermute | solution.py:36
  27.8 7.1 %collective-permute-start.6 = (bf16[4,2,32,256]{3,2,1,0:T(8,128)(2,1)S(1)}, bf16[4,2,32,256]{3,2,1,0:T(8,128)(2,1)S(1)}, u32[]{:S(2)}, u32[]{:S(2)}) collective-permute-start(bf16[4,2,32,256]{3,2,1,0:T(8,128)(2,1)S(1)} %get-tuple-element.38), channel_id=1, source_target_pairs={{0,1},{1,0},{2,3},{3,2},{4,5},{5,4},{6,7},{7,6},{8,9},{9,8},{10,11... | collective-permute-start | bytes 393224 | tf_op jit(solution)/shard_map/ppermute | solution.py:480
  29.4 7.1 %collective-permute-start.7 = (bf16[4,2,32,256]{3,2,1,0:T(8,128)(2,1)S(1)}, bf16[4,2,32,256]{3,2,1,0:T(8,128)(2,1)S(1)}, u32[]{:S(2)}, u32[]{:S(2)}) collective-permute-start(bf16[4,2,32,256]{3,2,1,0:T(8,128)(2,1)S(1)} %get-tuple-element.39), channel_id=1, source_target_pairs={{0,2},{1,3},{2,0},{3,1},{4,6},{5,7},{6,4},{7,5},{8,10},{9,11},{10,... | collective-permute-start | bytes 393224 | tf_op jit(solution)/shard_map/ppermute | solution.py:480
  29.5 13.7 %collective-permute-start.8 = (bf16[4,2,32,256]{3,2,1,0:T(8,128)(2,1)S(1)}, bf16[4,2,32,256]{3,2,1,0:T(8,128)(2,1)S(1)}, u32[]{:S(2)}, u32[]{:S(2)}) collective-permute-start(bf16[4,2,32,256]{3,2,1,0:T(8,128)(2,1)S(1)} %get-tuple-element.40), channel_id=1, source_target_pairs={{0,3},{1,2},{2,1},{3,0},{4,7},{5,6},{6,5},{7,4},{8,11},{9,10},{10,... | collective-permute-start | bytes 393224 | tf_op jit(solution)/shard_map/ppermute | solution.py:480
  31.4 18.3 %collective-permute-start.9 = (bf16[4,2,32,256]{3,2,1,0:T(8,128)(2,1)S(1)}, bf16[4,2,32,256]{3,2,1,0:T(8,128)(2,1)S(1)}, u32[]{:S(2)}, u32[]{:S(2)}) collective-permute-start(bf16[4,2,32,256]{3,2,1,0:T(8,128)(2,1)S(1)} %get-tuple-element.41), channel_id=1, source_target_pairs={{0,5},{1,4},{2,7},{3,6},{4,1},{5,0},{6,3},{7,2},{8,13},{9,12},{10,... | collective-permute-start | bytes 393224 | tf_op jit(solution)/shard_map/ppermute | solution.py:480
  34.9 17.6 %collective-permute-start.10 = (bf16[4,2,32,256]{3,2,1,0:T(8,128)(2,1)S(1)}, bf16[4,2,32,256]{3,2,1,0:T(8,128)(2,1)S(1)}, u32[]{:S(2)}, u32[]{:S(2)}) collective-permute-start(bf16[4,2,32,256]{3,2,1,0:T(8,128)(2,1)S(1)} %get-tuple-element.42), channel_id=1, source_target_pairs={{0,6},{1,7},{2,4},{3,5},{4,2},{5,3},{6,0},{7,1},{8,14},{9,15},{10,... | collective-permute-start | bytes 393224 | tf_op jit(solution)/shard_map/ppermute | solution.py:480
  34.9 20.4 %collective-permute-start.11 = (bf16[4,2,32,256]{3,2,1,0:T(8,128)(2,1)S(1)}, bf16[4,2,32,256]{3,2,1,0:T(8,128)(2,1)S(1)}, u32[]{:S(2)}, u32[]{:S(2)}) collective-permute-start(bf16[4,2,32,256]{3,2,1,0:T(8,128)(2,1)S(1)} %get-tuple-element.43), channel_id=1, source_target_pairs={{0,7},{1,6},{2,5},{3,4},{4,3},{5,2},{6,1},{7,0},{8,15},{9,14},{10,... | collective-permute-start | bytes 393224 | tf_op jit(solution)/shard_map/ppermute | solution.py:480
  36.4 20.3 %collective-permute-start.5 = (bf16[4,2,32,256]{3,2,1,0:T(8,128)(2,1)S(1)}, bf16[4,2,32,256]{3,2,1,0:T(8,128)(2,1)S(1)}, u32[]{:S(2)}, u32[]{:S(2)}) collective-permute-start(bf16[4,2,32,256]{3,2,1,0:T(8,128)(2,1)S(1)} %get-tuple-element.37), channel_id=1, source_target_pairs={{0,4},{1,5},{2,6},{3,7},{4,0},{5,1},{6,2},{7,3},{8,12},{9,13},{10,... | collective-permute-start | bytes 393224 | tf_op jit(solution)/shard_map/ppermute | solution.py:480
  61.6 7.8 %collective-permute-start.20 = (bf16[4,2,32,256]{3,2,1,0:T(8,128)(2,1)S(1)}, bf16[4,2,32,256]{3,2,1,0:T(8,128)(2,1)S(1)}, u32[]{:S(2)}, u32[]{:S(2)}) collective-permute-start(bf16[4,2,32,256]{3,2,1,0:T(8,128)(2,1)S(1)} %get-tuple-element.59), channel_id=1, source_target_pairs={{0,4},{1,5},{2,6},{3,7},{4,0},{5,1},{6,2},{7,3},{8,12},{9,13},{10,... | collective-permute-start | bytes 393224 | tf_op jit(solution)/shard_map/ppermute | solution.py:480
  65.0 6.3 %collective-permute-start.21 = (bf16[4,2,32,256]{3,2,1,0:T(8,128)(2,1)S(1)}, bf16[4,2,32,256]{3,2,1,0:T(8,128)(2,1)S(1)}, u32[]{:S(2)}, u32[]{:S(2)}) collective-permute-start(bf16[4,2,32,256]{3,2,1,0:T(8,128)(2,1)S(1)} %get-tuple-element.60), channel_id=1, source_target_pairs={{0,1},{1,0},{2,3},{3,2},{4,5},{5,4},{6,7},{7,6},{8,9},{9,8},{10,11... | collective-permute-start | bytes 393224 | tf_op jit(solution)/shard_map/ppermute | solution.py:480
  65.6 9.0 %collective-permute-start.22 = (bf16[4,2,32,256]{3,2,1,0:T(8,128)(2,1)S(1)}, bf16[4,2,32,256]{3,2,1,0:T(8,128)(2,1)S(1)}, u32[]{:S(2)}, u32[]{:S(2)}) collective-permute-start(bf16[4,2,32,256]{3,2,1,0:T(8,128)(2,1)S(1)} %get-tuple-element.61), channel_id=1, source_target_pairs={{0,2},{1,3},{2,0},{3,1},{4,6},{5,7},{6,4},{7,5},{8,10},{9,11},{10,... | collective-permute-start | bytes 393224 | tf_op jit(solution)/shard_map/ppermute | solution.py:480
  65.6 10.2 %collective-permute-start.23 = (bf16[4,2,32,256]{3,2,1,0:T(8,128)(2,1)S(1)}, bf16[4,2,32,256]{3,2,1,0:T(8,128)(2,1)S(1)}, u32[]{:S(2)}, u32[]{:S(2)}) collective-permute-start(bf16[4,2,32,256]{3,2,1,0:T(8,128)(2,1)S(1)} %get-tuple-element.62), channel_id=1, source_target_pairs={{0,3},{1,2},{2,1},{3,0},{4,7},{5,6},{6,5},{7,4},{8,11},{9,10},{10,... | collective-permute-start | bytes 393224 | tf_op jit(solution)/shard_map/ppermute | solution.py:480
  68.5 12.0 %collective-permute-start.24 = (bf16[4,2,32,256]{3,2,1,0:T(8,128)(2,1)S(1)}, bf16[4,2,32,256]{3,2,1,0:T(8,128)(2,1)S(1)}, u32[]{:S(2)}, u32[]{:S(2)}) collective-permute-start(bf16[4,2,32,256]{3,2,1,0:T(8,128)(2,1)S(1)} %get-tuple-element.63), channel_id=1, source_target_pairs={{0,5},{1,4},{2,7},{3,6},{4,1},{5,0},{6,3},{7,2},{8,13},{9,12},{10,... | collective-permute-start | bytes 393224 | tf_op jit(solution)/shard_map/ppermute | solution.py:480
  69.4 15.6 %collective-permute-start.25 = (bf16[4,2,32,256]{3,2,1,0:T(8,128)(2,1)S(1)}, bf16[4,2,32,256]{3,2,1,0:T(8,128)(2,1)S(1)}, u32[]{:S(2)}, u32[]{:S(2)}) collective-permute-start(bf16[4,2,32,256]{3,2,1,0:T(8,128)(2,1)S(1)} %get-tuple-element.64), channel_id=1, source_target_pairs={{0,6},{1,7},{2,4},{3,5},{4,2},{5,3},{6,0},{7,1},{8,14},{9,15},{10,... | collective-permute-start | bytes 393224 | tf_op jit(solution)/shard_map/ppermute | solution.py:480
  71.3 15.2 %collective-permute-start.26 = (bf16[4,2,32,256]{3,2,1,0:T(8,128)(2,1)S(1)}, bf16[4,2,32,256]{3,2,1,0:T(8,128)(2,1)S(1)}, u32[]{:S(2)}, u32[]{:S(2)}) collective-permute-start(bf16[4,2,32,256]{3,2,1,0:T(8,128)(2,1)S(1)} %get-tuple-element.65), channel_id=1, source_target_pairs={{0,7},{1,6},{2,5},{3,4},{4,3},{5,2},{6,1},{7,0},{8,15},{9,14},{10,... | collective-permute-start | bytes 393224 | tf_op jit(solution)/shard_map/ppermute | solution.py:480
  74.6 14.8 %collective-permute-start.16 = (bf16[2,128,512]{2,1,0:T(8,128)(2,1)S(1)}, bf16[2,128,512]{2,1,0:T(8,128)(2,1)S(1)}, u32[]{:S(2)}, u32[]{:S(2)}) collective-permute-start(bf16[2,128,512]{2,1,0:T(8,128)(2,1)S(1)} %get-tuple-element.53), channel_id=1, source_target_pairs={{0,8},{8,0},{16,24},{24,16},{1,9},{9,1},{17,25},{25,17},{2,10},{10... | collective-permute-start | bytes 786440 | tf_op jit(solution)/shard_map/ppermute | solution.py:36
  75.7 13.7 %collective-permute-start.17 = (bf16[2,128,512]{2,1,0:T(8,128)(2,1)S(1)}, bf16[2,128,512]{2,1,0:T(8,128)(2,1)S(1)}, u32[]{:S(2)}, u32[]{:S(2)}) collective-permute-start(bf16[2,128,512]{2,1,0:T(8,128)(2,1)S(1)} %get-tuple-element.54), channel_id=1, source_target_pairs={{8,16},{16,8},{9,17},{17,9},{10,18},{18,10},{11,19},{19,11},{12,20... | collective-permute-start | bytes 786440 | tf_op jit(solution)/shard_map/ppermute | solution.py:36
  88.1 11.6 %collective-permute-start.27 = (bf16[12,2,32,256]{3,2,1,0:T(8,128)(2,1)S(1)}, bf16[12,2,32,256]{3,2,1,0:T(8,128)(2,1)S(1)}, u32[]{:S(2)}, u32[]{:S(2)}) collective-permute-start(bf16[12,2,32,256]{3,2,1,0:T(8,128)(2,1)S(1)} %shard_map.116), channel_id=1, source_target_pairs={{0,8},{8,16},{16,24},{1,9},{9,17},{17,25},{2,10},{10,18},{18,26},{... | collective-permute-start | bytes 1179656 | tf_op jit(solution)/shard_map/ppermute | solution.py:26
  89.6 6.2 %collective-permute-start.18 = (bf16[2,256,128]{2,1,0:T(8,128)(2,1)S(1)}, bf16[2,256,128]{2,1,0:T(8,128)(2,1)S(1)}, u32[]{:S(2)}, u32[]{:S(2)}) collective-permute-start(bf16[2,256,128]{2,1,0:T(8,128)(2,1)S(1)} %get-tuple-element.56), channel_id=1, source_target_pairs={{0,1},{1,0},{2,3},{3,2},{4,5},{5,4},{6,7},{7,6},{8,9},{9,8},{10,11... | collective-permute-start | bytes 393224 | tf_op jit(solution)/shard_map/ppermute | solution.py:36
  91.0 7.7 %collective-permute-start.19 = (bf16[2,256,128]{2,1,0:T(8,128)(2,1)S(1)}, bf16[2,256,128]{2,1,0:T(8,128)(2,1)S(1)}, u32[]{:S(2)}, u32[]{:S(2)}) collective-permute-start(bf16[2,256,128]{2,1,0:T(8,128)(2,1)S(1)} %get-tuple-element.57), channel_id=1, source_target_pairs={{1,2},{2,1},{3,4},{4,3},{5,6},{6,5},{9,10},{10,9},{11,12},{12,11},... | collective-permute-start | bytes 393224 | tf_op jit(solution)/shard_map/ppermute | solution.py:36
  (6 other events, 103.8 us)

commit v7 on v6

--- a/solution.py
+++ b/solution.py
@@ -324,30 +324,48 @@
 
     for block, start in zip(blocks, starts):
         probes[:, :, pl.ds(start, rows)] = block[...]
-    for slot in range(windows.shape[0]):
-        probe_re = probes[slot, 0].astype(jnp.float32)
-        probe_im = probes[slot, 1].astype(jnp.float32)
-        window_re = windows[slot, 0].astype(jnp.float32)
-        window_im = windows[slot, 1].astype(jnp.float32)
-        leaving = jnp.concatenate(
-            [
-                (probe_re * window_re - probe_im * window_im).astype(jnp.bfloat16),
-                (probe_re * window_im + probe_im * window_re).astype(jnp.bfloat16),
-            ],
-            axis=0,
+    slots = range(windows.shape[0])
+
+    def held(ref, slot):
+        return ref[slot, 0].astype(jnp.float32), ref[slot, 1].astype(jnp.float32)
+
+    def stacked(re, im):
+        return jnp.concatenate([re.astype(jnp.bfloat16), im.astype(jnp.bfloat16)], axis=0)
+
+    def beside(products):
+        columns = [products[:, slot * size : (slot + 1) * size] for slot in slots]
+        turned = [jnp.concatenate([c[:size], c[size:]], axis=1) for c in columns]
+        return jnp.concatenate(turned, axis=0)
+
+    def parts(products, slot):
+        block = products[slot * size : (slot + 1) * size]
+        return block[:, :size], block[:, size:]
+
+    leaving = []
+    for slot in slots:
+        probe_re, probe_im = held(probes, slot)
+        window_re, window_im = held(windows, slot)
+        leaving.append(
+            stacked(
+                probe_re * window_re - probe_im * window_im,
+                probe_re * window_im + probe_im * window_re,
+            )
         )
-        half = dot(forward[...], leaving).astype(jnp.bfloat16)
-        far = dot(jnp.concatenate([half[:size], half[size:]], axis=1), inverse[...])
-        far_re, far_im = (far[:, :size], far[:, size:])
+    half = dot(forward[...], jnp.concatenate(leaving, axis=1)).astype(jnp.bfloat16)
+    far = dot(beside(half), inverse[...])
+    changes = []
+    for slot in slots:
+        far_re, far_im = parts(far, slot)
         power = jnp.maximum(far_re * far_re + far_im * far_im, FLOOR * FLOOR)
         live = jnp.where(slot < counts[0, 0], 1.0, 0.0).astype(jnp.float32)
         factor = (measured[slot] * lax.rsqrt(power) - 1.0) * live
-        change = jnp.concatenate(
-            [(far_re * factor).astype(jnp.bfloat16), (far_im * factor).astype(jnp.bfloat16)], axis=0
-        )
-        back = dot(inverse[...], change).astype(jnp.bfloat16)
-        update = dot(jnp.concatenate([back[:size], back[size:]], axis=1), forward[...])
-        update_re, update_im = (update[:, :size], update[:, size:])
+        changes.append(stacked(far_re * factor, far_im * factor))
+    back = dot(inverse[...], jnp.concatenate(changes, axis=1)).astype(jnp.bfloat16)
+    update = dot(beside(back), forward[...])
+    for slot in slots:
+        update_re, update_im = parts(update, slot)
+        probe_re, probe_im = held(probes, slot)
+        window_re, window_im = held(windows, slot)
         terms[slot, 0] = (window_re * update_re + window_im * update_im).astype(jnp.bfloat16)
         terms[slot, 1] = (window_re * update_im - window_im * update_re).astype(jnp.bfloat16)
         placed[slot, 0] = probe_re * update_re + probe_im * update_im

time: 101 us -> 99.3 us (0.983)
  Pallas kernels: 23 us -> 21.3 us
    pallas_call x13, Pallas kernels: 23 us -> 21.3 us  [call(): pl.pallas_call(body, out_shape=tuple(outs), in_specs=specs, out_specs=tup...]
where the time goes in v7:
time: 99.3 us; the launch traced here: 99 us
  waiting for transfers between devices  38.2 us (38%)
  starting transfers between devices  36.9 us (37%)
  Pallas kernels  21.3 us (21%)
  between operations  1.53 us (2%)
    ppermute x18, waiting for transfers between devices, move(): lax.ppermute(value, 'col', [(i, goes_to(i, step)) for i in range(count)])  28.1 us
    ppermute x18, starting transfers between devices, move(): lax.ppermute(value, 'col', [(i, goes_to(i, step)) for i in range(count)])  26 us
    pallas_call x13, Pallas kernels, call(): pl.pallas_call(body, out_shape=tuple(outs), in_specs=specs, out_specs=tup...  21.3 us
    ppermute x8, waiting for transfers between devices, swap(): lax.ppermute(value, axis, pairs)  10 us
    ppermute x8, starting transfers between devices, swap(): lax.ppermute(value, axis, pairs)  8.35 us
    ppermute x2, starting transfers between devices, shift(): return lax.ppermute(value, axis, pairs)  2.61 us
  transfers between devices with their start and end apart: 28, of which 15 were waited for; matrix products, arithmetic and copies ran while one was open for 0% of the time, Pallas kernels for 18%

profile of v7, /device:TPU:8, one launch (start us, length us, event | category | flops | bytes accessed | tf_op | source)
XLA Modules:
  0.0 99.0 jit_solution(15780037722318804796)
XLA Ops:
  4.7 1.9 %collective-permute-start.13 = (bf16[2,256,128]{2,1,0:T(8,128)(2,1)S(1)}, bf16[2,256,128]{2,1,0:T(8,128)(2,1)S(1)}, u32[]{:S(2)}, u32[]{:S(2)}) collective-permute-start(bf16[2,256,128]{2,1,0:T(8,128)(2,1)S(1)} %get-tuple-element.46), channel_id=1, source_target_pairs={{1,2},{2,1},{3,4},{4,3},{5,6},{6,5},{9,10},{10,9},{11,12},{12,11},... | collective-permute-start | bytes 393224 | tf_op jit(solution)/shard_map/ppermute | solution.py:36
  6.6 2.8 %collective-permute-done.12.even.side_even = bf16[2,256,128]{2,1,0:T(8,128)(2,1)S(1)} collective-permute-done((bf16[2,256,128]{2,1,0:T(8,128)(2,1)S(1)}, bf16[2,256,128]{2,1,0:T(8,128)(2,1)S(1)}, u32[]{:S(2)}, u32[]{:S(2)}) %collective-permute-start.12) | collective-permute-done | bytes 131104 | tf_op jit(solution)/shard_map/ppermute | solution.py:36
  9.4 4.3 %collective-permute-done.13.odd.side_odd = bf16[2,256,128]{2,1,0:T(8,128)(2,1)S(1)} collective-permute-done((bf16[2,256,128]{2,1,0:T(8,128)(2,1)S(1)}, bf16[2,256,128]{2,1,0:T(8,128)(2,1)S(1)}, u32[]{:S(2)}, u32[]{:S(2)}) %collective-permute-start.13) | collective-permute-done | bytes 131104 | tf_op jit(solution)/shard_map/ppermute | solution.py:36
  14.7 2.7 %collective-permute-start = (f32[5,128]{1,0:T(8,128)S(1)}, f32[5,128]{1,0:T(8,128)S(1)}, u32[]{:S(2)}, u32[]{:S(2)}) collective-permute-start(f32[5,128]{1,0:T(8,128)S(1)} %get-tuple-element.34.mine), channel_id=1, source_target_pairs={{0,4},{1,5},{2,6},{3,7},{4,0},{5,1},{6,2},{7,3},{8,12},{9,13},{10,... | collective-permute-start | bytes 7688 | tf_op jit(solution)/shard_map/ppermute | solution.py:498
  17.4 1.9 %collective-permute-done.across = f32[5,128]{1,0:T(8,128)S(1)} collective-permute-done((f32[5,128]{1,0:T(8,128)S(1)}, f32[5,128]{1,0:T(8,128)S(1)}, u32[]{:S(2)}, u32[]{:S(2)}) %collective-permute-start) | collective-permute-done | bytes 2592 | tf_op jit(solution)/shard_map/ppermute | solution.py:498
  19.4 1.9 %collective-permute-start.2 = (f32[2,5,128]{2,1,0:T(8,128)S(1)}, f32[2,5,128]{2,1,0:T(8,128)S(1)}, u32[]{:S(2)}, u32[]{:S(2)}) collective-permute-start(f32[2,5,128]{2,1,0:T(8,128)S(1)} %shard_map.105.weights.refs_0_), channel_id=1, source_target_pairs={{0,2},{1,3},{2,0},{3,1},{4,6},{5,7},{6,4},{7,5},{8,10},{9,11},{10,... | collective-permute-start | bytes 15368 | tf_op jit(solution)/shard_map/ppermute | solution.py:498
  24.9 2.8 %shard_map.107 = (bf16[4,2,32,256]{3,2,1,0:T(8,128)(2,1)S(1)}, bf16[4,2,32,256]{3,2,1,0:T(8,128)(2,1)S(1)}, bf16[4,2,32,256]{3,2,1,0:T(8,128)(2,1)S(1)}, bf16[4,...) custom-call(s32[1]{0:T(128)} %bitcast.1.row, ...), custom_call_target="tpu_custom_call" | custom-call | tf_op jit(solution)/shard_map/pallas_call | solution.py:96
  29.5 1.9 %collective-permute-start.8 = (bf16[4,2,32,256]{3,2,1,0:T(8,128)(2,1)S(1)}, bf16[4,2,32,256]{3,2,1,0:T(8,128)(2,1)S(1)}, u32[]{:S(2)}, u32[]{:S(2)}) collective-permute-start(bf16[4,2,32,256]{3,2,1,0:T(8,128)(2,1)S(1)} %get-tuple-element.40), channel_id=1, source_target_pairs={{0,3},{1,2},{2,1},{3,0},{4,7},{5,6},{6,5},{7,4},{8,11},{9,10},{10,... | collective-permute-start | bytes 393224 | tf_op jit(solution)/shard_map/ppermute | solution.py:498
  31.4 3.5 %collective-permute-start.9 = (bf16[4,2,32,256]{3,2,1,0:T(8,128)(2,1)S(1)}, bf16[4,2,32,256]{3,2,1,0:T(8,128)(2,1)S(1)}, u32[]{:S(2)}, u32[]{:S(2)}) collective-permute-start(bf16[4,2,32,256]{3,2,1,0:T(8,128)(2,1)S(1)} %get-tuple-element.41), channel_id=1, source_target_pairs={{0,5},{1,4},{2,7},{3,6},{4,1},{5,0},{6,3},{7,2},{8,13},{9,12},{10,... | collective-permute-start | bytes 393224 | tf_op jit(solution)/shard_map/ppermute | solution.py:498
  36.4 3.4 %collective-permute-start.5 = (bf16[4,2,32,256]{3,2,1,0:T(8,128)(2,1)S(1)}, bf16[4,2,32,256]{3,2,1,0:T(8,128)(2,1)S(1)}, u32[]{:S(2)}, u32[]{:S(2)}) collective-permute-start(bf16[4,2,32,256]{3,2,1,0:T(8,128)(2,1)S(1)} %get-tuple-element.37), channel_id=1, source_target_pairs={{0,4},{1,5},{2,6},{3,7},{4,0},{5,1},{6,2},{7,3},{8,12},{9,13},{10,... | collective-permute-start | bytes 393224 | tf_op jit(solution)/shard_map/ppermute | solution.py:498
  40.5 2.6 %shard_map.109 = (bf16[4,2,256,256]{3,2,1,0:T(8,128)(2,1)S(1)}, f32[4,256,256]{2,1,0:T(8,128)S(1)}) custom-call(s32[1]{0:T(128)} %bitcast.1.row, s32[1]{0:T(128)} %bitcast.me, s32[2,4]{1,0:T(2,128)} %bitcast.7, bf16[2,256,256]{2,1,0:T(8,128)(2,1)S(1)} %get-tuple-element.44.tile, bf16[2,256,128]{2,1,0:T(8,128)(2,1)S(1)} %collective-permute-done.12.even.side_even, ...), custom_call_target="tpu_custom_call" | custom-call | tf_op jit(solution)/shard_map/pallas_call | solution.py:96
  43.1 6.5 %collective-permute-done.9.refs_5_ = bf16[4,2,32,256]{3,2,1,0:T(8,128)(2,1)S(1)} collective-permute-done((bf16[4,2,32,256]{3,2,1,0:T(8,128)(2,1)S(1)}, bf16[4,2,32,256]{3,2,1,0:T(8,128)(2,1)S(1)}, u32[]{:S(2)}, u32[]{:S(2)}) %collective-permute-start.9) | collective-permute-done | bytes 131104 | tf_op jit(solution)/shard_map/ppermute | solution.py:498
  49.6 2.8 %collective-permute-done.10.refs_6_ = bf16[4,2,32,256]{3,2,1,0:T(8,128)(2,1)S(1)} collective-permute-done((bf16[4,2,32,256]{3,2,1,0:T(8,128)(2,1)S(1)}, bf16[4,2,32,256]{3,2,1,0:T(8,128)(2,1)S(1)}, u32[]{:S(2)}, u32[]{:S(2)}) %collective-permute-start.10) | collective-permute-done | bytes 131104 | tf_op jit(solution)/shard_map/ppermute | solution.py:498
  52.4 2.8 %collective-permute-done.11.refs_7_ = bf16[4,2,32,256]{3,2,1,0:T(8,128)(2,1)S(1)} collective-permute-done((bf16[4,2,32,256]{3,2,1,0:T(8,128)(2,1)S(1)}, bf16[4,2,32,256]{3,2,1,0:T(8,128)(2,1)S(1)}, u32[]{:S(2)}, u32[]{:S(2)}) %collective-permute-start.11) | collective-permute-done | bytes 131104 | tf_op jit(solution)/shard_map/ppermute | solution.py:498
  56.8 3.1 %shard_map.110 = (bf16[4,2,32,256]{3,2,1,0:T(8,128)(2,1)S(1)}, bf16[4,2,32,256]{3,2,1,0:T(8,128)(2,1)S(1)}, bf16[4,2,32,256]{3,2,1,0:T(8,128)(2,1)S(1)}, bf16[4,...) custom-call(s32[1,1]{1,0:T(1,128)S(6)} %copy.11.counts, ...), custom_call_target="tpu_custom_call" | custom-call | tf_op jit(solution)/shard_map/pallas_call | solution.py:96
  59.9 3.4 %collective-permute-start.20 = (bf16[4,2,32,256]{3,2,1,0:T(8,128)(2,1)S(1)}, bf16[4,2,32,256]{3,2,1,0:T(8,128)(2,1)S(1)}, u32[]{:S(2)}, u32[]{:S(2)}) collective-permute-start(bf16[4,2,32,256]{3,2,1,0:T(8,128)(2,1)S(1)} %get-tuple-element.59), channel_id=1, source_target_pairs={{0,4},{1,5},{2,6},{3,7},{4,0},{5,1},{6,2},{7,3},{8,12},{9,13},{10,... | collective-permute-start | bytes 393224 | tf_op jit(solution)/shard_map/ppermute | solution.py:498
  63.9 2.9 %collective-permute-start.23 = (bf16[4,2,32,256]{3,2,1,0:T(8,128)(2,1)S(1)}, bf16[4,2,32,256]{3,2,1,0:T(8,128)(2,1)S(1)}, u32[]{:S(2)}, u32[]{:S(2)}) collective-permute-start(bf16[4,2,32,256]{3,2,1,0:T(8,128)(2,1)S(1)} %get-tuple-element.62), channel_id=1, source_target_pairs={{0,3},{1,2},{2,1},{3,0},{4,7},{5,6},{6,5},{7,4},{8,11},{9,10},{10,... | collective-permute-start | bytes 393224 | tf_op jit(solution)/shard_map/ppermute | solution.py:498
  69.9 3.1 %shard_map.111 = (bf16[2,128,512]{2,1,0:T(8,128)(2,1)S(1)}, f32[2,256,512]{2,1,0:T(8,128)S(1)}, bf16[2,128,512]{2,1,0:T(8,128)(2,1)S(1)}) custom-call(s32[1]{0:T(128)} %bitcast.1.row, s32[2,4]{1,0:T(2,128)} %bitcast.8, f32[4,2,256,256]{3,2,1,0:T(8,128)S(1)} %get-tuple-element.51.pieces), custom_call_target="tpu_custom_call" | custom-call | tf_op jit(solution)/shard_map/pallas_call | solution.py:96
  76.2 2.6 %collective-permute-done.24.refs_9_.refs_5_ = bf16[4,2,32,256]{3,2,1,0:T(8,128)(2,1)S(1)} collective-permute-done((bf16[4,2,32,256]{3,2,1,0:T(8,128)(2,1)S(1)}, bf16[4,2,32,256]{3,2,1,0:T(8,128)(2,1)S(1)}, u32[]{:S(2)}, u32[]{:S(2)}) %collective-permute-start.24) | collective-permute-done | bytes 131104 | tf_op jit(solution)/shard_map/ppermute | solution.py:498
  78.8 4.5 %collective-permute-done.25.refs_10_.refs_6_ = bf16[4,2,32,256]{3,2,1,0:T(8,128)(2,1)S(1)} collective-permute-done((bf16[4,2,32,256]{3,2,1,0:T(8,128)(2,1)S(1)}, bf16[4,2,32,256]{3,2,1,0:T(8,128)(2,1)S(1)}, u32[]{:S(2)}, u32[]{:S(2)}) %collective-permute-start.25) | collective-permute-done | bytes 131104 | tf_op jit(solution)/shard_map/ppermute | solution.py:498
  83.3 1.6 %collective-permute-done.26.refs_11_.refs_7_ = bf16[4,2,32,256]{3,2,1,0:T(8,128)(2,1)S(1)} collective-permute-done((bf16[4,2,32,256]{3,2,1,0:T(8,128)(2,1)S(1)}, bf16[4,2,32,256]{3,2,1,0:T(8,128)(2,1)S(1)}, u32[]{:S(2)}, u32[]{:S(2)}) %collective-permute-start.26) | collective-permute-done | bytes 131104 | tf_op jit(solution)/shard_map/ppermute | solution.py:498
  89.3 1.9 %collective-permute-start.19 = (bf16[2,256,128]{2,1,0:T(8,128)(2,1)S(1)}, bf16[2,256,128]{2,1,0:T(8,128)(2,1)S(1)}, u32[]{:S(2)}, u32[]{:S(2)}) collective-permute-start(bf16[2,256,128]{2,1,0:T(8,128)(2,1)S(1)} %get-tuple-element.57), channel_id=1, source_target_pairs={{1,2},{2,1},{3,4},{4,3},{5,6},{6,5},{9,10},{10,9},{11,12},{12,11},... | collective-permute-start | bytes 393224 | tf_op jit(solution)/shard_map/ppermute | solution.py:36
  91.2 2.9 %shard_map.114 = f32[12,2,32,256]{3,2,1,0:T(8,128)S(1)} custom-call(s32[1]{0:T(128)} %bitcast.1.row, f32[2,5,128]{2,1,0:T(8,128)S(1)} %shard_map.105.weights.refs_0_, f32[2,5,128]{2,1,0:T(8,128)S(1)} %collective-permute-done.1.refs_1_, f32[2,5,128]{2,1,0:T(8,128)S(1)} %collective-permute-done.2.refs_2_, f32[2,5,128]{2,1,0:T(8,128)S(1)} %collective-permute-done.3.refs_3_, ...), custom_call_target="tpu_custom_call" | custom-call | tf_op jit(solution)/shard_map/pallas_call | solution.py:96
  94.1 2.9 %collective-permute-done.19.odd = bf16[2,256,128]{2,1,0:T(8,128)(2,1)S(1)} collective-permute-done((bf16[2,256,128]{2,1,0:T(8,128)(2,1)S(1)}, bf16[2,256,128]{2,1,0:T(8,128)(2,1)S(1)}, u32[]{:S(2)}, u32[]{:S(2)}) %collective-permute-start.19) | collective-permute-done | bytes 131104 | tf_op jit(solution)/shard_map/ppermute | solution.py:36
  (50 shorter events, 26.6 us)
Async XLA Ops:
  0.6 20.7 %collective-permute-start.4 = (bf16[1,12,2,32,256]{4,3,2,1,0:T(8,128)(2,1)}, bf16[1,12,2,32,256]{4,3,2,1,0:T(8,128)(2,1)S(1)}, u32[]{:S(2)}, u32[]{:S(2)}) collective-permute-start(bf16[1,12,2,32,256]{4,3,2,1,0:T(8,128)(2,1)} %own.1), channel_id=1, source_target_pairs={{8,0},{16,8},{24,16},{9,1},{17,9},{25,17},{10,2},{18,10},{26,18},{... | collective-permute-start | bytes 1179656 | tf_op jit(solution)/shard_map/ppermute | solution.py:26
  3.1 6.3 %collective-permute-start.12 = (bf16[2,256,128]{2,1,0:T(8,128)(2,1)S(1)}, bf16[2,256,128]{2,1,0:T(8,128)(2,1)S(1)}, u32[]{:S(2)}, u32[]{:S(2)}) collective-permute-start(bf16[2,256,128]{2,1,0:T(8,128)(2,1)S(1)} %get-tuple-element.45), channel_id=1, source_target_pairs={{0,1},{1,0},{2,3},{3,2},{4,5},{5,4},{6,7},{7,6},{8,9},{9,8},{10,11... | collective-permute-start | bytes 393224 | tf_op jit(solution)/shard_map/ppermute | solution.py:36
  4.7 9.0 %collective-permute-start.13 = (bf16[2,256,128]{2,1,0:T(8,128)(2,1)S(1)}, bf16[2,256,128]{2,1,0:T(8,128)(2,1)S(1)}, u32[]{:S(2)}, u32[]{:S(2)}) collective-permute-start(bf16[2,256,128]{2,1,0:T(8,128)(2,1)S(1)} %get-tuple-element.46), channel_id=1, source_target_pairs={{1,2},{2,1},{3,4},{4,3},{5,6},{6,5},{9,10},{10,9},{11,12},{12,11},... | collective-permute-start | bytes 393224 | tf_op jit(solution)/shard_map/ppermute | solution.py:36
  13.8 17.5 %collective-permute-start.14 = (bf16[2,128,512]{2,1,0:T(8,128)(2,1)S(1)}, bf16[2,128,512]{2,1,0:T(8,128)(2,1)S(1)}, u32[]{:S(2)}, u32[]{:S(2)}) collective-permute-start(bf16[2,128,512]{2,1,0:T(8,128)(2,1)S(1)} %get-tuple-element.47), channel_id=1, source_target_pairs={{0,8},{8,0},{16,24},{24,16},{1,9},{9,1},{17,25},{25,17},{2,10},{10... | collective-permute-start | bytes 786440 | tf_op jit(solution)/shard_map/ppermute | solution.py:36
  13.9 21.0 %collective-permute-start.15 = (bf16[2,128,512]{2,1,0:T(8,128)(2,1)S(1)}, bf16[2,128,512]{2,1,0:T(8,128)(2,1)S(1)}, u32[]{:S(2)}, u32[]{:S(2)}) collective-permute-start(bf16[2,128,512]{2,1,0:T(8,128)(2,1)S(1)} %get-tuple-element.48), channel_id=1, source_target_pairs={{8,16},{16,8},{9,17},{17,9},{10,18},{18,10},{11,19},{19,11},{12,20... | collective-permute-start | bytes 786440 | tf_op jit(solution)/shard_map/ppermute | solution.py:36
  27.8 7.1 %collective-permute-start.6 = (bf16[4,2,32,256]{3,2,1,0:T(8,128)(2,1)S(1)}, bf16[4,2,32,256]{3,2,1,0:T(8,128)(2,1)S(1)}, u32[]{:S(2)}, u32[]{:S(2)}) collective-permute-start(bf16[4,2,32,256]{3,2,1,0:T(8,128)(2,1)S(1)} %get-tuple-element.38), channel_id=1, source_target_pairs={{0,1},{1,0},{2,3},{3,2},{4,5},{5,4},{6,7},{7,6},{8,9},{9,8},{10,11... | collective-permute-start | bytes 393224 | tf_op jit(solution)/shard_map/ppermute | solution.py:498
  29.4 7.1 %collective-permute-start.7 = (bf16[4,2,32,256]{3,2,1,0:T(8,128)(2,1)S(1)}, bf16[4,2,32,256]{3,2,1,0:T(8,128)(2,1)S(1)}, u32[]{:S(2)}, u32[]{:S(2)}) collective-permute-start(bf16[4,2,32,256]{3,2,1,0:T(8,128)(2,1)S(1)} %get-tuple-element.39), channel_id=1, source_target_pairs={{0,2},{1,3},{2,0},{3,1},{4,6},{5,7},{6,4},{7,5},{8,10},{9,11},{10,... | collective-permute-start | bytes 393224 | tf_op jit(solution)/shard_map/ppermute | solution.py:498
  29.5 13.7 %collective-permute-start.8 = (bf16[4,2,32,256]{3,2,1,0:T(8,128)(2,1)S(1)}, bf16[4,2,32,256]{3,2,1,0:T(8,128)(2,1)S(1)}, u32[]{:S(2)}, u32[]{:S(2)}) collective-permute-start(bf16[4,2,32,256]{3,2,1,0:T(8,128)(2,1)S(1)} %get-tuple-element.40), channel_id=1, source_target_pairs={{0,3},{1,2},{2,1},{3,0},{4,7},{5,6},{6,5},{7,4},{8,11},{9,10},{10,... | collective-permute-start | bytes 393224 | tf_op jit(solution)/shard_map/ppermute | solution.py:498
  31.4 18.3 %collective-permute-start.9 = (bf16[4,2,32,256]{3,2,1,0:T(8,128)(2,1)S(1)}, bf16[4,2,32,256]{3,2,1,0:T(8,128)(2,1)S(1)}, u32[]{:S(2)}, u32[]{:S(2)}) collective-permute-start(bf16[4,2,32,256]{3,2,1,0:T(8,128)(2,1)S(1)} %get-tuple-element.41), channel_id=1, source_target_pairs={{0,5},{1,4},{2,7},{3,6},{4,1},{5,0},{6,3},{7,2},{8,13},{9,12},{10,... | collective-permute-start | bytes 393224 | tf_op jit(solution)/shard_map/ppermute | solution.py:498
  34.9 17.6 %collective-permute-start.10 = (bf16[4,2,32,256]{3,2,1,0:T(8,128)(2,1)S(1)}, bf16[4,2,32,256]{3,2,1,0:T(8,128)(2,1)S(1)}, u32[]{:S(2)}, u32[]{:S(2)}) collective-permute-start(bf16[4,2,32,256]{3,2,1,0:T(8,128)(2,1)S(1)} %get-tuple-element.42), channel_id=1, source_target_pairs={{0,6},{1,7},{2,4},{3,5},{4,2},{5,3},{6,0},{7,1},{8,14},{9,15},{10,... | collective-permute-start | bytes 393224 | tf_op jit(solution)/shard_map/ppermute | solution.py:498
  34.9 20.4 %collective-permute-start.11 = (bf16[4,2,32,256]{3,2,1,0:T(8,128)(2,1)S(1)}, bf16[4,2,32,256]{3,2,1,0:T(8,128)(2,1)S(1)}, u32[]{:S(2)}, u32[]{:S(2)}) collective-permute-start(bf16[4,2,32,256]{3,2,1,0:T(8,128)(2,1)S(1)} %get-tuple-element.43), channel_id=1, source_target_pairs={{0,7},{1,6},{2,5},{3,4},{4,3},{5,2},{6,1},{7,0},{8,15},{9,14},{10,... | collective-permute-start | bytes 393224 | tf_op jit(solution)/shard_map/ppermute | solution.py:498
  36.4 20.3 %collective-permute-start.5 = (bf16[4,2,32,256]{3,2,1,0:T(8,128)(2,1)S(1)}, bf16[4,2,32,256]{3,2,1,0:T(8,128)(2,1)S(1)}, u32[]{:S(2)}, u32[]{:S(2)}) collective-permute-start(bf16[4,2,32,256]{3,2,1,0:T(8,128)(2,1)S(1)} %get-tuple-element.37), channel_id=1, source_target_pairs={{0,4},{1,5},{2,6},{3,7},{4,0},{5,1},{6,2},{7,3},{8,12},{9,13},{10,... | collective-permute-start | bytes 393224 | tf_op jit(solution)/shard_map/ppermute | solution.py:498
  59.9 7.8 %collective-permute-start.20 = (bf16[4,2,32,256]{3,2,1,0:T(8,128)(2,1)S(1)}, bf16[4,2,32,256]{3,2,1,0:T(8,128)(2,1)S(1)}, u32[]{:S(2)}, u32[]{:S(2)}) collective-permute-start(bf16[4,2,32,256]{3,2,1,0:T(8,128)(2,1)S(1)} %get-tuple-element.59), channel_id=1, source_target_pairs={{0,4},{1,5},{2,6},{3,7},{4,0},{5,1},{6,2},{7,3},{8,12},{9,13},{10,... | collective-permute-start | bytes 393224 | tf_op jit(solution)/shard_map/ppermute | solution.py:498
  63.3 6.3 %collective-permute-start.21 = (bf16[4,2,32,256]{3,2,1,0:T(8,128)(2,1)S(1)}, bf16[4,2,32,256]{3,2,1,0:T(8,128)(2,1)S(1)}, u32[]{:S(2)}, u32[]{:S(2)}) collective-permute-start(bf16[4,2,32,256]{3,2,1,0:T(8,128)(2,1)S(1)} %get-tuple-element.60), channel_id=1, source_target_pairs={{0,1},{1,0},{2,3},{3,2},{4,5},{5,4},{6,7},{7,6},{8,9},{9,8},{10,11... | collective-permute-start | bytes 393224 | tf_op jit(solution)/shard_map/ppermute | solution.py:498
  63.9 9.0 %collective-permute-start.22 = (bf16[4,2,32,256]{3,2,1,0:T(8,128)(2,1)S(1)}, bf16[4,2,32,256]{3,2,1,0:T(8,128)(2,1)S(1)}, u32[]{:S(2)}, u32[]{:S(2)}) collective-permute-start(bf16[4,2,32,256]{3,2,1,0:T(8,128)(2,1)S(1)} %get-tuple-element.61), channel_id=1, source_target_pairs={{0,2},{1,3},{2,0},{3,1},{4,6},{5,7},{6,4},{7,5},{8,10},{9,11},{10,... | collective-permute-start | bytes 393224 | tf_op jit(solution)/shard_map/ppermute | solution.py:498
  63.9 10.2 %collective-permute-start.23 = (bf16[4,2,32,256]{3,2,1,0:T(8,128)(2,1)S(1)}, bf16[4,2,32,256]{3,2,1,0:T(8,128)(2,1)S(1)}, u32[]{:S(2)}, u32[]{:S(2)}) collective-permute-start(bf16[4,2,32,256]{3,2,1,0:T(8,128)(2,1)S(1)} %get-tuple-element.62), channel_id=1, source_target_pairs={{0,3},{1,2},{2,1},{3,0},{4,7},{5,6},{6,5},{7,4},{8,11},{9,10},{10,... | collective-permute-start | bytes 393224 | tf_op jit(solution)/shard_map/ppermute | solution.py:498
  66.8 12.0 %collective-permute-start.24 = (bf16[4,2,32,256]{3,2,1,0:T(8,128)(2,1)S(1)}, bf16[4,2,32,256]{3,2,1,0:T(8,128)(2,1)S(1)}, u32[]{:S(2)}, u32[]{:S(2)}) collective-permute-start(bf16[4,2,32,256]{3,2,1,0:T(8,128)(2,1)S(1)} %get-tuple-element.63), channel_id=1, source_target_pairs={{0,5},{1,4},{2,7},{3,6},{4,1},{5,0},{6,3},{7,2},{8,13},{9,12},{10,... | collective-permute-start | bytes 393224 | tf_op jit(solution)/shard_map/ppermute | solution.py:498
  67.7 15.6 %collective-permute-start.25 = (bf16[4,2,32,256]{3,2,1,0:T(8,128)(2,1)S(1)}, bf16[4,2,32,256]{3,2,1,0:T(8,128)(2,1)S(1)}, u32[]{:S(2)}, u32[]{:S(2)}) collective-permute-start(bf16[4,2,32,256]{3,2,1,0:T(8,128)(2,1)S(1)} %get-tuple-element.64), channel_id=1, source_target_pairs={{0,6},{1,7},{2,4},{3,5},{4,2},{5,3},{6,0},{7,1},{8,14},{9,15},{10,... | collective-permute-start | bytes 393224 | tf_op jit(solution)/shard_map/ppermute | solution.py:498
  69.7 15.2 %collective-permute-start.26 = (bf16[4,2,32,256]{3,2,1,0:T(8,128)(2,1)S(1)}, bf16[4,2,32,256]{3,2,1,0:T(8,128)(2,1)S(1)}, u32[]{:S(2)}, u32[]{:S(2)}) collective-permute-start(bf16[4,2,32,256]{3,2,1,0:T(8,128)(2,1)S(1)} %get-tuple-element.65), channel_id=1, source_target_pairs={{0,7},{1,6},{2,5},{3,4},{4,3},{5,2},{6,1},{7,0},{8,15},{9,14},{10,... | collective-permute-start | bytes 393224 | tf_op jit(solution)/shard_map/ppermute | solution.py:498
  72.9 14.8 %collective-permute-start.16 = (bf16[2,128,512]{2,1,0:T(8,128)(2,1)S(1)}, bf16[2,128,512]{2,1,0:T(8,128)(2,1)S(1)}, u32[]{:S(2)}, u32[]{:S(2)}) collective-permute-start(bf16[2,128,512]{2,1,0:T(8,128)(2,1)S(1)} %get-tuple-element.53), channel_id=1, source_target_pairs={{0,8},{8,0},{16,24},{24,16},{1,9},{9,1},{17,25},{25,17},{2,10},{10... | collective-permute-start | bytes 786440 | tf_op jit(solution)/shard_map/ppermute | solution.py:36
  74.1 13.7 %collective-permute-start.17 = (bf16[2,128,512]{2,1,0:T(8,128)(2,1)S(1)}, bf16[2,128,512]{2,1,0:T(8,128)(2,1)S(1)}, u32[]{:S(2)}, u32[]{:S(2)}) collective-permute-start(bf16[2,128,512]{2,1,0:T(8,128)(2,1)S(1)} %get-tuple-element.54), channel_id=1, source_target_pairs={{8,16},{16,8},{9,17},{17,9},{10,18},{18,10},{11,19},{19,11},{12,20... | collective-permute-start | bytes 786440 | tf_op jit(solution)/shard_map/ppermute | solution.py:36
  86.4 11.6 %collective-permute-start.27 = (bf16[12,2,32,256]{3,2,1,0:T(8,128)(2,1)S(1)}, bf16[12,2,32,256]{3,2,1,0:T(8,128)(2,1)S(1)}, u32[]{:S(2)}, u32[]{:S(2)}) collective-permute-start(bf16[12,2,32,256]{3,2,1,0:T(8,128)(2,1)S(1)} %shard_map.116), channel_id=1, source_target_pairs={{0,8},{8,16},{16,24},{1,9},{9,17},{17,25},{2,10},{10,18},{18,26},{... | collective-permute-start | bytes 1179656 | tf_op jit(solution)/shard_map/ppermute | solution.py:26
  87.9 6.2 %collective-permute-start.18 = (bf16[2,256,128]{2,1,0:T(8,128)(2,1)S(1)}, bf16[2,256,128]{2,1,0:T(8,128)(2,1)S(1)}, u32[]{:S(2)}, u32[]{:S(2)}) collective-permute-start(bf16[2,256,128]{2,1,0:T(8,128)(2,1)S(1)} %get-tuple-element.56), channel_id=1, source_target_pairs={{0,1},{1,0},{2,3},{3,2},{4,5},{5,4},{6,7},{7,6},{8,9},{9,8},{10,11... | collective-permute-start | bytes 393224 | tf_op jit(solution)/shard_map/ppermute | solution.py:36
  89.3 7.7 %collective-permute-start.19 = (bf16[2,256,128]{2,1,0:T(8,128)(2,1)S(1)}, bf16[2,256,128]{2,1,0:T(8,128)(2,1)S(1)}, u32[]{:S(2)}, u32[]{:S(2)}) collective-permute-start(bf16[2,256,128]{2,1,0:T(8,128)(2,1)S(1)} %get-tuple-element.57), channel_id=1, source_target_pairs={{1,2},{2,1},{3,4},{4,3},{5,6},{6,5},{9,10},{10,9},{11,12},{12,11},... | collective-permute-start | bytes 393224 | tf_op jit(solution)/shard_map/ppermute | solution.py:36
  (6 other events, 103.8 us)

commit v8 on v7

--- a/solution.py
+++ b/solution.py
@@ -198,16 +198,11 @@
     return [first, *rest]
 
 
-def prepare_kernel(
-    me, coeffs, region, tile, payload, low, even, odd, coeffs_held, region_held, tile_held, sem
-):
+def payload_kernel(coeffs, region, payload, coeffs_held, region_held, sem):
     slots, num_modes = coeffs.shape[2:]
-    half = even.shape[2]
     copies = [
-        pltpu.make_async_copy(source, held, sem.at[at])
-        for at, (source, held) in enumerate(
-            ((coeffs, coeffs_held), (region, region_held), (tile, tile_held))
-        )
+        pltpu.make_async_copy(coeffs, coeffs_held, sem.at[0]),
+        pltpu.make_async_copy(region, region_held, sem.at[1]),
     ]
     for copy in copies:
         copy.start()
@@ -216,7 +211,14 @@
         copy.wait()
     payload[:slots, :num_modes] = coeffs_held[0, 0]
     payload[slots:, :slots] = region_held[0].astype(jnp.float32)
-    low[...] = tile_held[...].astype(jnp.bfloat16)
+
+
+def edges_kernel(me, tile, low, even, odd, held, sem):
+    half = even.shape[2]
+    copy = pltpu.make_async_copy(tile, held, sem)
+    copy.start()
+    copy.wait()
+    low[...] = held[...].astype(jnp.bfloat16)
     first, second = by_side(me[0], low[:, :, :half], low[:, :, low.shape[2] - half :])
     even[...] = first
     odd[...] = second
@@ -250,11 +252,8 @@
 
 
 def window_kernel(
-    row, me, corners, tile, side_even, side_odd, end_even, end_odd, intensity, out, measured, ext,
-    held, sem,
+    row, me, corners, tile, side_even, side_odd, end_even, end_odd, out, ext
 ):
-    copy = pltpu.make_async_copy(intensity, held, sem)
-    copy.start()
     size = out.shape[-1]
     half = side_even.shape[-1]
     rows, cols = tile.shape[1:]
@@ -281,32 +280,30 @@
         return carry
 
     lax.fori_loop(0, out.shape[0], slot_step, 0)
+
+
+def levels_kernel(intensity, measured, held, sem):
+    copy = pltpu.make_async_copy(intensity, held, sem)
+    copy.start()
     copy.wait()
-    for slot in range(out.shape[0]):
+    for slot in range(measured.shape[0]):
         measured[slot] = jnp.sqrt(held[0, 0, slot].astype(jnp.float32))
 
 
-def windows_of(row, me, corners, tile, sides, ends, intensity):
-    slot_count = intensity.shape[2]
-    size = intensity.shape[-1]
+def windows_of(row, me, corners, tile, sides, ends, slot_count, size):
     half = sides[0].shape[-1]
     extent = (2, tile.shape[1] + 2 * half + SUBLANES, tile.shape[2] + 2 * half + LANES)
     return call(
         window_kernel,
-        [((slot_count, 2, size, size), jnp.bfloat16), ((slot_count, size, size), jnp.float32)],
+        [((slot_count, 2, size, size), jnp.bfloat16)],
         (row, SMEM),
         (me, SMEM),
         (corners, SMEM),
         tile,
         *sides,
         *ends,
-        (intensity, HBM),
-        scratch=[
-            pltpu.VMEM(extent, jnp.float32),
-            pltpu.VMEM(intensity.shape, intensity.dtype),
-            pltpu.SemaphoreType.DMA,
-        ],
-    )
+        scratch=[pltpu.VMEM(extent, jnp.float32)],
+    )[0]
 
 
 def dft_kernel(goes_to, comes_from, steps, counts, me, *refs):
@@ -498,16 +495,20 @@
         return lax.ppermute(value, "col", [(i, goes_to(i, step)) for i in range(count)])
 
     side = (2, rows, half)
-    payload, low, *edges = call(
-        prepare_kernel,
-        [((slot_count + 1, LANES), jnp.float32), (object_field.shape, jnp.bfloat16)]
-        + [(side, jnp.bfloat16)] * 2,
-        (me, SMEM),
+    (payload,) = call(
+        payload_kernel,
+        [((slot_count + 1, LANES), jnp.float32)],
         (coeffs, HBM),
         (region, HBM),
+        scratch=[pltpu.VMEM(x.shape, x.dtype) for x in (coeffs, region)]
+        + [pltpu.SemaphoreType.DMA((2,))],
+    )
+    low, *edges = call(
+        edges_kernel,
+        [(object_field.shape, jnp.bfloat16)] + [(side, jnp.bfloat16)] * 2,
+        (me, SMEM),
         (object_field, HBM),
-        scratch=[pltpu.VMEM(x.shape, x.dtype) for x in (coeffs, region, object_field)]
-        + [pltpu.SemaphoreType.DMA((3,))],
+        scratch=[pltpu.VMEM(object_field.shape, object_field.dtype), pltpu.SemaphoreType.DMA],
     )
     paired = count > 1 and count & (count - 1) == 0
     if paired:
@@ -544,7 +545,13 @@
         blocks[step] = move(slab, step) if step else slab
 
     corners = pltpu.with_memory_space_constraint(offsets[0, 0].T, pltpu.HBM)
-    windows, measured = windows_of(row, me, corners, low, sides, ends, intensity)
+    (measured,) = call(
+        levels_kernel,
+        [((slot_count, size, size), jnp.float32)],
+        (intensity, HBM),
+        scratch=[pltpu.VMEM(intensity.shape, intensity.dtype), pltpu.SemaphoreType.DMA],
+    )
+    windows = windows_of(row, me, corners, low, sides, ends, slot_count, size)
     whole = (slot_count, 2, size, size)
     *terms, placed = call(
         functools.partial(dft_kernel, goes_to, comes_from, every),
@@ -598,7 +605,9 @@
         )
 
     (following,) = add_up([0] + near, ((1, 1, False),), [], [jnp.float32])
-    (following,) = add_up(crossing, ((1, 1, True),), [following], [jnp.bfloat16])
+    if len(crossing) > 1:
+        (following,) = add_up(crossing[:-1], ((1, 1, True),), [following], [jnp.float32])
+    (following,) = add_up(crossing[-1:], ((1, 1, True),), [following], [jnp.bfloat16])
     passed = shift(following, "row", 1)
     (own,) = add_up(every, ((0, 0, False),), [], [jnp.float32])
     mode_grad = (own + passed.astype(jnp.float32))[None]

time: 99.3 us -> 99.3 us (level)
  waiting for transfers between devices: 38.2 us -> 35.8 us
  Pallas kernels: 21.3 us -> 23.7 us
    ppermute x18, waiting for transfers between devices: 28.1 us -> 25.8 us  [move(): lax.ppermute(value, 'col', [(i, goes_to(i, step)) for i in range(count)])]
    pallas_call x13 -> x16, Pallas kernels: 21.3 us -> 23.7 us  [call(): pl.pallas_call(body, out_shape=tuple(outs), in_specs=specs, out_specs=tup...]
  transfers between devices with their start and end apart: 28 -> 28, of which waited for: 15 -> 15; matrix products, arithmetic and copies ran while one was open for 0% -> 0% of each run, Pallas kernels for 18% -> 21%
where the time goes in v8:
time: 99.3 us; the launch traced here: 98.8 us
  starting transfers between devices  36.8 us (37%)
  waiting for transfers between devices  35.8 us (36%)
  Pallas kernels  23.7 us (24%)
  between operations  1.55 us (2%)
  other arithmetic  1 us (1%)
    ppermute x18, starting transfers between devices, move(): lax.ppermute(value, 'col', [(i, goes_to(i, step)) for i in range(count)])  26 us
    ppermute x18, waiting for transfers between devices, move(): lax.ppermute(value, 'col', [(i, goes_to(i, step)) for i in range(count)])  25.8 us
    pallas_call x16, Pallas kernels, call(): pl.pallas_call(body, out_shape=tuple(outs), in_specs=specs, out_specs=tup...  23.7 us
    ppermute x8, waiting for transfers between devices, swap(): lax.ppermute(value, axis, pairs)  10 us
    ppermute x8, starting transfers between devices, swap(): lax.ppermute(value, axis, pairs)  8.22 us
    ppermute x2, starting transfers between devices, shift(): return lax.ppermute(value, axis, pairs)  2.61 us
  transfers between devices with their start and end apart: 28, of which 15 were waited for; matrix products, arithmetic and copies ran while one was open for 0% of the time, Pallas kernels for 21%

profile of v8, /device:TPU:8, one launch (start us, length us, event | category | flops | bytes accessed | tf_op | source)
XLA Modules:
  0.0 98.8 jit_solution(11086417556398656461)
XLA Ops:
  4.6 1.9 %collective-permute-start.13 = (bf16[2,256,128]{2,1,0:T(8,128)(2,1)S(1)}, bf16[2,256,128]{2,1,0:T(8,128)(2,1)S(1)}, u32[]{:S(2)}, u32[]{:S(2)}) collective-permute-start(bf16[2,256,128]{2,1,0:T(8,128)(2,1)S(1)} %get-tuple-element.42), channel_id=1, source_target_pairs={{1,2},{2,1},{3,4},{4,3},{5,6},{6,5},{9,10},{10,9},{11,12},{12,11},... | collective-permute-start | bytes 393224 | tf_op jit(solution)/shard_map/ppermute | solution.py:36
  6.5 2.8 %collective-permute-done.12.even.side_even = bf16[2,256,128]{2,1,0:T(8,128)(2,1)S(1)} collective-permute-done((bf16[2,256,128]{2,1,0:T(8,128)(2,1)S(1)}, bf16[2,256,128]{2,1,0:T(8,128)(2,1)S(1)}, u32[]{:S(2)}, u32[]{:S(2)}) %collective-permute-start.12) | collective-permute-done | bytes 131104 | tf_op jit(solution)/shard_map/ppermute | solution.py:36
  9.4 4.3 %collective-permute-done.13.odd.side_odd = bf16[2,256,128]{2,1,0:T(8,128)(2,1)S(1)} collective-permute-done((bf16[2,256,128]{2,1,0:T(8,128)(2,1)S(1)}, bf16[2,256,128]{2,1,0:T(8,128)(2,1)S(1)}, u32[]{:S(2)}, u32[]{:S(2)}) %collective-permute-start.13) | collective-permute-done | bytes 131104 | tf_op jit(solution)/shard_map/ppermute | solution.py:36
  15.2 2.7 %collective-permute-start = (f32[5,128]{1,0:T(8,128)S(1)}, f32[5,128]{1,0:T(8,128)S(1)}, u32[]{:S(2)}, u32[]{:S(2)}) collective-permute-start(f32[5,128]{1,0:T(8,128)S(1)} %shard_map.104.mine), channel_id=1, source_target_pairs={{0,4},{1,5},{2,6},{3,7},{4,0},{5,1},{6,2},{7,3},{8,12},{9,13},{10,... | collective-permute-start | bytes 7688 | tf_op jit(solution)/shard_map/ppermute | solution.py:495
  17.9 1.9 %collective-permute-done.across = f32[5,128]{1,0:T(8,128)S(1)} collective-permute-done((f32[5,128]{1,0:T(8,128)S(1)}, f32[5,128]{1,0:T(8,128)S(1)}, u32[]{:S(2)}, u32[]{:S(2)}) %collective-permute-start) | collective-permute-done | bytes 2592 | tf_op jit(solution)/shard_map/ppermute | solution.py:495
  19.9 1.9 %collective-permute-start.2 = (f32[2,5,128]{2,1,0:T(8,128)S(1)}, f32[2,5,128]{2,1,0:T(8,128)S(1)}, u32[]{:S(2)}, u32[]{:S(2)}) collective-permute-start(f32[2,5,128]{2,1,0:T(8,128)S(1)} %shard_map.105.weights.refs_0_), channel_id=1, source_target_pairs={{0,2},{1,3},{2,0},{3,1},{4,6},{5,7},{6,4},{7,5},{8,10},{9,11},{10,... | collective-permute-start | bytes 15368 | tf_op jit(solution)/shard_map/ppermute | solution.py:495
  25.4 2.8 %shard_map.107 = (bf16[4,2,32,256]{3,2,1,0:T(8,128)(2,1)S(1)}, bf16[4,2,32,256]{3,2,1,0:T(8,128)(2,1)S(1)}, bf16[4,2,32,256]{3,2,1,0:T(8,128)(2,1)S(1)}, bf16[4,...) custom-call(s32[1]{0:T(128)} %bitcast.1.row, ...), custom_call_target="tpu_custom_call" | custom-call | tf_op jit(solution)/shard_map/pallas_call | solution.py:96
  28.3 1.6 %collective-permute-start.6 = (bf16[4,2,32,256]{3,2,1,0:T(8,128)(2,1)S(1)}, bf16[4,2,32,256]{3,2,1,0:T(8,128)(2,1)S(1)}, u32[]{:S(2)}, u32[]{:S(2)}) collective-permute-start(bf16[4,2,32,256]{3,2,1,0:T(8,128)(2,1)S(1)} %get-tuple-element.34), channel_id=1, source_target_pairs={{0,1},{1,0},{2,3},{3,2},{4,5},{5,4},{6,7},{7,6},{8,9},{9,8},{10,11... | collective-permute-start | bytes 393224 | tf_op jit(solution)/shard_map/ppermute | solution.py:495
  30.0 1.9 %collective-permute-start.8 = (bf16[4,2,32,256]{3,2,1,0:T(8,128)(2,1)S(1)}, bf16[4,2,32,256]{3,2,1,0:T(8,128)(2,1)S(1)}, u32[]{:S(2)}, u32[]{:S(2)}) collective-permute-start(bf16[4,2,32,256]{3,2,1,0:T(8,128)(2,1)S(1)} %get-tuple-element.36), channel_id=1, source_target_pairs={{0,3},{1,2},{2,1},{3,0},{4,7},{5,6},{6,5},{7,4},{8,11},{9,10},{10,... | collective-permute-start | bytes 393224 | tf_op jit(solution)/shard_map/ppermute | solution.py:495
  31.9 3.5 %collective-permute-start.9 = (bf16[4,2,32,256]{3,2,1,0:T(8,128)(2,1)S(1)}, bf16[4,2,32,256]{3,2,1,0:T(8,128)(2,1)S(1)}, u32[]{:S(2)}, u32[]{:S(2)}) collective-permute-start(bf16[4,2,32,256]{3,2,1,0:T(8,128)(2,1)S(1)} %get-tuple-element.37), channel_id=1, source_target_pairs={{0,5},{1,4},{2,7},{3,6},{4,1},{5,0},{6,3},{7,2},{8,13},{9,12},{10,... | collective-permute-start | bytes 393224 | tf_op jit(solution)/shard_map/ppermute | solution.py:495
  37.0 3.4 %collective-permute-start.5 = (bf16[4,2,32,256]{3,2,1,0:T(8,128)(2,1)S(1)}, bf16[4,2,32,256]{3,2,1,0:T(8,128)(2,1)S(1)}, u32[]{:S(2)}, u32[]{:S(2)}) collective-permute-start(bf16[4,2,32,256]{3,2,1,0:T(8,128)(2,1)S(1)} %get-tuple-element.33), channel_id=1, source_target_pairs={{0,4},{1,5},{2,6},{3,7},{4,0},{5,1},{6,2},{7,3},{8,12},{9,13},{10,... | collective-permute-start | bytes 393224 | tf_op jit(solution)/shard_map/ppermute | solution.py:495
  42.4 2.3 %shard_map.110.refs_8_ = bf16[4,2,256,256]{3,2,1,0:T(8,128)(2,1)S(1)} custom-call(s32[1]{0:T(128)} %bitcast.1.row, s32[1]{0:T(128)} %bitcast.me, s32[2,4]{1,0:T(2,128)} %bitcast.7, bf16[2,256,256]{2,1,0:T(8,128)(2,1)S(1)} %get-tuple-element.40.tile, bf16[2,256,128]{2,1,0:T(8,128)(2,1)S(1)} %collective-permute-done.12.even.side_even, ...), custom_call_target="tpu_custom_call" | custom-call | tf_op jit(solution)/shard_map/pallas_call | solution.py:96
  44.7 5.5 %collective-permute-done.9.refs_5_ = bf16[4,2,32,256]{3,2,1,0:T(8,128)(2,1)S(1)} collective-permute-done((bf16[4,2,32,256]{3,2,1,0:T(8,128)(2,1)S(1)}, bf16[4,2,32,256]{3,2,1,0:T(8,128)(2,1)S(1)}, u32[]{:S(2)}, u32[]{:S(2)}) %collective-permute-start.9) | collective-permute-done | bytes 131104 | tf_op jit(solution)/shard_map/ppermute | solution.py:495
  50.2 2.8 %collective-permute-done.10.refs_6_ = bf16[4,2,32,256]{3,2,1,0:T(8,128)(2,1)S(1)} collective-permute-done((bf16[4,2,32,256]{3,2,1,0:T(8,128)(2,1)S(1)}, bf16[4,2,32,256]{3,2,1,0:T(8,128)(2,1)S(1)}, u32[]{:S(2)}, u32[]{:S(2)}) %collective-permute-start.10) | collective-permute-done | bytes 131104 | tf_op jit(solution)/shard_map/ppermute | solution.py:495
  53.0 2.8 %collective-permute-done.11.refs_7_ = bf16[4,2,32,256]{3,2,1,0:T(8,128)(2,1)S(1)} collective-permute-done((bf16[4,2,32,256]{3,2,1,0:T(8,128)(2,1)S(1)}, bf16[4,2,32,256]{3,2,1,0:T(8,128)(2,1)S(1)}, u32[]{:S(2)}, u32[]{:S(2)}) %collective-permute-start.11) | collective-permute-done | bytes 131104 | tf_op jit(solution)/shard_map/ppermute | solution.py:495
  57.3 3.1 %shard_map.112 = (bf16[4,2,32,256]{3,2,1,0:T(8,128)(2,1)S(1)}, bf16[4,2,32,256]{3,2,1,0:T(8,128)(2,1)S(1)}, bf16[4,2,32,256]{3,2,1,0:T(8,128)(2,1)S(1)}, bf16[4,...) custom-call(s32[1,1]{1,0:T(1,128)S(6)} %copy.11.counts, ...), custom_call_target="tpu_custom_call" | custom-call | tf_op jit(solution)/shard_map/pallas_call | solution.py:96
  60.4 3.4 %collective-permute-start.20 = (bf16[4,2,32,256]{3,2,1,0:T(8,128)(2,1)S(1)}, bf16[4,2,32,256]{3,2,1,0:T(8,128)(2,1)S(1)}, u32[]{:S(2)}, u32[]{:S(2)}) collective-permute-start(bf16[4,2,32,256]{3,2,1,0:T(8,128)(2,1)S(1)} %get-tuple-element.53), channel_id=1, source_target_pairs={{0,4},{1,5},{2,6},{3,7},{4,0},{5,1},{6,2},{7,3},{8,12},{9,13},{10,... | collective-permute-start | bytes 393224 | tf_op jit(solution)/shard_map/ppermute | solution.py:495
  64.4 2.9 %collective-permute-start.23 = (bf16[4,2,32,256]{3,2,1,0:T(8,128)(2,1)S(1)}, bf16[4,2,32,256]{3,2,1,0:T(8,128)(2,1)S(1)}, u32[]{:S(2)}, u32[]{:S(2)}) collective-permute-start(bf16[4,2,32,256]{3,2,1,0:T(8,128)(2,1)S(1)} %get-tuple-element.56), channel_id=1, source_target_pairs={{0,3},{1,2},{2,1},{3,0},{4,7},{5,6},{6,5},{7,4},{8,11},{9,10},{10,... | collective-permute-start | bytes 393224 | tf_op jit(solution)/shard_map/ppermute | solution.py:495
  70.4 3.1 %shard_map.113 = (bf16[2,128,512]{2,1,0:T(8,128)(2,1)S(1)}, f32[2,256,512]{2,1,0:T(8,128)S(1)}, bf16[2,128,512]{2,1,0:T(8,128)(2,1)S(1)}) custom-call(s32[1]{0:T(128)} %bitcast.1.row, s32[2,4]{1,0:T(2,128)} %bitcast.8, f32[4,2,256,256]{3,2,1,0:T(8,128)S(1)} %get-tuple-element.45.pieces), custom_call_target="tpu_custom_call" | custom-call | tf_op jit(solution)/shard_map/pallas_call | solution.py:96
  76.8 2.6 %collective-permute-done.24.refs_9_.refs_5_ = bf16[4,2,32,256]{3,2,1,0:T(8,128)(2,1)S(1)} collective-permute-done((bf16[4,2,32,256]{3,2,1,0:T(8,128)(2,1)S(1)}, bf16[4,2,32,256]{3,2,1,0:T(8,128)(2,1)S(1)}, u32[]{:S(2)}, u32[]{:S(2)}) %collective-permute-start.24) | collective-permute-done | bytes 131104 | tf_op jit(solution)/shard_map/ppermute | solution.py:495
  79.4 4.5 %collective-permute-done.25.refs_10_.refs_6_ = bf16[4,2,32,256]{3,2,1,0:T(8,128)(2,1)S(1)} collective-permute-done((bf16[4,2,32,256]{3,2,1,0:T(8,128)(2,1)S(1)}, bf16[4,2,32,256]{3,2,1,0:T(8,128)(2,1)S(1)}, u32[]{:S(2)}, u32[]{:S(2)}) %collective-permute-start.25) | collective-permute-done | bytes 131104 | tf_op jit(solution)/shard_map/ppermute | solution.py:495
  89.1 1.9 %collective-permute-start.19 = (bf16[2,256,128]{2,1,0:T(8,128)(2,1)S(1)}, bf16[2,256,128]{2,1,0:T(8,128)(2,1)S(1)}, u32[]{:S(2)}, u32[]{:S(2)}) collective-permute-start(bf16[2,256,128]{2,1,0:T(8,128)(2,1)S(1)} %get-tuple-element.51), channel_id=1, source_target_pairs={{1,2},{2,1},{3,4},{4,3},{5,6},{6,5},{9,10},{10,9},{11,12},{12,11},... | collective-permute-start | bytes 393224 | tf_op jit(solution)/shard_map/ppermute | solution.py:36
  91.1 2.9 %shard_map.116 = f32[12,2,32,256]{3,2,1,0:T(8,128)S(1)} custom-call(s32[1]{0:T(128)} %bitcast.1.row, f32[2,5,128]{2,1,0:T(8,128)S(1)} %shard_map.105.weights.refs_0_, f32[2,5,128]{2,1,0:T(8,128)S(1)} %collective-permute-done.1.refs_1_, f32[2,5,128]{2,1,0:T(8,128)S(1)} %collective-permute-done.2.refs_2_, f32[2,5,128]{2,1,0:T(8,128)S(1)} %collective-permute-done.3.refs_3_, ...), custom_call_target="tpu_custom_call" | custom-call | tf_op jit(solution)/shard_map/pallas_call | solution.py:96
  94.0 2.9 %collective-permute-done.19.odd = bf16[2,256,128]{2,1,0:T(8,128)(2,1)S(1)} collective-permute-done((bf16[2,256,128]{2,1,0:T(8,128)(2,1)S(1)}, bf16[2,256,128]{2,1,0:T(8,128)(2,1)S(1)}, u32[]{:S(2)}, u32[]{:S(2)}) %collective-permute-start.19) | collective-permute-done | bytes 131104 | tf_op jit(solution)/shard_map/ppermute | solution.py:36
  (53 shorter events, 27.9 us)
Async XLA Ops:
  0.6 21.2 %collective-permute-start.4 = (bf16[1,12,2,32,256]{4,3,2,1,0:T(8,128)(2,1)}, bf16[1,12,2,32,256]{4,3,2,1,0:T(8,128)(2,1)S(1)}, u32[]{:S(2)}, u32[]{:S(2)}) collective-permute-start(bf16[1,12,2,32,256]{4,3,2,1,0:T(8,128)(2,1)} %own.1), channel_id=1, source_target_pairs={{8,0},{16,8},{24,16},{9,1},{17,9},{25,17},{10,2},{18,10},{26,18},{... | collective-permute-start | bytes 1179656 | tf_op jit(solution)/shard_map/ppermute | solution.py:26
  3.1 6.3 %collective-permute-start.12 = (bf16[2,256,128]{2,1,0:T(8,128)(2,1)S(1)}, bf16[2,256,128]{2,1,0:T(8,128)(2,1)S(1)}, u32[]{:S(2)}, u32[]{:S(2)}) collective-permute-start(bf16[2,256,128]{2,1,0:T(8,128)(2,1)S(1)} %get-tuple-element.41), channel_id=1, source_target_pairs={{0,1},{1,0},{2,3},{3,2},{4,5},{5,4},{6,7},{7,6},{8,9},{9,8},{10,11... | collective-permute-start | bytes 393224 | tf_op jit(solution)/shard_map/ppermute | solution.py:36
  4.6 9.0 %collective-permute-start.13 = (bf16[2,256,128]{2,1,0:T(8,128)(2,1)S(1)}, bf16[2,256,128]{2,1,0:T(8,128)(2,1)S(1)}, u32[]{:S(2)}, u32[]{:S(2)}) collective-permute-start(bf16[2,256,128]{2,1,0:T(8,128)(2,1)S(1)} %get-tuple-element.42), channel_id=1, source_target_pairs={{1,2},{2,1},{3,4},{4,3},{5,6},{6,5},{9,10},{10,9},{11,12},{12,11},... | collective-permute-start | bytes 393224 | tf_op jit(solution)/shard_map/ppermute | solution.py:36
  13.7 18.1 %collective-permute-start.14 = (bf16[2,128,512]{2,1,0:T(8,128)(2,1)S(1)}, bf16[2,128,512]{2,1,0:T(8,128)(2,1)S(1)}, u32[]{:S(2)}, u32[]{:S(2)}) collective-permute-start(bf16[2,128,512]{2,1,0:T(8,128)(2,1)S(1)} %get-tuple-element.43), channel_id=1, source_target_pairs={{0,8},{8,0},{16,24},{24,16},{1,9},{9,1},{17,25},{25,17},{2,10},{10... | collective-permute-start | bytes 786440 | tf_op jit(solution)/shard_map/ppermute | solution.py:36
  13.8 21.6 %collective-permute-start.15 = (bf16[2,128,512]{2,1,0:T(8,128)(2,1)S(1)}, bf16[2,128,512]{2,1,0:T(8,128)(2,1)S(1)}, u32[]{:S(2)}, u32[]{:S(2)}) collective-permute-start(bf16[2,128,512]{2,1,0:T(8,128)(2,1)S(1)} %get-tuple-element.44), channel_id=1, source_target_pairs={{8,16},{16,8},{9,17},{17,9},{10,18},{18,10},{11,19},{19,11},{12,20... | collective-permute-start | bytes 786440 | tf_op jit(solution)/shard_map/ppermute | solution.py:36
  28.3 7.1 %collective-permute-start.6 = (bf16[4,2,32,256]{3,2,1,0:T(8,128)(2,1)S(1)}, bf16[4,2,32,256]{3,2,1,0:T(8,128)(2,1)S(1)}, u32[]{:S(2)}, u32[]{:S(2)}) collective-permute-start(bf16[4,2,32,256]{3,2,1,0:T(8,128)(2,1)S(1)} %get-tuple-element.34), channel_id=1, source_target_pairs={{0,1},{1,0},{2,3},{3,2},{4,5},{5,4},{6,7},{7,6},{8,9},{9,8},{10,11... | collective-permute-start | bytes 393224 | tf_op jit(solution)/shard_map/ppermute | solution.py:495
  29.9 7.1 %collective-permute-start.7 = (bf16[4,2,32,256]{3,2,1,0:T(8,128)(2,1)S(1)}, bf16[4,2,32,256]{3,2,1,0:T(8,128)(2,1)S(1)}, u32[]{:S(2)}, u32[]{:S(2)}) collective-permute-start(bf16[4,2,32,256]{3,2,1,0:T(8,128)(2,1)S(1)} %get-tuple-element.35), channel_id=1, source_target_pairs={{0,2},{1,3},{2,0},{3,1},{4,6},{5,7},{6,4},{7,5},{8,10},{9,11},{10,... | collective-permute-start | bytes 393224 | tf_op jit(solution)/shard_map/ppermute | solution.py:495
  30.0 14.7 %collective-permute-start.8 = (bf16[4,2,32,256]{3,2,1,0:T(8,128)(2,1)S(1)}, bf16[4,2,32,256]{3,2,1,0:T(8,128)(2,1)S(1)}, u32[]{:S(2)}, u32[]{:S(2)}) collective-permute-start(bf16[4,2,32,256]{3,2,1,0:T(8,128)(2,1)S(1)} %get-tuple-element.36), channel_id=1, source_target_pairs={{0,3},{1,2},{2,1},{3,0},{4,7},{5,6},{6,5},{7,4},{8,11},{9,10},{10,... | collective-permute-start | bytes 393224 | tf_op jit(solution)/shard_map/ppermute | solution.py:495
  31.9 18.3 %collective-permute-start.9 = (bf16[4,2,32,256]{3,2,1,0:T(8,128)(2,1)S(1)}, bf16[4,2,32,256]{3,2,1,0:T(8,128)(2,1)S(1)}, u32[]{:S(2)}, u32[]{:S(2)}) collective-permute-start(bf16[4,2,32,256]{3,2,1,0:T(8,128)(2,1)S(1)} %get-tuple-element.37), channel_id=1, source_target_pairs={{0,5},{1,4},{2,7},{3,6},{4,1},{5,0},{6,3},{7,2},{8,13},{9,12},{10,... | collective-permute-start | bytes 393224 | tf_op jit(solution)/shard_map/ppermute | solution.py:495
  35.4 17.6 %collective-permute-start.10 = (bf16[4,2,32,256]{3,2,1,0:T(8,128)(2,1)S(1)}, bf16[4,2,32,256]{3,2,1,0:T(8,128)(2,1)S(1)}, u32[]{:S(2)}, u32[]{:S(2)}) collective-permute-start(bf16[4,2,32,256]{3,2,1,0:T(8,128)(2,1)S(1)} %get-tuple-element.38), channel_id=1, source_target_pairs={{0,6},{1,7},{2,4},{3,5},{4,2},{5,3},{6,0},{7,1},{8,14},{9,15},{10,... | collective-permute-start | bytes 393224 | tf_op jit(solution)/shard_map/ppermute | solution.py:495
  35.4 20.4 %collective-permute-start.11 = (bf16[4,2,32,256]{3,2,1,0:T(8,128)(2,1)S(1)}, bf16[4,2,32,256]{3,2,1,0:T(8,128)(2,1)S(1)}, u32[]{:S(2)}, u32[]{:S(2)}) collective-permute-start(bf16[4,2,32,256]{3,2,1,0:T(8,128)(2,1)S(1)} %get-tuple-element.39), channel_id=1, source_target_pairs={{0,7},{1,6},{2,5},{3,4},{4,3},{5,2},{6,1},{7,0},{8,15},{9,14},{10,... | collective-permute-start | bytes 393224 | tf_op jit(solution)/shard_map/ppermute | solution.py:495
  37.0 20.3 %collective-permute-start.5 = (bf16[4,2,32,256]{3,2,1,0:T(8,128)(2,1)S(1)}, bf16[4,2,32,256]{3,2,1,0:T(8,128)(2,1)S(1)}, u32[]{:S(2)}, u32[]{:S(2)}) collective-permute-start(bf16[4,2,32,256]{3,2,1,0:T(8,128)(2,1)S(1)} %get-tuple-element.33), channel_id=1, source_target_pairs={{0,4},{1,5},{2,6},{3,7},{4,0},{5,1},{6,2},{7,3},{8,12},{9,13},{10,... | collective-permute-start | bytes 393224 | tf_op jit(solution)/shard_map/ppermute | solution.py:495
  60.4 7.8 %collective-permute-start.20 = (bf16[4,2,32,256]{3,2,1,0:T(8,128)(2,1)S(1)}, bf16[4,2,32,256]{3,2,1,0:T(8,128)(2,1)S(1)}, u32[]{:S(2)}, u32[]{:S(2)}) collective-permute-start(bf16[4,2,32,256]{3,2,1,0:T(8,128)(2,1)S(1)} %get-tuple-element.53), channel_id=1, source_target_pairs={{0,4},{1,5},{2,6},{3,7},{4,0},{5,1},{6,2},{7,3},{8,12},{9,13},{10,... | collective-permute-start | bytes 393224 | tf_op jit(solution)/shard_map/ppermute | solution.py:495
  63.9 6.3 %collective-permute-start.21 = (bf16[4,2,32,256]{3,2,1,0:T(8,128)(2,1)S(1)}, bf16[4,2,32,256]{3,2,1,0:T(8,128)(2,1)S(1)}, u32[]{:S(2)}, u32[]{:S(2)}) collective-permute-start(bf16[4,2,32,256]{3,2,1,0:T(8,128)(2,1)S(1)} %get-tuple-element.54), channel_id=1, source_target_pairs={{0,1},{1,0},{2,3},{3,2},{4,5},{5,4},{6,7},{7,6},{8,9},{9,8},{10,11... | collective-permute-start | bytes 393224 | tf_op jit(solution)/shard_map/ppermute | solution.py:495
  64.4 9.0 %collective-permute-start.22 = (bf16[4,2,32,256]{3,2,1,0:T(8,128)(2,1)S(1)}, bf16[4,2,32,256]{3,2,1,0:T(8,128)(2,1)S(1)}, u32[]{:S(2)}, u32[]{:S(2)}) collective-permute-start(bf16[4,2,32,256]{3,2,1,0:T(8,128)(2,1)S(1)} %get-tuple-element.55), channel_id=1, source_target_pairs={{0,2},{1,3},{2,0},{3,1},{4,6},{5,7},{6,4},{7,5},{8,10},{9,11},{10,... | collective-permute-start | bytes 393224 | tf_op jit(solution)/shard_map/ppermute | solution.py:495
  64.4 10.2 %collective-permute-start.23 = (bf16[4,2,32,256]{3,2,1,0:T(8,128)(2,1)S(1)}, bf16[4,2,32,256]{3,2,1,0:T(8,128)(2,1)S(1)}, u32[]{:S(2)}, u32[]{:S(2)}) collective-permute-start(bf16[4,2,32,256]{3,2,1,0:T(8,128)(2,1)S(1)} %get-tuple-element.56), channel_id=1, source_target_pairs={{0,3},{1,2},{2,1},{3,0},{4,7},{5,6},{6,5},{7,4},{8,11},{9,10},{10,... | collective-permute-start | bytes 393224 | tf_op jit(solution)/shard_map/ppermute | solution.py:495
  67.4 12.0 %collective-permute-start.24 = (bf16[4,2,32,256]{3,2,1,0:T(8,128)(2,1)S(1)}, bf16[4,2,32,256]{3,2,1,0:T(8,128)(2,1)S(1)}, u32[]{:S(2)}, u32[]{:S(2)}) collective-permute-start(bf16[4,2,32,256]{3,2,1,0:T(8,128)(2,1)S(1)} %get-tuple-element.57), channel_id=1, source_target_pairs={{0,5},{1,4},{2,7},{3,6},{4,1},{5,0},{6,3},{7,2},{8,13},{9,12},{10,... | collective-permute-start | bytes 393224 | tf_op jit(solution)/shard_map/ppermute | solution.py:495
  68.2 15.6 %collective-permute-start.25 = (bf16[4,2,32,256]{3,2,1,0:T(8,128)(2,1)S(1)}, bf16[4,2,32,256]{3,2,1,0:T(8,128)(2,1)S(1)}, u32[]{:S(2)}, u32[]{:S(2)}) collective-permute-start(bf16[4,2,32,256]{3,2,1,0:T(8,128)(2,1)S(1)} %get-tuple-element.58), channel_id=1, source_target_pairs={{0,6},{1,7},{2,4},{3,5},{4,2},{5,3},{6,0},{7,1},{8,14},{9,15},{10,... | collective-permute-start | bytes 393224 | tf_op jit(solution)/shard_map/ppermute | solution.py:495
  70.2 15.2 %collective-permute-start.26 = (bf16[4,2,32,256]{3,2,1,0:T(8,128)(2,1)S(1)}, bf16[4,2,32,256]{3,2,1,0:T(8,128)(2,1)S(1)}, u32[]{:S(2)}, u32[]{:S(2)}) collective-permute-start(bf16[4,2,32,256]{3,2,1,0:T(8,128)(2,1)S(1)} %get-tuple-element.59), channel_id=1, source_target_pairs={{0,7},{1,6},{2,5},{3,4},{4,3},{5,2},{6,1},{7,0},{8,15},{9,14},{10,... | collective-permute-start | bytes 393224 | tf_op jit(solution)/shard_map/ppermute | solution.py:495
  73.5 14.1 %collective-permute-start.16 = (bf16[2,128,512]{2,1,0:T(8,128)(2,1)S(1)}, bf16[2,128,512]{2,1,0:T(8,128)(2,1)S(1)}, u32[]{:S(2)}, u32[]{:S(2)}) collective-permute-start(bf16[2,128,512]{2,1,0:T(8,128)(2,1)S(1)} %get-tuple-element.47), channel_id=1, source_target_pairs={{0,8},{8,0},{16,24},{24,16},{1,9},{9,1},{17,25},{25,17},{2,10},{10... | collective-permute-start | bytes 786440 | tf_op jit(solution)/shard_map/ppermute | solution.py:36
  74.6 13.0 %collective-permute-start.17 = (bf16[2,128,512]{2,1,0:T(8,128)(2,1)S(1)}, bf16[2,128,512]{2,1,0:T(8,128)(2,1)S(1)}, u32[]{:S(2)}, u32[]{:S(2)}) collective-permute-start(bf16[2,128,512]{2,1,0:T(8,128)(2,1)S(1)} %get-tuple-element.48), channel_id=1, source_target_pairs={{8,16},{16,8},{9,17},{17,9},{10,18},{18,10},{11,19},{19,11},{12,20... | collective-permute-start | bytes 786440 | tf_op jit(solution)/shard_map/ppermute | solution.py:36
  86.3 11.6 %collective-permute-start.27 = (bf16[12,2,32,256]{3,2,1,0:T(8,128)(2,1)S(1)}, bf16[12,2,32,256]{3,2,1,0:T(8,128)(2,1)S(1)}, u32[]{:S(2)}, u32[]{:S(2)}) collective-permute-start(bf16[12,2,32,256]{3,2,1,0:T(8,128)(2,1)S(1)} %shard_map.119), channel_id=1, source_target_pairs={{0,8},{8,16},{16,24},{1,9},{9,17},{17,25},{2,10},{10,18},{18,26},{... | collective-permute-start | bytes 1179656 | tf_op jit(solution)/shard_map/ppermute | solution.py:26
  87.8 6.2 %collective-permute-start.18 = (bf16[2,256,128]{2,1,0:T(8,128)(2,1)S(1)}, bf16[2,256,128]{2,1,0:T(8,128)(2,1)S(1)}, u32[]{:S(2)}, u32[]{:S(2)}) collective-permute-start(bf16[2,256,128]{2,1,0:T(8,128)(2,1)S(1)} %get-tuple-element.50), channel_id=1, source_target_pairs={{0,1},{1,0},{2,3},{3,2},{4,5},{5,4},{6,7},{7,6},{8,9},{9,8},{10,11... | collective-permute-start | bytes 393224 | tf_op jit(solution)/shard_map/ppermute | solution.py:36
  89.1 7.7 %collective-permute-start.19 = (bf16[2,256,128]{2,1,0:T(8,128)(2,1)S(1)}, bf16[2,256,128]{2,1,0:T(8,128)(2,1)S(1)}, u32[]{:S(2)}, u32[]{:S(2)}) collective-permute-start(bf16[2,256,128]{2,1,0:T(8,128)(2,1)S(1)} %get-tuple-element.51), channel_id=1, source_target_pairs={{1,2},{2,1},{3,4},{4,3},{5,6},{6,5},{9,10},{10,9},{11,12},{12,11},... | collective-permute-start | bytes 393224 | tf_op jit(solution)/shard_map/ppermute | solution.py:36
  (6 other events, 75.8 us)

commit v9 on v8

--- a/solution.py
+++ b/solution.py
@@ -83,7 +83,7 @@
     return steps, goes_to, comes_from
 
 
-def call(body, outs, *operands, scratch=(), limit=20):
+def call(body, outs, *operands, scratch=(), limit=20, aliases={}):
     arrays = [o[0] if isinstance(o, tuple) else o for o in operands]
     arrays = [
         pltpu.with_memory_space_constraint(a, pltpu.HBM)
@@ -99,6 +99,7 @@
         in_specs=specs,
         out_specs=tuple(VMEM for _ in outs),
         scratch_shapes=list(scratch),
+        input_output_aliases=aliases,
         compiler_params=pltpu.CompilerParams(vmem_limit_bytes=limit * 1024 * 1024),
     )(*arrays)
 
@@ -282,9 +283,10 @@
     lax.fori_loop(0, out.shape[0], slot_step, 0)
 
 
-def levels_kernel(intensity, measured, held, sem):
+def levels_kernel(intensity, measured, zeros, held, sem):
     copy = pltpu.make_async_copy(intensity, held, sem)
     copy.start()
+    zeros[...] = jnp.zeros_like(zeros)
     copy.wait()
     for slot in range(measured.shape[0]):
         measured[slot] = jnp.sqrt(held[0, 0, slot].astype(jnp.float32))
@@ -371,11 +373,10 @@
         out[...] = terms[:, :, pl.ds(start, rows)]
 
 
-def place_kernel(half, row, corners, pieces, first, middle, second, accum):
+def place_kernel(half, row, corners, pieces, zeros, first, accum, second):
     size = pieces.shape[-1]
-    rows = middle.shape[1]
-    width = middle.shape[2]
-    accum[...] = jnp.zeros_like(accum)
+    rows = accum.shape[1] - SUBLANES - 2 * half
+    width = first.shape[2]
     for slot in range(pieces.shape[0]):
         base_row, rest_row, base_col, rest_col = corner_of(
             corners, slot, half, rows + 2 * half - size
@@ -391,18 +392,16 @@
             block = pltpu.roll(block, rest_row, 0)
             where = (part, pl.ds(base_row, size + SUBLANES), pl.ds(base_col, size + LANES))
             accum[where] += block
-    middle[...] = accum[:, half : half + rows, :width]
     top = accum[:, :half, :width].astype(jnp.bfloat16)
     bottom = accum[:, half + rows : 2 * half + rows, :width].astype(jnp.bfloat16)
     first[...], second[...] = by_side(row[0], top, bottom)
 
 
-def rows_kernel(row, me, middle, even, odd, first, center, second, total):
+def rows_kernel(row, me, accum, even, odd, first, center, second, total):
     half = even.shape[1]
-    rows = middle.shape[1]
-    cols = center.shape[2]
+    rows, cols = center.shape[1:]
     got_top, got_bottom = from_sides(row[0], even[...], odd[...])
-    total[...] = middle[...]
+    total[...] = accum[:, half : half + rows, : cols + 2 * half]
     total[:, :half] += got_top.astype(jnp.float32)
     total[:, rows - half :] += got_bottom.astype(jnp.float32)
     center[...] = total[:, :, half : half + cols]
@@ -545,9 +544,10 @@
         blocks[step] = move(slab, step) if step else slab
 
     corners = pltpu.with_memory_space_constraint(offsets[0, 0].T, pltpu.HBM)
-    (measured,) = call(
+    extent = (2, rows + 2 * half + SUBLANES, cols + 2 * half + LANES)
+    measured, zeros = call(
         levels_kernel,
-        [((slot_count, size, size), jnp.float32)],
+        [((slot_count, size, size), jnp.float32), (extent, jnp.float32)],
         (intensity, HBM),
         scratch=[pltpu.VMEM(intensity.shape, intensity.dtype), pltpu.SemaphoreType.DMA],
     )
@@ -568,14 +568,14 @@
     terms = dict(zip(every, terms))
     received = {step: move(terms[step], step) if step else terms[step] for step in every}
 
-    extent = (2, rows + 2 * half + SUBLANES, cols + 2 * half + LANES)
-    even, middle, odd = call(
+    even, accum, odd = call(
         functools.partial(place_kernel, half),
-        [(wide, jnp.bfloat16), ((2, rows, cols + 2 * half), jnp.float32), (wide, jnp.bfloat16)],
+        [(wide, jnp.bfloat16), (extent, jnp.float32), (wide, jnp.bfloat16)],
         (row, SMEM),
         (corners, SMEM),
         placed,
-        scratch=[pltpu.VMEM(extent, jnp.float32)],
+        zeros,
+        aliases={3: 1},
     )
     over_ends = swap([even, odd], "row")
     even, center, odd = call(
@@ -583,7 +583,7 @@
         [(side, jnp.bfloat16), ((2, rows, cols), jnp.float32), (side, jnp.bfloat16)],
         (row, SMEM),
         (me, SMEM),
-        middle,
+        accum,
         *over_ends,
         scratch=[pltpu.VMEM((2, rows, cols + 2 * half), jnp.float32)],
     )
@@ -605,9 +605,7 @@
         )
 
     (following,) = add_up([0] + near, ((1, 1, False),), [], [jnp.float32])
-    if len(crossing) > 1:
-        (following,) = add_up(crossing[:-1], ((1, 1, True),), [following], [jnp.float32])
-    (following,) = add_up(crossing[-1:], ((1, 1, True),), [following], [jnp.bfloat16])
+    (following,) = add_up(crossing, ((1, 1, True),), [following], [jnp.bfloat16])
     passed = shift(following, "row", 1)
     (own,) = add_up(every, ((0, 0, False),), [], [jnp.float32])
     mode_grad = (own + passed.astype(jnp.float32))[None]

time: 99.3 us -> 102 us (1.027)
  starting transfers between devices: 36.8 us -> 40.4 us
    ppermute x18, starting transfers between devices: 26 us -> 29.6 us  [move(): lax.ppermute(value, 'col', [(i, goes_to(i, step)) for i in range(count)])]
    pallas_call x16 -> x15, Pallas kernels: 23.7 us -> 22.8 us  [call(): pl.pallas_call(body, out_shape=tuple(outs), in_specs=specs, out_specs=tup...]
  transfers between devices with their start and end apart: 28 -> 28, of which waited for: 15 -> 13; matrix products, arithmetic and copies ran while one was open for 0% -> 0% of each run, Pallas kernels for 21% -> 19%
where the time goes in v9:
time: 102 us
  starting transfers between devices  40.4 us (40%)
  waiting for transfers between devices  35.7 us (35%)
  Pallas kernels  22.8 us (22%)
  between operations  1.55 us (2%)
    ppermute x18, starting transfers between devices, move(): lax.ppermute(value, 'col', [(i, goes_to(i, step)) for i in range(count)])  29.6 us
    ppermute x18, waiting for transfers between devices, move(): lax.ppermute(value, 'col', [(i, goes_to(i, step)) for i in range(count)])  25.7 us
    pallas_call x15, Pallas kernels, call(): pl.pallas_call(body, out_shape=tuple(outs), in_specs=specs, out_specs=tup...  22.8 us
    ppermute x8, waiting for transfers between devices, swap(): lax.ppermute(value, axis, pairs)  10 us
    ppermute x8, starting transfers between devices, swap(): lax.ppermute(value, axis, pairs)  8.17 us
    ppermute x2, starting transfers between devices, shift(): return lax.ppermute(value, axis, pairs)  2.61 us
  transfers between devices with their start and end apart: 28, of which 13 were waited for; matrix products, arithmetic and copies ran while one was open for 0% of the time, Pallas kernels for 19%

profile of v9, /device:TPU:8, one launch (start us, length us, event | category | flops | bytes accessed | tf_op | source)
XLA Modules:
  0.0 101.6 jit_solution(8277475173517287542)
XLA Ops:
  4.6 1.9 %collective-permute-start.13 = (bf16[2,256,128]{2,1,0:T(8,128)(2,1)S(1)}, bf16[2,256,128]{2,1,0:T(8,128)(2,1)S(1)}, u32[]{:S(2)}, u32[]{:S(2)}) collective-permute-start(bf16[2,256,128]{2,1,0:T(8,128)(2,1)S(1)} %get-tuple-element.44), channel_id=1, source_target_pairs={{1,2},{2,1},{3,4},{4,3},{5,6},{6,5},{9,10},{10,9},{11,12},{12,11},... | collective-permute-start | bytes 393224 | tf_op jit(solution)/shard_map/ppermute | solution.py:36
  6.5 2.8 %collective-permute-done.12.even.side_even = bf16[2,256,128]{2,1,0:T(8,128)(2,1)S(1)} collective-permute-done((bf16[2,256,128]{2,1,0:T(8,128)(2,1)S(1)}, bf16[2,256,128]{2,1,0:T(8,128)(2,1)S(1)}, u32[]{:S(2)}, u32[]{:S(2)}) %collective-permute-start.12) | collective-permute-done | bytes 131104 | tf_op jit(solution)/shard_map/ppermute | solution.py:36
  9.4 4.3 %collective-permute-done.13.odd.side_odd = bf16[2,256,128]{2,1,0:T(8,128)(2,1)S(1)} collective-permute-done((bf16[2,256,128]{2,1,0:T(8,128)(2,1)S(1)}, bf16[2,256,128]{2,1,0:T(8,128)(2,1)S(1)}, u32[]{:S(2)}, u32[]{:S(2)}) %collective-permute-start.13) | collective-permute-done | bytes 131104 | tf_op jit(solution)/shard_map/ppermute | solution.py:36
  15.4 2.7 %collective-permute-start = (f32[5,128]{1,0:T(8,128)S(1)}, f32[5,128]{1,0:T(8,128)S(1)}, u32[]{:S(2)}, u32[]{:S(2)}) collective-permute-start(f32[5,128]{1,0:T(8,128)S(1)} %shard_map.104.mine), channel_id=1, source_target_pairs={{0,4},{1,5},{2,6},{3,7},{4,0},{5,1},{6,2},{7,3},{8,12},{9,13},{10,... | collective-permute-start | bytes 7688 | tf_op jit(solution)/shard_map/ppermute | solution.py:494
  18.0 1.9 %collective-permute-done.across = f32[5,128]{1,0:T(8,128)S(1)} collective-permute-done((f32[5,128]{1,0:T(8,128)S(1)}, f32[5,128]{1,0:T(8,128)S(1)}, u32[]{:S(2)}, u32[]{:S(2)}) %collective-permute-start) | collective-permute-done | bytes 2592 | tf_op jit(solution)/shard_map/ppermute | solution.py:494
  20.6 2.8 %collective-permute-start.3 = (f32[2,5,128]{2,1,0:T(8,128)S(1)}, f32[2,5,128]{2,1,0:T(8,128)S(1)}, u32[]{:S(2)}, u32[]{:S(2)}) collective-permute-start(f32[2,5,128]{2,1,0:T(8,128)S(1)} %shard_map.105.weights.refs_0_), channel_id=1, source_target_pairs={{0,3},{1,2},{2,1},{3,0},{4,7},{5,6},{6,5},{7,4},{8,11},{9,10},{10,... | collective-permute-start | bytes 15368 | tf_op jit(solution)/shard_map/ppermute | solution.py:494
  25.2 2.8 %shard_map.107 = (bf16[4,2,32,256]{3,2,1,0:T(8,128)(2,1)S(1)}, bf16[4,2,32,256]{3,2,1,0:T(8,128)(2,1)S(1)}, bf16[4,2,32,256]{3,2,1,0:T(8,128)(2,1)S(1)}, bf16[4,...) custom-call(s32[1]{0:T(128)} %bitcast.1.row, ...), custom_call_target="tpu_custom_call" | custom-call | tf_op jit(solution)/shard_map/pallas_call | solution.py:96
  28.0 2.6 %collective-permute-start.10 = (bf16[4,2,32,256]{3,2,1,0:T(8,128)(2,1)S(1)}, bf16[4,2,32,256]{3,2,1,0:T(8,128)(2,1)S(1)}, u32[]{:S(2)}, u32[]{:S(2)}) collective-permute-start(bf16[4,2,32,256]{3,2,1,0:T(8,128)(2,1)S(1)} %get-tuple-element.40), channel_id=1, source_target_pairs={{0,6},{1,7},{2,4},{3,5},{4,2},{5,3},{6,0},{7,1},{8,14},{9,15},{10,... | collective-permute-start | bytes 393224 | tf_op jit(solution)/shard_map/ppermute | solution.py:494
  32.6 2.7 %collective-permute-start.7 = (bf16[4,2,32,256]{3,2,1,0:T(8,128)(2,1)S(1)}, bf16[4,2,32,256]{3,2,1,0:T(8,128)(2,1)S(1)}, u32[]{:S(2)}, u32[]{:S(2)}) collective-permute-start(bf16[4,2,32,256]{3,2,1,0:T(8,128)(2,1)S(1)} %get-tuple-element.37), channel_id=1, source_target_pairs={{0,2},{1,3},{2,0},{3,1},{4,6},{5,7},{6,4},{7,5},{8,10},{9,11},{10,... | collective-permute-start | bytes 393224 | tf_op jit(solution)/shard_map/ppermute | solution.py:494
  36.3 4.3 %collective-permute-done.10.refs_6_ = bf16[4,2,32,256]{3,2,1,0:T(8,128)(2,1)S(1)} collective-permute-done((bf16[4,2,32,256]{3,2,1,0:T(8,128)(2,1)S(1)}, bf16[4,2,32,256]{3,2,1,0:T(8,128)(2,1)S(1)}, u32[]{:S(2)}, u32[]{:S(2)}) %collective-permute-start.10) | collective-permute-done | bytes 131104 | tf_op jit(solution)/shard_map/ppermute | solution.py:494
  40.5 5.5 %collective-permute-done.11.refs_7_ = bf16[4,2,32,256]{3,2,1,0:T(8,128)(2,1)S(1)} collective-permute-done((bf16[4,2,32,256]{3,2,1,0:T(8,128)(2,1)S(1)}, bf16[4,2,32,256]{3,2,1,0:T(8,128)(2,1)S(1)}, u32[]{:S(2)}, u32[]{:S(2)}) %collective-permute-start.11) | collective-permute-done | bytes 131104 | tf_op jit(solution)/shard_map/ppermute | solution.py:494
  48.0 2.3 %shard_map.110.refs_8_ = bf16[4,2,256,256]{3,2,1,0:T(8,128)(2,1)S(1)} custom-call(s32[1]{0:T(128)} %bitcast.1.row, s32[1]{0:T(128)} %bitcast.me, s32[2,4]{1,0:T(2,128)} %bitcast.7, bf16[2,256,256]{2,1,0:T(8,128)(2,1)S(1)} %get-tuple-element.42.tile, bf16[2,256,128]{2,1,0:T(8,128)(2,1)S(1)} %collective-permute-done.12.even.side_even, ...), custom_call_target="tpu_custom_call" | custom-call | tf_op jit(solution)/shard_map/pallas_call | solution.py:96
  50.4 1.9 %collective-permute-done.5.refs_1_ = bf16[4,2,32,256]{3,2,1,0:T(8,128)(2,1)S(1)} collective-permute-done((bf16[4,2,32,256]{3,2,1,0:T(8,128)(2,1)S(1)}, bf16[4,2,32,256]{3,2,1,0:T(8,128)(2,1)S(1)}, u32[]{:S(2)}, u32[]{:S(2)}) %collective-permute-start.5) | collective-permute-done | bytes 131104 | tf_op jit(solution)/shard_map/ppermute | solution.py:494
  52.3 3.1 %shard_map.112 = (bf16[4,2,32,256]{3,2,1,0:T(8,128)(2,1)S(1)}, bf16[4,2,32,256]{3,2,1,0:T(8,128)(2,1)S(1)}, bf16[4,2,32,256]{3,2,1,0:T(8,128)(2,1)S(1)}, bf16[4,...) custom-call(s32[1,1]{1,0:T(1,128)S(6)} %copy.13.counts, ...), custom_call_target="tpu_custom_call" | custom-call | tf_op jit(solution)/shard_map/pallas_call | solution.py:96
  55.4 5.4 %collective-permute-start.21 = (bf16[4,2,32,256]{3,2,1,0:T(8,128)(2,1)S(1)}, bf16[4,2,32,256]{3,2,1,0:T(8,128)(2,1)S(1)}, u32[]{:S(2)}, u32[]{:S(2)}) collective-permute-start(bf16[4,2,32,256]{3,2,1,0:T(8,128)(2,1)S(1)} %get-tuple-element.58), channel_id=1, source_target_pairs={{0,1},{1,0},{2,3},{3,2},{4,5},{5,4},{6,7},{7,6},{8,9},{9,8},{10,11... | collective-permute-start | bytes 393224 | tf_op jit(solution)/shard_map/ppermute | solution.py:494
  60.8 2.1 %collective-permute-start.22 = (bf16[4,2,32,256]{3,2,1,0:T(8,128)(2,1)S(1)}, bf16[4,2,32,256]{3,2,1,0:T(8,128)(2,1)S(1)}, u32[]{:S(2)}, u32[]{:S(2)}) collective-permute-start(bf16[4,2,32,256]{3,2,1,0:T(8,128)(2,1)S(1)} %get-tuple-element.59), channel_id=1, source_target_pairs={{0,2},{1,3},{2,0},{3,1},{4,6},{5,7},{6,4},{7,5},{8,10},{9,11},{10,... | collective-permute-start | bytes 393224 | tf_op jit(solution)/shard_map/ppermute | solution.py:494
  68.8 1.9 %collective-permute-start.26 = (bf16[4,2,32,256]{3,2,1,0:T(8,128)(2,1)S(1)}, bf16[4,2,32,256]{3,2,1,0:T(8,128)(2,1)S(1)}, u32[]{:S(2)}, u32[]{:S(2)}) collective-permute-start(bf16[4,2,32,256]{3,2,1,0:T(8,128)(2,1)S(1)} %get-tuple-element.63), channel_id=1, source_target_pairs={{0,7},{1,6},{2,5},{3,4},{4,3},{5,2},{6,1},{7,0},{8,15},{9,14},{10,... | collective-permute-start | bytes 393224 | tf_op jit(solution)/shard_map/ppermute | solution.py:494
  70.7 2.9 %shard_map.113 = (bf16[2,128,512]{2,1,0:T(8,128)(2,1)S(1)}, f32[2,520,640]{2,1,0:T(8,128)S(1)}, bf16[2,128,512]{2,1,0:T(8,128)(2,1)S(1)}) custom-call(s32[1]{0:T(128)} %bitcast.1.row, s32[2,4]{1,0:T(2,128)} %bitcast.8, f32[4,2,256,256]{3,2,1,0:T(8,128)S(1)} %get-tuple-element.48.pieces, ...), custom_call_target="tpu_custom_call", output_to_operand_aliasing={{1}: (3, {})} | custom-call | tf_op jit(solution)/shard_map/pallas_call | solution.py:96
  73.7 5.4 %collective-permute-done.20.refs_5_.refs_4_ = bf16[4,2,32,256]{3,2,1,0:T(8,128)(2,1)S(1)} collective-permute-done((bf16[4,2,32,256]{3,2,1,0:T(8,128)(2,1)S(1)}, bf16[4,2,32,256]{3,2,1,0:T(8,128)(2,1)S(1)}, u32[]{:S(2)}, u32[]{:S(2)}) %collective-permute-start.20) | collective-permute-done | bytes 131104 | tf_op jit(solution)/shard_map/ppermute | solution.py:494
  81.8 4.1 %collective-permute-done.25.refs_10_.refs_6_ = bf16[4,2,32,256]{3,2,1,0:T(8,128)(2,1)S(1)} collective-permute-done((bf16[4,2,32,256]{3,2,1,0:T(8,128)(2,1)S(1)}, bf16[4,2,32,256]{3,2,1,0:T(8,128)(2,1)S(1)}, u32[]{:S(2)}, u32[]{:S(2)}) %collective-permute-start.25) | collective-permute-done | bytes 131104 | tf_op jit(solution)/shard_map/ppermute | solution.py:494
  85.9 1.8 %collective-permute-done.26.refs_11_.refs_7_ = bf16[4,2,32,256]{3,2,1,0:T(8,128)(2,1)S(1)} collective-permute-done((bf16[4,2,32,256]{3,2,1,0:T(8,128)(2,1)S(1)}, bf16[4,2,32,256]{3,2,1,0:T(8,128)(2,1)S(1)}, u32[]{:S(2)}, u32[]{:S(2)}) %collective-permute-start.26) | collective-permute-done | bytes 131104 | tf_op jit(solution)/shard_map/ppermute | solution.py:494
  91.9 1.9 %collective-permute-start.19 = (bf16[2,256,128]{2,1,0:T(8,128)(2,1)S(1)}, bf16[2,256,128]{2,1,0:T(8,128)(2,1)S(1)}, u32[]{:S(2)}, u32[]{:S(2)}) collective-permute-start(bf16[2,256,128]{2,1,0:T(8,128)(2,1)S(1)} %get-tuple-element.55), channel_id=1, source_target_pairs={{1,2},{2,1},{3,4},{4,3},{5,6},{6,5},{9,10},{10,9},{11,12},{12,11},... | collective-permute-start | bytes 393224 | tf_op jit(solution)/shard_map/ppermute | solution.py:36
  93.8 2.9 %shard_map.116 = f32[12,2,32,256]{3,2,1,0:T(8,128)S(1)} custom-call(s32[1]{0:T(128)} %bitcast.1.row, f32[2,5,128]{2,1,0:T(8,128)S(1)} %shard_map.105.weights.refs_0_, f32[2,5,128]{2,1,0:T(8,128)S(1)} %collective-permute-done.1.refs_1_, f32[2,5,128]{2,1,0:T(8,128)S(1)} %collective-permute-done.2.refs_2_, f32[2,5,128]{2,1,0:T(8,128)S(1)} %collective-permute-done.3.refs_3_, ...), custom_call_target="tpu_custom_call" | custom-call | tf_op jit(solution)/shard_map/pallas_call | solution.py:96
  97.2 2.5 %collective-permute-done.19.odd = bf16[2,256,128]{2,1,0:T(8,128)(2,1)S(1)} collective-permute-done((bf16[2,256,128]{2,1,0:T(8,128)(2,1)S(1)}, bf16[2,256,128]{2,1,0:T(8,128)(2,1)S(1)}, u32[]{:S(2)}, u32[]{:S(2)}) %collective-permute-start.19) | collective-permute-done | bytes 131104 | tf_op jit(solution)/shard_map/ppermute | solution.py:36
  (52 shorter events, 27.6 us)
Async XLA Ops:
  0.6 20.0 %collective-permute-start.4 = (bf16[1,12,2,32,256]{4,3,2,1,0:T(8,128)(2,1)}, bf16[1,12,2,32,256]{4,3,2,1,0:T(8,128)(2,1)S(1)}, u32[]{:S(2)}, u32[]{:S(2)}) collective-permute-start(bf16[1,12,2,32,256]{4,3,2,1,0:T(8,128)(2,1)} %own.1), channel_id=1, source_target_pairs={{8,0},{16,8},{24,16},{9,1},{17,9},{25,17},{10,2},{18,10},{26,18},{... | collective-permute-start | bytes 1179656 | tf_op jit(solution)/shard_map/ppermute | solution.py:26
  3.1 6.3 %collective-permute-start.12 = (bf16[2,256,128]{2,1,0:T(8,128)(2,1)S(1)}, bf16[2,256,128]{2,1,0:T(8,128)(2,1)S(1)}, u32[]{:S(2)}, u32[]{:S(2)}) collective-permute-start(bf16[2,256,128]{2,1,0:T(8,128)(2,1)S(1)} %get-tuple-element.43), channel_id=1, source_target_pairs={{0,1},{1,0},{2,3},{3,2},{4,5},{5,4},{6,7},{7,6},{8,9},{9,8},{10,11... | collective-permute-start | bytes 393224 | tf_op jit(solution)/shard_map/ppermute | solution.py:36
  4.6 9.0 %collective-permute-start.13 = (bf16[2,256,128]{2,1,0:T(8,128)(2,1)S(1)}, bf16[2,256,128]{2,1,0:T(8,128)(2,1)S(1)}, u32[]{:S(2)}, u32[]{:S(2)}) collective-permute-start(bf16[2,256,128]{2,1,0:T(8,128)(2,1)S(1)} %get-tuple-element.44), channel_id=1, source_target_pairs={{1,2},{2,1},{3,4},{4,3},{5,6},{6,5},{9,10},{10,9},{11,12},{12,11},... | collective-permute-start | bytes 393224 | tf_op jit(solution)/shard_map/ppermute | solution.py:36
  13.8 18.8 %collective-permute-start.14 = (bf16[2,128,512]{2,1,0:T(8,128)(2,1)S(1)}, bf16[2,128,512]{2,1,0:T(8,128)(2,1)S(1)}, u32[]{:S(2)}, u32[]{:S(2)}) collective-permute-start(bf16[2,128,512]{2,1,0:T(8,128)(2,1)S(1)} %get-tuple-element.45), channel_id=1, source_target_pairs={{0,8},{8,0},{16,24},{24,16},{1,9},{9,1},{17,25},{25,17},{2,10},{10... | collective-permute-start | bytes 786440 | tf_op jit(solution)/shard_map/ppermute | solution.py:36
  13.8 21.4 %collective-permute-start.15 = (bf16[2,128,512]{2,1,0:T(8,128)(2,1)S(1)}, bf16[2,128,512]{2,1,0:T(8,128)(2,1)S(1)}, u32[]{:S(2)}, u32[]{:S(2)}) collective-permute-start(bf16[2,128,512]{2,1,0:T(8,128)(2,1)S(1)} %get-tuple-element.46), channel_id=1, source_target_pairs={{8,16},{16,8},{9,17},{17,9},{10,18},{18,10},{11,19},{19,11},{12,20... | collective-permute-start | bytes 786440 | tf_op jit(solution)/shard_map/ppermute | solution.py:36
  28.0 12.5 %collective-permute-start.10 = (bf16[4,2,32,256]{3,2,1,0:T(8,128)(2,1)S(1)}, bf16[4,2,32,256]{3,2,1,0:T(8,128)(2,1)S(1)}, u32[]{:S(2)}, u32[]{:S(2)}) collective-permute-start(bf16[4,2,32,256]{3,2,1,0:T(8,128)(2,1)S(1)} %get-tuple-element.40), channel_id=1, source_target_pairs={{0,6},{1,7},{2,4},{3,5},{4,2},{5,3},{6,0},{7,1},{8,14},{9,15},{10,... | collective-permute-start | bytes 393224 | tf_op jit(solution)/shard_map/ppermute | solution.py:494
  30.6 15.4 %collective-permute-start.11 = (bf16[4,2,32,256]{3,2,1,0:T(8,128)(2,1)S(1)}, bf16[4,2,32,256]{3,2,1,0:T(8,128)(2,1)S(1)}, u32[]{:S(2)}, u32[]{:S(2)}) collective-permute-start(bf16[4,2,32,256]{3,2,1,0:T(8,128)(2,1)S(1)} %get-tuple-element.41), channel_id=1, source_target_pairs={{0,7},{1,6},{2,5},{3,4},{4,3},{5,2},{6,1},{7,0},{8,15},{9,14},{10,... | collective-permute-start | bytes 393224 | tf_op jit(solution)/shard_map/ppermute | solution.py:494
  32.1 18.2 %collective-permute-start.6 = (bf16[4,2,32,256]{3,2,1,0:T(8,128)(2,1)S(1)}, bf16[4,2,32,256]{3,2,1,0:T(8,128)(2,1)S(1)}, u32[]{:S(2)}, u32[]{:S(2)}) collective-permute-start(bf16[4,2,32,256]{3,2,1,0:T(8,128)(2,1)S(1)} %get-tuple-element.36), channel_id=1, source_target_pairs={{0,1},{1,0},{2,3},{3,2},{4,5},{5,4},{6,7},{7,6},{8,9},{9,8},{10,11... | collective-permute-start | bytes 393224 | tf_op jit(solution)/shard_map/ppermute | solution.py:494
  32.6 17.8 %collective-permute-start.7 = (bf16[4,2,32,256]{3,2,1,0:T(8,128)(2,1)S(1)}, bf16[4,2,32,256]{3,2,1,0:T(8,128)(2,1)S(1)}, u32[]{:S(2)}, u32[]{:S(2)}) collective-permute-start(bf16[4,2,32,256]{3,2,1,0:T(8,128)(2,1)S(1)} %get-tuple-element.37), channel_id=1, source_target_pairs={{0,2},{1,3},{2,0},{3,1},{4,6},{5,7},{6,4},{7,5},{8,10},{9,11},{10,... | collective-permute-start | bytes 393224 | tf_op jit(solution)/shard_map/ppermute | solution.py:494
  35.3 15.1 %collective-permute-start.8 = (bf16[4,2,32,256]{3,2,1,0:T(8,128)(2,1)S(1)}, bf16[4,2,32,256]{3,2,1,0:T(8,128)(2,1)S(1)}, u32[]{:S(2)}, u32[]{:S(2)}) collective-permute-start(bf16[4,2,32,256]{3,2,1,0:T(8,128)(2,1)S(1)} %get-tuple-element.38), channel_id=1, source_target_pairs={{0,3},{1,2},{2,1},{3,0},{4,7},{5,6},{6,5},{7,4},{8,11},{9,10},{10,... | collective-permute-start | bytes 393224 | tf_op jit(solution)/shard_map/ppermute | solution.py:494
  40.5 9.9 %collective-permute-start.9 = (bf16[4,2,32,256]{3,2,1,0:T(8,128)(2,1)S(1)}, bf16[4,2,32,256]{3,2,1,0:T(8,128)(2,1)S(1)}, u32[]{:S(2)}, u32[]{:S(2)}) collective-permute-start(bf16[4,2,32,256]{3,2,1,0:T(8,128)(2,1)S(1)} %get-tuple-element.39), channel_id=1, source_target_pairs={{0,5},{1,4},{2,7},{3,6},{4,1},{5,0},{6,3},{7,2},{8,13},{9,12},{10,... | collective-permute-start | bytes 393224 | tf_op jit(solution)/shard_map/ppermute | solution.py:494
  46.0 6.2 %collective-permute-start.5 = (bf16[4,2,32,256]{3,2,1,0:T(8,128)(2,1)S(1)}, bf16[4,2,32,256]{3,2,1,0:T(8,128)(2,1)S(1)}, u32[]{:S(2)}, u32[]{:S(2)}) collective-permute-start(bf16[4,2,32,256]{3,2,1,0:T(8,128)(2,1)S(1)} %get-tuple-element.35), channel_id=1, source_target_pairs={{0,4},{1,5},{2,6},{3,7},{4,0},{5,1},{6,2},{7,3},{8,12},{9,13},{10,... | collective-permute-start | bytes 393224 | tf_op jit(solution)/shard_map/ppermute | solution.py:494
  55.4 11.8 %collective-permute-start.21 = (bf16[4,2,32,256]{3,2,1,0:T(8,128)(2,1)S(1)}, bf16[4,2,32,256]{3,2,1,0:T(8,128)(2,1)S(1)}, u32[]{:S(2)}, u32[]{:S(2)}) collective-permute-start(bf16[4,2,32,256]{3,2,1,0:T(8,128)(2,1)S(1)} %get-tuple-element.58), channel_id=1, source_target_pairs={{0,1},{1,0},{2,3},{3,2},{4,5},{5,4},{6,7},{7,6},{8,9},{9,8},{10,11... | collective-permute-start | bytes 393224 | tf_op jit(solution)/shard_map/ppermute | solution.py:494
  60.8 8.0 %collective-permute-start.22 = (bf16[4,2,32,256]{3,2,1,0:T(8,128)(2,1)S(1)}, bf16[4,2,32,256]{3,2,1,0:T(8,128)(2,1)S(1)}, u32[]{:S(2)}, u32[]{:S(2)}) collective-permute-start(bf16[4,2,32,256]{3,2,1,0:T(8,128)(2,1)S(1)} %get-tuple-element.59), channel_id=1, source_target_pairs={{0,2},{1,3},{2,0},{3,1},{4,6},{5,7},{6,4},{7,5},{8,10},{9,11},{10,... | collective-permute-start | bytes 393224 | tf_op jit(solution)/shard_map/ppermute | solution.py:494
  62.9 10.7 %collective-permute-start.23 = (bf16[4,2,32,256]{3,2,1,0:T(8,128)(2,1)S(1)}, bf16[4,2,32,256]{3,2,1,0:T(8,128)(2,1)S(1)}, u32[]{:S(2)}, u32[]{:S(2)}) collective-permute-start(bf16[4,2,32,256]{3,2,1,0:T(8,128)(2,1)S(1)} %get-tuple-element.60), channel_id=1, source_target_pairs={{0,3},{1,2},{2,1},{3,0},{4,7},{5,6},{6,5},{7,4},{8,11},{9,10},{10,... | collective-permute-start | bytes 393224 | tf_op jit(solution)/shard_map/ppermute | solution.py:494
  64.3 14.7 %collective-permute-start.20 = (bf16[4,2,32,256]{3,2,1,0:T(8,128)(2,1)S(1)}, bf16[4,2,32,256]{3,2,1,0:T(8,128)(2,1)S(1)}, u32[]{:S(2)}, u32[]{:S(2)}) collective-permute-start(bf16[4,2,32,256]{3,2,1,0:T(8,128)(2,1)S(1)} %get-tuple-element.57), channel_id=1, source_target_pairs={{0,4},{1,5},{2,6},{3,7},{4,0},{5,1},{6,2},{7,3},{8,12},{9,13},{10,... | collective-permute-start | bytes 393224 | tf_op jit(solution)/shard_map/ppermute | solution.py:494
  65.8 16.1 %collective-permute-start.24 = (bf16[4,2,32,256]{3,2,1,0:T(8,128)(2,1)S(1)}, bf16[4,2,32,256]{3,2,1,0:T(8,128)(2,1)S(1)}, u32[]{:S(2)}, u32[]{:S(2)}) collective-permute-start(bf16[4,2,32,256]{3,2,1,0:T(8,128)(2,1)S(1)} %get-tuple-element.61), channel_id=1, source_target_pairs={{0,5},{1,4},{2,7},{3,6},{4,1},{5,0},{6,3},{7,2},{8,13},{9,12},{10,... | collective-permute-start | bytes 393224 | tf_op jit(solution)/shard_map/ppermute | solution.py:494
  67.2 18.7 %collective-permute-start.25 = (bf16[4,2,32,256]{3,2,1,0:T(8,128)(2,1)S(1)}, bf16[4,2,32,256]{3,2,1,0:T(8,128)(2,1)S(1)}, u32[]{:S(2)}, u32[]{:S(2)}) collective-permute-start(bf16[4,2,32,256]{3,2,1,0:T(8,128)(2,1)S(1)} %get-tuple-element.62), channel_id=1, source_target_pairs={{0,6},{1,7},{2,4},{3,5},{4,2},{5,3},{6,0},{7,1},{8,14},{9,15},{10,... | collective-permute-start | bytes 393224 | tf_op jit(solution)/shard_map/ppermute | solution.py:494
  68.8 18.9 %collective-permute-start.26 = (bf16[4,2,32,256]{3,2,1,0:T(8,128)(2,1)S(1)}, bf16[4,2,32,256]{3,2,1,0:T(8,128)(2,1)S(1)}, u32[]{:S(2)}, u32[]{:S(2)}) collective-permute-start(bf16[4,2,32,256]{3,2,1,0:T(8,128)(2,1)S(1)} %get-tuple-element.63), channel_id=1, source_target_pairs={{0,7},{1,6},{2,5},{3,4},{4,3},{5,2},{6,1},{7,0},{8,15},{9,14},{10,... | collective-permute-start | bytes 393224 | tf_op jit(solution)/shard_map/ppermute | solution.py:494
  73.6 16.9 %collective-permute-start.16 = (bf16[2,128,512]{2,1,0:T(8,128)(2,1)S(1)}, bf16[2,128,512]{2,1,0:T(8,128)(2,1)S(1)}, u32[]{:S(2)}, u32[]{:S(2)}) collective-permute-start(bf16[2,128,512]{2,1,0:T(8,128)(2,1)S(1)} %get-tuple-element.51), channel_id=1, source_target_pairs={{0,8},{8,0},{16,24},{24,16},{1,9},{9,1},{17,25},{25,17},{2,10},{10... | collective-permute-start | bytes 786440 | tf_op jit(solution)/shard_map/ppermute | solution.py:36
  79.0 11.5 %collective-permute-start.17 = (bf16[2,128,512]{2,1,0:T(8,128)(2,1)S(1)}, bf16[2,128,512]{2,1,0:T(8,128)(2,1)S(1)}, u32[]{:S(2)}, u32[]{:S(2)}) collective-permute-start(bf16[2,128,512]{2,1,0:T(8,128)(2,1)S(1)} %get-tuple-element.52), channel_id=1, source_target_pairs={{8,16},{16,8},{9,17},{17,9},{10,18},{18,10},{11,19},{19,11},{12,20... | collective-permute-start | bytes 786440 | tf_op jit(solution)/shard_map/ppermute | solution.py:36
  89.2 11.4 %collective-permute-start.27 = (bf16[12,2,32,256]{3,2,1,0:T(8,128)(2,1)S(1)}, bf16[12,2,32,256]{3,2,1,0:T(8,128)(2,1)S(1)}, u32[]{:S(2)}, u32[]{:S(2)}) collective-permute-start(bf16[12,2,32,256]{3,2,1,0:T(8,128)(2,1)S(1)} %shard_map.118), channel_id=1, source_target_pairs={{0,8},{8,16},{16,24},{1,9},{9,17},{17,25},{2,10},{10,18},{18,26},{... | collective-permute-start | bytes 1179656 | tf_op jit(solution)/shard_map/ppermute | solution.py:26
  90.7 6.4 %collective-permute-start.18 = (bf16[2,256,128]{2,1,0:T(8,128)(2,1)S(1)}, bf16[2,256,128]{2,1,0:T(8,128)(2,1)S(1)}, u32[]{:S(2)}, u32[]{:S(2)}) collective-permute-start(bf16[2,256,128]{2,1,0:T(8,128)(2,1)S(1)} %get-tuple-element.54), channel_id=1, source_target_pairs={{0,1},{1,0},{2,3},{3,2},{4,5},{5,4},{6,7},{7,6},{8,9},{9,8},{10,11... | collective-permute-start | bytes 393224 | tf_op jit(solution)/shard_map/ppermute | solution.py:36
  91.9 7.7 %collective-permute-start.19 = (bf16[2,256,128]{2,1,0:T(8,128)(2,1)S(1)}, bf16[2,256,128]{2,1,0:T(8,128)(2,1)S(1)}, u32[]{:S(2)}, u32[]{:S(2)}) collective-permute-start(bf16[2,256,128]{2,1,0:T(8,128)(2,1)S(1)} %get-tuple-element.55), channel_id=1, source_target_pairs={{1,2},{2,1},{3,4},{4,3},{5,6},{6,5},{9,10},{10,9},{11,12},{12,11},... | collective-permute-start | bytes 393224 | tf_op jit(solution)/shard_map/ppermute | solution.py:36
  (6 other events, 95.4 us)

commit v10 on v9

--- a/solution.py
+++ b/solution.py
@@ -61,7 +61,8 @@
 
 def transfer_order(count):
     half = count // 2
-    return [half] * (half > 0) + list(range(1, half)) + list(range(half + 1, count))
+    far = list(range(half + 1, count))
+    return [half] * (half > 0) + list(range(1, half)) + far[:-2] + far[:-3:-1]
 
 
 def slab_order(count, paired):
@@ -252,6 +253,41 @@
     return base_row, rest_row, base_col, rest_col
 
 
+def beyond(shape, dim, bound):
+    return lax.broadcasted_iota(jnp.int32, shape, dim) >= bound
+
+
+def pushed(block, down, across):
+    rows, cols = block.shape
+    edge = jnp.zeros((rows, LANES), block.dtype)
+    tiles = [block[:, start : start + LANES] for start in range(0, cols, LANES)]
+    tiles = [pltpu.roll(tile, across, 1) for tile in tiles]
+    kept = beyond((rows, LANES), 1, across)
+    pairs = zip(tiles + [edge], [edge] + tiles)
+    block = jnp.concatenate([jnp.where(kept, tile, before) for tile, before in pairs], axis=1)
+    cols += LANES
+    tall = block.reshape(rows // SUBLANES, SUBLANES, cols)
+    tall = pltpu.roll(tall, down, 1)
+    edge = jnp.zeros((1, SUBLANES, cols), block.dtype)
+    below = jnp.concatenate([tall, edge], axis=0)
+    above = jnp.concatenate([edge, tall], axis=0)
+    tall = jnp.where(beyond(below.shape, 1, down), below, above)
+    return tall.reshape(rows + SUBLANES, cols)
+
+
+def pulled(block, up, back):
+    rows, cols = block.shape
+    tall = block.reshape(rows // SUBLANES, SUBLANES, cols)
+    tall = pltpu.roll(tall, (SUBLANES - up) & (SUBLANES - 1), 1)
+    kept = beyond(tall[1:].shape, 1, SUBLANES - up)
+    block = jnp.where(kept, tall[1:], tall[:-1]).reshape(rows - SUBLANES, cols)
+    tiles = [block[:, start : start + LANES] for start in range(0, cols, LANES)]
+    tiles = [pltpu.roll(tile, (LANES - back) & (LANES - 1), 1) for tile in tiles]
+    kept = beyond((rows - SUBLANES, LANES), 1, LANES - back)
+    pairs = zip(tiles[1:], tiles[:-1])
+    return jnp.concatenate([jnp.where(kept, after, tile) for after, tile in pairs], axis=1)
+
+
 def window_kernel(
     row, me, corners, tile, side_even, side_odd, end_even, end_odd, out, ext
 ):
@@ -275,9 +311,7 @@
         )
         for part in range(2):
             block = ext[part, pl.ds(base_row, tall), pl.ds(base_col, wide)]
-            block = pltpu.roll(block, lax.rem(tall - rest_row, tall), 0)[:size]
-            block = pltpu.roll(block, lax.rem(wide - rest_col, wide), 1)[:, :size]
-            out[slot, part] = block.astype(jnp.bfloat16)
+            out[slot, part] = pulled(block, rest_row, rest_col).astype(jnp.bfloat16)
         return carry
 
     lax.fori_loop(0, out.shape[0], slot_step, 0)
@@ -382,14 +416,7 @@
             corners, slot, half, rows + 2 * half - size
         )
         for part in range(2):
-            block = jnp.concatenate(
-                [pieces[slot, part], jnp.zeros((size, LANES), jnp.float32)], axis=1
-            )
-            block = pltpu.roll(block, rest_col, 1)
-            block = jnp.concatenate(
-                [block, jnp.zeros((SUBLANES, size + LANES), jnp.float32)], axis=0
-            )
-            block = pltpu.roll(block, rest_row, 0)
+            block = pushed(pieces[slot, part], rest_row, rest_col)
             where = (part, pl.ds(base_row, size + SUBLANES), pl.ds(base_col, size + LANES))
             accum[where] += block
     top = accum[:, :half, :width].astype(jnp.bfloat16)
@@ -488,7 +515,7 @@
     count = lax.axis_size("col")
     middle_step = count // 2
     near = list(range(1, middle_step))
-    crossing = list(range(max(middle_step, 1), count))
+    crossing = [step for step in steps if step >= middle_step]
 
     def move(value, step):
         return lax.ppermute(value, "col", [(i, goes_to(i, step)) for i in range(count)])
@@ -605,7 +632,9 @@
         )
 
     (following,) = add_up([0] + near, ((1, 1, False),), [], [jnp.float32])
-    (following,) = add_up(crossing, ((1, 1, True),), [following], [jnp.bfloat16])
+    if len(crossing) > 1:
+        (following,) = add_up(crossing[:-1], ((1, 1, True),), [following], [jnp.float32])
+    (following,) = add_up(crossing[-1:], ((1, 1, True),), [following], [jnp.bfloat16])
     passed = shift(following, "row", 1)
     (own,) = add_up(every, ((0, 0, False),), [], [jnp.float32])
     mode_grad = (own + passed.astype(jnp.float32))[None]

time: 102 us -> 101 us (level)
  the two profiles are of different devices: /device:TPU:8 before, /device:TPU:16 now
where the time goes in v10:
time: 101 us; the launch traced here: 100 us
  waiting for transfers between devices  40.1 us (40%)
  starting transfers between devices  36.3 us (36%)
  Pallas kernels  21.3 us (21%)
  between operations  1.57 us (2%)
    ppermute x18, waiting for transfers between devices, move(): lax.ppermute(value, 'col', [(i, goes_to(i, step)) for i in range(count)])  31.4 us
    ppermute x18, starting transfers between devices, move(): lax.ppermute(value, 'col', [(i, goes_to(i, step)) for i in range(count)])  23.9 us
    pallas_call x16, Pallas kernels, call(): pl.pallas_call(body, out_shape=tuple(outs), in_specs=specs, out_specs=tup...  21.3 us
    ppermute x8, starting transfers between devices, swap(): lax.ppermute(value, axis, pairs)  9.82 us
    ppermute x8, waiting for transfers between devices, swap(): lax.ppermute(value, axis, pairs)  8.68 us
    ppermute x2, starting transfers between devices, shift(): return lax.ppermute(value, axis, pairs)  2.61 us
  transfers between devices with their start and end apart: 28, of which 13 were waited for; matrix products, arithmetic and copies ran while one was open for 0% of the time, Pallas kernels for 18%

profile of v10, /device:TPU:16, one launch (start us, length us, event | category | flops | bytes accessed | tf_op | source)
XLA Modules:
  0.0 100.3 jit_solution(15594176172192404918)
XLA Ops:
  3.1 1.6 %collective-permute-start.12 = (bf16[2,256,128]{2,1,0:T(8,128)(2,1)S(1)}, bf16[2,256,128]{2,1,0:T(8,128)(2,1)S(1)}, u32[]{:S(2)}, u32[]{:S(2)}) collective-permute-start(bf16[2,256,128]{2,1,0:T(8,128)(2,1)S(1)} %get-tuple-element.43), channel_id=1, source_target_pairs={{0,1},{1,0},{2,3},{3,2},{4,5},{5,4},{6,7},{7,6},{8,9},{9,8},{10,11... | collective-permute-start | bytes 393224 | tf_op jit(solution)/shard_map/ppermute | solution.py:36
  4.6 2.3 %collective-permute-start.13 = (bf16[2,256,128]{2,1,0:T(8,128)(2,1)S(1)}, bf16[2,256,128]{2,1,0:T(8,128)(2,1)S(1)}, u32[]{:S(2)}, u32[]{:S(2)}) collective-permute-start(bf16[2,256,128]{2,1,0:T(8,128)(2,1)S(1)} %get-tuple-element.44), channel_id=1, source_target_pairs={{1,2},{2,1},{3,4},{4,3},{5,6},{6,5},{9,10},{10,9},{11,12},{12,11},... | collective-permute-start | bytes 393224 | tf_op jit(solution)/shard_map/ppermute | solution.py:36
  7.0 2.4 %collective-permute-done.12.even.side_even = bf16[2,256,128]{2,1,0:T(8,128)(2,1)S(1)} collective-permute-done((bf16[2,256,128]{2,1,0:T(8,128)(2,1)S(1)}, bf16[2,256,128]{2,1,0:T(8,128)(2,1)S(1)}, u32[]{:S(2)}, u32[]{:S(2)}) %collective-permute-start.12) | collective-permute-done | bytes 131104 | tf_op jit(solution)/shard_map/ppermute | solution.py:36
  9.4 4.3 %collective-permute-done.13.odd.side_odd = bf16[2,256,128]{2,1,0:T(8,128)(2,1)S(1)} collective-permute-done((bf16[2,256,128]{2,1,0:T(8,128)(2,1)S(1)}, bf16[2,256,128]{2,1,0:T(8,128)(2,1)S(1)}, u32[]{:S(2)}, u32[]{:S(2)}) %collective-permute-start.13) | collective-permute-done | bytes 131104 | tf_op jit(solution)/shard_map/ppermute | solution.py:36
  15.5 4.5 %collective-permute-done.across = f32[5,128]{1,0:T(8,128)S(1)} collective-permute-done((f32[5,128]{1,0:T(8,128)S(1)}, f32[5,128]{1,0:T(8,128)S(1)}, u32[]{:S(2)}, u32[]{:S(2)}) %collective-permute-start) | collective-permute-done | bytes 2592 | tf_op jit(solution)/shard_map/ppermute | solution.py:521
  21.5 1.9 %collective-permute-start.3 = (f32[2,5,128]{2,1,0:T(8,128)S(1)}, f32[2,5,128]{2,1,0:T(8,128)S(1)}, u32[]{:S(2)}, u32[]{:S(2)}) collective-permute-start(f32[2,5,128]{2,1,0:T(8,128)S(1)} %shard_map.105.weights.refs_0_), channel_id=1, source_target_pairs={{0,3},{1,2},{2,1},{3,0},{4,7},{5,6},{6,5},{7,4},{8,11},{9,10},{10,... | collective-permute-start | bytes 15368 | tf_op jit(solution)/shard_map/ppermute | solution.py:521
  26.1 2.8 %shard_map.107 = (bf16[4,2,32,256]{3,2,1,0:T(8,128)(2,1)S(1)}, bf16[4,2,32,256]{3,2,1,0:T(8,128)(2,1)S(1)}, bf16[4,2,32,256]{3,2,1,0:T(8,128)(2,1)S(1)}, bf16[4,...) custom-call(s32[1]{0:T(128)} %bitcast.1.row, ...), custom_call_target="tpu_custom_call" | custom-call | tf_op jit(solution)/shard_map/pallas_call | solution.py:97
  29.5 3.0 %collective-permute-start.11 = (bf16[4,2,32,256]{3,2,1,0:T(8,128)(2,1)S(1)}, bf16[4,2,32,256]{3,2,1,0:T(8,128)(2,1)S(1)}, u32[]{:S(2)}, u32[]{:S(2)}) collective-permute-start(bf16[4,2,32,256]{3,2,1,0:T(8,128)(2,1)S(1)} %get-tuple-element.41), channel_id=1, source_target_pairs={{0,6},{1,7},{2,4},{3,5},{4,2},{5,3},{6,0},{7,1},{8,14},{9,15},{10,... | collective-permute-start | bytes 393224 | tf_op jit(solution)/shard_map/ppermute | solution.py:521
  32.5 2.8 %collective-permute-start.7 = (bf16[4,2,32,256]{3,2,1,0:T(8,128)(2,1)S(1)}, bf16[4,2,32,256]{3,2,1,0:T(8,128)(2,1)S(1)}, u32[]{:S(2)}, u32[]{:S(2)}) collective-permute-start(bf16[4,2,32,256]{3,2,1,0:T(8,128)(2,1)S(1)} %get-tuple-element.37), channel_id=1, source_target_pairs={{0,2},{1,3},{2,0},{3,1},{4,6},{5,7},{6,4},{7,5},{8,10},{9,11},{10,... | collective-permute-start | bytes 393224 | tf_op jit(solution)/shard_map/ppermute | solution.py:521
  36.3 5.6 %collective-permute-done.10.refs_6_ = bf16[4,2,32,256]{3,2,1,0:T(8,128)(2,1)S(1)} collective-permute-done((bf16[4,2,32,256]{3,2,1,0:T(8,128)(2,1)S(1)}, bf16[4,2,32,256]{3,2,1,0:T(8,128)(2,1)S(1)}, u32[]{:S(2)}, u32[]{:S(2)}) %collective-permute-start.10) | collective-permute-done | bytes 131104 | tf_op jit(solution)/shard_map/ppermute | solution.py:521
  41.9 3.4 %collective-permute-done.11.refs_7_ = bf16[4,2,32,256]{3,2,1,0:T(8,128)(2,1)S(1)} collective-permute-done((bf16[4,2,32,256]{3,2,1,0:T(8,128)(2,1)S(1)}, bf16[4,2,32,256]{3,2,1,0:T(8,128)(2,1)S(1)}, u32[]{:S(2)}, u32[]{:S(2)}) %collective-permute-start.11) | collective-permute-done | bytes 131104 | tf_op jit(solution)/shard_map/ppermute | solution.py:521
  48.4 1.6 %shard_map.110.refs_8_ = bf16[4,2,256,256]{3,2,1,0:T(8,128)(2,1)S(1)} custom-call(s32[1]{0:T(128)} %bitcast.1.row, s32[1]{0:T(128)} %bitcast.me, s32[2,4]{1,0:T(2,128)} %bitcast.7, bf16[2,256,256]{2,1,0:T(8,128)(2,1)S(1)} %get-tuple-element.42.tile, bf16[2,256,128]{2,1,0:T(8,128)(2,1)S(1)} %collective-permute-done.12.even.side_even, ...), custom_call_target="tpu_custom_call" | custom-call | tf_op jit(solution)/shard_map/pallas_call | solution.py:97
  50.6 2.0 %collective-permute-done.5.refs_1_ = bf16[4,2,32,256]{3,2,1,0:T(8,128)(2,1)S(1)} collective-permute-done((bf16[4,2,32,256]{3,2,1,0:T(8,128)(2,1)S(1)}, bf16[4,2,32,256]{3,2,1,0:T(8,128)(2,1)S(1)}, u32[]{:S(2)}, u32[]{:S(2)}) %collective-permute-start.5) | collective-permute-done | bytes 131104 | tf_op jit(solution)/shard_map/ppermute | solution.py:521
  52.7 3.1 %shard_map.112 = (bf16[4,2,32,256]{3,2,1,0:T(8,128)(2,1)S(1)}, bf16[4,2,32,256]{3,2,1,0:T(8,128)(2,1)S(1)}, bf16[4,2,32,256]{3,2,1,0:T(8,128)(2,1)S(1)}, bf16[4,...) custom-call(s32[1,1]{1,0:T(1,128)S(6)} %copy.13.counts, ...), custom_call_target="tpu_custom_call" | custom-call | tf_op jit(solution)/shard_map/pallas_call | solution.py:97
  57.3 3.2 %collective-permute-start.22 = (bf16[4,2,32,256]{3,2,1,0:T(8,128)(2,1)S(1)}, bf16[4,2,32,256]{3,2,1,0:T(8,128)(2,1)S(1)}, u32[]{:S(2)}, u32[]{:S(2)}) collective-permute-start(bf16[4,2,32,256]{3,2,1,0:T(8,128)(2,1)S(1)} %get-tuple-element.59), channel_id=1, source_target_pairs={{0,2},{1,3},{2,0},{3,1},{4,6},{5,7},{6,4},{7,5},{8,10},{9,11},{10,... | collective-permute-start | bytes 393224 | tf_op jit(solution)/shard_map/ppermute | solution.py:521
  62.7 2.0 %collective-permute-start.24 = (bf16[4,2,32,256]{3,2,1,0:T(8,128)(2,1)S(1)}, bf16[4,2,32,256]{3,2,1,0:T(8,128)(2,1)S(1)}, u32[]{:S(2)}, u32[]{:S(2)}) collective-permute-start(bf16[4,2,32,256]{3,2,1,0:T(8,128)(2,1)S(1)} %get-tuple-element.61), channel_id=1, source_target_pairs={{0,5},{1,4},{2,7},{3,6},{4,1},{5,0},{6,3},{7,2},{8,13},{9,12},{10,... | collective-permute-start | bytes 393224 | tf_op jit(solution)/shard_map/ppermute | solution.py:521
  66.2 1.5 %collective-permute-start.26 = (bf16[4,2,32,256]{3,2,1,0:T(8,128)(2,1)S(1)}, bf16[4,2,32,256]{3,2,1,0:T(8,128)(2,1)S(1)}, u32[]{:S(2)}, u32[]{:S(2)}) collective-permute-start(bf16[4,2,32,256]{3,2,1,0:T(8,128)(2,1)S(1)} %get-tuple-element.63), channel_id=1, source_target_pairs={{0,6},{1,7},{2,4},{3,5},{4,2},{5,3},{6,0},{7,1},{8,14},{9,15},{10,... | collective-permute-start | bytes 393224 | tf_op jit(solution)/shard_map/ppermute | solution.py:521
  69.2 8.7 %collective-permute-done.20.refs_5_.refs_4_ = bf16[4,2,32,256]{3,2,1,0:T(8,128)(2,1)S(1)} collective-permute-done((bf16[4,2,32,256]{3,2,1,0:T(8,128)(2,1)S(1)}, bf16[4,2,32,256]{3,2,1,0:T(8,128)(2,1)S(1)}, u32[]{:S(2)}, u32[]{:S(2)}) %collective-permute-start.20) | collective-permute-done | bytes 131104 | tf_op jit(solution)/shard_map/ppermute | solution.py:521
  78.5 1.5 %shard_map.117.refs_7_ = f32[12,2,32,256]{3,2,1,0:T(8,128)S(1)} custom-call(s32[1]{0:T(128)} %bitcast.1.row, f32[2,5,128]{2,1,0:T(8,128)S(1)} %shard_map.105.weights.refs_0_, f32[2,5,128]{2,1,0:T(8,128)S(1)} %collective-permute-done.1.refs_1_, f32[2,5,128]{2,1,0:T(8,128)S(1)} %collective-permute-done.2.refs_2_, ...), custom_call_target="tpu_custom_call" | custom-call | tf_op jit(solution)/shard_map/pallas_call | solution.py:97
  80.7 4.5 %collective-permute-done.25.refs_10_.refs_6_ = bf16[4,2,32,256]{3,2,1,0:T(8,128)(2,1)S(1)} collective-permute-done((bf16[4,2,32,256]{3,2,1,0:T(8,128)(2,1)S(1)}, bf16[4,2,32,256]{3,2,1,0:T(8,128)(2,1)S(1)}, u32[]{:S(2)}, u32[]{:S(2)}) %collective-permute-start.25) | collective-permute-done | bytes 131104 | tf_op jit(solution)/shard_map/ppermute | solution.py:521
  89.1 1.5 %collective-permute-start.18 = (bf16[2,256,128]{2,1,0:T(8,128)(2,1)S(1)}, bf16[2,256,128]{2,1,0:T(8,128)(2,1)S(1)}, u32[]{:S(2)}, u32[]{:S(2)}) collective-permute-start(bf16[2,256,128]{2,1,0:T(8,128)(2,1)S(1)} %get-tuple-element.54), channel_id=1, source_target_pairs={{0,1},{1,0},{2,3},{3,2},{4,5},{5,4},{6,7},{7,6},{8,9},{9,8},{10,11... | collective-permute-start | bytes 393224 | tf_op jit(solution)/shard_map/ppermute | solution.py:36
  90.6 2.9 %collective-permute-start.19 = (bf16[2,256,128]{2,1,0:T(8,128)(2,1)S(1)}, bf16[2,256,128]{2,1,0:T(8,128)(2,1)S(1)}, u32[]{:S(2)}, u32[]{:S(2)}) collective-permute-start(bf16[2,256,128]{2,1,0:T(8,128)(2,1)S(1)} %get-tuple-element.55), channel_id=1, source_target_pairs={{1,2},{2,1},{3,4},{4,3},{5,6},{6,5},{9,10},{10,9},{11,12},{12,11},... | collective-permute-start | bytes 393224 | tf_op jit(solution)/shard_map/ppermute | solution.py:36
  93.5 2.9 %shard_map.116 = f32[12,2,32,256]{3,2,1,0:T(8,128)S(1)} custom-call(s32[1]{0:T(128)} %bitcast.1.row, f32[2,5,128]{2,1,0:T(8,128)S(1)} %shard_map.105.weights.refs_0_, f32[2,5,128]{2,1,0:T(8,128)S(1)} %collective-permute-done.1.refs_1_, f32[2,5,128]{2,1,0:T(8,128)S(1)} %collective-permute-done.2.refs_2_, f32[2,5,128]{2,1,0:T(8,128)S(1)} %collective-permute-done.3.refs_3_, ...), custom_call_target="tpu_custom_call" | custom-call | tf_op jit(solution)/shard_map/pallas_call | solution.py:97
  96.4 2.0 %collective-permute-done.19.odd = bf16[2,256,128]{2,1,0:T(8,128)(2,1)S(1)} collective-permute-done((bf16[2,256,128]{2,1,0:T(8,128)(2,1)S(1)}, bf16[2,256,128]{2,1,0:T(8,128)(2,1)S(1)}, u32[]{:S(2)}, u32[]{:S(2)}) %collective-permute-start.19) | collective-permute-done | bytes 131104 | tf_op jit(solution)/shard_map/ppermute | solution.py:36
  (53 shorter events, 26.8 us)
Async XLA Ops:
  0.6 20.9 %collective-permute-start.4 = (bf16[1,12,2,32,256]{4,3,2,1,0:T(8,128)(2,1)}, bf16[1,12,2,32,256]{4,3,2,1,0:T(8,128)(2,1)S(1)}, u32[]{:S(2)}, u32[]{:S(2)}) collective-permute-start(bf16[1,12,2,32,256]{4,3,2,1,0:T(8,128)(2,1)} %own.1), channel_id=1, source_target_pairs={{8,0},{16,8},{24,16},{9,1},{17,9},{25,17},{10,2},{18,10},{26,18},{... | collective-permute-start | bytes 1179656 | tf_op jit(solution)/shard_map/ppermute | solution.py:26
  3.1 6.3 %collective-permute-start.12 = (bf16[2,256,128]{2,1,0:T(8,128)(2,1)S(1)}, bf16[2,256,128]{2,1,0:T(8,128)(2,1)S(1)}, u32[]{:S(2)}, u32[]{:S(2)}) collective-permute-start(bf16[2,256,128]{2,1,0:T(8,128)(2,1)S(1)} %get-tuple-element.43), channel_id=1, source_target_pairs={{0,1},{1,0},{2,3},{3,2},{4,5},{5,4},{6,7},{7,6},{8,9},{9,8},{10,11... | collective-permute-start | bytes 393224 | tf_op jit(solution)/shard_map/ppermute | solution.py:36
  4.6 9.0 %collective-permute-start.13 = (bf16[2,256,128]{2,1,0:T(8,128)(2,1)S(1)}, bf16[2,256,128]{2,1,0:T(8,128)(2,1)S(1)}, u32[]{:S(2)}, u32[]{:S(2)}) collective-permute-start(bf16[2,256,128]{2,1,0:T(8,128)(2,1)S(1)} %get-tuple-element.44), channel_id=1, source_target_pairs={{1,2},{2,1},{3,4},{4,3},{5,6},{6,5},{9,10},{10,9},{11,12},{12,11},... | collective-permute-start | bytes 393224 | tf_op jit(solution)/shard_map/ppermute | solution.py:36
  13.8 18.7 %collective-permute-start.14 = (bf16[2,128,512]{2,1,0:T(8,128)(2,1)S(1)}, bf16[2,128,512]{2,1,0:T(8,128)(2,1)S(1)}, u32[]{:S(2)}, u32[]{:S(2)}) collective-permute-start(bf16[2,128,512]{2,1,0:T(8,128)(2,1)S(1)} %get-tuple-element.45), channel_id=1, source_target_pairs={{0,8},{8,0},{16,24},{24,16},{1,9},{9,1},{17,25},{25,17},{2,10},{10... | collective-permute-start | bytes 786440 | tf_op jit(solution)/shard_map/ppermute | solution.py:36
  13.8 21.5 %collective-permute-start.15 = (bf16[2,128,512]{2,1,0:T(8,128)(2,1)S(1)}, bf16[2,128,512]{2,1,0:T(8,128)(2,1)S(1)}, u32[]{:S(2)}, u32[]{:S(2)}) collective-permute-start(bf16[2,128,512]{2,1,0:T(8,128)(2,1)S(1)} %get-tuple-element.46), channel_id=1, source_target_pairs={{8,16},{16,8},{9,17},{17,9},{10,18},{18,10},{11,19},{19,11},{12,20... | collective-permute-start | bytes 786440 | tf_op jit(solution)/shard_map/ppermute | solution.py:36
  28.9 12.9 %collective-permute-start.10 = (bf16[4,2,32,256]{3,2,1,0:T(8,128)(2,1)S(1)}, bf16[4,2,32,256]{3,2,1,0:T(8,128)(2,1)S(1)}, u32[]{:S(2)}, u32[]{:S(2)}) collective-permute-start(bf16[4,2,32,256]{3,2,1,0:T(8,128)(2,1)S(1)} %get-tuple-element.40), channel_id=1, source_target_pairs={{0,7},{1,6},{2,5},{3,4},{4,3},{5,2},{6,1},{7,0},{8,15},{9,14},{10,... | collective-permute-start | bytes 393224 | tf_op jit(solution)/shard_map/ppermute | solution.py:521
  29.5 15.8 %collective-permute-start.11 = (bf16[4,2,32,256]{3,2,1,0:T(8,128)(2,1)S(1)}, bf16[4,2,32,256]{3,2,1,0:T(8,128)(2,1)S(1)}, u32[]{:S(2)}, u32[]{:S(2)}) collective-permute-start(bf16[4,2,32,256]{3,2,1,0:T(8,128)(2,1)S(1)} %get-tuple-element.41), channel_id=1, source_target_pairs={{0,6},{1,7},{2,4},{3,5},{4,2},{5,3},{6,0},{7,1},{8,14},{9,15},{10,... | collective-permute-start | bytes 393224 | tf_op jit(solution)/shard_map/ppermute | solution.py:521
  32.5 17.5 %collective-permute-start.6 = (bf16[4,2,32,256]{3,2,1,0:T(8,128)(2,1)S(1)}, bf16[4,2,32,256]{3,2,1,0:T(8,128)(2,1)S(1)}, u32[]{:S(2)}, u32[]{:S(2)}) collective-permute-start(bf16[4,2,32,256]{3,2,1,0:T(8,128)(2,1)S(1)} %get-tuple-element.36), channel_id=1, source_target_pairs={{0,1},{1,0},{2,3},{3,2},{4,5},{5,4},{6,7},{7,6},{8,9},{9,8},{10,11... | collective-permute-start | bytes 393224 | tf_op jit(solution)/shard_map/ppermute | solution.py:521
  32.5 17.5 %collective-permute-start.7 = (bf16[4,2,32,256]{3,2,1,0:T(8,128)(2,1)S(1)}, bf16[4,2,32,256]{3,2,1,0:T(8,128)(2,1)S(1)}, u32[]{:S(2)}, u32[]{:S(2)}) collective-permute-start(bf16[4,2,32,256]{3,2,1,0:T(8,128)(2,1)S(1)} %get-tuple-element.37), channel_id=1, source_target_pairs={{0,2},{1,3},{2,0},{3,1},{4,6},{5,7},{6,4},{7,5},{8,10},{9,11},{10,... | collective-permute-start | bytes 393224 | tf_op jit(solution)/shard_map/ppermute | solution.py:521
  35.3 14.7 %collective-permute-start.8 = (bf16[4,2,32,256]{3,2,1,0:T(8,128)(2,1)S(1)}, bf16[4,2,32,256]{3,2,1,0:T(8,128)(2,1)S(1)}, u32[]{:S(2)}, u32[]{:S(2)}) collective-permute-start(bf16[4,2,32,256]{3,2,1,0:T(8,128)(2,1)S(1)} %get-tuple-element.38), channel_id=1, source_target_pairs={{0,3},{1,2},{2,1},{3,0},{4,7},{5,6},{6,5},{7,4},{8,11},{9,10},{10,... | collective-permute-start | bytes 393224 | tf_op jit(solution)/shard_map/ppermute | solution.py:521
  41.9 8.8 %collective-permute-start.9 = (bf16[4,2,32,256]{3,2,1,0:T(8,128)(2,1)S(1)}, bf16[4,2,32,256]{3,2,1,0:T(8,128)(2,1)S(1)}, u32[]{:S(2)}, u32[]{:S(2)}) collective-permute-start(bf16[4,2,32,256]{3,2,1,0:T(8,128)(2,1)S(1)} %get-tuple-element.39), channel_id=1, source_target_pairs={{0,5},{1,4},{2,7},{3,6},{4,1},{5,0},{6,3},{7,2},{8,13},{9,12},{10,... | collective-permute-start | bytes 393224 | tf_op jit(solution)/shard_map/ppermute | solution.py:521
  45.2 7.4 %collective-permute-start.5 = (bf16[4,2,32,256]{3,2,1,0:T(8,128)(2,1)S(1)}, bf16[4,2,32,256]{3,2,1,0:T(8,128)(2,1)S(1)}, u32[]{:S(2)}, u32[]{:S(2)}) collective-permute-start(bf16[4,2,32,256]{3,2,1,0:T(8,128)(2,1)S(1)} %get-tuple-element.35), channel_id=1, source_target_pairs={{0,4},{1,5},{2,6},{3,7},{4,0},{5,1},{6,2},{7,3},{8,12},{9,13},{10,... | collective-permute-start | bytes 393224 | tf_op jit(solution)/shard_map/ppermute | solution.py:521
  55.8 8.9 %collective-permute-start.21 = (bf16[4,2,32,256]{3,2,1,0:T(8,128)(2,1)S(1)}, bf16[4,2,32,256]{3,2,1,0:T(8,128)(2,1)S(1)}, u32[]{:S(2)}, u32[]{:S(2)}) collective-permute-start(bf16[4,2,32,256]{3,2,1,0:T(8,128)(2,1)S(1)} %get-tuple-element.58), channel_id=1, source_target_pairs={{0,1},{1,0},{2,3},{3,2},{4,5},{5,4},{6,7},{7,6},{8,9},{9,8},{10,11... | collective-permute-start | bytes 393224 | tf_op jit(solution)/shard_map/ppermute | solution.py:521
  57.3 8.9 %collective-permute-start.22 = (bf16[4,2,32,256]{3,2,1,0:T(8,128)(2,1)S(1)}, bf16[4,2,32,256]{3,2,1,0:T(8,128)(2,1)S(1)}, u32[]{:S(2)}, u32[]{:S(2)}) collective-permute-start(bf16[4,2,32,256]{3,2,1,0:T(8,128)(2,1)S(1)} %get-tuple-element.59), channel_id=1, source_target_pairs={{0,2},{1,3},{2,0},{3,1},{4,6},{5,7},{6,4},{7,5},{8,10},{9,11},{10,... | collective-permute-start | bytes 393224 | tf_op jit(solution)/shard_map/ppermute | solution.py:521
  60.5 8.6 %collective-permute-start.23 = (bf16[4,2,32,256]{3,2,1,0:T(8,128)(2,1)S(1)}, bf16[4,2,32,256]{3,2,1,0:T(8,128)(2,1)S(1)}, u32[]{:S(2)}, u32[]{:S(2)}) collective-permute-start(bf16[4,2,32,256]{3,2,1,0:T(8,128)(2,1)S(1)} %get-tuple-element.60), channel_id=1, source_target_pairs={{0,3},{1,2},{2,1},{3,0},{4,7},{5,6},{6,5},{7,4},{8,11},{9,10},{10,... | collective-permute-start | bytes 393224 | tf_op jit(solution)/shard_map/ppermute | solution.py:521
  61.8 16.1 %collective-permute-start.20 = (bf16[4,2,32,256]{3,2,1,0:T(8,128)(2,1)S(1)}, bf16[4,2,32,256]{3,2,1,0:T(8,128)(2,1)S(1)}, u32[]{:S(2)}, u32[]{:S(2)}) collective-permute-start(bf16[4,2,32,256]{3,2,1,0:T(8,128)(2,1)S(1)} %get-tuple-element.57), channel_id=1, source_target_pairs={{0,4},{1,5},{2,6},{3,7},{4,0},{5,1},{6,2},{7,3},{8,12},{9,13},{10,... | collective-permute-start | bytes 393224 | tf_op jit(solution)/shard_map/ppermute | solution.py:521
  62.7 17.9 %collective-permute-start.24 = (bf16[4,2,32,256]{3,2,1,0:T(8,128)(2,1)S(1)}, bf16[4,2,32,256]{3,2,1,0:T(8,128)(2,1)S(1)}, u32[]{:S(2)}, u32[]{:S(2)}) collective-permute-start(bf16[4,2,32,256]{3,2,1,0:T(8,128)(2,1)S(1)} %get-tuple-element.61), channel_id=1, source_target_pairs={{0,5},{1,4},{2,7},{3,6},{4,1},{5,0},{6,3},{7,2},{8,13},{9,12},{10,... | collective-permute-start | bytes 393224 | tf_op jit(solution)/shard_map/ppermute | solution.py:521
  64.7 20.4 %collective-permute-start.25 = (bf16[4,2,32,256]{3,2,1,0:T(8,128)(2,1)S(1)}, bf16[4,2,32,256]{3,2,1,0:T(8,128)(2,1)S(1)}, u32[]{:S(2)}, u32[]{:S(2)}) collective-permute-start(bf16[4,2,32,256]{3,2,1,0:T(8,128)(2,1)S(1)} %get-tuple-element.62), channel_id=1, source_target_pairs={{0,7},{1,6},{2,5},{3,4},{4,3},{5,2},{6,1},{7,0},{8,15},{9,14},{10,... | collective-permute-start | bytes 393224 | tf_op jit(solution)/shard_map/ppermute | solution.py:521
  66.2 20.6 %collective-permute-start.26 = (bf16[4,2,32,256]{3,2,1,0:T(8,128)(2,1)S(1)}, bf16[4,2,32,256]{3,2,1,0:T(8,128)(2,1)S(1)}, u32[]{:S(2)}, u32[]{:S(2)}) collective-permute-start(bf16[4,2,32,256]{3,2,1,0:T(8,128)(2,1)S(1)} %get-tuple-element.63), channel_id=1, source_target_pairs={{0,6},{1,7},{2,4},{3,5},{4,2},{5,3},{6,0},{7,1},{8,14},{9,15},{10,... | collective-permute-start | bytes 393224 | tf_op jit(solution)/shard_map/ppermute | solution.py:521
  69.1 19.8 %collective-permute-start.16 = (bf16[2,128,512]{2,1,0:T(8,128)(2,1)S(1)}, bf16[2,128,512]{2,1,0:T(8,128)(2,1)S(1)}, u32[]{:S(2)}, u32[]{:S(2)}) collective-permute-start(bf16[2,128,512]{2,1,0:T(8,128)(2,1)S(1)} %get-tuple-element.51), channel_id=1, source_target_pairs={{0,8},{8,0},{16,24},{24,16},{1,9},{9,1},{17,25},{25,17},{2,10},{10... | collective-permute-start | bytes 786440 | tf_op jit(solution)/shard_map/ppermute | solution.py:36
  77.9 11.1 %collective-permute-start.17 = (bf16[2,128,512]{2,1,0:T(8,128)(2,1)S(1)}, bf16[2,128,512]{2,1,0:T(8,128)(2,1)S(1)}, u32[]{:S(2)}, u32[]{:S(2)}) collective-permute-start(bf16[2,128,512]{2,1,0:T(8,128)(2,1)S(1)} %get-tuple-element.52), channel_id=1, source_target_pairs={{8,16},{16,8},{9,17},{17,9},{10,18},{18,10},{11,19},{19,11},{12,20... | collective-permute-start | bytes 786440 | tf_op jit(solution)/shard_map/ppermute | solution.py:36
  87.6 11.7 %collective-permute-start.27 = (bf16[12,2,32,256]{3,2,1,0:T(8,128)(2,1)S(1)}, bf16[12,2,32,256]{3,2,1,0:T(8,128)(2,1)S(1)}, u32[]{:S(2)}, u32[]{:S(2)}) collective-permute-start(bf16[12,2,32,256]{3,2,1,0:T(8,128)(2,1)S(1)} %shard_map.119), channel_id=1, source_target_pairs={{0,8},{8,16},{16,24},{1,9},{9,17},{17,25},{2,10},{10,18},{18,26},{... | collective-permute-start | bytes 1179656 | tf_op jit(solution)/shard_map/ppermute | solution.py:26
  89.1 7.2 %collective-permute-start.18 = (bf16[2,256,128]{2,1,0:T(8,128)(2,1)S(1)}, bf16[2,256,128]{2,1,0:T(8,128)(2,1)S(1)}, u32[]{:S(2)}, u32[]{:S(2)}) collective-permute-start(bf16[2,256,128]{2,1,0:T(8,128)(2,1)S(1)} %get-tuple-element.54), channel_id=1, source_target_pairs={{0,1},{1,0},{2,3},{3,2},{4,5},{5,4},{6,7},{7,6},{8,9},{9,8},{10,11... | collective-permute-start | bytes 393224 | tf_op jit(solution)/shard_map/ppermute | solution.py:36
  90.6 7.7 %collective-permute-start.19 = (bf16[2,256,128]{2,1,0:T(8,128)(2,1)S(1)}, bf16[2,256,128]{2,1,0:T(8,128)(2,1)S(1)}, u32[]{:S(2)}, u32[]{:S(2)}) collective-permute-start(bf16[2,256,128]{2,1,0:T(8,128)(2,1)S(1)} %get-tuple-element.55), channel_id=1, source_target_pairs={{1,2},{2,1},{3,4},{4,3},{5,6},{6,5},{9,10},{10,9},{11,12},{12,11},... | collective-permute-start | bytes 393224 | tf_op jit(solution)/shard_map/ppermute | solution.py:36
  (6 other events, 96.2 us)

commit v11 on v10

--- a/solution.py
+++ b/solution.py
@@ -61,8 +61,7 @@
 
 def transfer_order(count):
     half = count // 2
-    far = list(range(half + 1, count))
-    return [half] * (half > 0) + list(range(1, half)) + far[:-2] + far[:-3:-1]
+    return [half] * (half > 0) + list(range(1, half)) + list(range(half + 1, count))
 
 
 def slab_order(count, paired):
@@ -515,7 +514,7 @@
     count = lax.axis_size("col")
     middle_step = count // 2
     near = list(range(1, middle_step))
-    crossing = [step for step in steps if step >= middle_step]
+    crossing = list(range(max(middle_step, 1), count))
 
     def move(value, step):
         return lax.ppermute(value, "col", [(i, goes_to(i, step)) for i in range(count)])

time: 101 us -> 101 us (level)
  the two profiles are of different devices: /device:TPU:16 before, /device:TPU:8 now
where the time goes in v11:
time: 101 us
  starting transfers between devices  40.4 us (40%)
  waiting for transfers between devices  36.7 us (36%)
  Pallas kernels  21.3 us (21%)
  between operations  1.55 us (2%)
    ppermute x18, starting transfers between devices, move(): lax.ppermute(value, 'col', [(i, goes_to(i, step)) for i in range(count)])  29.6 us
    ppermute x18, waiting for transfers between devices, move(): lax.ppermute(value, 'col', [(i, goes_to(i, step)) for i in range(count)])  26.6 us
    pallas_call x16, Pallas kernels, call(): pl.pallas_call(body, out_shape=tuple(outs), in_specs=specs, out_specs=tup...  21.3 us
    ppermute x8, waiting for transfers between devices, swap(): lax.ppermute(value, axis, pairs)  10 us
    ppermute x8, starting transfers between devices, swap(): lax.ppermute(value, axis, pairs)  8.17 us
    ppermute x2, starting transfers between devices, shift(): return lax.ppermute(value, axis, pairs)  2.61 us
  transfers between devices with their start and end apart: 28, of which 14 were waited for; matrix products, arithmetic and copies ran while one was open for 0% of the time, Pallas kernels for 18%

profile of v11, /device:TPU:8, one launch (start us, length us, event | category | flops | bytes accessed | tf_op | source)
XLA Modules:
  0.0 100.9 jit_solution(18147992468551058510)
XLA Ops:
  3.1 1.6 %collective-permute-start.12 = (bf16[2,256,128]{2,1,0:T(8,128)(2,1)S(1)}, bf16[2,256,128]{2,1,0:T(8,128)(2,1)S(1)}, u32[]{:S(2)}, u32[]{:S(2)}) collective-permute-start(bf16[2,256,128]{2,1,0:T(8,128)(2,1)S(1)} %get-tuple-element.43), channel_id=1, source_target_pairs={{0,1},{1,0},{2,3},{3,2},{4,5},{5,4},{6,7},{7,6},{8,9},{9,8},{10,11... | collective-permute-start | bytes 393224 | tf_op jit(solution)/shard_map/ppermute | solution.py:36
  4.6 1.9 %collective-permute-start.13 = (bf16[2,256,128]{2,1,0:T(8,128)(2,1)S(1)}, bf16[2,256,128]{2,1,0:T(8,128)(2,1)S(1)}, u32[]{:S(2)}, u32[]{:S(2)}) collective-permute-start(bf16[2,256,128]{2,1,0:T(8,128)(2,1)S(1)} %get-tuple-element.44), channel_id=1, source_target_pairs={{1,2},{2,1},{3,4},{4,3},{5,6},{6,5},{9,10},{10,9},{11,12},{12,11},... | collective-permute-start | bytes 393224 | tf_op jit(solution)/shard_map/ppermute | solution.py:36
  6.5 2.8 %collective-permute-done.12.even.side_even = bf16[2,256,128]{2,1,0:T(8,128)(2,1)S(1)} collective-permute-done((bf16[2,256,128]{2,1,0:T(8,128)(2,1)S(1)}, bf16[2,256,128]{2,1,0:T(8,128)(2,1)S(1)}, u32[]{:S(2)}, u32[]{:S(2)}) %collective-permute-start.12) | collective-permute-done | bytes 131104 | tf_op jit(solution)/shard_map/ppermute | solution.py:36
  9.4 4.3 %collective-permute-done.13.odd.side_odd = bf16[2,256,128]{2,1,0:T(8,128)(2,1)S(1)} collective-permute-done((bf16[2,256,128]{2,1,0:T(8,128)(2,1)S(1)}, bf16[2,256,128]{2,1,0:T(8,128)(2,1)S(1)}, u32[]{:S(2)}, u32[]{:S(2)}) %collective-permute-start.13) | collective-permute-done | bytes 131104 | tf_op jit(solution)/shard_map/ppermute | solution.py:36
  15.4 2.7 %collective-permute-start = (f32[5,128]{1,0:T(8,128)S(1)}, f32[5,128]{1,0:T(8,128)S(1)}, u32[]{:S(2)}, u32[]{:S(2)}) collective-permute-start(f32[5,128]{1,0:T(8,128)S(1)} %shard_map.104.mine), channel_id=1, source_target_pairs={{0,4},{1,5},{2,6},{3,7},{4,0},{5,1},{6,2},{7,3},{8,12},{9,13},{10,... | collective-permute-start | bytes 7688 | tf_op jit(solution)/shard_map/ppermute | solution.py:520
  18.0 1.9 %collective-permute-done.across = f32[5,128]{1,0:T(8,128)S(1)} collective-permute-done((f32[5,128]{1,0:T(8,128)S(1)}, f32[5,128]{1,0:T(8,128)S(1)}, u32[]{:S(2)}, u32[]{:S(2)}) %collective-permute-start) | collective-permute-done | bytes 2592 | tf_op jit(solution)/shard_map/ppermute | solution.py:520
  20.6 2.8 %collective-permute-start.3 = (f32[2,5,128]{2,1,0:T(8,128)S(1)}, f32[2,5,128]{2,1,0:T(8,128)S(1)}, u32[]{:S(2)}, u32[]{:S(2)}) collective-permute-start(f32[2,5,128]{2,1,0:T(8,128)S(1)} %shard_map.105.weights.refs_0_), channel_id=1, source_target_pairs={{0,3},{1,2},{2,1},{3,0},{4,7},{5,6},{6,5},{7,4},{8,11},{9,10},{10,... | collective-permute-start | bytes 15368 | tf_op jit(solution)/shard_map/ppermute | solution.py:520
  25.2 2.8 %shard_map.107 = (bf16[4,2,32,256]{3,2,1,0:T(8,128)(2,1)S(1)}, bf16[4,2,32,256]{3,2,1,0:T(8,128)(2,1)S(1)}, bf16[4,2,32,256]{3,2,1,0:T(8,128)(2,1)S(1)}, bf16[4,...) custom-call(s32[1]{0:T(128)} %bitcast.1.row, ...), custom_call_target="tpu_custom_call" | custom-call | tf_op jit(solution)/shard_map/pallas_call | solution.py:96
  28.0 2.6 %collective-permute-start.10 = (bf16[4,2,32,256]{3,2,1,0:T(8,128)(2,1)S(1)}, bf16[4,2,32,256]{3,2,1,0:T(8,128)(2,1)S(1)}, u32[]{:S(2)}, u32[]{:S(2)}) collective-permute-start(bf16[4,2,32,256]{3,2,1,0:T(8,128)(2,1)S(1)} %get-tuple-element.40), channel_id=1, source_target_pairs={{0,6},{1,7},{2,4},{3,5},{4,2},{5,3},{6,0},{7,1},{8,14},{9,15},{10,... | collective-permute-start | bytes 393224 | tf_op jit(solution)/shard_map/ppermute | solution.py:520
  32.6 2.7 %collective-permute-start.7 = (bf16[4,2,32,256]{3,2,1,0:T(8,128)(2,1)S(1)}, bf16[4,2,32,256]{3,2,1,0:T(8,128)(2,1)S(1)}, u32[]{:S(2)}, u32[]{:S(2)}) collective-permute-start(bf16[4,2,32,256]{3,2,1,0:T(8,128)(2,1)S(1)} %get-tuple-element.37), channel_id=1, source_target_pairs={{0,2},{1,3},{2,0},{3,1},{4,6},{5,7},{6,4},{7,5},{8,10},{9,11},{10,... | collective-permute-start | bytes 393224 | tf_op jit(solution)/shard_map/ppermute | solution.py:520
  36.3 4.3 %collective-permute-done.10.refs_6_ = bf16[4,2,32,256]{3,2,1,0:T(8,128)(2,1)S(1)} collective-permute-done((bf16[4,2,32,256]{3,2,1,0:T(8,128)(2,1)S(1)}, bf16[4,2,32,256]{3,2,1,0:T(8,128)(2,1)S(1)}, u32[]{:S(2)}, u32[]{:S(2)}) %collective-permute-start.10) | collective-permute-done | bytes 131104 | tf_op jit(solution)/shard_map/ppermute | solution.py:520
  40.5 5.5 %collective-permute-done.11.refs_7_ = bf16[4,2,32,256]{3,2,1,0:T(8,128)(2,1)S(1)} collective-permute-done((bf16[4,2,32,256]{3,2,1,0:T(8,128)(2,1)S(1)}, bf16[4,2,32,256]{3,2,1,0:T(8,128)(2,1)S(1)}, u32[]{:S(2)}, u32[]{:S(2)}) %collective-permute-start.11) | collective-permute-done | bytes 131104 | tf_op jit(solution)/shard_map/ppermute | solution.py:520
  48.0 1.6 %shard_map.110.refs_8_ = bf16[4,2,256,256]{3,2,1,0:T(8,128)(2,1)S(1)} custom-call(s32[1]{0:T(128)} %bitcast.1.row, s32[1]{0:T(128)} %bitcast.me, s32[2,4]{1,0:T(2,128)} %bitcast.7, bf16[2,256,256]{2,1,0:T(8,128)(2,1)S(1)} %get-tuple-element.42.tile, bf16[2,256,128]{2,1,0:T(8,128)(2,1)S(1)} %collective-permute-done.12.even.side_even, ...), custom_call_target="tpu_custom_call" | custom-call | tf_op jit(solution)/shard_map/pallas_call | solution.py:96
  50.2 2.1 %collective-permute-done.5.refs_1_ = bf16[4,2,32,256]{3,2,1,0:T(8,128)(2,1)S(1)} collective-permute-done((bf16[4,2,32,256]{3,2,1,0:T(8,128)(2,1)S(1)}, bf16[4,2,32,256]{3,2,1,0:T(8,128)(2,1)S(1)}, u32[]{:S(2)}, u32[]{:S(2)}) %collective-permute-start.5) | collective-permute-done | bytes 131104 | tf_op jit(solution)/shard_map/ppermute | solution.py:520
  52.3 3.1 %shard_map.112 = (bf16[4,2,32,256]{3,2,1,0:T(8,128)(2,1)S(1)}, bf16[4,2,32,256]{3,2,1,0:T(8,128)(2,1)S(1)}, bf16[4,2,32,256]{3,2,1,0:T(8,128)(2,1)S(1)}, bf16[4,...) custom-call(s32[1,1]{1,0:T(1,128)S(6)} %copy.13.counts, ...), custom_call_target="tpu_custom_call" | custom-call | tf_op jit(solution)/shard_map/pallas_call | solution.py:96
  55.4 5.4 %collective-permute-start.21 = (bf16[4,2,32,256]{3,2,1,0:T(8,128)(2,1)S(1)}, bf16[4,2,32,256]{3,2,1,0:T(8,128)(2,1)S(1)}, u32[]{:S(2)}, u32[]{:S(2)}) collective-permute-start(bf16[4,2,32,256]{3,2,1,0:T(8,128)(2,1)S(1)} %get-tuple-element.58), channel_id=1, source_target_pairs={{0,1},{1,0},{2,3},{3,2},{4,5},{5,4},{6,7},{7,6},{8,9},{9,8},{10,11... | collective-permute-start | bytes 393224 | tf_op jit(solution)/shard_map/ppermute | solution.py:520
  63.6 2.2 %collective-permute-start.20 = (bf16[4,2,32,256]{3,2,1,0:T(8,128)(2,1)S(1)}, bf16[4,2,32,256]{3,2,1,0:T(8,128)(2,1)S(1)}, u32[]{:S(2)}, u32[]{:S(2)}) collective-permute-start(bf16[4,2,32,256]{3,2,1,0:T(8,128)(2,1)S(1)} %get-tuple-element.57), channel_id=1, source_target_pairs={{0,4},{1,5},{2,6},{3,7},{4,0},{5,1},{6,2},{7,3},{8,12},{9,13},{10,... | collective-permute-start | bytes 393224 | tf_op jit(solution)/shard_map/ppermute | solution.py:520
  66.6 2.2 %collective-permute-start.25 = (bf16[4,2,32,256]{3,2,1,0:T(8,128)(2,1)S(1)}, bf16[4,2,32,256]{3,2,1,0:T(8,128)(2,1)S(1)}, u32[]{:S(2)}, u32[]{:S(2)}) collective-permute-start(bf16[4,2,32,256]{3,2,1,0:T(8,128)(2,1)S(1)} %get-tuple-element.62), channel_id=1, source_target_pairs={{0,6},{1,7},{2,4},{3,5},{4,2},{5,3},{6,0},{7,1},{8,14},{9,15},{10,... | collective-permute-start | bytes 393224 | tf_op jit(solution)/shard_map/ppermute | solution.py:520
  68.8 1.9 %collective-permute-start.26 = (bf16[4,2,32,256]{3,2,1,0:T(8,128)(2,1)S(1)}, bf16[4,2,32,256]{3,2,1,0:T(8,128)(2,1)S(1)}, u32[]{:S(2)}, u32[]{:S(2)}) collective-permute-start(bf16[4,2,32,256]{3,2,1,0:T(8,128)(2,1)S(1)} %get-tuple-element.63), channel_id=1, source_target_pairs={{0,7},{1,6},{2,5},{3,4},{4,3},{5,2},{6,1},{7,0},{8,15},{9,14},{10,... | collective-permute-start | bytes 393224 | tf_op jit(solution)/shard_map/ppermute | solution.py:520
  72.2 6.9 %collective-permute-done.20.refs_5_.refs_4_ = bf16[4,2,32,256]{3,2,1,0:T(8,128)(2,1)S(1)} collective-permute-done((bf16[4,2,32,256]{3,2,1,0:T(8,128)(2,1)S(1)}, bf16[4,2,32,256]{3,2,1,0:T(8,128)(2,1)S(1)}, u32[]{:S(2)}, u32[]{:S(2)}) %collective-permute-start.20) | collective-permute-done | bytes 131104 | tf_op jit(solution)/shard_map/ppermute | solution.py:520
  82.0 4.0 %collective-permute-done.25.refs_10_.refs_6_ = bf16[4,2,32,256]{3,2,1,0:T(8,128)(2,1)S(1)} collective-permute-done((bf16[4,2,32,256]{3,2,1,0:T(8,128)(2,1)S(1)}, bf16[4,2,32,256]{3,2,1,0:T(8,128)(2,1)S(1)}, u32[]{:S(2)}, u32[]{:S(2)}) %collective-permute-start.25) | collective-permute-done | bytes 131104 | tf_op jit(solution)/shard_map/ppermute | solution.py:520
  91.2 1.9 %collective-permute-start.19 = (bf16[2,256,128]{2,1,0:T(8,128)(2,1)S(1)}, bf16[2,256,128]{2,1,0:T(8,128)(2,1)S(1)}, u32[]{:S(2)}, u32[]{:S(2)}) collective-permute-start(bf16[2,256,128]{2,1,0:T(8,128)(2,1)S(1)} %get-tuple-element.55), channel_id=1, source_target_pairs={{1,2},{2,1},{3,4},{4,3},{5,6},{6,5},{9,10},{10,9},{11,12},{12,11},... | collective-permute-start | bytes 393224 | tf_op jit(solution)/shard_map/ppermute | solution.py:36
  93.2 2.9 %shard_map.116 = f32[12,2,32,256]{3,2,1,0:T(8,128)S(1)} custom-call(s32[1]{0:T(128)} %bitcast.1.row, f32[2,5,128]{2,1,0:T(8,128)S(1)} %shard_map.105.weights.refs_0_, f32[2,5,128]{2,1,0:T(8,128)S(1)} %collective-permute-done.1.refs_1_, f32[2,5,128]{2,1,0:T(8,128)S(1)} %collective-permute-done.2.refs_2_, f32[2,5,128]{2,1,0:T(8,128)S(1)} %collective-permute-done.3.refs_3_, ...), custom_call_target="tpu_custom_call" | custom-call | tf_op jit(solution)/shard_map/pallas_call | solution.py:96
  96.5 2.5 %collective-permute-done.19.odd = bf16[2,256,128]{2,1,0:T(8,128)(2,1)S(1)} collective-permute-done((bf16[2,256,128]{2,1,0:T(8,128)(2,1)S(1)}, bf16[2,256,128]{2,1,0:T(8,128)(2,1)S(1)}, u32[]{:S(2)}, u32[]{:S(2)}) %collective-permute-start.19) | collective-permute-done | bytes 131104 | tf_op jit(solution)/shard_map/ppermute | solution.py:36
  (53 shorter events, 26.9 us)
Async XLA Ops:
  0.6 20.0 %collective-permute-start.4 = (bf16[1,12,2,32,256]{4,3,2,1,0:T(8,128)(2,1)}, bf16[1,12,2,32,256]{4,3,2,1,0:T(8,128)(2,1)S(1)}, u32[]{:S(2)}, u32[]{:S(2)}) collective-permute-start(bf16[1,12,2,32,256]{4,3,2,1,0:T(8,128)(2,1)} %own.1), channel_id=1, source_target_pairs={{8,0},{16,8},{24,16},{9,1},{17,9},{25,17},{10,2},{18,10},{26,18},{... | collective-permute-start | bytes 1179656 | tf_op jit(solution)/shard_map/ppermute | solution.py:26
  3.1 6.3 %collective-permute-start.12 = (bf16[2,256,128]{2,1,0:T(8,128)(2,1)S(1)}, bf16[2,256,128]{2,1,0:T(8,128)(2,1)S(1)}, u32[]{:S(2)}, u32[]{:S(2)}) collective-permute-start(bf16[2,256,128]{2,1,0:T(8,128)(2,1)S(1)} %get-tuple-element.43), channel_id=1, source_target_pairs={{0,1},{1,0},{2,3},{3,2},{4,5},{5,4},{6,7},{7,6},{8,9},{9,8},{10,11... | collective-permute-start | bytes 393224 | tf_op jit(solution)/shard_map/ppermute | solution.py:36
  4.6 9.0 %collective-permute-start.13 = (bf16[2,256,128]{2,1,0:T(8,128)(2,1)S(1)}, bf16[2,256,128]{2,1,0:T(8,128)(2,1)S(1)}, u32[]{:S(2)}, u32[]{:S(2)}) collective-permute-start(bf16[2,256,128]{2,1,0:T(8,128)(2,1)S(1)} %get-tuple-element.44), channel_id=1, source_target_pairs={{1,2},{2,1},{3,4},{4,3},{5,6},{6,5},{9,10},{10,9},{11,12},{12,11},... | collective-permute-start | bytes 393224 | tf_op jit(solution)/shard_map/ppermute | solution.py:36
  13.8 18.8 %collective-permute-start.14 = (bf16[2,128,512]{2,1,0:T(8,128)(2,1)S(1)}, bf16[2,128,512]{2,1,0:T(8,128)(2,1)S(1)}, u32[]{:S(2)}, u32[]{:S(2)}) collective-permute-start(bf16[2,128,512]{2,1,0:T(8,128)(2,1)S(1)} %get-tuple-element.45), channel_id=1, source_target_pairs={{0,8},{8,0},{16,24},{24,16},{1,9},{9,1},{17,25},{25,17},{2,10},{10... | collective-permute-start | bytes 786440 | tf_op jit(solution)/shard_map/ppermute | solution.py:36
  13.8 21.4 %collective-permute-start.15 = (bf16[2,128,512]{2,1,0:T(8,128)(2,1)S(1)}, bf16[2,128,512]{2,1,0:T(8,128)(2,1)S(1)}, u32[]{:S(2)}, u32[]{:S(2)}) collective-permute-start(bf16[2,128,512]{2,1,0:T(8,128)(2,1)S(1)} %get-tuple-element.46), channel_id=1, source_target_pairs={{8,16},{16,8},{9,17},{17,9},{10,18},{18,10},{11,19},{19,11},{12,20... | collective-permute-start | bytes 786440 | tf_op jit(solution)/shard_map/ppermute | solution.py:36
  28.0 12.5 %collective-permute-start.10 = (bf16[4,2,32,256]{3,2,1,0:T(8,128)(2,1)S(1)}, bf16[4,2,32,256]{3,2,1,0:T(8,128)(2,1)S(1)}, u32[]{:S(2)}, u32[]{:S(2)}) collective-permute-start(bf16[4,2,32,256]{3,2,1,0:T(8,128)(2,1)S(1)} %get-tuple-element.40), channel_id=1, source_target_pairs={{0,6},{1,7},{2,4},{3,5},{4,2},{5,3},{6,0},{7,1},{8,14},{9,15},{10,... | collective-permute-start | bytes 393224 | tf_op jit(solution)/shard_map/ppermute | solution.py:520
  30.6 15.4 %collective-permute-start.11 = (bf16[4,2,32,256]{3,2,1,0:T(8,128)(2,1)S(1)}, bf16[4,2,32,256]{3,2,1,0:T(8,128)(2,1)S(1)}, u32[]{:S(2)}, u32[]{:S(2)}) collective-permute-start(bf16[4,2,32,256]{3,2,1,0:T(8,128)(2,1)S(1)} %get-tuple-element.41), channel_id=1, source_target_pairs={{0,7},{1,6},{2,5},{3,4},{4,3},{5,2},{6,1},{7,0},{8,15},{9,14},{10,... | collective-permute-start | bytes 393224 | tf_op jit(solution)/shard_map/ppermute | solution.py:520
  32.1 17.5 %collective-permute-start.6 = (bf16[4,2,32,256]{3,2,1,0:T(8,128)(2,1)S(1)}, bf16[4,2,32,256]{3,2,1,0:T(8,128)(2,1)S(1)}, u32[]{:S(2)}, u32[]{:S(2)}) collective-permute-start(bf16[4,2,32,256]{3,2,1,0:T(8,128)(2,1)S(1)} %get-tuple-element.36), channel_id=1, source_target_pairs={{0,1},{1,0},{2,3},{3,2},{4,5},{5,4},{6,7},{7,6},{8,9},{9,8},{10,11... | collective-permute-start | bytes 393224 | tf_op jit(solution)/shard_map/ppermute | solution.py:520
  32.6 17.0 %collective-permute-start.7 = (bf16[4,2,32,256]{3,2,1,0:T(8,128)(2,1)S(1)}, bf16[4,2,32,256]{3,2,1,0:T(8,128)(2,1)S(1)}, u32[]{:S(2)}, u32[]{:S(2)}) collective-permute-start(bf16[4,2,32,256]{3,2,1,0:T(8,128)(2,1)S(1)} %get-tuple-element.37), channel_id=1, source_target_pairs={{0,2},{1,3},{2,0},{3,1},{4,6},{5,7},{6,4},{7,5},{8,10},{9,11},{10,... | collective-permute-start | bytes 393224 | tf_op jit(solution)/shard_map/ppermute | solution.py:520
  35.3 14.4 %collective-permute-start.8 = (bf16[4,2,32,256]{3,2,1,0:T(8,128)(2,1)S(1)}, bf16[4,2,32,256]{3,2,1,0:T(8,128)(2,1)S(1)}, u32[]{:S(2)}, u32[]{:S(2)}) collective-permute-start(bf16[4,2,32,256]{3,2,1,0:T(8,128)(2,1)S(1)} %get-tuple-element.38), channel_id=1, source_target_pairs={{0,3},{1,2},{2,1},{3,0},{4,7},{5,6},{6,5},{7,4},{8,11},{9,10},{10,... | collective-permute-start | bytes 393224 | tf_op jit(solution)/shard_map/ppermute | solution.py:520
  40.5 9.7 %collective-permute-start.9 = (bf16[4,2,32,256]{3,2,1,0:T(8,128)(2,1)S(1)}, bf16[4,2,32,256]{3,2,1,0:T(8,128)(2,1)S(1)}, u32[]{:S(2)}, u32[]{:S(2)}) collective-permute-start(bf16[4,2,32,256]{3,2,1,0:T(8,128)(2,1)S(1)} %get-tuple-element.39), channel_id=1, source_target_pairs={{0,5},{1,4},{2,7},{3,6},{4,1},{5,0},{6,3},{7,2},{8,13},{9,12},{10,... | collective-permute-start | bytes 393224 | tf_op jit(solution)/shard_map/ppermute | solution.py:520
  46.0 6.2 %collective-permute-start.5 = (bf16[4,2,32,256]{3,2,1,0:T(8,128)(2,1)S(1)}, bf16[4,2,32,256]{3,2,1,0:T(8,128)(2,1)S(1)}, u32[]{:S(2)}, u32[]{:S(2)}) collective-permute-start(bf16[4,2,32,256]{3,2,1,0:T(8,128)(2,1)S(1)} %get-tuple-element.35), channel_id=1, source_target_pairs={{0,4},{1,5},{2,6},{3,7},{4,0},{5,1},{6,2},{7,3},{8,12},{9,13},{10,... | collective-permute-start | bytes 393224 | tf_op jit(solution)/shard_map/ppermute | solution.py:520
  55.4 11.2 %collective-permute-start.21 = (bf16[4,2,32,256]{3,2,1,0:T(8,128)(2,1)S(1)}, bf16[4,2,32,256]{3,2,1,0:T(8,128)(2,1)S(1)}, u32[]{:S(2)}, u32[]{:S(2)}) collective-permute-start(bf16[4,2,32,256]{3,2,1,0:T(8,128)(2,1)S(1)} %get-tuple-element.58), channel_id=1, source_target_pairs={{0,1},{1,0},{2,3},{3,2},{4,5},{5,4},{6,7},{7,6},{8,9},{9,8},{10,11... | collective-permute-start | bytes 393224 | tf_op jit(solution)/shard_map/ppermute | solution.py:520
  60.8 8.0 %collective-permute-start.22 = (bf16[4,2,32,256]{3,2,1,0:T(8,128)(2,1)S(1)}, bf16[4,2,32,256]{3,2,1,0:T(8,128)(2,1)S(1)}, u32[]{:S(2)}, u32[]{:S(2)}) collective-permute-start(bf16[4,2,32,256]{3,2,1,0:T(8,128)(2,1)S(1)} %get-tuple-element.59), channel_id=1, source_target_pairs={{0,2},{1,3},{2,0},{3,1},{4,6},{5,7},{6,4},{7,5},{8,10},{9,11},{10,... | collective-permute-start | bytes 393224 | tf_op jit(solution)/shard_map/ppermute | solution.py:520
  62.2 9.9 %collective-permute-start.23 = (bf16[4,2,32,256]{3,2,1,0:T(8,128)(2,1)S(1)}, bf16[4,2,32,256]{3,2,1,0:T(8,128)(2,1)S(1)}, u32[]{:S(2)}, u32[]{:S(2)}) collective-permute-start(bf16[4,2,32,256]{3,2,1,0:T(8,128)(2,1)S(1)} %get-tuple-element.60), channel_id=1, source_target_pairs={{0,3},{1,2},{2,1},{3,0},{4,7},{5,6},{6,5},{7,4},{8,11},{9,10},{10,... | collective-permute-start | bytes 393224 | tf_op jit(solution)/shard_map/ppermute | solution.py:520
  63.6 15.6 %collective-permute-start.20 = (bf16[4,2,32,256]{3,2,1,0:T(8,128)(2,1)S(1)}, bf16[4,2,32,256]{3,2,1,0:T(8,128)(2,1)S(1)}, u32[]{:S(2)}, u32[]{:S(2)}) collective-permute-start(bf16[4,2,32,256]{3,2,1,0:T(8,128)(2,1)S(1)} %get-tuple-element.57), channel_id=1, source_target_pairs={{0,4},{1,5},{2,6},{3,7},{4,0},{5,1},{6,2},{7,3},{8,12},{9,13},{10,... | collective-permute-start | bytes 393224 | tf_op jit(solution)/shard_map/ppermute | solution.py:520
  65.8 16.2 %collective-permute-start.24 = (bf16[4,2,32,256]{3,2,1,0:T(8,128)(2,1)S(1)}, bf16[4,2,32,256]{3,2,1,0:T(8,128)(2,1)S(1)}, u32[]{:S(2)}, u32[]{:S(2)}) collective-permute-start(bf16[4,2,32,256]{3,2,1,0:T(8,128)(2,1)S(1)} %get-tuple-element.61), channel_id=1, source_target_pairs={{0,5},{1,4},{2,7},{3,6},{4,1},{5,0},{6,3},{7,2},{8,13},{9,12},{10,... | collective-permute-start | bytes 393224 | tf_op jit(solution)/shard_map/ppermute | solution.py:520
  66.6 19.3 %collective-permute-start.25 = (bf16[4,2,32,256]{3,2,1,0:T(8,128)(2,1)S(1)}, bf16[4,2,32,256]{3,2,1,0:T(8,128)(2,1)S(1)}, u32[]{:S(2)}, u32[]{:S(2)}) collective-permute-start(bf16[4,2,32,256]{3,2,1,0:T(8,128)(2,1)S(1)} %get-tuple-element.62), channel_id=1, source_target_pairs={{0,6},{1,7},{2,4},{3,5},{4,2},{5,3},{6,0},{7,1},{8,14},{9,15},{10,... | collective-permute-start | bytes 393224 | tf_op jit(solution)/shard_map/ppermute | solution.py:520
  68.8 18.9 %collective-permute-start.26 = (bf16[4,2,32,256]{3,2,1,0:T(8,128)(2,1)S(1)}, bf16[4,2,32,256]{3,2,1,0:T(8,128)(2,1)S(1)}, u32[]{:S(2)}, u32[]{:S(2)}) collective-permute-start(bf16[4,2,32,256]{3,2,1,0:T(8,128)(2,1)S(1)} %get-tuple-element.63), channel_id=1, source_target_pairs={{0,7},{1,6},{2,5},{3,4},{4,3},{5,2},{6,1},{7,0},{8,15},{9,14},{10,... | collective-permute-start | bytes 393224 | tf_op jit(solution)/shard_map/ppermute | solution.py:520
  72.1 17.8 %collective-permute-start.16 = (bf16[2,128,512]{2,1,0:T(8,128)(2,1)S(1)}, bf16[2,128,512]{2,1,0:T(8,128)(2,1)S(1)}, u32[]{:S(2)}, u32[]{:S(2)}) collective-permute-start(bf16[2,128,512]{2,1,0:T(8,128)(2,1)S(1)} %get-tuple-element.51), channel_id=1, source_target_pairs={{0,8},{8,0},{16,24},{24,16},{1,9},{9,1},{17,25},{25,17},{2,10},{10... | collective-permute-start | bytes 786440 | tf_op jit(solution)/shard_map/ppermute | solution.py:36
  79.1 10.7 %collective-permute-start.17 = (bf16[2,128,512]{2,1,0:T(8,128)(2,1)S(1)}, bf16[2,128,512]{2,1,0:T(8,128)(2,1)S(1)}, u32[]{:S(2)}, u32[]{:S(2)}) collective-permute-start(bf16[2,128,512]{2,1,0:T(8,128)(2,1)S(1)} %get-tuple-element.52), channel_id=1, source_target_pairs={{8,16},{16,8},{9,17},{17,9},{10,18},{18,10},{11,19},{19,11},{12,20... | collective-permute-start | bytes 786440 | tf_op jit(solution)/shard_map/ppermute | solution.py:36
  88.5 11.4 %collective-permute-start.27 = (bf16[12,2,32,256]{3,2,1,0:T(8,128)(2,1)S(1)}, bf16[12,2,32,256]{3,2,1,0:T(8,128)(2,1)S(1)}, u32[]{:S(2)}, u32[]{:S(2)}) collective-permute-start(bf16[12,2,32,256]{3,2,1,0:T(8,128)(2,1)S(1)} %shard_map.119), channel_id=1, source_target_pairs={{0,8},{8,16},{16,24},{1,9},{9,17},{17,25},{2,10},{10,18},{18,26},{... | collective-permute-start | bytes 1179656 | tf_op jit(solution)/shard_map/ppermute | solution.py:26
  90.1 6.4 %collective-permute-start.18 = (bf16[2,256,128]{2,1,0:T(8,128)(2,1)S(1)}, bf16[2,256,128]{2,1,0:T(8,128)(2,1)S(1)}, u32[]{:S(2)}, u32[]{:S(2)}) collective-permute-start(bf16[2,256,128]{2,1,0:T(8,128)(2,1)S(1)} %get-tuple-element.54), channel_id=1, source_target_pairs={{0,1},{1,0},{2,3},{3,2},{4,5},{5,4},{6,7},{7,6},{8,9},{9,8},{10,11... | collective-permute-start | bytes 393224 | tf_op jit(solution)/shard_map/ppermute | solution.py:36
  91.2 7.7 %collective-permute-start.19 = (bf16[2,256,128]{2,1,0:T(8,128)(2,1)S(1)}, bf16[2,256,128]{2,1,0:T(8,128)(2,1)S(1)}, u32[]{:S(2)}, u32[]{:S(2)}) collective-permute-start(bf16[2,256,128]{2,1,0:T(8,128)(2,1)S(1)} %get-tuple-element.55), channel_id=1, source_target_pairs={{1,2},{2,1},{3,4},{4,3},{5,6},{6,5},{9,10},{10,9},{11,12},{12,11},... | collective-permute-start | bytes 393224 | tf_op jit(solution)/shard_map/ppermute | solution.py:36
  (6 other events, 95.4 us)
